TPU v7x, 32 devices: a whole 2x2x4 slice. The times are simulated.
32 devices in a mesh: groups: 2 (over y), seq: 4 (over z), head: 2 (over x), batch: 2 (over core).
Axes of the slice: x: 2, y: 2, z: 4, core: 2. Of those that a mesh axis runs over, the one named last changes fastest.
Arguments:
- hidden_in: bfloat16 [4, 1024, 8192], P(('groups', 'batch'), 'seq', 'head'), parts along dimension 0, may hold values from -6 to 6
- teacher_query: bfloat16 [4, 1024, 4096], P(('groups', 'batch'), 'seq', 'head'), parts along dimension 0, may hold values from -48 to 48
- teacher_key: bfloat16 [4, 1024, 512], P(('groups', 'batch'), 'seq'), parts along dimension 0, may hold values from -6 to 6
- proj_c: bfloat16 [8192, 4096], P('seq', 'head'), may hold values from -0.00390625 to 0.00390625
- proj_b: bfloat16 [8192, 512], P('seq'), may hold values from -0.0029296875 to 0.0029296875
- proj_step: bfloat16 [8192, 32], P('seq', 'head'), may hold values from -0.0625 to 0.0625
- decay_rate: float32 [32], P('head'), may hold values from 0.0001 to 0.06
Outputs:
- row_loss: float32 [4, 32, 1024], P(('groups', 'batch'), 'head', 'seq'), parts along dimension 0
There are 2 independent parts, one for each index of `groups`. A program takes and returns all parts, laid end to end along the dimension named above; an argument that names none is the same for every part. Nothing has to cross between parts.
All inputs are finite; a program needn't handle non-finite values.
Results may differ from a plain program's by a relative error of at most 0.0015.
Values may be sent and summed in bfloat16 or wider, within the bound.
No kernel may reach another device: no remote copies, remote signals or barrier semaphores. Data moves between devices by JAX's collectives and lax.ppermute only.
A program may use at most 128 MiB of HBM per device.

v0:
```python
import jax
import jax.numpy as jnp
from jax import lax
from jax.sharding import PartitionSpec as P

HEADS = 32
KV_HEADS = 4
HEAD_DIM = 128


NEG_FILL = -1e30


def carried_in(shard, axis, combine, identity):
    length, mine = (lax.axis_size(axis), lax.axis_index(axis))
    everything = lax.all_gather(shard, axis)
    start = jnp.broadcast_to(jnp.asarray(identity, shard.dtype), shard.shape)

    def hop(k, before):
        reached = k < mine
        new = combine(before, everything[k])
        return jnp.where(reached, new, before)

    return lax.fori_loop(0, length, hop, start)


def local(hidden_in, teacher_query, teacher_key, proj_c, proj_b, proj_step, decay_rate):
    seq_count, tok_count, _ = hidden_in.shape
    head_count = proj_step.shape[1]
    per_model_group = HEADS // KV_HEADS
    group_count = max(1, head_count // per_model_group)
    per_group = head_count // group_count
    group_first = lax.axis_index("head") * head_count // per_model_group
    width_b = group_count * HEAD_DIM
    local_b = lax.dynamic_slice_in_dim(proj_b, group_first * HEAD_DIM, width_b, 1)
    local_key = lax.dynamic_slice_in_dim(teacher_key, group_first * HEAD_DIM, width_b, 2)
    features = lax.all_gather(hidden_in, "head", axis=2, tiled=True)
    token_rows = features.reshape(seq_count * tok_count, features.shape[2])
    pieces = (
        lax.all_gather(proj_c, "seq", axis=0, tiled=True),
        lax.all_gather(local_b, "seq", axis=0, tiled=True),
        lax.all_gather(proj_step, "seq", axis=0, tiled=True),
    )
    readout, inputs, step_raw = tuple(
        (jnp.dot(token_rows, one_piece, preferred_element_type=jnp.float32) for one_piece in pieces)
    )
    query_c = readout.astype(jnp.bfloat16).reshape(
        seq_count, tok_count, group_count, per_group, HEAD_DIM
    )
    key_b = inputs.astype(jnp.bfloat16).reshape(seq_count, tok_count, width_b)
    step_size = jax.nn.softplus(step_raw).reshape(seq_count, tok_count, head_count)
    local_cum = jnp.cumsum(-decay_rate[None, None, :] * step_size, axis=1)
    prefix = carried_in(
        local_cum[:, -1, :],
        "seq",
        lambda earlier, later: earlier + later,
        jnp.zeros((seq_count, head_count), jnp.float32),
    )
    cumulated = prefix[:, None, :] + local_cum
    all_steps, all_cumul = (
        lax.all_gather(step_size, "seq", axis=1, tiled=True),
        lax.all_gather(cumulated, "seq", axis=1, tiled=True),
    )
    query_t = teacher_query.reshape(seq_count, tok_count, group_count, per_group, HEAD_DIM)
    first_row = lax.axis_index("seq") * tok_count
    query_pos = first_row + jnp.arange(tok_count, dtype=jnp.int32)
    last_query = first_row + tok_count - 1
    cum_query = jnp.transpose(
        cumulated.reshape(seq_count, tok_count, group_count, per_group), (0, 2, 3, 1)
    )[..., None]

    def by_head(values, block_rows):
        shaped = values.reshape(seq_count, block_rows, group_count, per_group)
        return jnp.transpose(shaped, (0, 2, 3, 1))[:, :, :, None, :]

    def tile_update(totals_in, key_tile, input_tile, key_start):
        block_rows = key_tile.shape[1]
        keys_here = key_tile.reshape(seq_count, block_rows, group_count, HEAD_DIM)
        inputs_here = input_tile.reshape(seq_count, block_rows, group_count, HEAD_DIM)
        maxima, normal, squares, crossed, student = totals_in
        scores = jnp.einsum(
            "sqgpn,skgn->sgpqk", query_t, keys_here, preferred_element_type=jnp.float32
        ) * HEAD_DIM ** (-0.5)
        key_pos = key_start + jnp.arange(block_rows, dtype=jnp.int32)
        allowed = key_pos[None, :] <= query_pos[:, None]
        new_max = jnp.maximum(maxima, jnp.max(jnp.where(allowed, scores, NEG_FILL), axis=-1))
        weights = jnp.exp(jnp.where(allowed, scores - new_max[..., None], -jnp.inf))
        rescale = jnp.exp(maxima - new_max)
        steps_k = by_head(lax.dynamic_slice_in_dim(all_steps, key_start, block_rows, 1), block_rows)
        cum_k = by_head(lax.dynamic_slice_in_dim(all_cumul, key_start, block_rows, 1), block_rows)
        log_gap = jnp.where(allowed, cum_query - cum_k, -jnp.inf)
        inner_prod = jnp.einsum(
            "sqgpn,skgn->sgpqk", query_c, inputs_here, preferred_element_type=jnp.float32
        )
        mixer_tile = inner_prod * steps_k * jnp.exp(log_gap)
        return (
            new_max,
            normal * rescale + jnp.sum(weights, axis=-1),
            squares * rescale * rescale + jnp.sum(weights * weights, axis=-1),
            crossed * rescale + jnp.sum(weights * mixer_tile, axis=-1),
            student + jnp.sum(mixer_tile * mixer_tile, axis=-1),
        )

    shape_rows = (seq_count, group_count, per_group, tok_count)
    starting_rows = (
        jnp.full(shape_rows, NEG_FILL, jnp.float32),
        jnp.zeros(shape_rows, jnp.float32),
        jnp.zeros(shape_rows, jnp.float32),
        jnp.zeros(shape_rows, jnp.float32),
        jnp.zeros(shape_rows, jnp.float32),
    )
    pieces = (
        lax.all_gather(local_key, "seq", axis=1, tiled=True),
        lax.all_gather(key_b, "seq", axis=1, tiled=True),
    )
    key_span = pieces[0].shape[1]
    block_rows = 512

    def one_block(block_index, running):
        key_start = block_index * block_rows
        key_tile = lax.dynamic_slice_in_dim(pieces[0], block_index * block_rows, block_rows, 1)
        input_tile = lax.dynamic_slice_in_dim(pieces[1], block_index * block_rows, block_rows, 1)
        return lax.cond(
            key_start > last_query,
            lambda current: current,
            lambda current: tile_update(current, key_tile, input_tile, key_start),
            running,
        )

    maxima, normal, squares, crossed, student = lax.fori_loop(
        0, key_span // block_rows, one_block, starting_rows
    )
    row_loss = squares / (normal * normal) - 2.0 * crossed / normal + student
    return row_loss.reshape(seq_count, head_count, tok_count)


def solution(mesh):
    in_specs = (
        P(("groups", "batch"), "seq", "head"),
        P(("groups", "batch"), "seq", "head"),
        P(("groups", "batch"), "seq", None),
        P("seq", "head"),
        P("seq", None),
        P("seq", "head"),
        P("head"),
    )
    out_specs = P(("groups", "batch"), "head", "seq")
    return jax.shard_map(local, mesh=mesh, in_specs=in_specs, out_specs=out_specs, check_vma=False)
```

profile of v0, /device:TPU:24, one launch (start us, length us, event | category | flops | bytes accessed | tf_op | source)
XLA Modules:
  0.0 752.1 jit_solution(7828328314470015174)
XLA Ops:
  6.5 0.0 copy-start
  6.5 0.0 copy-start.5
  6.5 0.0 copy-start.2
  6.5 0.0 all-gather.8.cloned.1.call-start
  6.5 0.7 all-gather.8.cloned.1.call-update
  7.3 0.0 copy-start.3
  7.3 0.0 all-gather.6.cloned.1.call-start
  7.3 0.8 copy-done
  8.1 1.0 constant_dynamic-slice_fusion.2
  9.2 0.0 copy-start.4
  9.2 0.0 all-gather.6.cloned.1.call-update
  9.2 0.0 all-gather.10.cloned.1.call-start
  9.2 0.7 all-gather.10.cloned.1.call-update
  9.9 0.0 copy-done.5
  10.0 0.2 copy-done.4
  10.1 0.1 copy.42
  10.2 0.0 copy-done.2
  10.2 0.5 copy.27
  10.8 0.7 copy.32
  11.4 0.0 copy-done.3
  11.5 14.6 %all_gather.32 = bf16[8192,16]{0,1:T(8,128)(2,1)S(1)} all-gather(bf16[2048,16]{0,1:T(8,128)(2,1)S(1)} %copy-done.3), channel_id=1, replica_groups=mesh['groups'=2,'seq'=4,'head'=2,'batch'=2] {'seq'}, dimensions={0}, use_global_device_ids=true | all-gather | bytes 327680 | tf_op jit(solution)/shard_map/all_gather | solution.py:42
  26.0 15.0 %all_gather.27 = bf16[1,1024,256]{1,2,0:T(8,128)(2,1)S(1)} all-gather(bf16[1,256,256]{1,2,0:T(8,128)(2,1)S(1)} %copy.42), channel_id=1, replica_groups=mesh['groups'=2,'seq'=4,'head'=2,'batch'=2] {'seq'}, dimensions={1}, use_global_device_ids=true | all-gather | bytes 655360 | tf_op jit(solution)/shard_map/all_gather | solution.py:113
  41.0 25.6 %all-gather.8.cloned.1.call-done = bf16[1,256,8192]{2,1,0:T(8,128)(2,1)} async-done(((bf16[1,256,4096]{2,1,0:T(8,128)(2,1)}), bf16[1,256,8192]{2,1,0:T(8,128)(2,1)}) %all-gather.8.cloned.1.call-update) | async-done | bytes 4194320 | tf_op jit(solution)/shard_map/all_gather | solution.py:37
  66.7 3.4 compare_select_fusion
  70.1 0.1 copy_bitcast_fusion
  70.1 0.6 reduce-window.6
  70.7 0.2 slice_reduce_fusion
  70.9 0.1 copy.30
  71.0 0.1 broadcast.83
  71.1 0.1 slice.13
  71.2 0.1 copy.31
  71.3 7.3 all_gather.34
  78.6 0.1 while.37
  78.7 0.1 broadcast_add_fusion.1
  78.8 12.2 %all_gather.35 = f32[1,1024,16]{1,0,2:T(1,128)S(1)} all-gather(f32[1,256,16]{1,0,2:T(1,128)S(1)} %broadcast_add_fusion.1), channel_id=1, replica_groups=mesh['groups'=2,'seq'=4,'head'=2,'batch'=2] {'seq'}, dimensions={1}, use_global_device_ids=true | all-gather | bytes 81920 | tf_op jit(solution)/shard_map/all_gather | solution.py:62
  91.0 13.7 %all-gather.1 = f32[1024,16]{0,1:T(8,128)S(1)} all-gather(f32[256,16]{0,1:T(8,128)S(1)} %compare_select_fusion), channel_id=3, replica_groups=mesh['groups'=2,'seq'=4,'head'=2,'batch'=2] {'seq'}, dimensions={0}, use_global_device_ids=true | all-gather | bytes 81920 | tf_op jit(solution)/shard_map/all_gather | solution.py:61
  104.7 43.6 %all-gather.6.cloned.1.call-done = bf16[8192,256]{1,0:T(8,128)(2,1)} async-done(((bf16[2048,256]{1,0:T(8,128)(2,1)}), bf16[8192,256]{1,0:T(8,128)(2,1)}) %all-gather.6.cloned.1.call-update) | async-done | bytes 4194320 | tf_op jit(solution)/shard_map/all_gather | solution.py:41
  148.3 4.8 fusion.27
  153.0 15.5 %all-gather = bf16[1024,256]{0,1:T(8,128)(2,1)S(1)} all-gather(bf16[256,256]{0,1:T(8,128)(2,1)S(1)} %fusion.27), channel_id=2, replica_groups=mesh['groups'=2,'seq'=4,'head'=2,'batch'=2] {'seq'}, dimensions={0}, use_global_device_ids=true | all-gather | bytes 655360 | tf_op jit(solution)/shard_map/all_gather | solution.py:114
  168.5 541.0 %all-gather.10.cloned.1.call-done = bf16[8192,2048]{1,0:T(8,128)(2,1)} async-done(((bf16[2048,2048]{1,0:T(8,128)(2,1)}), bf16[8192,2048]{1,0:T(8,128)(2,1)}) %all-gather.10.cloned.1.call-update) | async-done | bytes 33554448 | tf_op jit(solution)/shard_map/all_gather | solution.py:40
  709.5 16.2 %fusion.21 = bf16[32,8,16,128]{3,1,2,0:T(8,128)(2,1)S(1)} fusion(bf16[8192,2048]{1,0:T(8,128)(2,1)} %all-gather.10.cloned.1.call-done, bf16[1,256,8192]{2,1,0:T(8,128)(2,1)} %all-gather.8.cloned.1.call-done), kind=kOutput, calls=%fused_computation.39 | convolution fusion | flops 8590458880 | bytes 38797312 | tf_op jit(solution)/shard_map/dot_general | solution.py:45
  725.8 0.2 copy.44
  726.0 0.3 copy.33
  726.3 17.6 %while.36 = (s32[]{:T(128)}, f32[1,2,8,256]{3,2,1,0:T(8,128)S(1)}, f32[1,2,8,256]{3,2,1,0:T(8,128)S(1)}, f32[1,2,8,256]{3,2,1,0:T(8,128)S(1)}, f32[1,2,8,256]{3,...) while((s32[]{:T(128)}, f32[1,2,8,256]{3,2,1,0:T(8,128)S(1)}, ...), condition=%wide.region_12.13_spmd.clone, body=%wide.region_4.12_spmd.clone.sunk | while | flops 1109545728 | bytes 21471664 | solution.py:130
  726.4 8.7 %conditional.3 = (f32[1,2,8,256]{3,2,1,0:T(8,128)S(1)}, f32[1,2,8,256]{3,2,1,0:T(8,128)S(1)}, f32[1,2,8,256]{3,2,1,0:T(8,128)S(1)}, f32[1,2,8,256]{3,2,1,0:T(8,128)S(1)}, f32[1,2,8,256]{3,2,1,0:T(8,128)S(1)}) conditional(s32[]{:T(128)} %convert_element_type.27, (s32[]{:T(128)}, s32[]{:T(128)}, bf16[1,1024,256]{1,2,0:T(8,128)(2,1)S(1)}, ...), branch_computations={%region_5.10_spmd, %region_11.11_spmd} | conditional | flops 1109545728 | bytes 21437530 | solution.py:123
  726.5 0.1 broadcast_compare_fusion
  726.6 1.5 fusion.3
  728.2 6.9 multiply_reduce_fusion
  735.2 8.7 %conditional.3 = (f32[1,2,8,256]{3,2,1,0:T(8,128)S(1)}, f32[1,2,8,256]{3,2,1,0:T(8,128)S(1)}, f32[1,2,8,256]{3,2,1,0:T(8,128)S(1)}, f32[1,2,8,256]{3,2,1,0:T(8,128)S(1)}, f32[1,2,8,256]{3,2,1,0:T(8,128)S(1)}) conditional(s32[]{:T(128)} %convert_element_type.27, (s32[]{:T(128)}, s32[]{:T(128)}, bf16[1,1024,256]{1,2,0:T(8,128)(2,1)S(1)}, ...), branch_computations={%region_5.10_spmd, %region_11.11_spmd} | conditional | flops 1109545728 | bytes 21437530 | solution.py:123
  735.3 0.1 broadcast_compare_fusion
  735.4 1.5 fusion.3
  737.0 6.9 multiply_reduce_fusion
  743.9 0.0 copy-start.1
  743.9 0.6 add_bitcast_fusion
  744.6 1.0 copy-done.1
  (36 shorter events, 0.4 us)
Async XLA Ops:
  6.5 1.6 copy-start
  6.5 3.4 copy-start.5
  6.5 3.7 copy-start.2
  6.5 60.1 %all-gather.8.cloned.1.call-start = ((), (), s32[]{:S(2)}) async-start(), calls=%async_computation.1 | async-start | bytes 6291456 | tf_op jit(solution)/shard_map/all_gather | solution.py:37
  7.3 4.2 copy-start.3
  7.3 141.0 %all-gather.6.cloned.1.call-start = ((), (), s32[]{:S(2)}) async-start(), calls=%async_computation | async-start | bytes 5242880 | tf_op jit(solution)/shard_map/all_gather | solution.py:41
  9.2 0.9 copy-start.4
  9.2 700.3 %all-gather.10.cloned.1.call-start = ((), (), s32[]{:S(2)}) async-start(), calls=%async_computation.2 | async-start | bytes 41943040 | tf_op jit(solution)/shard_map/all_gather | solution.py:40
  743.9 1.6 copy-start.1
Sparse Core Ops, SparseCore 0:
  8.9 57.7 all-gather.7
  68.2 79.9 all-gather.5
  149.8 559.6 all-gather.9
where the time goes:
time: 754 us; the launch traced here: 752 us
  waiting for transfers between devices  612 us (81%)
  blocking collectives  78.2 us (10%)
  matrix products  41.2 us (5%)
  between operations  13.4 us (2%)
    all_gather x1, waiting for transfers between devices, local(): lax.all_gather(proj_c, 'seq', axis=0, tiled=True)  541 us
    all_gather x1, waiting for transfers between devices, local(): lax.all_gather(local_b, 'seq', axis=0, tiled=True)  43.6 us
    all_gather x1, waiting for transfers between devices, local(): features = lax.all_gather(hidden_in, 'head', axis=2, tiled=True)  25.6 us
    dot_general x3, matrix products, local(): jnp.dot(token_rows, one_piece, preferred_element_type=jnp.float32)  24.4 us
    all_gather x1, blocking collectives, local(): lax.all_gather(key_b, 'seq', axis=1, tiled=True)  15.5 us
  transfers between devices with their start and end apart: 3, of which 3 were waited for; matrix products, arithmetic and copies ran while one was open for 2% of the time, Pallas kernels for 0%

commit v1 on v0

v1 whole, which is shorter than its diff:
```python
import functools
import math

import jax
import jax.numpy as jnp
from jax import lax
from jax.experimental import pallas as pl
from jax.experimental.pallas import tpu as pltpu
from jax.sharding import PartitionSpec as P

HEADS = 32
KV_HEADS = 4
HEAD_DIM = 128
LOG2E = math.log2(math.e)
BF16 = jnp.bfloat16
F32 = jnp.float32
VMEM_LIMIT = 48 * 1024 * 1024

NT = (((1,), (1,)), ((), ()))


def xor_permute(value, axis, offset):
    size = lax.axis_size(axis)
    return lax.ppermute(value, axis, [(i, i ^ offset) for i in range(size)])


def whole(shape):
    return pl.BlockSpec(shape, lambda *_: (0,) * len(shape))


def columns(rows, width, index):
    return pl.BlockSpec((rows, width), lambda *_: (0, index))


def smem():
    return pl.BlockSpec(memory_space=pltpu.SMEM)


def call(kernel, args, in_specs, out_shapes, name, scratch=()):
    return pl.pallas_call(
        kernel,
        grid=(1,),
        in_specs=in_specs,
        out_specs=tuple(whole(s.shape) for s in out_shapes),
        out_shape=tuple(out_shapes),
        scratch_shapes=list(scratch),
        compiler_params=pltpu.CompilerParams(vmem_limit_bytes=VMEM_LIMIT),
        name=name,
    )(*args)


def product(place, act, own, pieces, model):
    block, quarter = place[0], place[1]
    rows = own.shape[0]
    total = jnp.dot(
        act[:, pl.ds(pl.multiple_of(block * rows, rows), rows)], own[...], preferred_element_type=F32
    )
    for piece, (step, turn) in zip(pieces, model):
        part = piece.shape[0]
        start = (block ^ step) * rows + (quarter ^ turn) * part
        total += jnp.dot(
            act[:, pl.ds(pl.multiple_of(start, part), part)], piece[...], preferred_element_type=F32
        )
    return total


def partial_kernel(model, place, act, own, *rest):
    pieces, out = rest[:-1], rest[-1]
    out[...] = product(place, act, own, pieces, model).astype(out.dtype)


def extra_kernel(model, step_model, place, act_own, act_other, own, *rest):
    n = len(model)
    pieces = rest[:n]
    step_pieces = rest[n : n + len(step_model)]
    full, rounded, raw = rest[-3:]
    tokens = act_own.shape[0]
    for at, act in enumerate((act_own, act_other)):
        here = slice(at * tokens, (at + 1) * tokens)
        value = product(place, act, own, pieces, model)
        full[here, :] = value
        rounded[here, :] = value.astype(BF16)
        total = None
        for piece, step in zip(step_pieces, step_model):
            rows = piece.shape[1]
            start = pl.multiple_of((place[0] ^ step) * rows, rows)
            part = lax.dot_general(piece[...], act[:, pl.ds(start, rows)], NT, preferred_element_type=F32)
            total = part if total is None else total + part
        raw[:, here] = total


def decay_kernel(offsets, place, raw, rate, factor, log_row, log_col, gain_col):
    mine = place[2]
    heads, tokens = raw.shape[1], raw.shape[2]
    lane = lax.broadcasted_iota(jnp.int32, (heads, tokens), 1)
    steps, logs, totals = [], [], []
    for at in range(len(offsets)):
        value = raw[at]
        step = jnp.maximum(value, 0.0) + jnp.log1p(jnp.exp(-jnp.abs(value)))
        log = step * (-LOG2E * rate[...])
        shift = 1
        while shift < tokens:
            log = log + jnp.where(lane >= shift, pltpu.roll(log, shift, 1), 0.0)
            shift *= 2
        steps.append(step)
        logs.append(log)
        totals.append(log[:, tokens - 1 :])
    for at, offset in enumerate(offsets):
        here = slice(at * tokens, (at + 1) * tokens)
        if at == 0:
            factor[:, here] = steps[0]
            continue
        between = jnp.zeros_like(totals[0])
        first = mine ^ offset
        for other, distance in enumerate(offsets):
            block = mine ^ distance
            inside = jnp.logical_and(block > first, block < mine)
            between += jnp.where(inside, totals[other], 0.0)
        factor[:, here] = steps[at] * jnp.exp2(totals[at] - logs[at] + between)
    log_row[...] = logs[0]
    wide = jnp.concatenate([logs[0], jnp.zeros((128 - heads, tokens), F32)], axis=0)
    turned = wide.T
    log_col[...] = turned
    gain_col[...] = jnp.exp2(turned)


def causal_of(tokens):
    row = lax.broadcasted_iota(jnp.int32, (tokens, tokens), 0)
    col = lax.broadcasted_iota(jnp.int32, (tokens, tokens), 1)
    return col <= row


def folded(combine, value):
    parts = [value[:, i : i + 128] for i in range(0, value.shape[1], 128)]
    return functools.reduce(combine, parts)


SCALE = LOG2E * HEAD_DIM ** -0.5


def teacher_kernel(offsets, place, query, keys, norm, scores, top, mass):
    tokens = query.shape[0]
    mine = place[2]
    own = lax.dot_general(query[...], keys[pl.ds(0, tokens), :], NT, preferred_element_type=F32) * SCALE
    own = jnp.where(causal_of(tokens), own, -jnp.inf)
    scores[0] = own
    top[...] = folded(jnp.maximum, own)
    for at in range(1, len(offsets)):

        @pl.when((mine ^ offsets[at]) < mine)
        def _(at=at):
            value = lax.dot_general(
                query[...], keys[pl.ds(at * tokens, tokens), :], NT, preferred_element_type=F32
            ) * SCALE
            scores[at] = value
            top[...] = jnp.maximum(top[...], folded(jnp.maximum, value))

    peak = jnp.max(top[...], axis=1, keepdims=True)
    mass[...] = folded(jnp.add, jnp.exp2(scores[0] - peak))
    for at in range(1, len(offsets)):

        @pl.when((mine ^ offsets[at]) < mine)
        def _(at=at):
            mass[...] += folded(jnp.add, jnp.exp2(scores[at] - peak))

    total = jnp.sum(mass[...], axis=1, keepdims=True)
    norm[0] = jnp.broadcast_to(peak + jnp.log2(total), (tokens, 128))


def loss_kernel(
    offsets, first, heads, place, query, kept, came, keys, inputs, norm, factor, log_row, log_col, gain_col, out, sums
):
    tokens = query.shape[0]
    mine = place[2]
    causal = causal_of(tokens)
    for i in range(heads):
        head = first + i
        cols = slice(i * HEAD_DIM, (i + 1) * HEAD_DIM)
        asked = query[:, cols]
        read = (kept[:, cols] + came[:, cols].astype(F32)).astype(BF16)
        lse = norm[i]
        wide = tokens // 128
        lse_wide = jnp.concatenate([lse] * wide, axis=1)

        def pair(at):
            rows = pl.ds(at * tokens, tokens)
            score = lax.dot_general(asked, keys[rows, :], NT, preferred_element_type=F32) * SCALE
            inner = lax.dot_general(read, inputs[rows, :], NT, preferred_element_type=F32)
            return jnp.exp2(score - lse_wide), inner * factor[head : head + 1, at * tokens : (at + 1) * tokens]

        prob, inner = pair(0)
        gap = log_col[:, head : head + 1] - log_row[head : head + 1, :]
        diff = jnp.where(causal, prob - inner * jnp.exp2(gap), 0.0)
        sums[...] = folded(jnp.add, diff * diff)
        gain = gain_col[:, head : head + 1]
        for at in range(1, len(offsets)):

            @pl.when((mine ^ offsets[at]) < mine)
            def _(at=at):
                prob, inner = pair(at)
                diff = prob - inner * gain
                sums[...] += folded(jnp.add, diff * diff)

        out[i] = jnp.sum(sums[...].T, axis=0, keepdims=True)


def gather_half(value, half):
    return [value] + [xor_permute(value, "seq", d) for d in range(1, half)]


def activations(hidden, half):
    tokens = hidden.shape[0]
    seq, heads = lax.axis_size("seq"), lax.axis_size("head")
    z, x = lax.axis_index("seq"), lax.axis_index("head")
    side = z // half
    if heads == 2:
        cut = tokens // 2
        spots = [(i, j) for i in range(seq) for j in range(2)]
        flat = lambda i, j: i * 2 + j
        both = ("seq", "head")
        level = side == x
        even = [s for s in spots if s[0] // half == s[1]]
        odd = [s for s in spots if s[0] // half != s[1]]
        over = lambda group: [(flat(i, j), flat(i ^ half, j)) for i, j in group]
        low, high = hidden[:cut], hidden[cut:]
        direct = lax.ppermute(low, both, over(odd))
        swapped = xor_permute(high, "head", 1)
        relayed = lax.ppermute(swapped, both, over(even))
        moved = lax.ppermute(low, both, [(flat(i, j), flat(i, 1 - j)) for i, j in even])
        mine = jnp.where(level, hidden, jnp.concatenate([moved, swapped], axis=0))
        first = jnp.where(level, direct, relayed)
        second = xor_permute(first, "head", 1)
        other = jnp.concatenate([jnp.where(level, first, second), jnp.where(level, second, first)], axis=0)
        return mine, other
    full = lax.all_gather(hidden, "head", axis=1, tiled=True)
    width = full.shape[1] // 2
    share = tokens // heads
    mine = lax.dynamic_slice_in_dim(full, side * width, width, 1)
    sent = lax.dynamic_slice(full, (x * share, (1 - side) * width), (share, width))
    came = xor_permute(sent, "seq", half)
    return mine, lax.all_gather(came, "head", axis=0, tiled=True)


def local(hidden_in, teacher_query, teacher_key, proj_c, proj_b, proj_step, decay_rate):
    _, tokens, _ = hidden_in.shape
    rows, width = proj_c.shape
    head_count = proj_step.shape[1]
    seq = lax.axis_size("seq")
    half = seq // 2
    copies_y, copies_c = lax.axis_size("groups"), lax.axis_size("batch")
    copies = copies_y * copies_c
    z, x = lax.axis_index("seq"), lax.axis_index("head")
    quarter = lax.axis_index("groups") * copies_c + lax.axis_index("batch")
    place = jnp.stack([z % half, quarter, z]).astype(jnp.int32)
    per_model_group = HEADS // KV_HEADS
    group_count = max(1, head_count // per_model_group)
    per_group = head_count // group_count
    group_first = x * head_count // per_model_group
    width_b = group_count * HEAD_DIM
    local_b = lax.dynamic_slice_in_dim(proj_b, group_first * HEAD_DIM, width_b, 1)
    local_key = lax.dynamic_slice_in_dim(teacher_key[0], group_first * HEAD_DIM, width_b, 1)
    offsets = [0, half]
    for d in range(1, half):
        offsets += [d, d ^ half]
    padded = max(16, head_count)

    act_own, act_other = activations(hidden_in[0], half)

    key_pair = jnp.concatenate([local_key, xor_permute(local_key, "seq", half)], axis=0)
    keys = jnp.concatenate(gather_half(key_pair, half), axis=0)

    chunk = max(HEAD_DIM, width // 4)
    count = width // chunk
    part = rows // copies

    def spread(piece):
        got = [piece]
        d = 1
        while d < copies_y:
            got += [xor_permute(g, "groups", d) for g in got]
            d *= 2
        d = 1
        while d < copies_c:
            got += [xor_permute(g, "batch", d) for g in got]
            d *= 2
        return got

    turns = [0]
    d = 1
    while d < copies_y:
        turns += [t ^ (d * copies_c) for t in turns]
        d *= 2
    d = 1
    while d < copies_c:
        turns += [t ^ d for t in turns]
        d *= 2
    model = [(d, t) for d in range(1, half) for t in turns]

    def weights(j):
        piece = lax.dynamic_slice(proj_c, (quarter * part, j * chunk), (part, chunk))
        if j == 0:
            extra = lax.dynamic_slice(local_b, (quarter * part, 0), (part, width_b))
            piece = jnp.concatenate([piece, extra], axis=1)
        return [g for d in range(1, half) for g in spread(xor_permute(piece, "seq", d))]

    pieces = [weights(j) for j in range(count)]
    step_t = jnp.pad(proj_step.T, ((0, padded - head_count), (0, 0)))
    step_pieces = gather_half(step_t, half)

    def partial(act, j, dtype):
        specs = [smem(), whole(act.shape), columns(rows, chunk, j)] + [columns(part, chunk, 0)] * len(model)
        return call(
            functools.partial(partial_kernel, model),
            (place, act, proj_c, *pieces[j]),
            specs,
            [jax.ShapeDtypeStruct((tokens, chunk), dtype)],
            "partial",
        )[0]

    extra_out = [
        jax.ShapeDtypeStruct((2 * tokens, width_b), F32),
        jax.ShapeDtypeStruct((2 * tokens, width_b), BF16),
        jax.ShapeDtypeStruct((padded, 2 * tokens), F32),
    ]
    extra_cols = [g[:, chunk:] for g in pieces[0]]
    full, rounded, raw = call(
        functools.partial(extra_kernel, model, list(range(half))),
        (place, act_own, act_other, local_b, *extra_cols, *step_pieces),
        [smem(), whole(act_own.shape), whole(act_other.shape), whole(local_b.shape)]
        + [whole((part, width_b))] * len(model)
        + [whole(step_t.shape)] * half,
        extra_out,
        "extra",
    )
    came = xor_permute(rounded, "seq", half).astype(F32)
    came_raw = xor_permute(raw, "seq", half)
    inputs_pair = (full + jnp.concatenate([came[tokens:], came[:tokens]], axis=0)).astype(BF16)
    raw_pair = raw + jnp.concatenate([came_raw[:, tokens:], came_raw[:, :tokens]], axis=1)
    inputs = jnp.concatenate(gather_half(inputs_pair, half), axis=0)
    raw_all = jnp.stack([r[:, i * tokens : (i + 1) * tokens] for r in gather_half(raw_pair, half) for i in range(2)])

    sent = [partial(act_other, j, BF16) for j in range(count)]
    arrived = [xor_permute(s, "seq", half) for s in sent]
    kept = [partial(act_own, j, F32) for j in range(count)]

    span = seq * tokens
    rate = jnp.pad(decay_rate, (0, padded - head_count))[:, None]
    factor, log_row, log_col, gain_col = call(
        functools.partial(decay_kernel, offsets),
        (place, raw_all, rate),
        [smem(), whole(raw_all.shape), whole(rate.shape)],
        [
            jax.ShapeDtypeStruct((padded, span), F32),
            jax.ShapeDtypeStruct((padded, tokens), F32),
            jax.ShapeDtypeStruct((tokens, 128), F32),
            jax.ShapeDtypeStruct((tokens, 128), F32),
        ],
        "decay",
    )
    query = teacher_query[0]
    norm = pl.pallas_call(
        functools.partial(teacher_kernel, offsets),
        grid=(head_count,),
        in_specs=[
            smem(),
            pl.BlockSpec((tokens, HEAD_DIM), lambda h: (0, h)),
            pl.BlockSpec((span, HEAD_DIM), lambda h: (0, h // per_group)),
        ],
        out_specs=pl.BlockSpec((1, tokens, 128), lambda h: (h, 0, 0)),
        out_shape=jax.ShapeDtypeStruct((head_count, tokens, 128), F32),
        scratch_shapes=[
            pltpu.VMEM((seq, tokens, tokens), F32),
            pltpu.VMEM((tokens, 128), F32),
            pltpu.VMEM((tokens, 128), F32),
        ],
        compiler_params=pltpu.CompilerParams(vmem_limit_bytes=VMEM_LIMIT),
        name="teacher",
    )(place, query, keys)

    heads = chunk // HEAD_DIM
    losses = []
    for j in range(count):
        group = j * heads // per_group
        losses.append(
            call(
                functools.partial(loss_kernel, offsets, j * heads, heads),
                (place, query, kept[j], arrived[j], keys, inputs, norm, factor, log_row, log_col, gain_col),
                [
                    smem(),
                    columns(tokens, chunk, j),
                    whole((tokens, chunk)),
                    whole((tokens, chunk)),
                    columns(span, HEAD_DIM, group),
                    columns(span, HEAD_DIM, group),
                    pl.BlockSpec((heads, tokens, 128), lambda *_, j=j: (j, 0, 0)),
                    whole(factor.shape),
                    whole(log_row.shape),
                    whole(log_col.shape),
                    whole(gain_col.shape),
                ],
                [jax.ShapeDtypeStruct((heads, 1, tokens), F32)],
                "loss",
                [pltpu.VMEM((tokens, 128), F32)],
            )[0]
        )
    return jnp.concatenate(losses, axis=0).reshape(1, head_count, tokens)


def solution(mesh):
    in_specs = (
        P(("groups", "batch"), "seq", "head"),
        P(("groups", "batch"), "seq", "head"),
        P(("groups", "batch"), "seq", None),
        P("seq", "head"),
        P("seq", None),
        P("seq", "head"),
        P("head"),
    )
    out_specs = P(("groups", "batch"), "head", "seq")
    return jax.shard_map(local, mesh=mesh, in_specs=in_specs, out_specs=out_specs, check_vma=False)
```

time: 754 us -> 273 us (0.36)
  waiting for transfers between devices: 612 us -> 138 us
  blocking collectives: 78.2 us -> 0 us
  Pallas kernels: 0 us -> 67.5 us
  starting transfers between devices: 0.08 us -> 48.2 us
  matrix products: 41.2 us -> 0 us
  between operations: 13.4 us -> 0.64 us
    all_gather x3 -> x0, waiting for transfers between devices: 610 us -> none  [the longest x1 541 us: local(): lax.all_gather(proj_c, 'seq', axis=0, tiled=True)]
    ppermute x0 -> x32, waiting for transfers between devices: none -> 138 us  [the longest x29 116 us: xor_permute(): return lax.ppermute(value, axis, [(i, i ^ offset) for i in range(size)])]
    all_gather x6 -> x0, blocking collectives: 78.2 us -> none  [the longest x1 15.5 us: local(): lax.all_gather(key_b, 'seq', axis=1, tiled=True)]
    pallas_call x0 -> x15, Pallas kernels: none -> 67.5 us  [the longest x14 48.1 us: call(): pl.pallas_call(kernel, grid=(1,), in_specs=in_specs, out_specs=tuple((who...]
    ppermute x0 -> x32, starting transfers between devices: none -> 48.2 us  [the longest x29 42.4 us: xor_permute(): return lax.ppermute(value, axis, [(i, i ^ offset) for i in range(size)])]
    dot_general x7 -> x0, matrix products: 41.2 us -> none  [the longest x3 24.4 us: local(): jnp.dot(token_rows, one_piece, preferred_element_type=jnp.float32)]
  transfers between devices with their start and end apart: 3 -> 32, of which waited for: 3 -> 13; matrix products, arithmetic and copies ran while one was open for 2% -> 5% of each run, Pallas kernels for 0% -> 23%
where the time goes in v1:
time: 273 us; the launch traced here: 272 us
  waiting for transfers between devices  138 us (51%)
  Pallas kernels  67.5 us (25%)
  starting transfers between devices  48.2 us (18%)
  local copies, waits for them, and re-layouts  10.9 us (4%)
  other arithmetic  7.3 us (3%)
    ppermute x29, waiting for transfers between devices, xor_permute(): return lax.ppermute(value, axis, [(i, i ^ offset) for i in range(size)])  116 us
    pallas_call x14, Pallas kernels, call(): pl.pallas_call(kernel, grid=(1,), in_specs=in_specs, out_specs=tuple((who...  48.1 us
    ppermute x29, starting transfers between devices, xor_permute(): return lax.ppermute(value, axis, [(i, i ^ offset) for i in range(size)])  42.4 us
    pallas_call x1, Pallas kernels, local(): pl.pallas_call(functools.partial(teacher_kernel, offsets), grid=(head_cou...  19.4 us
    ppermute x1, waiting for transfers between devices, activations(): relayed = lax.ppermute(swapped, both, over(even))  18.7 us
  transfers between devices with their start and end apart: 32, of which 13 were waited for; matrix products, arithmetic and copies ran while one was open for 5% of the time, Pallas kernels for 23%

profile of v1, /device:TPU:24, one launch (start us, length us, event | category | flops | bytes accessed | tf_op | source)
XLA Modules:
  0.0 272.4 jit_solution(10985282409282217987)
XLA Ops:
  0.0 3.1 %slice_bitcast_fusion.1 = (bf16[128,4096]{1,0:T(8,128)(2,1)}, bf16[128,4096]{1,0:T(8,128)(2,1)}) fusion(bf16[1,256,4096]{2,1,0:T(8,128)(2,1)} %param.7), kind=kLoop, calls=%fused_computation.3 | loop fusion | bytes 4194304 | tf_op jit(solution)/shard_map/slice | solution.py:225
  3.1 1.5 collective-permute-start.1
  4.6 1.2 dynamic_slice.24
  5.8 2.7 constant_dynamic-slice_fusion.4
  8.6 0.5 collective-permute-start.2
  9.1 3.2 %collective-permute-start.6 = (bf16[128,4096]{1,0:T(8,128)(2,1)}, bf16[128,4096]{1,0:T(8,128)(2,1)}, u32[]{:S(2)}, u32[]{:S(2)}) collective-permute-start(bf16[128,4096]{1,0:T(8,128)(2,1)} %get-tuple-element.25), channel_id=1, source_target_pairs={{2,10},{6,14},{8,0},{12,4},{3,11},{7,15},{9,1},{13,5},{18,26},{22,... | collective-permute-start | bytes 3145736 | tf_op jit(solution)/shard_map/ppermute | solution.py:226
  12.3 15.9 %collective-permute-done.1 = bf16[128,4096]{1,0:T(8,128)(2,1)S(1)} collective-permute-done((bf16[128,4096]{1,0:T(8,128)(2,1)}, bf16[128,4096]{1,0:T(8,128)(2,1)S(1)}, u32[]{:S(2)}, u32[]{:S(2)}) %collective-permute-start.1) | collective-permute-done | bytes 1048608 | tf_op jit(solution)/shard_map/ppermute | solution.py:24
  28.3 1.3 collective-permute-start.7
  29.6 1.6 collective-permute-start.3
  31.1 1.3 collective-permute-start
  32.5 12.0 %collective-permute-start.10 = (bf16[256,256]{1,0:T(8,128)(2,1)S(1)}, bf16[256,256]{1,0:T(8,128)(2,1)}, u32[]{:S(2)}, u32[]{:S(2)}) collective-permute-start(bf16[256,256]{1,0:T(8,128)(2,1)S(1)} %dynamic-slice_bitcast_fusion), channel_id=1, source_target_pairs={{0,8},{4,12},{8,0},{12,4},{1,9},{5,13},{9,1},{13,5},{2,10},{6,14},... | collective-permute-start | bytes 393224 | tf_op jit(solution)/shard_map/ppermute | solution.py:24
  44.5 0.1 copy.8.rate
  44.6 0.1 pad_add_fusion.place
  44.6 1.3 constant_dynamic-slice_fusion.own
  46.0 3.6 %collective-permute-done.6 = bf16[128,4096]{1,0:T(8,128)(2,1)} collective-permute-done((bf16[128,4096]{1,0:T(8,128)(2,1)}, bf16[128,4096]{1,0:T(8,128)(2,1)}, u32[]{:S(2)}, u32[]{:S(2)}) %collective-permute-start.6) | collective-permute-done | bytes 1048608 | tf_op jit(solution)/shard_map/ppermute | solution.py:226
  49.6 12.2 %collective-permute-start.17 = (bf16[512,512]{1,0:T(8,128)(2,1)S(1)}, bf16[512,512]{1,0:T(8,128)(2,1)S(1)}, u32[]{:S(2)}, u32[]{:S(2)}) collective-permute-start(bf16[512,512]{1,0:T(8,128)(2,1)S(1)} %copy-done.28), channel_id=1, source_target_pairs={{0,4},{4,0},{8,12},{12,8},{1,5},{5,1},{9,13},{13,9},{2,6},{6,2},{1... | collective-permute-start | bytes 1572872 | tf_op jit(solution)/shard_map/ppermute | solution.py:24
  61.9 18.7 %collective-permute-done.7 = bf16[128,4096]{1,0:T(8,128)(2,1)} collective-permute-done((bf16[128,4096]{1,0:T(8,128)(2,1)S(1)}, bf16[128,4096]{1,0:T(8,128)(2,1)}, u32[]{:S(2)}, u32[]{:S(2)}) %collective-permute-start.7) | collective-permute-done | bytes 1048608 | tf_op jit(solution)/shard_map/ppermute | solution.py:228
  80.5 1.3 broadcast_select_fusion.2
  81.9 1.4 collective-permute-done.10
  83.3 0.9 pad_maximum_fusion.4
  84.2 10.1 %collective-permute-done.17.rest_0_ = bf16[512,512]{1,0:T(8,128)(2,1)S(1)} collective-permute-done((bf16[512,512]{1,0:T(8,128)(2,1)S(1)}, bf16[512,512]{1,0:T(8,128)(2,1)S(1)}, u32[]{:S(2)}, u32[]{:S(2)}) %collective-permute-start.17) | collective-permute-done | bytes 524320 | tf_op jit(solution)/shard_map/ppermute | solution.py:24
  94.3 2.0 collective-permute-start.22
  96.3 0.1 collective-permute-start.27
  96.4 1.5 collective-permute-start.18
  97.9 2.0 maximum_select_fusion.act.act_own
  100.0 2.0 collective-permute-start.11
  102.0 8.5 %collective-permute-done.22.rest_0_ = bf16[512,512]{1,0:T(8,128)(2,1)S(1)} collective-permute-done((bf16[512,512]{1,0:T(8,128)(2,1)S(1)}, bf16[512,512]{1,0:T(8,128)(2,1)S(1)}, u32[]{:S(2)}, u32[]{:S(2)}) %collective-permute-start.22) | collective-permute-done | bytes 524320 | tf_op jit(solution)/shard_map/ppermute | solution.py:24
  110.5 11.2 %collective-permute-done.27.rest_0_ = bf16[512,512]{1,0:T(8,128)(2,1)S(1)} collective-permute-done((bf16[512,512]{1,0:T(8,128)(2,1)S(1)}, bf16[512,512]{1,0:T(8,128)(2,1)S(1)}, u32[]{:S(2)}, u32[]{:S(2)}) %collective-permute-start.27) | collective-permute-done | bytes 524320 | tf_op jit(solution)/shard_map/ppermute | solution.py:24
  121.7 1.5 collective-permute-start.23
  123.2 0.5 collective-permute-start.28
  123.7 0.1 broadcast_select_fusion.1
  123.9 2.5 collective-permute-done.11
  126.4 0.5 collective-permute-start.29
  126.9 9.7 %collective-permute-done.23.rest_1_ = bf16[512,512]{1,0:T(8,128)(2,1)S(1)} collective-permute-done((bf16[512,512]{1,0:T(8,128)(2,1)S(1)}, bf16[512,512]{1,0:T(8,128)(2,1)S(1)}, u32[]{:S(2)}, u32[]{:S(2)}) %collective-permute-start.23) | collective-permute-done | bytes 524320 | tf_op jit(solution)/shard_map/ppermute | solution.py:24
  136.6 8.4 %collective-permute-done.28.rest_1_ = bf16[512,512]{1,0:T(8,128)(2,1)S(1)} collective-permute-done((bf16[512,512]{1,0:T(8,128)(2,1)S(1)}, bf16[512,512]{1,0:T(8,128)(2,1)S(1)}, u32[]{:S(2)}, u32[]{:S(2)}) %collective-permute-start.28) | collective-permute-done | bytes 524320 | tf_op jit(solution)/shard_map/ppermute | solution.py:24
  145.0 1.6 pad_maximum_fusion.act.act_other
  146.6 4.0 %extra.1 = (f32[512,256]{1,0:T(8,128)S(1)}, bf16[512,256]{1,0:T(8,128)(2,1)S(1)}, f32[16,512]{1,0:T(8,128)S(1)}) custom-call(s32[3]{0:T(128)S(1)} %pad_add_fusion.place, bf16[256,4096]{1,0:T(8,128)(2,1)S(1)} %maximum_select_fusion.act.act_own, bf16[256,4096]{1,0:T(8,128)(2,1)} %pad_maximum_fusion.act.act_other, ...), custom_call_target="tpu_custom_call" | custom-call | tf_op jit(solution)/shard_map/extra/pallas_call | solution.py:40
  150.6 0.1 collective-permute-start.15
  150.7 1.1 pad_maximum_fusion.2.keys
  151.8 19.4 %teacher.1.norm = f32[16,256,128]{2,1,0:T(8,128)S(1)} custom-call(s32[3]{0:T(128)S(1)} %pad_add_fusion.place, bf16[256,2048]{1,0:T(8,128)(2,1)S(1)} %bitcast.24, bf16[1024,256]{1,0:T(8,128)(2,1)S(1)} %pad_maximum_fusion.2.keys), custom_call_target="tpu_custom_call" | custom-call | tf_op jit(solution)/shard_map/teacher/pallas_call | solution.py:361
  171.3 2.9 %partial.10.kept = f32[256,512]{1,0:T(8,128)S(1)} custom-call(s32[3]{0:T(128)S(1)} %pad_add_fusion.place, bf16[256,4096]{1,0:T(8,128)(2,1)S(1)} %maximum_select_fusion.act.act_own, bf16[2048,2048]{1,0:T(8,128)(2,1)} %own.15, bf16[512,512]{1,0:T(8,128)(2,1)S(1)} %collective-permute-done.17.rest_0_, bf16[512,512]{1,0:T(8,128)(2,1)S(1)} %collective-permute-done.18.rest_1_, ...), custom_call_target="tpu_custom_call" | custom-call | tf_op jit(solution)/shard_map/partial/pallas_call | solution.py:40
  174.1 0.8 copy-done.7
  175.0 3.1 %partial.12.kept = f32[256,512]{1,0:T(8,128)S(1)} custom-call(s32[3]{0:T(128)S(1)} %pad_add_fusion.place, bf16[256,4096]{1,0:T(8,128)(2,1)S(1)} %maximum_select_fusion.act.act_own, bf16[2048,2048]{1,0:T(8,128)(2,1)} %own.15, bf16[512,512]{1,0:T(8,128)(2,1)S(1)} %collective-permute-done.22.rest_0_, bf16[512,512]{1,0:T(8,128)(2,1)S(1)} %collective-permute-done.23.rest_1_, ...), custom_call_target="tpu_custom_call" | custom-call | tf_op jit(solution)/shard_map/partial/pallas_call | solution.py:40
  178.2 3.3 %partial.14.kept = f32[256,512]{1,0:T(8,128)S(1)} custom-call(s32[3]{0:T(128)S(1)} %pad_add_fusion.place, bf16[256,4096]{1,0:T(8,128)(2,1)S(1)} %maximum_select_fusion.act.act_own, bf16[2048,2048]{1,0:T(8,128)(2,1)} %own.15, bf16[512,512]{1,0:T(8,128)(2,1)S(1)} %collective-permute-done.27.rest_0_, bf16[512,512]{1,0:T(8,128)(2,1)S(1)} %collective-permute-done.28.rest_1_, ...), custom_call_target="tpu_custom_call" | custom-call | tf_op jit(solution)/shard_map/partial/pallas_call | solution.py:40
  181.5 3.0 %partial.8.kept = f32[256,512]{1,0:T(8,128)S(1)} custom-call(s32[3]{0:T(128)S(1)} %pad_add_fusion.place, bf16[256,4096]{1,0:T(8,128)(2,1)S(1)} %maximum_select_fusion.act.act_own, bf16[2048,2048]{1,0:T(8,128)(2,1)} %own.15, bf16[512,768]{1,0:T(8,128)(2,1)S(1)} %collective-permute-done.2.rest_0_, bf16[512,768]{1,0:T(8,128)(2,1)S(1)} %collective-permute-done.3.rest_1_, ...), custom_call_target="tpu_custom_call" | custom-call | tf_op jit(solution)/shard_map/partial/pallas_call | solution.py:40
  184.5 0.8 copy-done.17
  185.3 3.0 %partial.9 = bf16[256,512]{1,0:T(8,128)(2,1)S(1)} custom-call(s32[3]{0:T(128)S(1)} %pad_add_fusion.place, bf16[256,4096]{1,0:T(8,128)(2,1)S(1)} %copy-done.1, bf16[2048,2048]{1,0:T(8,128)(2,1)} %own.15, bf16[512,768]{1,0:T(8,128)(2,1)S(1)} %collective-permute-done.2.rest_0_, bf16[512,768]{1,0:T(8,128)(2,1)S(1)} %collective-permute-done.3.rest_1_, ...), custom_call_target="tpu_custom_call" | custom-call | tf_op jit(solution)/shard_map/partial/pallas_call | solution.py:40
  188.5 2.9 %collective-permute-start.13 = (bf16[512,256]{1,0:T(8,128)(2,1)S(1)}, bf16[512,256]{1,0:T(8,128)(2,1)S(1)}, u32[]{:S(2)}, u32[]{:S(2)}) collective-permute-start(bf16[512,256]{1,0:T(8,128)(2,1)S(1)} %copy-done.25), channel_id=1, source_target_pairs={{0,8},{4,12},{8,0},{12,4},{1,9},{5,13},{9,1},{13,5},{2,10},{6,14},... | collective-permute-start | bytes 786440 | tf_op jit(solution)/shard_map/ppermute | solution.py:24
  191.4 2.9 %partial.11 = bf16[256,512]{1,0:T(8,128)(2,1)S(1)} custom-call(s32[3]{0:T(128)S(1)} %pad_add_fusion.place, bf16[256,4096]{1,0:T(8,128)(2,1)S(1)} %copy-done.1, bf16[2048,2048]{1,0:T(8,128)(2,1)} %own.15, bf16[512,512]{1,0:T(8,128)(2,1)S(1)} %collective-permute-done.17.rest_0_, bf16[512,512]{1,0:T(8,128)(2,1)S(1)} %copy-done.6, ...), custom_call_target="tpu_custom_call" | custom-call | tf_op jit(solution)/shard_map/partial/pallas_call | solution.py:40
  194.2 0.3 collective-permute-start.21
  194.5 3.1 %partial.13 = bf16[256,512]{1,0:T(8,128)(2,1)S(1)} custom-call(s32[3]{0:T(128)S(1)} %pad_add_fusion.place, bf16[256,4096]{1,0:T(8,128)(2,1)S(1)} %copy-done.1, bf16[2048,2048]{1,0:T(8,128)(2,1)} %own.15, bf16[512,512]{1,0:T(8,128)(2,1)S(1)} %copy-done.4, bf16[512,512]{1,0:T(8,128)(2,1)S(1)} %copy-done.16, bf16[512,512]{1,0:T(8,128)(2,1)} %collective-permute-done.24.rest_2_, ...), custom_call_target="tpu_custom_call" | custom-call | tf_op jit(solution)/shard_map/partial/pallas_call | solution.py:40
  197.6 2.8 %collective-permute-start.26 = (bf16[256,512]{1,0:T(8,128)(2,1)S(1)}, bf16[256,512]{1,0:T(8,128)(2,1)S(1)}, u32[]{:S(2)}, u32[]{:S(2)}) collective-permute-start(bf16[256,512]{1,0:T(8,128)(2,1)S(1)} %partial.13), channel_id=1, source_target_pairs={{0,8},{4,12},{8,0},{12,4},{1,9},{5,13},{9,1},{13,5},{2,10},{6,14},... | collective-permute-start | bytes 786440 | tf_op jit(solution)/shard_map/ppermute | solution.py:24
  200.4 3.1 %partial.15 = bf16[256,512]{1,0:T(8,128)(2,1)S(1)} custom-call(s32[3]{0:T(128)S(1)} %pad_add_fusion.place, bf16[256,4096]{1,0:T(8,128)(2,1)S(1)} %copy-done.1, bf16[2048,2048]{1,0:T(8,128)(2,1)} %own.15, bf16[512,512]{1,0:T(8,128)(2,1)S(1)} %collective-permute-done.27.rest_0_, bf16[512,512]{1,0:T(8,128)(2,1)S(1)} %copy-done.12, ...), custom_call_target="tpu_custom_call" | custom-call | tf_op jit(solution)/shard_map/partial/pallas_call | solution.py:40
  203.6 0.3 collective-permute-start.31
  203.9 23.6 %collective-permute-done.13 = bf16[512,256]{1,0:T(8,128)(2,1)S(1)} collective-permute-done((bf16[512,256]{1,0:T(8,128)(2,1)S(1)}, bf16[512,256]{1,0:T(8,128)(2,1)S(1)}, u32[]{:S(2)}, u32[]{:S(2)}) %collective-permute-start.13) | collective-permute-done | bytes 262176 | tf_op jit(solution)/shard_map/ppermute | solution.py:24
  227.5 0.1 fusion
  227.6 17.4 %collective-permute-done.16 = f32[16,512]{1,0:T(8,128)S(1)} collective-permute-done((f32[16,512]{1,0:T(8,128)S(1)}, f32[16,512]{1,0:T(8,128)S(1)}, u32[]{:S(2)}, u32[]{:S(2)}) %collective-permute-start.16) | collective-permute-done | bytes 32800 | tf_op jit(solution)/shard_map/ppermute | solution.py:24
  245.0 1.3 decay.1
  246.3 6.9 %collective-permute-done.14 = bf16[512,256]{1,0:T(8,128)(2,1)S(1)} collective-permute-done((bf16[512,256]{1,0:T(8,128)(2,1)S(1)}, bf16[512,256]{1,0:T(8,128)(2,1)S(1)}, u32[]{:S(2)}, u32[]{:S(2)}) %collective-permute-start.14) | collective-permute-done | bytes 262176 | tf_op jit(solution)/shard_map/ppermute | solution.py:24
  253.3 4.6 %loss.4 = f32[4,1,256]{2,1,0:T(1,128)S(1)} custom-call(s32[3]{0:T(128)S(1)} %pad_add_fusion.place, bf16[256,2048]{1,0:T(8,128)(2,1)S(1)} %bitcast.25, f32[256,512]{1,0:T(8,128)S(1)} %copy-done.18, bf16[256,512]{1,0:T(8,128)(2,1)S(1)} %collective-permute-done.9.came, bf16[1024,256]{1,0:T(8,128)(2,1)S(1)} %pad_maximum_fusion.2.keys, ...), custom_call_target="tpu_custom_call" | custom-call | tf_op jit(solution)/shard_map/loss/pallas_call | solution.py:40
  257.9 4.8 %loss.5 = f32[4,1,256]{2,1,0:T(1,128)S(1)} custom-call(s32[3]{0:T(128)S(1)} %pad_add_fusion.place, bf16[256,2048]{1,0:T(8,128)(2,1)S(1)} %bitcast.26, f32[256,512]{1,0:T(8,128)S(1)} %copy-done.8, bf16[256,512]{1,0:T(8,128)(2,1)S(1)} %collective-permute-done.21.came, bf16[1024,256]{1,0:T(8,128)(2,1)S(1)} %pad_maximum_fusion.2.keys, ...), custom_call_target="tpu_custom_call" | custom-call | tf_op jit(solution)/shard_map/loss/pallas_call | solution.py:40
  262.7 4.5 %loss.6 = f32[4,1,256]{2,1,0:T(1,128)S(1)} custom-call(s32[3]{0:T(128)S(1)} %pad_add_fusion.place, bf16[256,2048]{1,0:T(8,128)(2,1)S(1)} %bitcast.27, f32[256,512]{1,0:T(8,128)S(1)} %copy-done.10, bf16[256,512]{1,0:T(8,128)(2,1)S(1)} %collective-permute-done.26.came, bf16[1024,256]{1,0:T(8,128)(2,1)S(1)} %pad_maximum_fusion.2.keys, ...), custom_call_target="tpu_custom_call" | custom-call | tf_op jit(solution)/shard_map/loss/pallas_call | solution.py:40
  267.2 4.5 %loss.7 = f32[4,1,256]{2,1,0:T(1,128)S(1)} custom-call(s32[3]{0:T(128)S(1)} %pad_add_fusion.place, bf16[256,2048]{1,0:T(8,128)(2,1)S(1)} %bitcast.28, f32[256,512]{1,0:T(8,128)S(1)} %partial.14.kept, bf16[256,512]{1,0:T(8,128)(2,1)S(1)} %collective-permute-done.31.came, bf16[1024,256]{1,0:T(8,128)(2,1)S(1)} %pad_maximum_fusion.2.keys, ...), custom_call_target="tpu_custom_call" | custom-call | tf_op jit(solution)/shard_map/loss/pallas_call | solution.py:40
  271.8 0.6 copy.9
  (103 shorter events, 0.5 us)
Async XLA Ops:
  0.0 32.4 %copy-start = (bf16[1,256,512]{2,1,0:T(8,128)(2,1)S(1)}, bf16[1,256,512]{2,1,0:T(8,128)(2,1)}, u32[]{:S(2)}) copy-start(bf16[1,256,512]{2,1,0:T(8,128)(2,1)} %param.9) | copy-start | bytes 786436
  3.1 25.1 %collective-permute-start.1 = (bf16[128,4096]{1,0:T(8,128)(2,1)}, bf16[128,4096]{1,0:T(8,128)(2,1)S(1)}, u32[]{:S(2)}, u32[]{:S(2)}) collective-permute-start(bf16[128,4096]{1,0:T(8,128)(2,1)} %get-tuple-element.26), channel_id=1, source_target_pairs={{0,2},{2,0},{1,3},{3,1},{4,6},{6,4},{5,7},{7,5},{8,10},{10,8},{9,1... | collective-permute-start | bytes 3145736 | tf_op jit(solution)/shard_map/ppermute | solution.py:24
  5.8 38.7 %copy-start.29 = (f32[16]{0:T(128)S(1)}, f32[16]{0:T(128)}, u32[]{:S(2)}) copy-start(f32[16]{0:T(128)} %param.13) | copy-start | bytes 196
  8.6 21.0 %collective-permute-start.2 = (bf16[512,768]{1,0:T(8,128)(2,1)S(1)}, bf16[512,768]{1,0:T(8,128)(2,1)S(1)}, u32[]{:S(2)}, u32[]{:S(2)}) collective-permute-start(bf16[512,768]{1,0:T(8,128)(2,1)S(1)} %pad_maximum_fusion.1), channel_id=1, source_target_pairs={{0,4},{4,0},{8,12},{12,8},{1,5},{5,1},{9,13},{13,9},{2,6},{6,2},{1... | collective-permute-start | bytes 2359304 | tf_op jit(solution)/shard_map/ppermute | solution.py:24
  9.1 40.5 %collective-permute-start.6 = (bf16[128,4096]{1,0:T(8,128)(2,1)}, bf16[128,4096]{1,0:T(8,128)(2,1)}, u32[]{:S(2)}, u32[]{:S(2)}) collective-permute-start(bf16[128,4096]{1,0:T(8,128)(2,1)} %get-tuple-element.25), channel_id=1, source_target_pairs={{2,10},{6,14},{8,0},{12,4},{3,11},{7,15},{9,1},{13,5},{18,26},{22,... | collective-permute-start | bytes 3145736 | tf_op jit(solution)/shard_map/ppermute | solution.py:226
  28.3 52.3 %collective-permute-start.7 = (bf16[128,4096]{1,0:T(8,128)(2,1)S(1)}, bf16[128,4096]{1,0:T(8,128)(2,1)}, u32[]{:S(2)}, u32[]{:S(2)}) collective-permute-start(bf16[128,4096]{1,0:T(8,128)(2,1)S(1)} %collective-permute-done.1), channel_id=1, source_target_pairs={{0,8},{4,12},{10,2},{14,6},{1,9},{5,13},{11,3},{15,7},{16,24},{20,... | collective-permute-start | bytes 3145736 | tf_op jit(solution)/shard_map/ppermute | solution.py:228
  29.6 32.3 %collective-permute-start.3 = (bf16[512,768]{1,0:T(8,128)(2,1)S(1)}, bf16[512,768]{1,0:T(8,128)(2,1)S(1)}, u32[]{:S(2)}, u32[]{:S(2)}) collective-permute-start(bf16[512,768]{1,0:T(8,128)(2,1)S(1)} %collective-permute-done.2.rest_0_), channel_id=1, source_target_pairs={{0,16},{16,0},{1,17},{17,1},{2,18},{18,2},{3,19},{19,3},{4,20},{20... | collective-permute-start | bytes 2359304 | tf_op jit(solution)/shard_map/ppermute | solution.py:24
  31.1 63.1 %collective-permute-start = (bf16[128,4096]{1,0:T(8,128)(2,1)}, bf16[128,4096]{1,0:T(8,128)(2,1)}, u32[]{:S(2)}, u32[]{:S(2)}) collective-permute-start(bf16[128,4096]{1,0:T(8,128)(2,1)} %get-tuple-element.25), channel_id=1, source_target_pairs={{0,2},{4,6},{10,8},{14,12},{1,3},{5,7},{11,9},{15,13},{16,18},{20,... | collective-permute-start | bytes 3145736 | tf_op jit(solution)/shard_map/ppermute | solution.py:229
  32.5 50.8 %collective-permute-start.10 = (bf16[256,256]{1,0:T(8,128)(2,1)S(1)}, bf16[256,256]{1,0:T(8,128)(2,1)}, u32[]{:S(2)}, u32[]{:S(2)}) collective-permute-start(bf16[256,256]{1,0:T(8,128)(2,1)S(1)} %dynamic-slice_bitcast_fusion), channel_id=1, source_target_pairs={{0,8},{4,12},{8,0},{12,4},{1,9},{5,13},{9,1},{13,5},{2,10},{6,14},... | collective-permute-start | bytes 393224 | tf_op jit(solution)/shard_map/ppermute | solution.py:24
  44.6 5.1 %copy-start.28 = (bf16[512,512]{1,0:T(8,128)(2,1)S(1)}, bf16[512,512]{1,0:T(8,128)(2,1)}, u32[]{:S(2)}) copy-start(bf16[512,512]{1,0:T(8,128)(2,1)} %get-tuple-element.19) | copy-start | bytes 1572868
  49.6 44.6 %copy-start.23 = (bf16[2048,16]{0,1:T(8,128)(2,1)S(1)}, bf16[2048,16]{0,1:T(8,128)(2,1)}, u32[]{:S(2)}) copy-start(bf16[2048,16]{0,1:T(8,128)(2,1)} %param.12) | copy-start | bytes 196612
  49.6 44.6 %copy-start.27 = (bf16[512,512]{1,0:T(8,128)(2,1)S(1)}, bf16[512,512]{1,0:T(8,128)(2,1)}, u32[]{:S(2)}) copy-start(bf16[512,512]{1,0:T(8,128)(2,1)} %get-tuple-element.21) | copy-start | bytes 1572868
  49.6 48.3 %copy-start.26 = (bf16[1,256,4096]{2,1,0:T(8,128)(2,1)S(1)}, bf16[1,256,4096]{2,1,0:T(8,128)(2,1)}, u32[]{:S(2)}) copy-start(bf16[1,256,4096]{2,1,0:T(8,128)(2,1)} %param.7) | copy-start | bytes 6291460
  49.6 44.6 %collective-permute-start.17 = (bf16[512,512]{1,0:T(8,128)(2,1)S(1)}, bf16[512,512]{1,0:T(8,128)(2,1)S(1)}, u32[]{:S(2)}, u32[]{:S(2)}) collective-permute-start(bf16[512,512]{1,0:T(8,128)(2,1)S(1)} %copy-done.28), channel_id=1, source_target_pairs={{0,4},{4,0},{8,12},{12,8},{1,5},{5,1},{9,13},{13,9},{2,6},{6,2},{1... | collective-permute-start | bytes 1572872 | tf_op jit(solution)/shard_map/ppermute | solution.py:24
  61.9 34.4 %collective-permute-start.4 = (bf16[512,768]{1,0:T(8,128)(2,1)S(1)}, bf16[512,768]{1,0:T(8,128)(2,1)S(1)}, u32[]{:S(2)}, u32[]{:S(2)}) collective-permute-start(bf16[512,768]{1,0:T(8,128)(2,1)S(1)} %collective-permute-done.2.rest_0_), channel_id=1, source_target_pairs={{0,1},{1,0},{2,3},{3,2},{4,5},{5,4},{6,7},{7,6},{8,9},{9,8},{10,11... | collective-permute-start | bytes 2359304 | tf_op jit(solution)/shard_map/ppermute | solution.py:24
  80.5 15.9 %collective-permute-start.5 = (bf16[512,768]{1,0:T(8,128)(2,1)S(1)}, bf16[512,768]{1,0:T(8,128)(2,1)S(1)}, u32[]{:S(2)}, u32[]{:S(2)}) collective-permute-start(bf16[512,768]{1,0:T(8,128)(2,1)S(1)} %collective-permute-done.3.rest_1_), channel_id=1, source_target_pairs={{0,1},{1,0},{2,3},{3,2},{4,5},{5,4},{6,7},{7,6},{8,9},{9,8},{10,11... | collective-permute-start | bytes 2359304 | tf_op jit(solution)/shard_map/ppermute | solution.py:24
  83.2 40.5 %collective-permute-start.8 = (bf16[128,4096]{1,0:T(8,128)(2,1)S(1)}, bf16[128,4096]{1,0:T(8,128)(2,1)S(1)}, u32[]{:S(2)}, u32[]{:S(2)}) collective-permute-start(bf16[128,4096]{1,0:T(8,128)(2,1)S(1)} %broadcast_select_fusion.2), channel_id=1, source_target_pairs={{0,2},{2,0},{1,3},{3,1},{4,6},{6,4},{5,7},{7,5},{8,10},{10,8},{9,1... | collective-permute-start | bytes 3145736 | tf_op jit(solution)/shard_map/ppermute | solution.py:24
  94.3 5.7 %collective-permute-start.12 = (bf16[16,2048]{1,0:T(8,128)(2,1)S(1)}, bf16[16,2048]{1,0:T(8,128)(2,1)S(1)}, u32[]{:S(2)}, u32[]{:S(2)}) collective-permute-start(bf16[16,2048]{1,0:T(8,128)(2,1)S(1)} %bitcast.29), channel_id=1, source_target_pairs={{0,4},{4,0},{8,12},{12,8},{1,5},{5,1},{9,13},{13,9},{2,6},{6,2},{1... | collective-permute-start | bytes 196616 | tf_op jit(solution)/shard_map/ppermute | solution.py:24
  94.3 16.2 %collective-permute-start.22 = (bf16[512,512]{1,0:T(8,128)(2,1)S(1)}, bf16[512,512]{1,0:T(8,128)(2,1)S(1)}, u32[]{:S(2)}, u32[]{:S(2)}) collective-permute-start(bf16[512,512]{1,0:T(8,128)(2,1)S(1)} %copy-done.27), channel_id=1, source_target_pairs={{0,4},{4,0},{8,12},{12,8},{1,5},{5,1},{9,13},{13,9},{2,6},{6,2},{1... | collective-permute-start | bytes 1572872 | tf_op jit(solution)/shard_map/ppermute | solution.py:24
  96.3 25.4 %collective-permute-start.27 = (bf16[512,512]{1,0:T(8,128)(2,1)S(1)}, bf16[512,512]{1,0:T(8,128)(2,1)S(1)}, u32[]{:S(2)}, u32[]{:S(2)}) collective-permute-start(bf16[512,512]{1,0:T(8,128)(2,1)S(1)} %get-tuple-element.20), channel_id=1, source_target_pairs={{0,4},{4,0},{8,12},{12,8},{1,5},{5,1},{9,13},{13,9},{2,6},{6,2},{1... | collective-permute-start | bytes 1572872 | tf_op jit(solution)/shard_map/ppermute | solution.py:24
  96.4 26.8 %collective-permute-start.18 = (bf16[512,512]{1,0:T(8,128)(2,1)S(1)}, bf16[512,512]{1,0:T(8,128)(2,1)S(1)}, u32[]{:S(2)}, u32[]{:S(2)}) collective-permute-start(bf16[512,512]{1,0:T(8,128)(2,1)S(1)} %collective-permute-done.17.rest_0_), channel_id=1, source_target_pairs={{0,16},{16,0},{1,17},{17,1},{2,18},{18,2},{3,19},{19,3},{4,20},{20... | collective-permute-start | bytes 1572872 | tf_op jit(solution)/shard_map/ppermute | solution.py:24
  100.0 26.4 %collective-permute-start.11 = (bf16[512,256]{1,0:T(8,128)(2,1)S(1)}, bf16[512,256]{1,0:T(8,128)(2,1)S(1)}, u32[]{:S(2)}, u32[]{:S(2)}) collective-permute-start(bf16[512,256]{1,0:T(8,128)(2,1)S(1)} %pad_maximum_fusion.4), channel_id=1, source_target_pairs={{0,4},{4,0},{8,12},{12,8},{1,5},{5,1},{9,13},{13,9},{2,6},{6,2},{1... | collective-permute-start | bytes 786440 | tf_op jit(solution)/shard_map/ppermute | solution.py:24
  110.5 64.5 %copy-start.3 = (bf16[512,512]{1,0:T(8,128)(2,1)}, bf16[512,512]{1,0:T(8,128)(2,1)S(1)}, u32[]{:S(2)}) copy-start(bf16[512,512]{1,0:T(8,128)(2,1)S(1)} %collective-permute-done.22.rest_0_) | copy-start | bytes 1572868
  110.5 15.9 %collective-permute-start.19 = (bf16[512,512]{1,0:T(8,128)(2,1)S(1)}, bf16[512,512]{1,0:T(8,128)(2,1)S(1)}, u32[]{:S(2)}, u32[]{:S(2)}) collective-permute-start(bf16[512,512]{1,0:T(8,128)(2,1)S(1)} %collective-permute-done.17.rest_0_), channel_id=1, source_target_pairs={{0,1},{1,0},{2,3},{3,2},{4,5},{5,4},{6,7},{7,6},{8,9},{9,8},{10,11... | collective-permute-start | bytes 1572872 | tf_op jit(solution)/shard_map/ppermute | solution.py:24
  121.7 14.9 %collective-permute-start.23 = (bf16[512,512]{1,0:T(8,128)(2,1)S(1)}, bf16[512,512]{1,0:T(8,128)(2,1)S(1)}, u32[]{:S(2)}, u32[]{:S(2)}) collective-permute-start(bf16[512,512]{1,0:T(8,128)(2,1)S(1)} %collective-permute-done.22.rest_0_), channel_id=1, source_target_pairs={{0,16},{16,0},{1,17},{17,1},{2,18},{18,2},{3,19},{19,3},{4,20},{20... | collective-permute-start | bytes 1572872 | tf_op jit(solution)/shard_map/ppermute | solution.py:24
  123.2 48.0 %copy-start.5 = (bf16[512,512]{1,0:T(8,128)(2,1)}, bf16[512,512]{1,0:T(8,128)(2,1)S(1)}, u32[]{:S(2)}) copy-start(bf16[512,512]{1,0:T(8,128)(2,1)S(1)} %collective-permute-done.18.rest_1_) | copy-start | bytes 1572868
  123.2 21.8 %collective-permute-start.28 = (bf16[512,512]{1,0:T(8,128)(2,1)S(1)}, bf16[512,512]{1,0:T(8,128)(2,1)S(1)}, u32[]{:S(2)}, u32[]{:S(2)}) collective-permute-start(bf16[512,512]{1,0:T(8,128)(2,1)S(1)} %collective-permute-done.27.rest_0_), channel_id=1, source_target_pairs={{0,16},{16,0},{1,17},{17,1},{2,18},{18,2},{3,19},{19,3},{4,20},{20... | collective-permute-start | bytes 1572872 | tf_op jit(solution)/shard_map/ppermute | solution.py:24
  123.7 26.9 %collective-permute-start.20 = (bf16[512,512]{1,0:T(8,128)(2,1)S(1)}, bf16[512,512]{1,0:T(8,128)(2,1)S(1)}, u32[]{:S(2)}, u32[]{:S(2)}) collective-permute-start(bf16[512,512]{1,0:T(8,128)(2,1)S(1)} %collective-permute-done.18.rest_1_), channel_id=1, source_target_pairs={{0,1},{1,0},{2,3},{3,2},{4,5},{5,4},{6,7},{7,6},{8,9},{9,8},{10,11... | collective-permute-start | bytes 1572872 | tf_op jit(solution)/shard_map/ppermute | solution.py:24
  126.4 48.6 %collective-permute-start.24 = (bf16[512,512]{1,0:T(8,128)(2,1)S(1)}, bf16[512,512]{1,0:T(8,128)(2,1)}, u32[]{:S(2)}, u32[]{:S(2)}) collective-permute-start(bf16[512,512]{1,0:T(8,128)(2,1)S(1)} %collective-permute-done.22.rest_0_), channel_id=1, source_target_pairs={{0,1},{1,0},{2,3},{3,2},{4,5},{5,4},{6,7},{7,6},{8,9},{9,8},{10,11... | collective-permute-start | bytes 1572872 | tf_op jit(solution)/shard_map/ppermute | solution.py:24
  126.4 44.9 %copy-start.13 = (bf16[512,512]{1,0:T(8,128)(2,1)}, bf16[512,512]{1,0:T(8,128)(2,1)S(1)}, u32[]{:S(2)}) copy-start(bf16[512,512]{1,0:T(8,128)(2,1)S(1)} %collective-permute-done.19.rest_2_) | copy-start | bytes 1572868
  126.4 51.7 %collective-permute-start.29 = (bf16[512,512]{1,0:T(8,128)(2,1)S(1)}, bf16[512,512]{1,0:T(8,128)(2,1)}, u32[]{:S(2)}, u32[]{:S(2)}) collective-permute-start(bf16[512,512]{1,0:T(8,128)(2,1)S(1)} %collective-permute-done.27.rest_0_), channel_id=1, source_target_pairs={{0,1},{1,0},{2,3},{3,2},{4,5},{5,4},{6,7},{7,6},{8,9},{9,8},{10,11... | collective-permute-start | bytes 1572872 | tf_op jit(solution)/shard_map/ppermute | solution.py:24
  136.6 38.4 %copy-start.15 = (bf16[512,512]{1,0:T(8,128)(2,1)}, bf16[512,512]{1,0:T(8,128)(2,1)S(1)}, u32[]{:S(2)}) copy-start(bf16[512,512]{1,0:T(8,128)(2,1)S(1)} %collective-permute-done.23.rest_1_) | copy-start | bytes 1572868
  136.6 38.4 %collective-permute-start.25 = (bf16[512,512]{1,0:T(8,128)(2,1)S(1)}, bf16[512,512]{1,0:T(8,128)(2,1)}, u32[]{:S(2)}, u32[]{:S(2)}) collective-permute-start(bf16[512,512]{1,0:T(8,128)(2,1)S(1)} %collective-permute-done.23.rest_1_), channel_id=1, source_target_pairs={{0,1},{1,0},{2,3},{3,2},{4,5},{5,4},{6,7},{7,6},{8,9},{9,8},{10,11... | collective-permute-start | bytes 1572872 | tf_op jit(solution)/shard_map/ppermute | solution.py:24
  145.0 33.2 %copy-start.11 = (bf16[512,512]{1,0:T(8,128)(2,1)}, bf16[512,512]{1,0:T(8,128)(2,1)S(1)}, u32[]{:S(2)}) copy-start(bf16[512,512]{1,0:T(8,128)(2,1)S(1)} %collective-permute-done.28.rest_1_) | copy-start | bytes 1572868
  145.0 33.1 %collective-permute-start.30 = (bf16[512,512]{1,0:T(8,128)(2,1)S(1)}, bf16[512,512]{1,0:T(8,128)(2,1)}, u32[]{:S(2)}, u32[]{:S(2)}) collective-permute-start(bf16[512,512]{1,0:T(8,128)(2,1)S(1)} %collective-permute-done.28.rest_1_), channel_id=1, source_target_pairs={{0,1},{1,0},{2,3},{3,2},{4,5},{5,4},{6,7},{7,6},{8,9},{9,8},{10,11... | collective-permute-start | bytes 1572872 | tf_op jit(solution)/shard_map/ppermute | solution.py:24
  146.6 5.2 %copy-start.2 = (bf16[1,256,2048]{2,1,0:T(8,128)(2,1)S(1)}, bf16[1,256,2048]{2,1,0:T(8,128)(2,1)}, u32[]{:S(2)}) copy-start(bf16[1,256,2048]{2,1,0:T(8,128)(2,1)} %param.8) | copy-start | bytes 3145732
  150.6 1.2 copy-start.21
  150.6 20.7 %copy-start.24 = (bf16[512,256]{1,0:T(8,128)(2,1)}, bf16[512,256]{1,0:T(8,128)(2,1)S(1)}, u32[]{:S(2)}) copy-start(bf16[512,256]{1,0:T(8,128)(2,1)S(1)} %get-tuple-element.13) | copy-start | bytes 786436
  150.6 20.7 %copy-start.19 = (bf16[512,512]{1,0:T(8,128)(2,1)}, bf16[512,512]{1,0:T(8,128)(2,1)S(1)}, u32[]{:S(2)}) copy-start(bf16[512,512]{1,0:T(8,128)(2,1)S(1)} %collective-permute-done.20.rest_3_) | copy-start | bytes 1572868
  150.6 53.0 %collective-permute-start.15 = (f32[16,512]{1,0:T(8,128)S(1)}, f32[16,512]{1,0:T(8,128)S(1)}, u32[]{:S(2)}, u32[]{:S(2)}) collective-permute-start(f32[16,512]{1,0:T(8,128)S(1)} %get-tuple-element.14), channel_id=1, source_target_pairs={{0,8},{4,12},{8,0},{12,4},{1,9},{5,13},{9,1},{13,5},{2,10},{6,14},... | collective-permute-start | bytes 98312 | tf_op jit(solution)/shard_map/ppermute | solution.py:24
  174.1 0.8 copy-start.7
  178.1 3.3 %copy-start.9 = (f32[256,512]{1,0:T(8,128)}, f32[256,512]{1,0:T(8,128)S(1)}, u32[]{:S(2)}) copy-start(f32[256,512]{1,0:T(8,128)S(1)} %partial.12.kept) | copy-start | bytes 1572868
  181.5 3.8 %copy-start.1 = (bf16[256,4096]{1,0:T(8,128)(2,1)S(1)}, bf16[256,4096]{1,0:T(8,128)(2,1)}, u32[]{:S(2)}) copy-start(bf16[256,4096]{1,0:T(8,128)(2,1)} %pad_maximum_fusion.act.act_other) | copy-start | bytes 6291460
  184.5 0.8 copy-start.17
  185.3 3.1 %copy-start.25 = (bf16[512,256]{1,0:T(8,128)(2,1)S(1)}, bf16[512,256]{1,0:T(8,128)(2,1)}, u32[]{:S(2)}) copy-start(bf16[512,256]{1,0:T(8,128)(2,1)} %copy-done.24) | copy-start | bytes 786436
  185.3 6.0 %copy-start.6 = (bf16[512,512]{1,0:T(8,128)(2,1)S(1)}, bf16[512,512]{1,0:T(8,128)(2,1)}, u32[]{:S(2)}) copy-start(bf16[512,512]{1,0:T(8,128)(2,1)} %copy-done.5) | copy-start | bytes 1572868
  185.3 6.0 %copy-start.14 = (bf16[512,512]{1,0:T(8,128)(2,1)S(1)}, bf16[512,512]{1,0:T(8,128)(2,1)}, u32[]{:S(2)}) copy-start(bf16[512,512]{1,0:T(8,128)(2,1)} %copy-done.13) | copy-start | bytes 1572868
  185.3 6.0 %copy-start.20 = (bf16[512,512]{1,0:T(8,128)(2,1)S(1)}, bf16[512,512]{1,0:T(8,128)(2,1)}, u32[]{:S(2)}) copy-start(bf16[512,512]{1,0:T(8,128)(2,1)} %copy-done.19) | copy-start | bytes 1572868
  188.3 64.9 %collective-permute-start.9 = (bf16[256,512]{1,0:T(8,128)(2,1)S(1)}, bf16[256,512]{1,0:T(8,128)(2,1)S(1)}, u32[]{:S(2)}, u32[]{:S(2)}) collective-permute-start(bf16[256,512]{1,0:T(8,128)(2,1)S(1)} %partial.9), channel_id=1, source_target_pairs={{0,8},{4,12},{8,0},{12,4},{1,9},{5,13},{9,1},{13,5},{2,10},{6,14},... | collective-permute-start | bytes 786440 | tf_op jit(solution)/shard_map/ppermute | solution.py:24
  188.4 6.1 %copy-start.4 = (bf16[512,512]{1,0:T(8,128)(2,1)S(1)}, bf16[512,512]{1,0:T(8,128)(2,1)}, u32[]{:S(2)}) copy-start(bf16[512,512]{1,0:T(8,128)(2,1)} %copy-done.3) | copy-start | bytes 1572868
  188.4 6.1 %copy-start.16 = (bf16[512,512]{1,0:T(8,128)(2,1)S(1)}, bf16[512,512]{1,0:T(8,128)(2,1)}, u32[]{:S(2)}) copy-start(bf16[512,512]{1,0:T(8,128)(2,1)} %copy-done.15) | copy-start | bytes 1572868
  188.5 39.0 %collective-permute-start.13 = (bf16[512,256]{1,0:T(8,128)(2,1)S(1)}, bf16[512,256]{1,0:T(8,128)(2,1)S(1)}, u32[]{:S(2)}, u32[]{:S(2)}) collective-permute-start(bf16[512,256]{1,0:T(8,128)(2,1)S(1)} %copy-done.25), channel_id=1, source_target_pairs={{0,8},{4,12},{8,0},{12,4},{1,9},{5,13},{9,1},{13,5},{2,10},{6,14},... | collective-permute-start | bytes 786440 | tf_op jit(solution)/shard_map/ppermute | solution.py:24
  194.2 6.2 %copy-start.12 = (bf16[512,512]{1,0:T(8,128)(2,1)S(1)}, bf16[512,512]{1,0:T(8,128)(2,1)}, u32[]{:S(2)}) copy-start(bf16[512,512]{1,0:T(8,128)(2,1)} %copy-done.11) | copy-start | bytes 1572868
  194.2 63.6 %collective-permute-start.21 = (bf16[256,512]{1,0:T(8,128)(2,1)S(1)}, bf16[256,512]{1,0:T(8,128)(2,1)S(1)}, u32[]{:S(2)}, u32[]{:S(2)}) collective-permute-start(bf16[256,512]{1,0:T(8,128)(2,1)S(1)} %partial.11), channel_id=1, source_target_pairs={{0,8},{4,12},{8,0},{12,4},{1,9},{5,13},{9,1},{13,5},{2,10},{6,14},... | collective-permute-start | bytes 786440 | tf_op jit(solution)/shard_map/ppermute | solution.py:24
  197.6 29.9 %copy-start.22 = (f32[512,256]{1,0:T(8,128)S(1)}, f32[512,256]{1,0:T(8,128)}, u32[]{:S(2)}) copy-start(f32[512,256]{1,0:T(8,128)} %copy-done.21) | copy-start | bytes 1572868
  197.6 65.0 %collective-permute-start.26 = (bf16[256,512]{1,0:T(8,128)(2,1)S(1)}, bf16[256,512]{1,0:T(8,128)(2,1)S(1)}, u32[]{:S(2)}, u32[]{:S(2)}) collective-permute-start(bf16[256,512]{1,0:T(8,128)(2,1)S(1)} %partial.13), channel_id=1, source_target_pairs={{0,8},{4,12},{8,0},{12,4},{1,9},{5,13},{9,1},{13,5},{2,10},{6,14},... | collective-permute-start | bytes 786440 | tf_op jit(solution)/shard_map/ppermute | solution.py:24
  203.6 49.7 %copy-start.18 = (f32[256,512]{1,0:T(8,128)S(1)}, f32[256,512]{1,0:T(8,128)}, u32[]{:S(2)}) copy-start(f32[256,512]{1,0:T(8,128)} %copy-done.17) | copy-start | bytes 1572868
  203.6 63.7 %collective-permute-start.31 = (bf16[256,512]{1,0:T(8,128)(2,1)S(1)}, bf16[256,512]{1,0:T(8,128)(2,1)S(1)}, u32[]{:S(2)}, u32[]{:S(2)}) collective-permute-start(bf16[256,512]{1,0:T(8,128)(2,1)S(1)} %partial.15), channel_id=1, source_target_pairs={{0,8},{4,12},{8,0},{12,4},{1,9},{5,13},{9,1},{13,5},{2,10},{6,14},... | collective-permute-start | bytes 786440 | tf_op jit(solution)/shard_map/ppermute | solution.py:24
  227.5 17.5 %collective-permute-start.16 = (f32[16,512]{1,0:T(8,128)S(1)}, f32[16,512]{1,0:T(8,128)S(1)}, u32[]{:S(2)}, u32[]{:S(2)}) collective-permute-start(f32[16,512]{1,0:T(8,128)S(1)} %maximum_add_fusion.1), channel_id=1, source_target_pairs={{0,4},{4,0},{8,12},{12,8},{1,5},{5,1},{9,13},{13,9},{2,6},{6,2},{1... | collective-permute-start | bytes 98312 | tf_op jit(solution)/shard_map/ppermute | solution.py:24
  245.0 8.2 %collective-permute-start.14 = (bf16[512,256]{1,0:T(8,128)(2,1)S(1)}, bf16[512,256]{1,0:T(8,128)(2,1)S(1)}, u32[]{:S(2)}, u32[]{:S(2)}) collective-permute-start(bf16[512,256]{1,0:T(8,128)(2,1)S(1)} %fusion), channel_id=1, source_target_pairs={{0,4},{4,0},{8,12},{12,8},{1,5},{5,1},{9,13},{13,9},{2,6},{6,2},{1... | collective-permute-start | bytes 786440 | tf_op jit(solution)/shard_map/ppermute | solution.py:24
  253.3 4.6 %copy-start.8 = (f32[256,512]{1,0:T(8,128)S(1)}, f32[256,512]{1,0:T(8,128)}, u32[]{:S(2)}) copy-start(f32[256,512]{1,0:T(8,128)} %copy-done.7) | copy-start | bytes 1572868
  257.8 4.8 %copy-start.10 = (f32[256,512]{1,0:T(8,128)S(1)}, f32[256,512]{1,0:T(8,128)}, u32[]{:S(2)}) copy-start(f32[256,512]{1,0:T(8,128)} %copy-done.9) | copy-start | bytes 1572868

commit v2 on v1

v2 whole, which is shorter than its diff:
```python
import functools
import math

import jax
import jax.numpy as jnp
from jax import lax
from jax.experimental import pallas as pl
from jax.experimental.pallas import tpu as pltpu
from jax.sharding import PartitionSpec as P

HEADS = 32
KV_HEADS = 4
HEAD_DIM = 128
LOG2E = math.log2(math.e)
BF16 = jnp.bfloat16
F32 = jnp.float32
VMEM_LIMIT = 48 * 1024 * 1024

NT = (((1,), (1,)), ((), ()))


def xor_permute(value, axis, offset):
    size = lax.axis_size(axis)
    return lax.ppermute(value, axis, [(i, i ^ offset) for i in range(size)])


def whole(shape):
    return pl.BlockSpec(shape, lambda *_: (0,) * len(shape))


def columns(rows, width, index):
    return pl.BlockSpec((rows, width), lambda *_: (0, index))


def smem():
    return pl.BlockSpec(memory_space=pltpu.SMEM)


def call(kernel, args, in_specs, out_shapes, name, scratch=()):
    return pl.pallas_call(
        kernel,
        grid=(1,),
        in_specs=in_specs,
        out_specs=tuple(whole(s.shape) for s in out_shapes),
        out_shape=tuple(out_shapes),
        scratch_shapes=list(scratch),
        compiler_params=pltpu.CompilerParams(vmem_limit_bytes=VMEM_LIMIT),
        name=name,
    )(*args)


def product(place, act, own, pieces, model):
    block, quarter = place[0], place[1]
    rows = own.shape[0]
    total = jnp.dot(
        act[:, pl.ds(pl.multiple_of(block * rows, rows), rows)], own[...], preferred_element_type=F32
    )
    for piece, (step, turn) in zip(pieces, model):
        part = piece.shape[0]
        start = (block ^ step) * rows + (quarter ^ turn) * part
        total += jnp.dot(
            act[:, pl.ds(pl.multiple_of(start, part), part)], piece[...], preferred_element_type=F32
        )
    return total


def partial_kernel(model, number, place, *rest):
    acts, own, pieces, outs = rest[:number], rest[number], rest[number + 1 : -number], rest[-number:]
    for act, out in zip(acts, outs):
        out[...] = product(place, act, own, pieces, model).astype(out.dtype)


def extra_kernel(model, step_model, place, act_own, act_low, act_high, own, *rest):
    n = len(model)
    pieces = rest[:n]
    step_pieces = rest[n : n + len(step_model)]
    full, rounded, raw = rest[-3:]
    first = 0
    for act in (act_own, act_low, act_high):
        here = slice(first, first + act.shape[0])
        first += act.shape[0]
        value = product(place, act, own, pieces, model)
        full[here, :] = value
        rounded[here, :] = value.astype(BF16)
        total = None
        for piece, step in zip(step_pieces, step_model):
            rows = piece.shape[1]
            start = pl.multiple_of((place[0] ^ step) * rows, rows)
            part = lax.dot_general(piece[...], act[:, pl.ds(start, rows)], NT, preferred_element_type=F32)
            total = part if total is None else total + part
        raw[:, here] = total


def decay_kernel(offsets, place, raw, rate, factor, log_row, log_col, gain_col):
    mine = place[2]
    heads, tokens = raw.shape[1], raw.shape[2]
    lane = lax.broadcasted_iota(jnp.int32, (heads, tokens), 1)
    steps, logs, totals = [], [], []
    for at in range(len(offsets)):
        value = raw[at]
        step = jnp.maximum(value, 0.0) + jnp.log1p(jnp.exp(-jnp.abs(value)))
        log = step * (-LOG2E * rate[...])
        shift = 1
        while shift < tokens:
            log = log + jnp.where(lane >= shift, pltpu.roll(log, shift, 1), 0.0)
            shift *= 2
        steps.append(step)
        logs.append(log)
        totals.append(log[:, tokens - 1 :])
    for at, offset in enumerate(offsets):
        here = slice(at * tokens, (at + 1) * tokens)
        if at == 0:
            factor[:, here] = steps[0]
            continue
        between = jnp.zeros_like(totals[0])
        first = mine ^ offset
        for other, distance in enumerate(offsets):
            block = mine ^ distance
            inside = jnp.logical_and(block > first, block < mine)
            between += jnp.where(inside, totals[other], 0.0)
        factor[:, here] = steps[at] * jnp.exp2(totals[at] - logs[at] + between)
    log_row[...] = logs[0]
    wide = jnp.concatenate([logs[0], jnp.zeros((128 - heads, tokens), F32)], axis=0)
    turned = wide.T
    log_col[...] = turned
    gain_col[...] = jnp.exp2(turned)


def causal_of(tokens):
    row = lax.broadcasted_iota(jnp.int32, (tokens, tokens), 0)
    col = lax.broadcasted_iota(jnp.int32, (tokens, tokens), 1)
    return col <= row


def folded(combine, value):
    parts = [value[:, i : i + 128] for i in range(0, value.shape[1], 128)]
    return functools.reduce(combine, parts)


SCALE = LOG2E * HEAD_DIM ** -0.5


def teacher_kernel(offsets, place, query, keys, norm, scores, top, mass):
    tokens = query.shape[0]
    mine = place[2]
    own = lax.dot_general(query[...], keys[pl.ds(0, tokens), :], NT, preferred_element_type=F32) * SCALE
    own = jnp.where(causal_of(tokens), own, -jnp.inf)
    scores[0] = own
    top[...] = folded(jnp.maximum, own)
    for at in range(1, len(offsets)):

        @pl.when((mine ^ offsets[at]) < mine)
        def _(at=at):
            value = lax.dot_general(
                query[...], keys[pl.ds(at * tokens, tokens), :], NT, preferred_element_type=F32
            ) * SCALE
            scores[at] = value
            top[...] = jnp.maximum(top[...], folded(jnp.maximum, value))

    peak = jnp.max(top[...], axis=1, keepdims=True)
    mass[...] = folded(jnp.add, jnp.exp2(scores[0] - peak))
    for at in range(1, len(offsets)):

        @pl.when((mine ^ offsets[at]) < mine)
        def _(at=at):
            mass[...] += folded(jnp.add, jnp.exp2(scores[at] - peak))

    total = jnp.sum(mass[...], axis=1, keepdims=True)
    norm[0] = jnp.broadcast_to(peak + jnp.log2(total), (tokens, 128))


def loss_kernel(
    offsets, first, heads, place, query, kept, came_low, came_high, keys, inputs, norm, factor, log_row, log_col, gain_col, out, sums
):
    tokens = query.shape[0]
    mine = place[2]
    causal = causal_of(tokens)
    for i in range(heads):
        head = first + i
        cols = slice(i * HEAD_DIM, (i + 1) * HEAD_DIM)
        asked = query[:, cols]
        came = jnp.concatenate([came_low[:, cols], came_high[:, cols]], axis=0)
        read = (kept[:, cols] + came.astype(F32)).astype(BF16)
        lse = norm[i]
        wide = tokens // 128
        lse_wide = jnp.concatenate([lse] * wide, axis=1)

        def pair(at):
            rows = pl.ds(at * tokens, tokens)
            score = lax.dot_general(asked, keys[rows, :], NT, preferred_element_type=F32) * SCALE
            inner = lax.dot_general(read, inputs[rows, :], NT, preferred_element_type=F32)
            return jnp.exp2(score - lse_wide), inner * factor[head : head + 1, at * tokens : (at + 1) * tokens]

        prob, inner = pair(0)
        gap = log_col[:, head : head + 1] - log_row[head : head + 1, :]
        diff = jnp.where(causal, prob - inner * jnp.exp2(gap), 0.0)
        sums[...] = folded(jnp.add, diff * diff)
        gain = gain_col[:, head : head + 1]
        for at in range(1, len(offsets)):

            @pl.when((mine ^ offsets[at]) < mine)
            def _(at=at):
                prob, inner = pair(at)
                diff = prob - inner * gain
                sums[...] += folded(jnp.add, diff * diff)

        out[i] = jnp.sum(sums[...].T, axis=0, keepdims=True)


class Order:
    def __init__(self):
        self.last = ()

    def gate(self, value):
        if not self.last:
            return value
        value, self.last = lax.optimization_barrier((value, self.last))
        return value

    def wait(self, value):
        value, _ = lax.optimization_barrier((value, self.last))
        self.last = tuple(jax.tree.leaves(value))
        return value


def xor_sums(offset_size, scale):
    got = [0]
    d = 1
    while d < offset_size:
        got += [g ^ (d * scale) for g in got]
        d *= 2
    return got


def spread(pieces, axis):
    got = list(pieces)
    d = 1
    while d < lax.axis_size(axis):
        got += [xor_permute(g, axis, d) for g in got]
        d *= 2
    return got


def local(hidden_in, teacher_query, teacher_key, proj_c, proj_b, proj_step, decay_rate):
    _, tokens, _ = hidden_in.shape
    hidden = hidden_in[0]
    rows, width = proj_c.shape
    head_count = proj_step.shape[1]
    seq, sides = lax.axis_size("seq"), lax.axis_size("head")
    half = seq // 2
    copies_y, copies_c = lax.axis_size("groups"), lax.axis_size("batch")
    copies = copies_y * copies_c
    z, x = lax.axis_index("seq"), lax.axis_index("head")
    side = z // half
    quarter = lax.axis_index("groups") * copies_c + lax.axis_index("batch")
    place = jnp.stack([z % half, quarter, z]).astype(jnp.int32)
    per_model_group = HEADS // KV_HEADS
    group_count = max(1, head_count // per_model_group)
    per_group = head_count // group_count
    group_first = x * head_count // per_model_group
    width_b = group_count * HEAD_DIM
    offsets = [0, half]
    for d in range(1, half):
        offsets += [d, d ^ half]
    padded = max(16, head_count)
    span = seq * tokens
    chunk = max(HEAD_DIM, width // 4)
    count = width // chunk
    heads = chunk // HEAD_DIM
    part = rows // copies
    turns = xor_sums(copies_y, copies_c)
    turns = [t ^ c for c in xor_sums(copies_c, 1) for t in turns]
    model = [(d, t) for d in range(1, half) for t in turns]
    query = teacher_query[0]
    order = Order()

    def over_half(value):
        return [xor_permute(value, "seq", d) for d in range(1, half)]

    def start_weights(first, last):
        piece = lax.dynamic_slice(proj_c, (quarter * part, first * chunk), (part, (last - first) * chunk))
        if first == 0:
            extra = lax.dynamic_slice(proj_b, (quarter * part, group_first * HEAD_DIM), (part, width_b))
            piece = jnp.concatenate([piece, extra], axis=1)
        return over_half(piece)

    def partial(acts, j):
        first, _, pieces = next(w for w in weights if w[0] <= j < w[1])
        return order.wait(
            call(
                functools.partial(partial_kernel, model, len(acts)),
                (order.gate(place), *[a for a, _ in acts], proj_c, *pieces),
                [smem()]
                + [whole(a.shape) for a, _ in acts]
                + [columns(rows, chunk, j)]
                + [columns(part, chunk, j - first)] * len(model),
                [jax.ShapeDtypeStruct((a.shape[0], chunk), dtype) for a, dtype in acts],
                "partial",
            )
        )

    def send(value):
        return xor_permute(value, "seq", half)

    def teacher(first, number):
        return pl.pallas_call(
            functools.partial(teacher_kernel, offsets),
            grid=(number,),
            in_specs=[
                smem(),
                pl.BlockSpec((tokens, HEAD_DIM), lambda h: (0, first + h)),
                pl.BlockSpec((span, HEAD_DIM), lambda h: (0, (first + h) // per_group)),
            ],
            out_specs=pl.BlockSpec((1, tokens, 128), lambda h: (h, 0, 0)),
            out_shape=jax.ShapeDtypeStruct((number, tokens, 128), F32),
            scratch_shapes=[
                pltpu.VMEM((seq, tokens, tokens), F32),
                pltpu.VMEM((tokens, 128), F32),
                pltpu.VMEM((tokens, 128), F32),
            ],
            compiler_params=pltpu.CompilerParams(vmem_limit_bytes=VMEM_LIMIT),
            name="teacher",
        )(order.gate(place), query, keys)

    spans = [(0, 1), (1, 2), (2, 4)]
    weights = []
    local_key = lax.dynamic_slice_in_dim(teacher_key[0], group_first * HEAD_DIM, width_b, 1)
    local_b = lax.dynamic_slice_in_dim(proj_b, group_first * HEAD_DIM, width_b, 1)
    step_t = jnp.pad(proj_step.T, ((0, padded - head_count), (0, 0)))

    if sides == 2:
        cut = tokens // 4
        spots = [(i, j) for i in range(seq) for j in range(2)]
        flat = lambda i, j: i * 2 + j
        both = ("seq", "head")
        level = side == x
        even = [s for s in spots if s[0] // half == s[1]]
        odd = [s for s in spots if s[0] // half != s[1]]
        over = lambda value, group: lax.ppermute(value, both, [(flat(i, j), flat(i ^ half, j)) for i, j in group])
        row = [hidden[i * cut : (i + 1) * cut] for i in range(4)]
        across = lambda value: lax.ppermute(value, both, [(flat(i, j), flat(i, 1 - j)) for i, j in even])
        direct = [over(row[0], odd), over(row[2], odd)]
        swapped = [xor_permute(row[1], "head", 1), xor_permute(row[3], "head", 1)]
        key_half = xor_permute(local_key, "seq", half)
        w0 = start_weights(0, 1)
        w1 = start_weights(1, 2)
        w2 = start_weights(2, 4)
        step_rest = over_half(step_t)
        swapped[0] = order.wait(swapped[0])
        relayed = [over(swapped[0], even), None]
        swapped[1] = order.wait(swapped[1])
        relayed[1] = over(swapped[1], even)
        moved = [across(order.gate(row[0])), None]
        w0 = spread(order.wait(w0), "groups")

        def swap(i):
            got = order.wait((direct[i], relayed[i]))
            first = jnp.where(level, got[0], got[1])
            return first, xor_permute(first, "head", 1)

        def join(first, second):
            second = order.wait(second)
            return jnp.concatenate([jnp.where(level, first, second), jnp.where(level, second, first)], axis=0)

        first0, second0 = swap(0)
        moved[0] = order.wait(moved[0])
        moved[1] = across(order.gate(row[2]))
        w0 = spread(order.wait(w0), "batch")
        w1 = spread(order.wait(w1), "groups")
        others = [join(first0, second0)]
        weights.append((0, 1, order.wait(w0)))
        arrived = {(0, 0): send(partial([(others[0], BF16)], 0)[0])}
        first1, second1 = swap(1)
        moved[1] = order.wait(moved[1])
        w1 = spread(order.wait(w1), "batch")
        key_half = order.wait(key_half)
        key_pair = jnp.concatenate([local_key, key_half], axis=0)
        key_rest = over_half(key_pair)
        w2 = spread(order.wait(w2), "groups")
        mine = jnp.where(
            level, hidden, jnp.concatenate([moved[0], swapped[0], moved[1], swapped[1]], axis=0)
        )
        weights.append((1, 2, order.wait(w1)))
        arrived[0, 1] = send(partial([(others[0], BF16)], 1)[0])
        step_rest = order.wait(step_rest)
        others.append(join(first1, second1))
        norms = []
    else:
        full = lax.all_gather(hidden, "head", axis=1, tiled=True)
        span_half = full.shape[1] // 2
        share = tokens // sides
        mine = lax.dynamic_slice_in_dim(full, side * span_half, span_half, 1)
        leaving = lax.dynamic_slice(full, (x * share, (1 - side) * span_half), (share, span_half))
        came = lax.all_gather(xor_permute(leaving, "seq", half), "head", axis=0, tiled=True)
        others = [came[: tokens // 2], came[tokens // 2 :]]
        key_pair = jnp.concatenate([local_key, xor_permute(local_key, "seq", half)], axis=0)
        step_rest = over_half(step_t)
        weights.append((0, 1, spread(spread(start_weights(0, 1), "groups"), "batch")))
        weights.append((1, 2, spread(spread(start_weights(1, 2), "groups"), "batch")))
        w2 = spread(start_weights(2, 4), "groups")
        norms = []
        key_rest = over_half(key_pair)
        arrived = {(0, j): send(partial([(others[0], BF16)], j)[0]) for j in range(2)}

    extra_out = [
        jax.ShapeDtypeStruct((2 * tokens, width_b), F32),
        jax.ShapeDtypeStruct((2 * tokens, width_b), BF16),
        jax.ShapeDtypeStruct((padded, 2 * tokens), F32),
    ]
    extra_cols = [g[:, chunk:] for g in weights[0][2]]
    acts = (mine, *others)
    full, rounded, raw = order.wait(
        call(
            functools.partial(extra_kernel, model, list(range(half))),
            (order.gate(place), *acts, local_b, *extra_cols, step_t, *step_rest),
            [smem()]
            + [whole(a.shape) for a in acts]
            + [whole(local_b.shape)]
            + [whole((part, width_b))] * len(model)
            + [whole(step_t.shape)] * half,
            extra_out,
            "extra",
        )
    )
    came = send(rounded)
    came_raw = send(raw)
    kept = []
    for j in range(2):
        leaving, stays = partial([(others[1], BF16), (mine, F32)], j)
        arrived[1, j] = send(leaving)
        kept.append(stays)
    w2 = spread(order.wait(w2), "batch")
    key_rest = order.wait(key_rest)
    keys = jnp.concatenate([key_pair] + key_rest, axis=0)
    norms.append(order.wait(teacher(0, heads)))
    came, came_raw = order.wait((came, came_raw))
    came = came.astype(F32)
    inputs_pair = (full + jnp.concatenate([came[tokens:], came[:tokens]], axis=0)).astype(BF16)
    raw_pair = raw + jnp.concatenate([came_raw[:, tokens:], came_raw[:, :tokens]], axis=1)
    inputs_rest = over_half(inputs_pair)
    raw_rest = over_half(raw_pair)
    norms.append(order.wait(teacher(heads, heads)))
    weights.append((2, 4, order.wait(w2)))
    for j in range(2, count):
        if j == count - 1:
            inputs_rest, raw_rest = order.wait((inputs_rest, raw_rest))
        low, high, stays = partial([(others[0], BF16), (others[1], BF16), (mine, F32)], j)
        arrived[0, j], arrived[1, j] = send(low), send(high)
        kept.append(stays)
        norms.append(order.wait(teacher(j * heads, heads)))
    inputs = jnp.concatenate([inputs_pair] + inputs_rest, axis=0)
    raw_all = jnp.stack([r[:, i * tokens : (i + 1) * tokens] for r in [raw_pair] + raw_rest for i in range(2)])
    rate = jnp.pad(decay_rate, (0, padded - head_count))[:, None]
    factor, log_row, log_col, gain_col = call(
        functools.partial(decay_kernel, offsets),
        (order.gate(place), raw_all, rate),
        [smem(), whole(raw_all.shape), whole(rate.shape)],
        [
            jax.ShapeDtypeStruct((padded, span), F32),
            jax.ShapeDtypeStruct((padded, tokens), F32),
            jax.ShapeDtypeStruct((tokens, 128), F32),
            jax.ShapeDtypeStruct((tokens, 128), F32),
        ],
        "decay",
    )
    factor = order.wait(factor)

    losses = []
    for j in range(count):
        group = j * heads // per_group
        came = order.wait((arrived[0, j], arrived[1, j]))
        losses.append(
            order.wait(
                call(
                    functools.partial(loss_kernel, offsets, j * heads, heads),
                    (place, query, kept[j], *came, keys, inputs, norms[j], factor, log_row, log_col, gain_col),
                    [
                        smem(),
                        columns(tokens, chunk, j),
                        whole((tokens, chunk)),
                        whole((tokens // 2, chunk)),
                        whole((tokens // 2, chunk)),
                        columns(span, HEAD_DIM, group),
                        columns(span, HEAD_DIM, group),
                        whole(norms[j].shape),
                        whole(factor.shape),
                        whole(log_row.shape),
                        whole(log_col.shape),
                        whole(gain_col.shape),
                    ],
                    [jax.ShapeDtypeStruct((heads, 1, tokens), F32)],
                    "loss",
                    [pltpu.VMEM((tokens, 128), F32)],
                )[0]
            )
        )
    return jnp.concatenate(losses, axis=0).reshape(1, head_count, tokens)


def solution(mesh):
    in_specs = (
        P(("groups", "batch"), "seq", "head"),
        P(("groups", "batch"), "seq", "head"),
        P(("groups", "batch"), "seq", None),
        P("seq", "head"),
        P("seq", None),
        P("seq", "head"),
        P("head"),
    )
    out_specs = P(("groups", "batch"), "head", "seq")
    return jax.shard_map(local, mesh=mesh, in_specs=in_specs, out_specs=out_specs, check_vma=False)
```

time: 273 us -> 192 us (0.70)
  waiting for transfers between devices: 138 us -> 57.3 us
  starting transfers between devices: 48.2 us -> 45.2 us
    ppermute x29 -> x31, waiting for transfers between devices: 116 us -> 34.8 us  [xor_permute(): return lax.ppermute(value, axis, [(i, i ^ offset) for i in range(size)])]
    ppermute x29 -> x31, starting transfers between devices: 42.4 us -> 35.1 us  [xor_permute(): return lax.ppermute(value, axis, [(i, i ^ offset) for i in range(size)])]
    ppermute x3 -> x6, starting transfers between devices: 5.79 us -> 10.1 us  [the longest x4 7.5 us: local(): lax.ppermute(value, both, [(flat(i, j), flat(i ^ half, j)) for i, j in gr...]
    unnamed x60, local copies, waits for them, and re-layouts: 1.73 us -> 5.04 us
    pallas_call x1 -> x4, Pallas kernels: 19.4 us -> 20.9 us  [teacher(): pl.pallas_call(functools.partial(teacher_kernel, offsets), grid=(number,)...]
    pallas_call x14 -> x12, Pallas kernels: 48.1 us -> 47.2 us  [call(): pl.pallas_call(kernel, grid=(1,), in_specs=in_specs, out_specs=tuple((who...]
    ppermute x3 -> x6, waiting for transfers between devices: 22.3 us -> 22.5 us  [the longest x4 16.8 us: local(): lax.ppermute(value, both, [(flat(i, j), flat(i ^ half, j)) for i, j in gr...]
  transfers between devices with their start and end apart: 32 -> 37, of which waited for: 13 -> 12; matrix products, arithmetic and copies ran while one was open for 5% -> 6% of each run, Pallas kernels for 23% -> 33%
where the time goes in v2:
time: 192 us; the launch traced here: 191 us
  Pallas kernels  68.2 us (36%)
  waiting for transfers between devices  57.3 us (30%)
  starting transfers between devices  45.2 us (24%)
  local copies, waits for them, and re-layouts  13.2 us (7%)
  other arithmetic  6.64 us (3%)
    pallas_call x12, Pallas kernels, call(): pl.pallas_call(kernel, grid=(1,), in_specs=in_specs, out_specs=tuple((who...  47.2 us
    ppermute x31, starting transfers between devices, xor_permute(): return lax.ppermute(value, axis, [(i, i ^ offset) for i in range(size)])  35.1 us
    ppermute x31, waiting for transfers between devices, xor_permute(): return lax.ppermute(value, axis, [(i, i ^ offset) for i in range(size)])  34.8 us
    pallas_call x4, Pallas kernels, teacher(): pl.pallas_call(functools.partial(teacher_kernel, offsets), grid=(number,)...  20.9 us
    ppermute x4, waiting for transfers between devices, local(): lax.ppermute(value, both, [(flat(i, j), flat(i ^ half, j)) for i, j in gr...  16.8 us
    ppermute x4, starting transfers between devices, local(): lax.ppermute(value, both, [(flat(i, j), flat(i ^ half, j)) for i, j in gr...  7.5 us
    ppermute x2, waiting for transfers between devices, local(): lax.ppermute(value, both, [(flat(i, j), flat(i, 1 - j)) for i, j in even])  5.7 us
    unnamed x60, local copies, waits for them, and re-layouts  5.04 us
  transfers between devices with their start and end apart: 37, of which 12 were waited for; matrix products, arithmetic and copies ran while one was open for 6% of the time, Pallas kernels for 33%

profile of v2, /device:TPU:24, one launch (start us, length us, event | category | flops | bytes accessed | tf_op | source)
XLA Modules:
  0.0 191.3 jit_solution(12565692077921350103)
XLA Ops:
  0.0 2.8 %slice_bitcast_fusion = (bf16[64,4096]{1,0:T(8,128)(2,1)}, bf16[64,4096]{1,0:T(8,128)(2,1)S(1)}, bf16[64,4096]{1,0:T(8,128)(2,1)}, bf16[64,4096]{1,0:T(8,128)(2,1)}) fusion(bf16[1,256,4096]{2,1,0:T(8,128)(2,1)} %param.7), kind=kLoop, calls=%fused_computation.8 | loop fusion | bytes 4194304 | tf_op jit(solution)/shard_map/slice | solution.py:340
  2.8 1.5 collective-permute-start.2
  4.3 2.1 %constant_dynamic-slice_fusion.3 = (bf16[512,512]{1,0:T(8,128)(2,1)}, bf16[512,512]{1,0:T(8,128)(2,1)S(1)}) fusion(bf16[2048,2048]{1,0:T(8,128)(2,1)} %rest_3_.3, s32[]{:T(128)} %select_n.64), kind=kLoop, calls=%fused_computation.31 | loop fusion | bytes 2097156 | tf_op jit(solution)/shard_map/dynamic_slice | solution.py:281
  6.5 0.5 collective-permute-start.4
  7.0 0.5 collective-permute-start.1
  7.6 2.7 %collective-permute-start.8 = (bf16[64,4096]{1,0:T(8,128)(2,1)}, bf16[64,4096]{1,0:T(8,128)(2,1)}, u32[]{:S(2)}, u32[]{:S(2)}) collective-permute-start(bf16[64,4096]{1,0:T(8,128)(2,1)} %get-tuple-element.98), channel_id=1, source_target_pairs={{2,10},{6,14},{8,0},{12,4},{3,11},{7,15},{9,1},{13,5},{18,26},{22,... | collective-permute-start | bytes 1572872 | tf_op jit(solution)/shard_map/ppermute | solution.py:339
  10.2 7.4 %collective-permute-done.2 = bf16[64,4096]{1,0:T(8,128)(2,1)S(1)} collective-permute-done((bf16[64,4096]{1,0:T(8,128)(2,1)S(1)}, bf16[64,4096]{1,0:T(8,128)(2,1)S(1)}, u32[]{:S(2)}, u32[]{:S(2)}) %collective-permute-start.2) | collective-permute-done | bytes 524320 | tf_op jit(solution)/shard_map/ppermute | solution.py:24
  17.6 1.3 collective-permute-start.9
  18.9 0.5 collective-permute-start.11
  19.4 8.4 %collective-permute-done.1 = bf16[64,4096]{1,0:T(8,128)(2,1)} collective-permute-done((bf16[64,4096]{1,0:T(8,128)(2,1)}, bf16[64,4096]{1,0:T(8,128)(2,1)}, u32[]{:S(2)}, u32[]{:S(2)}) %collective-permute-start.1) | collective-permute-done | bytes 524320 | tf_op jit(solution)/shard_map/ppermute | solution.py:24
  27.8 2.3 %collective-permute-start = (bf16[64,4096]{1,0:T(8,128)(2,1)}, bf16[64,4096]{1,0:T(8,128)(2,1)S(1)}, u32[]{:S(2)}, u32[]{:S(2)}) collective-permute-start(bf16[64,4096]{1,0:T(8,128)(2,1)} %get-tuple-element.100), channel_id=1, source_target_pairs={{2,10},{6,14},{8,0},{12,4},{3,11},{7,15},{9,1},{13,5},{18,26},{22,... | collective-permute-start | bytes 1572872 | tf_op jit(solution)/shard_map/ppermute | solution.py:339
  30.1 1.5 collective-permute-done.4.rest_2_.rest_3_
  31.6 1.3 collective-permute-start.15
  32.9 3.5 %collective-permute-done.8 = bf16[64,4096]{1,0:T(8,128)(2,1)} collective-permute-done((bf16[64,4096]{1,0:T(8,128)(2,1)}, bf16[64,4096]{1,0:T(8,128)(2,1)}, u32[]{:S(2)}, u32[]{:S(2)}) %collective-permute-start.8) | collective-permute-done | bytes 524320 | tf_op jit(solution)/shard_map/ppermute | solution.py:339
  36.4 1.5 collective-permute-start.5
  37.9 5.6 %collective-permute-done.9 = bf16[64,4096]{1,0:T(8,128)(2,1)} collective-permute-done((bf16[64,4096]{1,0:T(8,128)(2,1)S(1)}, bf16[64,4096]{1,0:T(8,128)(2,1)}, u32[]{:S(2)}, u32[]{:S(2)}) %collective-permute-start.9) | collective-permute-done | bytes 524320 | tf_op jit(solution)/shard_map/ppermute | solution.py:339
  43.6 1.1 broadcast_select_fusion.5
  44.7 9.6 %collective-permute-start.10 = (bf16[64,4096]{1,0:T(8,128)(2,1)S(1)}, bf16[64,4096]{1,0:T(8,128)(2,1)S(1)}, u32[]{:S(2)}, u32[]{:S(2)}) collective-permute-start(bf16[64,4096]{1,0:T(8,128)(2,1)S(1)} %broadcast_select_fusion.5), channel_id=1, source_target_pairs={{0,2},{2,0},{1,3},{3,1},{4,6},{6,4},{5,7},{7,5},{8,10},{10,8},{9,1... | collective-permute-start | bytes 1572872 | tf_op jit(solution)/shard_map/ppermute | solution.py:24
  54.3 1.3 constant_dynamic-slice_fusion.2
  55.8 3.0 %collective-permute-done.15 = bf16[64,4096]{1,0:T(8,128)(2,1)S(1)} collective-permute-done((bf16[64,4096]{1,0:T(8,128)(2,1)}, bf16[64,4096]{1,0:T(8,128)(2,1)S(1)}, u32[]{:S(2)}, u32[]{:S(2)}) %collective-permute-start.15) | collective-permute-done | bytes 524320 | tf_op jit(solution)/shard_map/ppermute | solution.py:341
  58.8 1.3 collective-permute-start.3
  60.2 4.2 %collective-permute-done.10 = bf16[64,4096]{1,0:T(8,128)(2,1)S(1)} collective-permute-done((bf16[64,4096]{1,0:T(8,128)(2,1)S(1)}, bf16[64,4096]{1,0:T(8,128)(2,1)S(1)}, u32[]{:S(2)}, u32[]{:S(2)}) %collective-permute-start.10) | collective-permute-done | bytes 524320 | tf_op jit(solution)/shard_map/ppermute | solution.py:24
  64.7 2.0 %collective-permute-done.7.rest_5_.rest_6_ = bf16[512,768]{1,0:T(8,128)(2,1)S(1)} collective-permute-done((bf16[512,768]{1,0:T(8,128)(2,1)S(1)}, bf16[512,768]{1,0:T(8,128)(2,1)S(1)}, u32[]{:S(2)}, u32[]{:S(2)}) %collective-permute-start.7) | collective-permute-done | bytes 786464 | tf_op jit(solution)/shard_map/ppermute | solution.py:24
  66.7 1.3 collective-permute-start.16
  68.0 2.5 %partial.6 = bf16[128,512]{1,0:T(8,128)(2,1)S(1)} custom-call(s32[3]{0:T(128)S(1)} %pad_add_fusion.place, bf16[128,4096]{1,0:T(8,128)(2,1)S(1)} %pad_maximum_fusion.rest_0_.act_low, bf16[2048,2048]{1,0:T(8,128)(2,1)} %rest_3_.3, bf16[512,768]{1,0:T(8,128)(2,1)S(1)} %collective-permute-done.4.rest_2_.rest_3_, ...), custom_call_target="tpu_custom_call" | custom-call | tf_op jit(solution)/shard_map/partial/pallas_call | solution.py:40
  70.5 1.6 collective-permute-start.14
  72.1 7.7 %collective-permute-done.3 = bf16[64,4096]{1,0:T(8,128)(2,1)S(1)} collective-permute-done((bf16[64,4096]{1,0:T(8,128)(2,1)}, bf16[64,4096]{1,0:T(8,128)(2,1)S(1)}, u32[]{:S(2)}, u32[]{:S(2)}) %collective-permute-start.3) | collective-permute-done | bytes 524320 | tf_op jit(solution)/shard_map/ppermute | solution.py:339
  79.8 2.7 %collective-permute-done.16 = bf16[64,4096]{1,0:T(8,128)(2,1)S(1)} collective-permute-done((bf16[64,4096]{1,0:T(8,128)(2,1)S(1)}, bf16[64,4096]{1,0:T(8,128)(2,1)S(1)}, u32[]{:S(2)}, u32[]{:S(2)}) %collective-permute-start.16) | collective-permute-done | bytes 524320 | tf_op jit(solution)/shard_map/ppermute | solution.py:341
  82.5 2.0 %collective-permute-done.14.rest_3_.rest_4_ = bf16[512,512]{1,0:T(8,128)(2,1)S(1)} collective-permute-done((bf16[512,512]{1,0:T(8,128)(2,1)S(1)}, bf16[512,512]{1,0:T(8,128)(2,1)S(1)}, u32[]{:S(2)}, u32[]{:S(2)}) %collective-permute-start.14) | collective-permute-done | bytes 524320 | tf_op jit(solution)/shard_map/ppermute | solution.py:24
  84.5 0.5 collective-permute-start.18
  85.0 2.4 %collective-permute-start.12 = (bf16[64,4096]{1,0:T(8,128)(2,1)S(1)}, bf16[64,4096]{1,0:T(8,128)(2,1)S(1)}, u32[]{:S(2)}, u32[]{:S(2)}) collective-permute-start(bf16[64,4096]{1,0:T(8,128)(2,1)S(1)} %broadcast_select_fusion.2), channel_id=1, source_target_pairs={{0,2},{2,0},{1,3},{3,1},{4,6},{6,4},{5,7},{7,5},{8,10},{10,8},{9,1... | collective-permute-start | bytes 1572872 | tf_op jit(solution)/shard_map/ppermute | solution.py:24
  87.4 3.1 %maximum_select_fusion.act_own.rest_1_.rest_2_ = bf16[256,4096]{1,0:T(8,128)(2,1)} fusion(bf16[64,4096]{1,0:T(8,128)(2,1)} %collective-permute-done.1, bf16[64,4096]{1,0:T(8,128)(2,1)S(1)} %collective-permute-done.16, bf16[64,4096]{1,0:T(8,128)(2,1)S(1)} %collective-permute-done.2, bf16[64,4096]{1,0:T(8,128)(2,1)S(1)} %collective-permute-done.15, ...), kind=kLoop, calls=%fused_computation | loop fusion | flops 9437184 | bytes 6291457 | tf_op jit(solution)/shard_map/jit(_where)/select_n | solution.py:380
  90.7 0.7 copy-done.20
  91.5 9.2 %collective-permute-done.19.rest_4_ = bf16[512,1024]{1,0:T(8,128)(2,1)} collective-permute-done((bf16[512,1024]{1,0:T(8,128)(2,1)S(1)}, bf16[512,1024]{1,0:T(8,128)(2,1)}, u32[]{:S(2)}, u32[]{:S(2)}) %collective-permute-start.19) | collective-permute-done | bytes 1048608 | tf_op jit(solution)/shard_map/ppermute | solution.py:24
  100.7 1.5 collective-permute-start.26
  102.2 0.7 pad_maximum_fusion.5
  103.0 2.7 %partial.7 = bf16[128,512]{1,0:T(8,128)(2,1)S(1)} custom-call(s32[3]{0:T(128)S(1)} %pad_add_fusion.place, bf16[128,4096]{1,0:T(8,128)(2,1)S(1)} %pad_maximum_fusion.rest_0_.act_low, bf16[2048,2048]{1,0:T(8,128)(2,1)} %rest_3_.3, bf16[512,512]{1,0:T(8,128)(2,1)S(1)} %copy-done.10, bf16[512,512]{1,0:T(8,128)(2,1)S(1)} %collective-permute-done.14.rest_3_.rest_4_, ...), custom_call_target="tpu_custom_call" | custom-call | tf_op jit(solution)/shard_map/partial/pallas_call | solution.py:40
  106.0 4.7 %extra.1 = (f32[512,256]{1,0:T(8,128)S(1)}, bf16[512,256]{1,0:T(8,128)(2,1)}, f32[16,512]{1,0:T(8,128)S(1)}) custom-call(s32[3]{0:T(128)S(1)} %pad_add_fusion.place, bf16[256,4096]{1,0:T(8,128)(2,1)} %maximum_select_fusion.act_own.rest_1_.rest_2_, bf16[128,4096]{1,0:T(8,128)(2,1)S(1)} %pad_maximum_fusion.rest_0_.act_low, ...), custom_call_target="tpu_custom_call" | custom-call | tf_op jit(solution)/shard_map/extra/pallas_call | solution.py:40
  110.7 0.8 copy-done.18
  111.6 2.9 %collective-permute-start.21 = (bf16[128,512]{1,0:T(8,128)(2,1)S(1)}, bf16[128,512]{1,0:T(8,128)(2,1)S(1)}, u32[]{:S(2)}, u32[]{:S(2)}) collective-permute-start(bf16[128,512]{1,0:T(8,128)(2,1)S(1)} %partial.6), channel_id=1, source_target_pairs={{0,8},{4,12},{8,0},{12,4},{1,9},{5,13},{9,1},{13,5},{2,10},{6,14},... | collective-permute-start | bytes 393224 | tf_op jit(solution)/shard_map/ppermute | solution.py:24
  114.6 1.1 copy-done.4
  115.7 1.1 copy-done.6
  116.9 1.1 copy-done.8
  118.0 4.2 %partial.8 = (bf16[128,512]{1,0:T(8,128)(2,1)S(1)}, f32[256,512]{1,0:T(8,128)S(1)}) custom-call(s32[3]{0:T(128)S(1)} %pad_add_fusion.place, bf16[128,4096]{1,0:T(8,128)(2,1)S(1)} %pad_maximum_fusion.1.act_high.rest_0_.rest_1_, bf16[256,4096]{1,0:T(8,128)(2,1)} %maximum_select_fusion.act_own.rest_1_.rest_2_, bf16[2048,2048]{1,0:T(8,128)(2,1)} %rest_3_.3, ...), custom_call_target="tpu_custom_call" | custom-call | tf_op jit(solution)/shard_map/partial/pallas_call | solution.py:40
  122.3 3.5 %partial.9 = (bf16[128,512]{1,0:T(8,128)(2,1)S(1)}, f32[256,512]{1,0:T(8,128)S(1)}) custom-call(s32[3]{0:T(128)S(1)} %pad_add_fusion.place, bf16[128,4096]{1,0:T(8,128)(2,1)S(1)} %pad_maximum_fusion.1.act_high.rest_0_.rest_1_, bf16[256,4096]{1,0:T(8,128)(2,1)S(1)} %copy-done.1, bf16[2048,2048]{1,0:T(8,128)(2,1)} %rest_3_.3, bf16[512,512]{1,0:T(8,128)(2,1)S(1)} %copy-done.11, ...), custom_call_target="tpu_custom_call" | custom-call | tf_op jit(solution)/shard_map/partial/pallas_call | solution.py:40
  125.9 1.0 pad_maximum_fusion.3.keys
  127.5 5.2 %teacher.4.norm = f32[4,256,128]{2,1,0:T(8,128)S(1)} custom-call(s32[3]{0:T(128)S(1)} %pad_add_fusion.place, bf16[256,2048]{1,0:T(8,128)(2,1)S(1)} %bitcast.28, bf16[1024,256]{1,0:T(8,128)(2,1)S(1)} %pad_maximum_fusion.3.keys), custom_call_target="tpu_custom_call" | custom-call | tf_op jit(solution)/shard_map/teacher/pallas_call | solution.py:306
  132.8 1.0 fusion.1
  133.9 1.0 collective-permute-start.27
  134.9 1.2 collective-permute-start.28
  136.1 5.2 %teacher.5.norm = f32[4,256,128]{2,1,0:T(8,128)S(1)} custom-call(s32[3]{0:T(128)S(1)} %pad_add_fusion.place, bf16[256,2048]{1,0:T(8,128)(2,1)S(1)} %bitcast.29, bf16[1024,256]{1,0:T(8,128)(2,1)S(1)} %pad_maximum_fusion.3.keys), custom_call_target="tpu_custom_call" | custom-call | tf_op jit(solution)/shard_map/teacher/pallas_call | solution.py:306
  141.4 2.9 %collective-permute-start.32 = (bf16[128,512]{1,0:T(8,128)(2,1)S(1)}, bf16[128,512]{1,0:T(8,128)(2,1)S(1)}, u32[]{:S(2)}, u32[]{:S(2)}) collective-permute-start(bf16[128,512]{1,0:T(8,128)(2,1)S(1)} %get-tuple-element.121), channel_id=1, source_target_pairs={{0,8},{4,12},{8,0},{12,4},{1,9},{5,13},{9,1},{13,5},{2,10},{6,14},... | collective-permute-start | bytes 393224 | tf_op jit(solution)/shard_map/ppermute | solution.py:24
  144.3 5.0 %partial.10 = (bf16[128,512]{1,0:T(8,128)(2,1)S(1)}, bf16[128,512]{1,0:T(8,128)(2,1)S(1)}, f32[256,512]{1,0:T(8,128)S(1)}) custom-call(s32[3]{0:T(128)S(1)} %pad_add_fusion.place, bf16[128,4096]{1,0:T(8,128)(2,1)S(1)} %pad_maximum_fusion.rest_0_.act_low, bf16[128,4096]{1,0:T(8,128)(2,1)S(1)} %pad_maximum_fusion.1.act_high.rest_0_.rest_1_, ...), custom_call_target="tpu_custom_call" | custom-call | tf_op jit(solution)/shard_map/partial/pallas_call | solution.py:40
  149.3 5.3 %teacher.6.norm = f32[4,256,128]{2,1,0:T(8,128)S(1)} custom-call(s32[3]{0:T(128)S(1)} %pad_add_fusion.place, bf16[256,2048]{1,0:T(8,128)(2,1)S(1)} %bitcast.30, bf16[1024,256]{1,0:T(8,128)(2,1)S(1)} %pad_maximum_fusion.3.keys), custom_call_target="tpu_custom_call" | custom-call | tf_op jit(solution)/shard_map/teacher/pallas_call | solution.py:306
  154.7 2.9 %collective-permute-start.33 = (bf16[128,512]{1,0:T(8,128)(2,1)S(1)}, bf16[128,512]{1,0:T(8,128)(2,1)S(1)}, u32[]{:S(2)}, u32[]{:S(2)}) collective-permute-start(bf16[128,512]{1,0:T(8,128)(2,1)S(1)} %get-tuple-element.135), channel_id=1, source_target_pairs={{0,8},{4,12},{8,0},{12,4},{1,9},{5,13},{9,1},{13,5},{2,10},{6,14},... | collective-permute-start | bytes 393224 | tf_op jit(solution)/shard_map/ppermute | solution.py:24
  157.6 5.0 %partial.11 = (bf16[128,512]{1,0:T(8,128)(2,1)S(1)}, bf16[128,512]{1,0:T(8,128)(2,1)S(1)}, f32[256,512]{1,0:T(8,128)S(1)}) custom-call(s32[3]{0:T(128)S(1)} %pad_add_fusion.place, bf16[128,4096]{1,0:T(8,128)(2,1)S(1)} %pad_maximum_fusion.rest_0_.act_low, bf16[128,4096]{1,0:T(8,128)(2,1)S(1)} %pad_maximum_fusion.1.act_high.rest_0_.rest_1_, ...), custom_call_target="tpu_custom_call" | custom-call | tf_op jit(solution)/shard_map/partial/pallas_call | solution.py:40
  162.8 2.8 %collective-permute-start.35 = (bf16[128,512]{1,0:T(8,128)(2,1)S(1)}, bf16[128,512]{1,0:T(8,128)(2,1)S(1)}, u32[]{:S(2)}, u32[]{:S(2)}) collective-permute-start(bf16[128,512]{1,0:T(8,128)(2,1)S(1)} %get-tuple-element.142), channel_id=1, source_target_pairs={{0,8},{4,12},{8,0},{12,4},{1,9},{5,13},{9,1},{13,5},{2,10},{6,14},... | collective-permute-start | bytes 393224 | tf_op jit(solution)/shard_map/ppermute | solution.py:24
  165.7 5.2 %teacher.7.norm = f32[4,256,128]{2,1,0:T(8,128)S(1)} custom-call(s32[3]{0:T(128)S(1)} %pad_add_fusion.place, bf16[256,2048]{1,0:T(8,128)(2,1)S(1)} %bitcast.31, bf16[1024,256]{1,0:T(8,128)(2,1)S(1)} %pad_maximum_fusion.3.keys), custom_call_target="tpu_custom_call" | custom-call | tf_op jit(solution)/shard_map/teacher/pallas_call | solution.py:306
  170.9 1.3 decay.1
  172.3 4.5 %loss.4 = f32[4,1,256]{2,1,0:T(1,128)S(1)} custom-call(s32[3]{0:T(128)S(1)} %pad_add_fusion.place, bf16[256,2048]{1,0:T(8,128)(2,1)S(1)} %bitcast.32, f32[256,512]{1,0:T(8,128)S(1)} %get-tuple-element.118.kept, bf16[128,512]{1,0:T(8,128)(2,1)S(1)} %collective-permute-done.21.came_low, bf16[128,512]{1,0:T(8,128)(2,1)S(1)} %collective-permute-done.22.came_high, ...), custom_call_target="tpu_custom_call" | custom-call | tf_op jit(solution)/shard_map/loss/pallas_call | solution.py:40
  176.8 4.7 %loss.5 = f32[4,1,256]{2,1,0:T(1,128)S(1)} custom-call(s32[3]{0:T(128)S(1)} %pad_add_fusion.place, bf16[256,2048]{1,0:T(8,128)(2,1)S(1)} %bitcast.33, f32[256,512]{1,0:T(8,128)S(1)} %get-tuple-element.122.kept, bf16[128,512]{1,0:T(8,128)(2,1)S(1)} %collective-permute-done.31.came_low, bf16[128,512]{1,0:T(8,128)(2,1)S(1)} %collective-permute-done.32.came_high, ...), custom_call_target="tpu_custom_call" | custom-call | tf_op jit(solution)/shard_map/loss/pallas_call | solution.py:40
  181.6 4.5 %loss.6 = f32[4,1,256]{2,1,0:T(1,128)S(1)} custom-call(s32[3]{0:T(128)S(1)} %pad_add_fusion.place, bf16[256,2048]{1,0:T(8,128)(2,1)S(1)} %bitcast.34, f32[256,512]{1,0:T(8,128)S(1)} %get-tuple-element.137.kept, bf16[128,512]{1,0:T(8,128)(2,1)S(1)} %collective-permute-done.33.came_low, bf16[128,512]{1,0:T(8,128)(2,1)S(1)} %collective-permute-done.34.came_high, ...), custom_call_target="tpu_custom_call" | custom-call | tf_op jit(solution)/shard_map/loss/pallas_call | solution.py:40
  186.1 4.5 %loss.7 = f32[4,1,256]{2,1,0:T(1,128)S(1)} custom-call(s32[3]{0:T(128)S(1)} %pad_add_fusion.place, bf16[256,2048]{1,0:T(8,128)(2,1)S(1)} %bitcast.35, f32[256,512]{1,0:T(8,128)S(1)} %get-tuple-element.144.kept, bf16[128,512]{1,0:T(8,128)(2,1)S(1)} %collective-permute-done.35.came_low, bf16[128,512]{1,0:T(8,128)(2,1)S(1)} %collective-permute-done.36.came_high, ...), custom_call_target="tpu_custom_call" | custom-call | tf_op jit(solution)/shard_map/loss/pallas_call | solution.py:40
  190.7 0.6 copy.9
  (119 shorter events, 2.3 us)
Async XLA Ops:
  0.0 54.3 %copy-start = (bf16[1,256,512]{2,1,0:T(8,128)(2,1)S(1)}, bf16[1,256,512]{2,1,0:T(8,128)(2,1)}, u32[]{:S(2)}) copy-start(bf16[1,256,512]{2,1,0:T(8,128)(2,1)} %param.9) | copy-start | bytes 786436
  2.8 14.8 %collective-permute-start.2 = (bf16[64,4096]{1,0:T(8,128)(2,1)S(1)}, bf16[64,4096]{1,0:T(8,128)(2,1)S(1)}, u32[]{:S(2)}, u32[]{:S(2)}) collective-permute-start(bf16[64,4096]{1,0:T(8,128)(2,1)S(1)} %get-tuple-element.166), channel_id=1, source_target_pairs={{0,2},{2,0},{1,3},{3,1},{4,6},{6,4},{5,7},{7,5},{8,10},{10,8},{9,1... | collective-permute-start | bytes 1572872 | tf_op jit(solution)/shard_map/ppermute | solution.py:24
  4.3 2.1 %dynamic-slice-start = ((bf16[2048,512]{1,0:T(8,128)(2,1)}, s32[]{:T(128)}, s32[]{:T(128)}), bf16[512,256]{1,0:T(8,128)(2,1)S(1)}, s32[]{:S(2)}) async-start(bf16[2048,512]{1,0:T(8,128)(2,1)} %param.11, s32[]{:T(128)} %select_n.64, s32[]{:T(128)} %select_n.66), calls=%async_computation | async-start | bytes 524800 | tf_op jit(solution)/shard_map/dynamic_slice | solution.py:283
  6.5 25.1 %collective-permute-start.4 = (bf16[512,768]{1,0:T(8,128)(2,1)S(1)}, bf16[512,768]{1,0:T(8,128)(2,1)S(1)}, u32[]{:S(2)}, u32[]{:S(2)}) collective-permute-start(bf16[512,768]{1,0:T(8,128)(2,1)S(1)} %pad_maximum_fusion.2), channel_id=1, source_target_pairs={{0,4},{4,0},{8,12},{12,8},{1,5},{5,1},{9,13},{13,9},{2,6},{6,2},{1... | collective-permute-start | bytes 2359304 | tf_op jit(solution)/shard_map/ppermute | solution.py:24
  7.0 20.8 %collective-permute-start.1 = (bf16[64,4096]{1,0:T(8,128)(2,1)}, bf16[64,4096]{1,0:T(8,128)(2,1)}, u32[]{:S(2)}, u32[]{:S(2)}) collective-permute-start(bf16[64,4096]{1,0:T(8,128)(2,1)} %get-tuple-element.167), channel_id=1, source_target_pairs={{0,2},{2,0},{1,3},{3,1},{4,6},{6,4},{5,7},{7,5},{8,10},{10,8},{9,1... | collective-permute-start | bytes 1572872 | tf_op jit(solution)/shard_map/ppermute | solution.py:24
  7.6 28.8 %collective-permute-start.8 = (bf16[64,4096]{1,0:T(8,128)(2,1)}, bf16[64,4096]{1,0:T(8,128)(2,1)}, u32[]{:S(2)}, u32[]{:S(2)}) collective-permute-start(bf16[64,4096]{1,0:T(8,128)(2,1)} %get-tuple-element.98), channel_id=1, source_target_pairs={{2,10},{6,14},{8,0},{12,4},{3,11},{7,15},{9,1},{13,5},{18,26},{22,... | collective-permute-start | bytes 1572872 | tf_op jit(solution)/shard_map/ppermute | solution.py:339
  17.6 25.9 %collective-permute-start.9 = (bf16[64,4096]{1,0:T(8,128)(2,1)S(1)}, bf16[64,4096]{1,0:T(8,128)(2,1)}, u32[]{:S(2)}, u32[]{:S(2)}) collective-permute-start(bf16[64,4096]{1,0:T(8,128)(2,1)S(1)} %collective-permute-done.2), channel_id=1, source_target_pairs={{0,8},{4,12},{10,2},{14,6},{1,9},{5,13},{11,3},{15,7},{16,24},{20,... | collective-permute-start | bytes 1572872 | tf_op jit(solution)/shard_map/ppermute | solution.py:339
  18.9 41.2 %collective-permute-start.11 = (bf16[512,512]{1,0:T(8,128)(2,1)}, bf16[512,512]{1,0:T(8,128)(2,1)S(1)}, u32[]{:S(2)}, u32[]{:S(2)}) collective-permute-start(bf16[512,512]{1,0:T(8,128)(2,1)} %get-tuple-element.163), channel_id=1, source_target_pairs={{0,4},{4,0},{8,12},{12,8},{1,5},{5,1},{9,13},{13,9},{2,6},{6,2},{1... | collective-permute-start | bytes 1572872 | tf_op jit(solution)/shard_map/ppermute | solution.py:24
  19.4 36.2 %copy-start.25 = (bf16[2048,512]{1,0:T(8,128)(2,1)S(1)}, bf16[2048,512]{1,0:T(8,128)(2,1)}, u32[]{:S(2)}) copy-start(bf16[2048,512]{1,0:T(8,128)(2,1)} %param.11) | copy-start | bytes 6291460
  27.8 42.7 %collective-permute-start = (bf16[64,4096]{1,0:T(8,128)(2,1)}, bf16[64,4096]{1,0:T(8,128)(2,1)S(1)}, u32[]{:S(2)}, u32[]{:S(2)}) collective-permute-start(bf16[64,4096]{1,0:T(8,128)(2,1)} %get-tuple-element.100), channel_id=1, source_target_pairs={{2,10},{6,14},{8,0},{12,4},{3,11},{7,15},{9,1},{13,5},{18,26},{22,... | collective-permute-start | bytes 1572872 | tf_op jit(solution)/shard_map/ppermute | solution.py:339
  31.6 27.2 %collective-permute-start.15 = (bf16[64,4096]{1,0:T(8,128)(2,1)}, bf16[64,4096]{1,0:T(8,128)(2,1)S(1)}, u32[]{:S(2)}, u32[]{:S(2)}) collective-permute-start(bf16[64,4096]{1,0:T(8,128)(2,1)} %get-tuple-element.98), channel_id=1, source_target_pairs={{0,2},{4,6},{10,8},{14,12},{1,3},{5,7},{11,9},{15,13},{16,18},{20,... | collective-permute-start | bytes 1572872 | tf_op jit(solution)/shard_map/ppermute | solution.py:341
  36.4 22.4 %collective-permute-start.5 = (bf16[512,768]{1,0:T(8,128)(2,1)S(1)}, bf16[512,768]{1,0:T(8,128)(2,1)S(1)}, u32[]{:S(2)}, u32[]{:S(2)}) collective-permute-start(bf16[512,768]{1,0:T(8,128)(2,1)S(1)} %collective-permute-done.4.rest_2_.rest_3_), channel_id=1, source_target_pairs={{0,16},{16,0},{1,17},{17,1},{2,18},{18,2},{3,19},{19,3},{4,20},{20... | collective-permute-start | bytes 2359304 | tf_op jit(solution)/shard_map/ppermute | solution.py:24
  44.7 19.7 %collective-permute-start.10 = (bf16[64,4096]{1,0:T(8,128)(2,1)S(1)}, bf16[64,4096]{1,0:T(8,128)(2,1)S(1)}, u32[]{:S(2)}, u32[]{:S(2)}) collective-permute-start(bf16[64,4096]{1,0:T(8,128)(2,1)S(1)} %broadcast_select_fusion.5), channel_id=1, source_target_pairs={{0,2},{2,0},{1,3},{3,1},{4,6},{6,4},{5,7},{7,5},{8,10},{10,8},{9,1... | collective-permute-start | bytes 1572872 | tf_op jit(solution)/shard_map/ppermute | solution.py:24
  54.3 47.9 %copy-start.23 = (bf16[256,256]{1,0:T(8,128)(2,1)}, bf16[256,256]{1,0:T(8,128)(2,1)S(1)}, u32[]{:S(2)}) copy-start(bf16[256,256]{1,0:T(8,128)(2,1)S(1)} %dynamic-slice_bitcast_fusion) | copy-start | bytes 393220
  55.8 10.9 %copy-start.28 = (bf16[64,4096]{1,0:T(8,128)(2,1)S(1)}, bf16[64,4096]{1,0:T(8,128)(2,1)}, u32[]{:S(2)}) copy-start(bf16[64,4096]{1,0:T(8,128)(2,1)} %get-tuple-element.100) | copy-start | bytes 1572868
  58.8 32.0 %collective-permute-start.20 = (bf16[256,256]{1,0:T(8,128)(2,1)S(1)}, bf16[256,256]{1,0:T(8,128)(2,1)S(1)}, u32[]{:S(2)}, u32[]{:S(2)}) collective-permute-start(bf16[256,256]{1,0:T(8,128)(2,1)S(1)} %dynamic-slice_bitcast_fusion), channel_id=1, source_target_pairs={{0,8},{4,12},{8,0},{12,4},{1,9},{5,13},{9,1},{13,5},{2,10},{6,14},... | collective-permute-start | bytes 393224 | tf_op jit(solution)/shard_map/ppermute | solution.py:24
  58.8 31.8 %copy-start.3 = (bf16[512,768]{1,0:T(8,128)(2,1)}, bf16[512,768]{1,0:T(8,128)(2,1)S(1)}, u32[]{:S(2)}) copy-start(bf16[512,768]{1,0:T(8,128)(2,1)S(1)} %collective-permute-done.5.rest_3_.rest_4_) | copy-start | bytes 2359300
  58.8 21.0 %collective-permute-start.3 = (bf16[64,4096]{1,0:T(8,128)(2,1)}, bf16[64,4096]{1,0:T(8,128)(2,1)S(1)}, u32[]{:S(2)}, u32[]{:S(2)}) collective-permute-start(bf16[64,4096]{1,0:T(8,128)(2,1)} %collective-permute-done.1), channel_id=1, source_target_pairs={{0,8},{4,12},{10,2},{14,6},{1,9},{5,13},{11,3},{15,7},{16,24},{20,... | collective-permute-start | bytes 1572872 | tf_op jit(solution)/shard_map/ppermute | solution.py:339
  60.1 4.4 %copy-start.9 = (bf16[512,512]{1,0:T(8,128)(2,1)}, bf16[512,512]{1,0:T(8,128)(2,1)S(1)}, u32[]{:S(2)}) copy-start(bf16[512,512]{1,0:T(8,128)(2,1)S(1)} %collective-permute-done.11.rest_2_.rest_3_) | copy-start | bytes 1572868
  60.1 4.5 %collective-permute-start.6 = (bf16[512,768]{1,0:T(8,128)(2,1)S(1)}, bf16[512,768]{1,0:T(8,128)(2,1)S(1)}, u32[]{:S(2)}, u32[]{:S(2)}) collective-permute-start(bf16[512,768]{1,0:T(8,128)(2,1)S(1)} %collective-permute-done.4.rest_2_.rest_3_), channel_id=1, source_target_pairs={{0,1},{1,0},{2,3},{3,2},{4,5},{5,4},{6,7},{7,6},{8,9},{9,8},{10,11... | collective-permute-start | bytes 2359304 | tf_op jit(solution)/shard_map/ppermute | solution.py:24
  64.4 2.3 %collective-permute-start.7 = (bf16[512,768]{1,0:T(8,128)(2,1)S(1)}, bf16[512,768]{1,0:T(8,128)(2,1)S(1)}, u32[]{:S(2)}, u32[]{:S(2)}) collective-permute-start(bf16[512,768]{1,0:T(8,128)(2,1)S(1)} %collective-permute-done.5.rest_3_.rest_4_), channel_id=1, source_target_pairs={{0,1},{1,0},{2,3},{3,2},{4,5},{5,4},{6,7},{7,6},{8,9},{9,8},{10,11... | collective-permute-start | bytes 2359304 | tf_op jit(solution)/shard_map/ppermute | solution.py:24
  64.6 5.9 %copy-start.10 = (bf16[512,512]{1,0:T(8,128)(2,1)S(1)}, bf16[512,512]{1,0:T(8,128)(2,1)}, u32[]{:S(2)}) copy-start(bf16[512,512]{1,0:T(8,128)(2,1)} %copy-done.9) | copy-start | bytes 1572868
  64.6 26.1 %copy-start.5 = (bf16[512,768]{1,0:T(8,128)(2,1)}, bf16[512,768]{1,0:T(8,128)(2,1)S(1)}, u32[]{:S(2)}) copy-start(bf16[512,768]{1,0:T(8,128)(2,1)S(1)} %collective-permute-done.6.rest_4_.rest_5_) | copy-start | bytes 2359300
  64.6 36.1 %collective-permute-start.19 = (bf16[512,1024]{1,0:T(8,128)(2,1)S(1)}, bf16[512,1024]{1,0:T(8,128)(2,1)}, u32[]{:S(2)}, u32[]{:S(2)}) collective-permute-start(bf16[512,1024]{1,0:T(8,128)(2,1)S(1)} %constant_dynamic-slice_fusion.2), channel_id=1, source_target_pairs={{0,4},{4,0},{8,12},{12,8},{1,5},{5,1},{9,13},{13,9},{2,6},{6,2},{1... | collective-permute-start | bytes 3145736 | tf_op jit(solution)/shard_map/ppermute | solution.py:24
  66.7 24.0 %copy-start.7 = (bf16[512,768]{1,0:T(8,128)(2,1)}, bf16[512,768]{1,0:T(8,128)(2,1)S(1)}, u32[]{:S(2)}) copy-start(bf16[512,768]{1,0:T(8,128)(2,1)S(1)} %collective-permute-done.7.rest_5_.rest_6_) | copy-start | bytes 2359300
  66.7 15.8 %collective-permute-start.16 = (bf16[64,4096]{1,0:T(8,128)(2,1)S(1)}, bf16[64,4096]{1,0:T(8,128)(2,1)S(1)}, u32[]{:S(2)}, u32[]{:S(2)}) collective-permute-start(bf16[64,4096]{1,0:T(8,128)(2,1)S(1)} %copy-done.28), channel_id=1, source_target_pairs={{0,2},{4,6},{10,8},{14,12},{1,3},{5,7},{11,9},{15,13},{16,18},{20,... | collective-permute-start | bytes 1572872 | tf_op jit(solution)/shard_map/ppermute | solution.py:341
  68.0 19.5 %copy-start.21 = (bf16[1,256,4096]{2,1,0:T(8,128)(2,1)S(1)}, bf16[1,256,4096]{2,1,0:T(8,128)(2,1)}, u32[]{:S(2)}) copy-start(bf16[1,256,4096]{2,1,0:T(8,128)(2,1)} %param.7) | copy-start | bytes 6291460
  70.5 14.0 %collective-permute-start.14 = (bf16[512,512]{1,0:T(8,128)(2,1)S(1)}, bf16[512,512]{1,0:T(8,128)(2,1)S(1)}, u32[]{:S(2)}, u32[]{:S(2)}) collective-permute-start(bf16[512,512]{1,0:T(8,128)(2,1)S(1)} %copy-done.10), channel_id=1, source_target_pairs={{0,16},{16,0},{1,17},{17,1},{2,18},{18,2},{3,19},{19,3},{4,20},{20... | collective-permute-start | bytes 1572872 | tf_op jit(solution)/shard_map/ppermute | solution.py:24
  84.5 18.5 %copy-start.12 = (bf16[512,512]{1,0:T(8,128)(2,1)}, bf16[512,512]{1,0:T(8,128)(2,1)S(1)}, u32[]{:S(2)}) copy-start(bf16[512,512]{1,0:T(8,128)(2,1)S(1)} %collective-permute-done.14.rest_3_.rest_4_) | copy-start | bytes 1572868
  84.5 18.4 %collective-permute-start.17 = (bf16[512,512]{1,0:T(8,128)(2,1)S(1)}, bf16[512,512]{1,0:T(8,128)(2,1)S(1)}, u32[]{:S(2)}, u32[]{:S(2)}) collective-permute-start(bf16[512,512]{1,0:T(8,128)(2,1)S(1)} %copy-done.10), channel_id=1, source_target_pairs={{0,1},{1,0},{2,3},{3,2},{4,5},{5,4},{6,7},{7,6},{8,9},{9,8},{10,11... | collective-permute-start | bytes 1572872 | tf_op jit(solution)/shard_map/ppermute | solution.py:24
  84.5 18.5 %collective-permute-start.18 = (bf16[512,512]{1,0:T(8,128)(2,1)S(1)}, bf16[512,512]{1,0:T(8,128)(2,1)S(1)}, u32[]{:S(2)}, u32[]{:S(2)}) collective-permute-start(bf16[512,512]{1,0:T(8,128)(2,1)S(1)} %collective-permute-done.14.rest_3_.rest_4_), channel_id=1, source_target_pairs={{0,1},{1,0},{2,3},{3,2},{4,5},{5,4},{6,7},{7,6},{8,9},{9,8},{10,11... | collective-permute-start | bytes 1572872 | tf_op jit(solution)/shard_map/ppermute | solution.py:24
  85.0 20.7 %collective-permute-start.12 = (bf16[64,4096]{1,0:T(8,128)(2,1)S(1)}, bf16[64,4096]{1,0:T(8,128)(2,1)S(1)}, u32[]{:S(2)}, u32[]{:S(2)}) collective-permute-start(bf16[64,4096]{1,0:T(8,128)(2,1)S(1)} %broadcast_select_fusion.2), channel_id=1, source_target_pairs={{0,2},{2,0},{1,3},{3,1},{4,6},{6,4},{5,7},{7,5},{8,10},{10,8},{9,1... | collective-permute-start | bytes 1572872 | tf_op jit(solution)/shard_map/ppermute | solution.py:24
  90.7 12.3 %copy-start.26 = (bf16[256,256]{1,0:T(8,128)(2,1)}, bf16[256,256]{1,0:T(8,128)(2,1)S(1)}, u32[]{:S(2)}) copy-start(bf16[256,256]{1,0:T(8,128)(2,1)S(1)} %collective-permute-done.20) | copy-start | bytes 393220
  91.4 14.3 %collective-permute-start.13 = (bf16[16,2048]{1,0:T(8,128)(2,1)S(1)}, bf16[16,2048]{1,0:T(8,128)(2,1)S(1)}, u32[]{:S(2)}, u32[]{:S(2)}) collective-permute-start(bf16[16,2048]{1,0:T(8,128)(2,1)S(1)} %bitcast.36), channel_id=1, source_target_pairs={{0,4},{4,0},{8,12},{12,8},{1,5},{5,1},{9,13},{13,9},{2,6},{6,2},{1... | collective-permute-start | bytes 196616 | tf_op jit(solution)/shard_map/ppermute | solution.py:24
  100.7 25.1 %collective-permute-start.26 = (bf16[512,1024]{1,0:T(8,128)(2,1)}, bf16[512,1024]{1,0:T(8,128)(2,1)}, u32[]{:S(2)}, u32[]{:S(2)}) collective-permute-start(bf16[512,1024]{1,0:T(8,128)(2,1)} %collective-permute-done.19.rest_4_), channel_id=1, source_target_pairs={{0,16},{16,0},{1,17},{17,1},{2,18},{18,2},{3,19},{19,3},{4,20},{20... | collective-permute-start | bytes 3145736 | tf_op jit(solution)/shard_map/ppermute | solution.py:24
  103.0 2.8 %copy-start.14 = (bf16[512,512]{1,0:T(8,128)(2,1)}, bf16[512,512]{1,0:T(8,128)(2,1)S(1)}, u32[]{:S(2)}) copy-start(bf16[512,512]{1,0:T(8,128)(2,1)S(1)} %collective-permute-done.17.rest_4_.rest_5_) | copy-start | bytes 1572868
  103.0 22.9 %collective-permute-start.25 = (bf16[512,256]{1,0:T(8,128)(2,1)}, bf16[512,256]{1,0:T(8,128)(2,1)}, u32[]{:S(2)}, u32[]{:S(2)}) collective-permute-start(bf16[512,256]{1,0:T(8,128)(2,1)} %pad_maximum_fusion.5), channel_id=1, source_target_pairs={{0,4},{4,0},{8,12},{12,8},{1,5},{5,1},{9,13},{13,9},{2,6},{6,2},{1... | collective-permute-start | bytes 786440 | tf_op jit(solution)/shard_map/ppermute | solution.py:24
  103.0 2.7 %copy-start.16 = (bf16[512,512]{1,0:T(8,128)(2,1)}, bf16[512,512]{1,0:T(8,128)(2,1)S(1)}, u32[]{:S(2)}) copy-start(bf16[512,512]{1,0:T(8,128)(2,1)S(1)} %collective-permute-done.18.rest_5_.rest_6_) | copy-start | bytes 1572868
  106.0 5.6 %copy-start.29 = (f32[16]{0:T(128)S(1)}, f32[16]{0:T(128)}, u32[]{:S(2)}) copy-start(f32[16]{0:T(128)} %param.13) | copy-start | bytes 196
  111.5 21.3 %collective-permute-start.23 = (bf16[512,256]{1,0:T(8,128)(2,1)}, bf16[512,256]{1,0:T(8,128)(2,1)}, u32[]{:S(2)}, u32[]{:S(2)}) collective-permute-start(bf16[512,256]{1,0:T(8,128)(2,1)} %get-tuple-element.115), channel_id=1, source_target_pairs={{0,8},{4,12},{8,0},{12,4},{1,9},{5,13},{9,1},{13,5},{2,10},{6,14},... | collective-permute-start | bytes 786440 | tf_op jit(solution)/shard_map/ppermute | solution.py:24
  111.6 51.0 %collective-permute-start.21 = (bf16[128,512]{1,0:T(8,128)(2,1)S(1)}, bf16[128,512]{1,0:T(8,128)(2,1)S(1)}, u32[]{:S(2)}, u32[]{:S(2)}) collective-permute-start(bf16[128,512]{1,0:T(8,128)(2,1)S(1)} %partial.6), channel_id=1, source_target_pairs={{0,8},{4,12},{8,0},{12,4},{1,9},{5,13},{9,1},{13,5},{2,10},{6,14},... | collective-permute-start | bytes 393224 | tf_op jit(solution)/shard_map/ppermute | solution.py:24
  114.5 18.2 %collective-permute-start.24 = (f32[16,512]{1,0:T(8,128)S(1)}, f32[16,512]{1,0:T(8,128)S(1)}, u32[]{:S(2)}, u32[]{:S(2)}) collective-permute-start(f32[16,512]{1,0:T(8,128)S(1)} %get-tuple-element.116), channel_id=1, source_target_pairs={{0,8},{4,12},{8,0},{12,4},{1,9},{5,13},{9,1},{13,5},{2,10},{6,14},... | collective-permute-start | bytes 98312 | tf_op jit(solution)/shard_map/ppermute | solution.py:24
  115.7 1.1 copy-start.6
  118.0 4.2 %copy-start.1 = (bf16[256,4096]{1,0:T(8,128)(2,1)S(1)}, bf16[256,4096]{1,0:T(8,128)(2,1)}, u32[]{:S(2)}) copy-start(bf16[256,4096]{1,0:T(8,128)(2,1)} %maximum_select_fusion.act_own.rest_1_.rest_2_) | copy-start | bytes 6291460
  118.0 4.2 %copy-start.11 = (bf16[512,512]{1,0:T(8,128)(2,1)S(1)}, bf16[512,512]{1,0:T(8,128)(2,1)}, u32[]{:S(2)}) copy-start(bf16[512,512]{1,0:T(8,128)(2,1)} %copy-done.9) | copy-start | bytes 1572868
  118.0 4.3 %copy-start.13 = (bf16[512,512]{1,0:T(8,128)(2,1)S(1)}, bf16[512,512]{1,0:T(8,128)(2,1)}, u32[]{:S(2)}) copy-start(bf16[512,512]{1,0:T(8,128)(2,1)} %copy-done.12) | copy-start | bytes 1572868
  118.0 4.3 %copy-start.15 = (bf16[512,512]{1,0:T(8,128)(2,1)S(1)}, bf16[512,512]{1,0:T(8,128)(2,1)}, u32[]{:S(2)}) copy-start(bf16[512,512]{1,0:T(8,128)(2,1)} %copy-done.14) | copy-start | bytes 1572868
  118.0 4.3 %copy-start.17 = (bf16[512,512]{1,0:T(8,128)(2,1)S(1)}, bf16[512,512]{1,0:T(8,128)(2,1)}, u32[]{:S(2)}) copy-start(bf16[512,512]{1,0:T(8,128)(2,1)} %copy-done.16) | copy-start | bytes 1572868
  122.3 3.6 %copy-start.24 = (bf16[256,256]{1,0:T(8,128)(2,1)S(1)}, bf16[256,256]{1,0:T(8,128)(2,1)}, u32[]{:S(2)}) copy-start(bf16[256,256]{1,0:T(8,128)(2,1)} %copy-done.23) | copy-start | bytes 393220
  122.3 3.6 %copy-start.27 = (bf16[256,256]{1,0:T(8,128)(2,1)S(1)}, bf16[256,256]{1,0:T(8,128)(2,1)}, u32[]{:S(2)}) copy-start(bf16[256,256]{1,0:T(8,128)(2,1)} %copy-done.26) | copy-start | bytes 393220
  122.3 5.2 %copy-start.2 = (bf16[1,256,2048]{2,1,0:T(8,128)(2,1)S(1)}, bf16[1,256,2048]{2,1,0:T(8,128)(2,1)}, u32[]{:S(2)}) copy-start(bf16[1,256,2048]{2,1,0:T(8,128)(2,1)} %param.8) | copy-start | bytes 3145732
  125.9 7.9 %copy-start.19 = (f32[512,256]{1,0:T(8,128)S(1)}, f32[512,256]{1,0:T(8,128)}, u32[]{:S(2)}) copy-start(f32[512,256]{1,0:T(8,128)} %copy-done.18) | copy-start | bytes 1572868
  126.9 14.3 %collective-permute-start.29 = (bf16[512,1024]{1,0:T(8,128)(2,1)}, bf16[512,1024]{1,0:T(8,128)(2,1)S(1)}, u32[]{:S(2)}, u32[]{:S(2)}) collective-permute-start(bf16[512,1024]{1,0:T(8,128)(2,1)} %collective-permute-done.19.rest_4_), channel_id=1, source_target_pairs={{0,1},{1,0},{2,3},{3,2},{4,5},{5,4},{6,7},{7,6},{8,9},{9,8},{10,11... | collective-permute-start | bytes 3145736 | tf_op jit(solution)/shard_map/ppermute | solution.py:24
  127.0 14.4 %collective-permute-start.30 = (bf16[512,1024]{1,0:T(8,128)(2,1)}, bf16[512,1024]{1,0:T(8,128)(2,1)S(1)}, u32[]{:S(2)}, u32[]{:S(2)}) collective-permute-start(bf16[512,1024]{1,0:T(8,128)(2,1)} %collective-permute-done.26.rest_5_), channel_id=1, source_target_pairs={{0,1},{1,0},{2,3},{3,2},{4,5},{5,4},{6,7},{7,6},{8,9},{9,8},{10,11... | collective-permute-start | bytes 3145736 | tf_op jit(solution)/shard_map/ppermute | solution.py:24
  133.9 20.8 %collective-permute-start.27 = (bf16[512,256]{1,0:T(8,128)(2,1)S(1)}, bf16[512,256]{1,0:T(8,128)(2,1)S(1)}, u32[]{:S(2)}, u32[]{:S(2)}) collective-permute-start(bf16[512,256]{1,0:T(8,128)(2,1)S(1)} %fusion), channel_id=1, source_target_pairs={{0,4},{4,0},{8,12},{12,8},{1,5},{5,1},{9,13},{13,9},{2,6},{6,2},{1... | collective-permute-start | bytes 786440 | tf_op jit(solution)/shard_map/ppermute | solution.py:24
  134.9 19.7 %collective-permute-start.28 = (f32[16,512]{1,0:T(8,128)S(1)}, f32[16,512]{1,0:T(8,128)S(1)}, u32[]{:S(2)}, u32[]{:S(2)}) collective-permute-start(f32[16,512]{1,0:T(8,128)S(1)} %maximum_add_fusion.1), channel_id=1, source_target_pairs={{0,4},{4,0},{8,12},{12,8},{1,5},{5,1},{9,13},{13,9},{2,6},{6,2},{1... | collective-permute-start | bytes 98312 | tf_op jit(solution)/shard_map/ppermute | solution.py:24
  141.3 21.5 %collective-permute-start.22 = (bf16[128,512]{1,0:T(8,128)(2,1)S(1)}, bf16[128,512]{1,0:T(8,128)(2,1)S(1)}, u32[]{:S(2)}, u32[]{:S(2)}) collective-permute-start(bf16[128,512]{1,0:T(8,128)(2,1)S(1)} %get-tuple-element.119), channel_id=1, source_target_pairs={{0,8},{4,12},{8,0},{12,4},{1,9},{5,13},{9,1},{13,5},{2,10},{6,14},... | collective-permute-start | bytes 393224 | tf_op jit(solution)/shard_map/ppermute | solution.py:24
  141.4 2.9 %copy-start.22 = (bf16[512,1024]{1,0:T(8,128)(2,1)}, bf16[512,1024]{1,0:T(8,128)(2,1)S(1)}, u32[]{:S(2)}) copy-start(bf16[512,1024]{1,0:T(8,128)(2,1)S(1)} %collective-permute-done.30.rest_7_) | copy-start | bytes 3145732
  141.4 24.2 %collective-permute-start.32 = (bf16[128,512]{1,0:T(8,128)(2,1)S(1)}, bf16[128,512]{1,0:T(8,128)(2,1)S(1)}, u32[]{:S(2)}, u32[]{:S(2)}) collective-permute-start(bf16[128,512]{1,0:T(8,128)(2,1)S(1)} %get-tuple-element.121), channel_id=1, source_target_pairs={{0,8},{4,12},{8,0},{12,4},{1,9},{5,13},{9,1},{13,5},{2,10},{6,14},... | collective-permute-start | bytes 393224 | tf_op jit(solution)/shard_map/ppermute | solution.py:24
  154.6 22.2 %collective-permute-start.31 = (bf16[128,512]{1,0:T(8,128)(2,1)S(1)}, bf16[128,512]{1,0:T(8,128)(2,1)S(1)}, u32[]{:S(2)}, u32[]{:S(2)}) collective-permute-start(bf16[128,512]{1,0:T(8,128)(2,1)S(1)} %partial.7), channel_id=1, source_target_pairs={{0,8},{4,12},{8,0},{12,4},{1,9},{5,13},{9,1},{13,5},{2,10},{6,14},... | collective-permute-start | bytes 393224 | tf_op jit(solution)/shard_map/ppermute | solution.py:24
  154.7 26.9 %collective-permute-start.33 = (bf16[128,512]{1,0:T(8,128)(2,1)S(1)}, bf16[128,512]{1,0:T(8,128)(2,1)S(1)}, u32[]{:S(2)}, u32[]{:S(2)}) collective-permute-start(bf16[128,512]{1,0:T(8,128)(2,1)S(1)} %get-tuple-element.135), channel_id=1, source_target_pairs={{0,8},{4,12},{8,0},{12,4},{1,9},{5,13},{9,1},{13,5},{2,10},{6,14},... | collective-permute-start | bytes 393224 | tf_op jit(solution)/shard_map/ppermute | solution.py:24
  162.6 18.9 %collective-permute-start.34 = (bf16[128,512]{1,0:T(8,128)(2,1)S(1)}, bf16[128,512]{1,0:T(8,128)(2,1)S(1)}, u32[]{:S(2)}, u32[]{:S(2)}) collective-permute-start(bf16[128,512]{1,0:T(8,128)(2,1)S(1)} %get-tuple-element.136), channel_id=1, source_target_pairs={{0,8},{4,12},{8,0},{12,4},{1,9},{5,13},{9,1},{13,5},{2,10},{6,14},... | collective-permute-start | bytes 393224 | tf_op jit(solution)/shard_map/ppermute | solution.py:24
  162.8 23.3 %collective-permute-start.35 = (bf16[128,512]{1,0:T(8,128)(2,1)S(1)}, bf16[128,512]{1,0:T(8,128)(2,1)S(1)}, u32[]{:S(2)}, u32[]{:S(2)}) collective-permute-start(bf16[128,512]{1,0:T(8,128)(2,1)S(1)} %get-tuple-element.142), channel_id=1, source_target_pairs={{0,8},{4,12},{8,0},{12,4},{1,9},{5,13},{9,1},{13,5},{2,10},{6,14},... | collective-permute-start | bytes 393224 | tf_op jit(solution)/shard_map/ppermute | solution.py:24
  165.6 20.5 %collective-permute-start.36 = (bf16[128,512]{1,0:T(8,128)(2,1)S(1)}, bf16[128,512]{1,0:T(8,128)(2,1)S(1)}, u32[]{:S(2)}, u32[]{:S(2)}) collective-permute-start(bf16[128,512]{1,0:T(8,128)(2,1)S(1)} %get-tuple-element.143), channel_id=1, source_target_pairs={{0,8},{4,12},{8,0},{12,4},{1,9},{5,13},{9,1},{13,5},{2,10},{6,14},... | collective-permute-start | bytes 393224 | tf_op jit(solution)/shard_map/ppermute | solution.py:24
  (4 other events, 4.0 us)

commit v3 on v2

--- a/solution.py
+++ b/solution.py
@@ -64,10 +64,16 @@
     return total
 
 
-def partial_kernel(model, number, place, *rest):
-    acts, own, pieces, outs = rest[:number], rest[number], rest[number + 1 : -number], rest[-number:]
-    for act, out in zip(acts, outs):
-        out[...] = product(place, act, own, pieces, model).astype(out.dtype)
+def partial_kernel(model, groups, place, *rest):
+    number = sum(groups)
+    acts, own, pieces, outs = rest[:number], rest[number], rest[number + 1 : -len(groups)], rest[-len(groups) :]
+    acts = list(acts)
+    for size, out in zip(groups, outs):
+        row = 0
+        for act in acts[:size]:
+            out[row : row + act.shape[0], :] = product(place, act, own, pieces, model).astype(out.dtype)
+            row += act.shape[0]
+        del acts[:size]
 
 
 def extra_kernel(model, step_model, place, act_own, act_low, act_high, own, *rest):
@@ -140,71 +146,72 @@
 SCALE = LOG2E * HEAD_DIM ** -0.5
 
 
-def teacher_kernel(offsets, place, query, keys, norm, scores, top, mass):
+def for_place(mine, offsets, body):
+    for position in range(len(offsets)):
+        earlier = [at for at in range(1, len(offsets)) if (position ^ offsets[at]) < position]
+        pl.when(mine == position)(functools.partial(body, earlier))
+
+
+def teacher_kernel(offsets, place, query, keys, norm):
     tokens = query.shape[0]
-    mine = place[2]
-    own = lax.dot_general(query[...], keys[pl.ds(0, tokens), :], NT, preferred_element_type=F32) * SCALE
-    own = jnp.where(causal_of(tokens), own, -jnp.inf)
-    scores[0] = own
-    top[...] = folded(jnp.maximum, own)
-    for at in range(1, len(offsets)):
-
-        @pl.when((mine ^ offsets[at]) < mine)
-        def _(at=at):
-            value = lax.dot_general(
-                query[...], keys[pl.ds(at * tokens, tokens), :], NT, preferred_element_type=F32
-            ) * SCALE
-            scores[at] = value
-            top[...] = jnp.maximum(top[...], folded(jnp.maximum, value))
-
-    peak = jnp.max(top[...], axis=1, keepdims=True)
-    mass[...] = folded(jnp.add, jnp.exp2(scores[0] - peak))
-    for at in range(1, len(offsets)):
-
-        @pl.when((mine ^ offsets[at]) < mine)
-        def _(at=at):
-            mass[...] += folded(jnp.add, jnp.exp2(scores[at] - peak))
-
-    total = jnp.sum(mass[...], axis=1, keepdims=True)
-    norm[0] = jnp.broadcast_to(peak + jnp.log2(total), (tokens, 128))
+
+    def body(earlier):
+        asked = query[...]
+        scores = []
+        for at in [0] + earlier:
+            key = keys[pl.ds(at * tokens, tokens), :]
+            scores.append(lax.dot_general(asked, key, NT, preferred_element_type=F32) * SCALE)
+        scores[0] = jnp.where(causal_of(tokens), scores[0], -jnp.inf)
+        top = functools.reduce(jnp.maximum, [folded(jnp.maximum, s) for s in scores])
+        peak = jnp.max(top, axis=1, keepdims=True)
+        mass = functools.reduce(jnp.add, [folded(jnp.add, jnp.exp2(s - peak)) for s in scores])
+        total = jnp.sum(mass, axis=1, keepdims=True)
+        norm[0] = jnp.broadcast_to(peak + jnp.log2(total), (tokens, 128))
+
+    for_place(place[2], offsets, body)
 
 
 def loss_kernel(
-    offsets, first, heads, place, query, kept, came_low, came_high, keys, inputs, norm, factor, log_row, log_col, gain_col, out, sums
+    offsets, first, heads, place, query, kept, keys, inputs, norm, factor, log_row, log_col, gain_col, *rest
 ):
+    arrived, out = rest[:-1], rest[-1]
     tokens = query.shape[0]
-    mine = place[2]
-    causal = causal_of(tokens)
-    for i in range(heads):
-        head = first + i
-        cols = slice(i * HEAD_DIM, (i + 1) * HEAD_DIM)
-        asked = query[:, cols]
-        came = jnp.concatenate([came_low[:, cols], came_high[:, cols]], axis=0)
-        read = (kept[:, cols] + came.astype(F32)).astype(BF16)
-        lse = norm[i]
-        wide = tokens // 128
-        lse_wide = jnp.concatenate([lse] * wide, axis=1)
-
-        def pair(at):
-            rows = pl.ds(at * tokens, tokens)
-            score = lax.dot_general(asked, keys[rows, :], NT, preferred_element_type=F32) * SCALE
-            inner = lax.dot_general(read, inputs[rows, :], NT, preferred_element_type=F32)
-            return jnp.exp2(score - lse_wide), inner * factor[head : head + 1, at * tokens : (at + 1) * tokens]
-
-        prob, inner = pair(0)
-        gap = log_col[:, head : head + 1] - log_row[head : head + 1, :]
-        diff = jnp.where(causal, prob - inner * jnp.exp2(gap), 0.0)
-        sums[...] = folded(jnp.add, diff * diff)
-        gain = gain_col[:, head : head + 1]
-        for at in range(1, len(offsets)):
-
-            @pl.when((mine ^ offsets[at]) < mine)
-            def _(at=at):
-                prob, inner = pair(at)
-                diff = prob - inner * gain
-                sums[...] += folded(jnp.add, diff * diff)
-
-        out[i] = jnp.sum(sums[...].T, axis=0, keepdims=True)
+
+    lane = lax.broadcasted_iota(jnp.int32, (tokens, 128), 1)
+
+    def body(earlier):
+        def one_head(i, carry):
+            head = first + i
+            cols = pl.ds(pl.multiple_of(i * HEAD_DIM, HEAD_DIM), HEAD_DIM)
+
+            def column(ref):
+                return jnp.sum(jnp.where(lane == head, ref[...], 0.0), axis=1, keepdims=True)
+
+            asked = query[:, cols]
+            came = jnp.concatenate([a[:, cols] for a in arrived], axis=0)
+            read = (kept[:, cols] + came.astype(F32)).astype(BF16)
+            lse = jnp.concatenate([norm[i]] * (tokens // 128), axis=1)
+            gain = column(gain_col)
+            sums = None
+            for at in [0] + earlier:
+                rows = pl.ds(at * tokens, tokens)
+                score = lax.dot_general(asked, keys[rows, :], NT, preferred_element_type=F32) * SCALE
+                inner = lax.dot_general(read, inputs[rows, :], NT, preferred_element_type=F32)
+                inner = inner * factor[pl.ds(head, 1), at * tokens : (at + 1) * tokens]
+                prob = jnp.exp2(score - lse)
+                if at == 0:
+                    gap = column(log_col) - log_row[pl.ds(head, 1), :]
+                    diff = jnp.where(causal_of(tokens), prob - inner * jnp.exp2(gap), 0.0)
+                else:
+                    diff = prob - inner * gain
+                square = folded(jnp.add, diff * diff)
+                sums = square if sums is None else sums + square
+            out[i] = jnp.sum(sums.T, axis=0, keepdims=True)
+            return carry
+
+        lax.fori_loop(0, heads, one_head, 0)
+
+    for_place(place[2], offsets, body)
 
 
 class Order:
@@ -284,23 +291,24 @@
             piece = jnp.concatenate([piece, extra], axis=1)
         return over_half(piece)
 
+    def send(value):
+        return xor_permute(value, "seq", half)
+
     def partial(acts, j):
         first, _, pieces = next(w for w in weights if w[0] <= j < w[1])
+        flat_acts = [a for blocks, _ in acts for a in blocks]
         return order.wait(
             call(
-                functools.partial(partial_kernel, model, len(acts)),
-                (order.gate(place), *[a for a, _ in acts], proj_c, *pieces),
+                functools.partial(partial_kernel, model, [len(blocks) for blocks, _ in acts]),
+                (order.gate(place), *flat_acts, proj_c, *pieces),
                 [smem()]
-                + [whole(a.shape) for a, _ in acts]
+                + [whole(a.shape) for a in flat_acts]
                 + [columns(rows, chunk, j)]
                 + [columns(part, chunk, j - first)] * len(model),
-                [jax.ShapeDtypeStruct((a.shape[0], chunk), dtype) for a, dtype in acts],
+                [jax.ShapeDtypeStruct((sum(a.shape[0] for a in blocks), chunk), dtype) for blocks, dtype in acts],
                 "partial",
             )
         )
-
-    def send(value):
-        return xor_permute(value, "seq", half)
 
     def teacher(first, number):
         return pl.pallas_call(
@@ -313,11 +321,6 @@
             ],
             out_specs=pl.BlockSpec((1, tokens, 128), lambda h: (h, 0, 0)),
             out_shape=jax.ShapeDtypeStruct((number, tokens, 128), F32),
-            scratch_shapes=[
-                pltpu.VMEM((seq, tokens, tokens), F32),
-                pltpu.VMEM((tokens, 128), F32),
-                pltpu.VMEM((tokens, 128), F32),
-            ],
             compiler_params=pltpu.CompilerParams(vmem_limit_bytes=VMEM_LIMIT),
             name="teacher",
         )(order.gate(place), query, keys)
@@ -369,22 +372,19 @@
         w1 = spread(order.wait(w1), "groups")
         others = [join(first0, second0)]
         weights.append((0, 1, order.wait(w0)))
-        arrived = {(0, 0): send(partial([(others[0], BF16)], 0)[0])}
+        early = send(partial([([others[0]], BF16)], 0)[0])
         first1, second1 = swap(1)
         moved[1] = order.wait(moved[1])
         w1 = spread(order.wait(w1), "batch")
+        mine = order.wait(
+            jnp.where(level, hidden, jnp.concatenate([moved[0], swapped[0], moved[1], swapped[1]], axis=0))
+        )
         key_half = order.wait(key_half)
         key_pair = jnp.concatenate([local_key, key_half], axis=0)
         key_rest = over_half(key_pair)
-        w2 = spread(order.wait(w2), "groups")
-        mine = jnp.where(
-            level, hidden, jnp.concatenate([moved[0], swapped[0], moved[1], swapped[1]], axis=0)
-        )
-        weights.append((1, 2, order.wait(w1)))
-        arrived[0, 1] = send(partial([(others[0], BF16)], 1)[0])
         step_rest = order.wait(step_rest)
         others.append(join(first1, second1))
-        norms = []
+
     else:
         full = lax.all_gather(hidden, "head", axis=1, tiled=True)
         span_half = full.shape[1] // 2
@@ -396,11 +396,10 @@
         key_pair = jnp.concatenate([local_key, xor_permute(local_key, "seq", half)], axis=0)
         step_rest = over_half(step_t)
         weights.append((0, 1, spread(spread(start_weights(0, 1), "groups"), "batch")))
-        weights.append((1, 2, spread(spread(start_weights(1, 2), "groups"), "batch")))
-        w2 = spread(start_weights(2, 4), "groups")
-        norms = []
+        w1 = spread(spread(start_weights(1, 2), "groups"), "batch")
+        w2 = start_weights(2, 4)
         key_rest = over_half(key_pair)
-        arrived = {(0, j): send(partial([(others[0], BF16)], j)[0]) for j in range(2)}
+        early = send(partial([([others[0]], BF16)], 0)[0])
 
     extra_out = [
         jax.ShapeDtypeStruct((2 * tokens, width_b), F32),
@@ -424,15 +423,24 @@
     )
     came = send(rounded)
     came_raw = send(raw)
-    kept = []
-    for j in range(2):
-        leaving, stays = partial([(others[1], BF16), (mine, F32)], j)
-        arrived[1, j] = send(leaving)
+    w2 = spread(order.wait(w2), "groups")
+    kept, arrived, norms = [], [], []
+    early = order.wait(early)
+    leaving, stays = partial([([others[1]], BF16), ([mine], F32)], 0)
+    arrived.append([early, send(leaving)])
+    kept.append(stays)
+
+    def full_partial(j):
+        leaving, stays = partial([(others, BF16), ([mine], F32)], j)
+        arrived.append([send(leaving)])
         kept.append(stays)
-    w2 = spread(order.wait(w2), "batch")
+
+    weights.append((1, 2, order.wait(w1)))
+    full_partial(1)
     key_rest = order.wait(key_rest)
     keys = jnp.concatenate([key_pair] + key_rest, axis=0)
     norms.append(order.wait(teacher(0, heads)))
+    w2 = spread(order.wait(w2), "batch")
     came, came_raw = order.wait((came, came_raw))
     came = came.astype(F32)
     inputs_pair = (full + jnp.concatenate([came[tokens:], came[:tokens]], axis=0)).astype(BF16)
@@ -440,14 +448,14 @@
     inputs_rest = over_half(inputs_pair)
     raw_rest = over_half(raw_pair)
     norms.append(order.wait(teacher(heads, heads)))
+    arrived[0] = order.wait(arrived[0])
     weights.append((2, 4, order.wait(w2)))
-    for j in range(2, count):
-        if j == count - 1:
-            inputs_rest, raw_rest = order.wait((inputs_rest, raw_rest))
-        low, high, stays = partial([(others[0], BF16), (others[1], BF16), (mine, F32)], j)
-        arrived[0, j], arrived[1, j] = send(low), send(high)
-        kept.append(stays)
-        norms.append(order.wait(teacher(j * heads, heads)))
+    full_partial(2)
+    norms.append(order.wait(teacher(2 * heads, heads)))
+    arrived[1] = order.wait(arrived[1])
+    full_partial(3)
+    norms.append(order.wait(teacher(3 * heads, heads)))
+    inputs_rest, raw_rest = order.wait((inputs_rest, raw_rest))
     inputs = jnp.concatenate([inputs_pair] + inputs_rest, axis=0)
     raw_all = jnp.stack([r[:, i * tokens : (i + 1) * tokens] for r in [raw_pair] + raw_rest for i in range(2)])
     rate = jnp.pad(decay_rate, (0, padded - head_count))[:, None]
@@ -468,18 +476,16 @@
     losses = []
     for j in range(count):
         group = j * heads // per_group
-        came = order.wait((arrived[0, j], arrived[1, j]))
+        came = order.wait(arrived[j])
         losses.append(
             order.wait(
                 call(
                     functools.partial(loss_kernel, offsets, j * heads, heads),
-                    (place, query, kept[j], *came, keys, inputs, norms[j], factor, log_row, log_col, gain_col),
+                    (place, query, kept[j], keys, inputs, norms[j], factor, log_row, log_col, gain_col, *came),
                     [
                         smem(),
                         columns(tokens, chunk, j),
                         whole((tokens, chunk)),
-                        whole((tokens // 2, chunk)),
-                        whole((tokens // 2, chunk)),
                         columns(span, HEAD_DIM, group),
                         columns(span, HEAD_DIM, group),
                         whole(norms[j].shape),
@@ -487,10 +493,10 @@
                         whole(log_row.shape),
                         whole(log_col.shape),
                         whole(gain_col.shape),
-                    ],
+                    ]
+                    + [whole(c.shape) for c in came],
                     [jax.ShapeDtypeStruct((heads, 1, tokens), F32)],
                     "loss",
-                    [pltpu.VMEM((tokens, 128), F32)],
                 )[0]
             )
         )

time: 192 us -> 180 us (0.938)
  waiting for transfers between devices: 57.3 us -> 76.4 us
  Pallas kernels: 68.2 us -> 51.5 us
  starting transfers between devices: 45.2 us -> 29.1 us
    ppermute x31 -> x28, starting transfers between devices: 35.1 us -> 20.7 us  [xor_permute(): return lax.ppermute(value, axis, [(i, i ^ offset) for i in range(size)])]
    pallas_call x4, Pallas kernels: 20.9 us -> 12 us  [teacher(): pl.pallas_call(functools.partial(teacher_kernel, offsets), grid=(number,)...]
    pallas_call x12 -> x11, Pallas kernels: 47.2 us -> 39.5 us  [call(): pl.pallas_call(kernel, grid=(1,), in_specs=in_specs, out_specs=tuple((who...]
    ppermute x31 -> x28, waiting for transfers between devices: 34.8 us -> 42 us  [xor_permute(): return lax.ppermute(value, axis, [(i, i ^ offset) for i in range(size)])]
    ppermute x4, waiting for transfers between devices: 16.8 us -> 23.3 us  [local(): lax.ppermute(value, both, [(flat(i, j), flat(i ^ half, j)) for i, j in gr...]
    ppermute x2, waiting for transfers between devices: 5.7 us -> 11.1 us  [local(): lax.ppermute(value, both, [(flat(i, j), flat(i, 1 - j)) for i, j in even])]
    unnamed x60 -> x34, local copies, waits for them, and re-layouts: 5.04 us -> 5.29 us
  transfers between devices with their start and end apart: 37 -> 34, of which waited for: 12 -> 15; matrix products, arithmetic and copies ran while one was open for 6% -> 7% of each run, Pallas kernels for 33% -> 27%
where the time goes in v3:
time: 180 us; the launch traced here: 179 us
  waiting for transfers between devices  76.4 us (42%)
  Pallas kernels  51.5 us (29%)
  starting transfers between devices  29.1 us (16%)
  local copies, waits for them, and re-layouts  14.6 us (8%)
  other arithmetic  6.69 us (4%)
    ppermute x28, waiting for transfers between devices, xor_permute(): return lax.ppermute(value, axis, [(i, i ^ offset) for i in range(size)])  42 us
    pallas_call x11, Pallas kernels, call(): pl.pallas_call(kernel, grid=(1,), in_specs=in_specs, out_specs=tuple((who...  39.5 us
    ppermute x4, waiting for transfers between devices, local(): lax.ppermute(value, both, [(flat(i, j), flat(i ^ half, j)) for i, j in gr...  23.3 us
    ppermute x28, starting transfers between devices, xor_permute(): return lax.ppermute(value, axis, [(i, i ^ offset) for i in range(size)])  20.7 us
    pallas_call x4, Pallas kernels, teacher(): pl.pallas_call(functools.partial(teacher_kernel, offsets), grid=(number,)...  12 us
    ppermute x2, waiting for transfers between devices, local(): lax.ppermute(value, both, [(flat(i, j), flat(i, 1 - j)) for i, j in even])  11.1 us
    ppermute x4, starting transfers between devices, local(): lax.ppermute(value, both, [(flat(i, j), flat(i ^ half, j)) for i, j in gr...  5.77 us
    unnamed x34, local copies, waits for them, and re-layouts  5.29 us
  transfers between devices with their start and end apart: 34, of which 15 were waited for; matrix products, arithmetic and copies ran while one was open for 7% of the time, Pallas kernels for 27%

profile of v3, /device:TPU:24, one launch (start us, length us, event | category | flops | bytes accessed | tf_op | source)
XLA Modules:
  0.0 178.9 jit_solution(10174576275904124140)
XLA Ops:
  0.0 2.7 %slice_bitcast_fusion.2 = (bf16[64,4096]{1,0:T(8,128)(2,1)}, bf16[64,4096]{1,0:T(8,128)(2,1)}, bf16[64,4096]{1,0:T(8,128)(2,1)}, bf16[64,4096]{1,0:T(8,128)(2,1)S(1)}) fusion(bf16[1,256,4096]{2,1,0:T(8,128)(2,1)} %param.7), kind=kLoop, calls=%fused_computation.10 | loop fusion | bytes 4194304 | tf_op jit(solution)/shard_map/slice | solution.py:343
  2.7 1.5 collective-permute-start.5
  4.2 2.1 %constant_dynamic-slice_fusion.1 = (bf16[512,512]{1,0:T(8,128)(2,1)S(1)}, bf16[512,512]{1,0:T(8,128)(2,1)}) fusion(bf16[2048,2048]{1,0:T(8,128)(2,1)} %rest_3_.5, s32[]{:T(128)} %select_n.62), kind=kLoop, calls=%fused_computation.28 | loop fusion | bytes 2097156 | tf_op jit(solution)/shard_map/dynamic_slice | solution.py:288
  6.4 0.5 collective-permute-start
  6.9 0.5 collective-permute-start.12
  7.5 1.9 %collective-permute-start.4 = (bf16[64,4096]{1,0:T(8,128)(2,1)}, bf16[64,4096]{1,0:T(8,128)(2,1)S(1)}, u32[]{:S(2)}, u32[]{:S(2)}) collective-permute-start(bf16[64,4096]{1,0:T(8,128)(2,1)} %get-tuple-element.97), channel_id=1, source_target_pairs={{2,10},{6,14},{8,0},{12,4},{3,11},{7,15},{9,1},{13,5},{18,26},{22,... | collective-permute-start | bytes 1572872 | tf_op jit(solution)/shard_map/ppermute | solution.py:342
  9.4 8.4 %collective-permute-done.5 = bf16[64,4096]{1,0:T(8,128)(2,1)S(1)} collective-permute-done((bf16[64,4096]{1,0:T(8,128)(2,1)}, bf16[64,4096]{1,0:T(8,128)(2,1)S(1)}, u32[]{:S(2)}, u32[]{:S(2)}) %collective-permute-start.5) | collective-permute-done | bytes 524320 | tf_op jit(solution)/shard_map/ppermute | solution.py:24
  17.8 1.3 collective-permute-start.6
  19.1 0.5 collective-permute-start.15
  19.6 8.4 %collective-permute-done.12 = bf16[64,4096]{1,0:T(8,128)(2,1)} collective-permute-done((bf16[64,4096]{1,0:T(8,128)(2,1)S(1)}, bf16[64,4096]{1,0:T(8,128)(2,1)}, u32[]{:S(2)}, u32[]{:S(2)}) %collective-permute-start.12) | collective-permute-done | bytes 524320 | tf_op jit(solution)/shard_map/ppermute | solution.py:24
  28.4 2.9 %collective-permute-done.rest_2_.rest_3_ = bf16[512,768]{1,0:T(8,128)(2,1)S(1)} collective-permute-done((bf16[512,768]{1,0:T(8,128)(2,1)S(1)}, bf16[512,768]{1,0:T(8,128)(2,1)S(1)}, u32[]{:S(2)}, u32[]{:S(2)}) %collective-permute-start) | collective-permute-done | bytes 786464 | tf_op jit(solution)/shard_map/ppermute | solution.py:24
  31.3 1.3 collective-permute-start.17
  32.6 3.7 %collective-permute-done.4 = bf16[64,4096]{1,0:T(8,128)(2,1)S(1)} collective-permute-done((bf16[64,4096]{1,0:T(8,128)(2,1)}, bf16[64,4096]{1,0:T(8,128)(2,1)S(1)}, u32[]{:S(2)}, u32[]{:S(2)}) %collective-permute-start.4) | collective-permute-done | bytes 524320 | tf_op jit(solution)/shard_map/ppermute | solution.py:342
  36.3 1.5 collective-permute-start.1
  37.8 5.9 %collective-permute-done.6 = bf16[64,4096]{1,0:T(8,128)(2,1)} collective-permute-done((bf16[64,4096]{1,0:T(8,128)(2,1)S(1)}, bf16[64,4096]{1,0:T(8,128)(2,1)}, u32[]{:S(2)}, u32[]{:S(2)}) %collective-permute-start.6) | collective-permute-done | bytes 524320 | tf_op jit(solution)/shard_map/ppermute | solution.py:342
  43.7 1.1 broadcast_select_fusion.5
  45.0 1.4 constant_dynamic-slice_fusion.2
  46.3 1.3 constant_dynamic-slice_fusion.own
  47.6 5.4 %collective-permute-done.17 = bf16[64,4096]{1,0:T(8,128)(2,1)S(1)} collective-permute-done((bf16[64,4096]{1,0:T(8,128)(2,1)}, bf16[64,4096]{1,0:T(8,128)(2,1)S(1)}, u32[]{:S(2)}, u32[]{:S(2)}) %collective-permute-start.17) | collective-permute-done | bytes 524320 | tf_op jit(solution)/shard_map/ppermute | solution.py:344
  53.0 1.3 collective-permute-start.11
  54.4 1.3 collective-permute-start.13
  55.8 4.9 %collective-permute-done.7 = bf16[64,4096]{1,0:T(8,128)(2,1)S(1)} collective-permute-done((bf16[64,4096]{1,0:T(8,128)(2,1)S(1)}, bf16[64,4096]{1,0:T(8,128)(2,1)S(1)}, u32[]{:S(2)}, u32[]{:S(2)}) %collective-permute-start.7) | collective-permute-done | bytes 524320 | tf_op jit(solution)/shard_map/ppermute | solution.py:24
  60.9 0.7 collective-permute-start.16
  61.6 1.4 collective-permute-done.3.rest_5_.rest_6_
  63.0 2.7 %partial.5 = bf16[128,512]{1,0:T(8,128)(2,1)S(1)} custom-call(s32[3]{0:T(128)S(1)} %pad_add_fusion.place, bf16[128,4096]{1,0:T(8,128)(2,1)S(1)} %pad_maximum_fusion.rest_0_.act_low, bf16[2048,2048]{1,0:T(8,128)(2,1)} %rest_3_.5, bf16[512,768]{1,0:T(8,128)(2,1)S(1)} %collective-permute-done.rest_2_.rest_3_, ...), custom_call_target="tpu_custom_call" | custom-call | tf_op jit(solution)/shard_map/partial/pallas_call | solution.py:40
  65.7 1.3 collective-permute-start.18
  67.0 13.7 %collective-permute-done.13 = bf16[64,4096]{1,0:T(8,128)(2,1)S(1)} collective-permute-done((bf16[64,4096]{1,0:T(8,128)(2,1)}, bf16[64,4096]{1,0:T(8,128)(2,1)S(1)}, u32[]{:S(2)}, u32[]{:S(2)}) %collective-permute-start.13) | collective-permute-done | bytes 524320 | tf_op jit(solution)/shard_map/ppermute | solution.py:342
  80.7 1.5 collective-permute-start.19
  82.3 5.7 %collective-permute-done.18 = bf16[64,4096]{1,0:T(8,128)(2,1)S(1)} collective-permute-done((bf16[64,4096]{1,0:T(8,128)(2,1)S(1)}, bf16[64,4096]{1,0:T(8,128)(2,1)S(1)}, u32[]{:S(2)}, u32[]{:S(2)}) %collective-permute-start.18) | collective-permute-done | bytes 524320 | tf_op jit(solution)/shard_map/ppermute | solution.py:344
  88.0 3.2 %maximum_select_fusion.act_own.rest_1_.rest_2_ = bf16[256,4096]{1,0:T(8,128)(2,1)} fusion(bf16[64,4096]{1,0:T(8,128)(2,1)} %collective-permute-done.12, bf16[64,4096]{1,0:T(8,128)(2,1)S(1)} %collective-permute-done.18, bf16[64,4096]{1,0:T(8,128)(2,1)S(1)} %collective-permute-done.5, bf16[64,4096]{1,0:T(8,128)(2,1)S(1)} %collective-permute-done.17, ...), kind=kLoop, calls=%fused_computation | loop fusion | flops 9437184 | bytes 6291457 | tf_op jit(solution)/shard_map/jit(_where)/select_n | solution.py:380
  91.3 2.6 %collective-permute-done.19.rest_5_ = bf16[512,512]{1,0:T(8,128)(2,1)} collective-permute-done((bf16[512,512]{1,0:T(8,128)(2,1)}, bf16[512,512]{1,0:T(8,128)(2,1)}, u32[]{:S(2)}, u32[]{:S(2)}) %collective-permute-start.19) | collective-permute-done | bytes 524320 | tf_op jit(solution)/shard_map/ppermute | solution.py:24
  93.9 3.6 %collective-permute-done.14 = bf16[64,4096]{1,0:T(8,128)(2,1)S(1)} collective-permute-done((bf16[64,4096]{1,0:T(8,128)(2,1)S(1)}, bf16[64,4096]{1,0:T(8,128)(2,1)S(1)}, u32[]{:S(2)}, u32[]{:S(2)}) %collective-permute-start.14) | collective-permute-done | bytes 524320 | tf_op jit(solution)/shard_map/ppermute | solution.py:24
  97.7 4.6 %extra.1 = (f32[512,256]{1,0:T(8,128)S(1)}, bf16[512,256]{1,0:T(8,128)(2,1)}, f32[16,512]{1,0:T(8,128)S(1)}) custom-call(s32[3]{0:T(128)S(1)} %pad_add_fusion.place, bf16[256,4096]{1,0:T(8,128)(2,1)} %maximum_select_fusion.act_own.rest_1_.rest_2_, bf16[128,4096]{1,0:T(8,128)(2,1)S(1)} %pad_maximum_fusion.rest_0_.act_low, ...), custom_call_target="tpu_custom_call" | custom-call | tf_op jit(solution)/shard_map/extra/pallas_call | solution.py:40
  102.3 0.8 copy-done.8
  103.1 1.5 collective-permute-start.25
  104.6 0.5 collective-permute-start.22
  105.2 0.7 pad_maximum_fusion.5
  105.9 2.1 %collective-permute-start.20 = (bf16[512,256]{1,0:T(8,128)(2,1)}, bf16[512,256]{1,0:T(8,128)(2,1)}, u32[]{:S(2)}, u32[]{:S(2)}) collective-permute-start(bf16[512,256]{1,0:T(8,128)(2,1)} %pad_maximum_fusion.5), channel_id=1, source_target_pairs={{0,4},{4,0},{8,12},{12,8},{1,5},{5,1},{9,13},{13,9},{2,6},{6,2},{1... | collective-permute-start | bytes 786440 | tf_op jit(solution)/shard_map/ppermute | solution.py:24
  108.0 6.3 %collective-permute-done.9.rest_0_ = bf16[128,512]{1,0:T(8,128)(2,1)S(1)} collective-permute-done((bf16[128,512]{1,0:T(8,128)(2,1)S(1)}, bf16[128,512]{1,0:T(8,128)(2,1)S(1)}, u32[]{:S(2)}, u32[]{:S(2)}) %collective-permute-start.9) | collective-permute-done | bytes 131104 | tf_op jit(solution)/shard_map/ppermute | solution.py:24
  114.5 1.1 copy-done.3
  115.6 1.1 copy-done.5
  116.7 1.1 copy-done.7
  117.9 4.1 %partial.6 = (bf16[128,512]{1,0:T(8,128)(2,1)S(1)}, f32[256,512]{1,0:T(8,128)S(1)}) custom-call(s32[3]{0:T(128)S(1)} %pad_add_fusion.place, bf16[128,4096]{1,0:T(8,128)(2,1)S(1)} %pad_maximum_fusion.1.act_high.rest_0_.rest_1_, bf16[256,4096]{1,0:T(8,128)(2,1)} %maximum_select_fusion.act_own.rest_1_.rest_2_, bf16[2048,2048]{1,0:T(8,128)(2,1)} %rest_3_.5, ...), custom_call_target="tpu_custom_call" | custom-call | tf_op jit(solution)/shard_map/partial/pallas_call | solution.py:40
  122.0 3.0 %collective-permute-start.24 = (f32[16,512]{1,0:T(8,128)S(1)}, f32[16,512]{1,0:T(8,128)S(1)}, u32[]{:S(2)}, u32[]{:S(2)}) collective-permute-start(f32[16,512]{1,0:T(8,128)S(1)} %get-tuple-element.110), channel_id=1, source_target_pairs={{0,8},{4,12},{8,0},{12,4},{1,9},{5,13},{9,1},{13,5},{2,10},{6,14},... | collective-permute-start | bytes 98312 | tf_op jit(solution)/shard_map/ppermute | solution.py:24
  125.1 5.4 %partial.7 = (bf16[256,512]{1,0:T(8,128)(2,1)S(1)}, f32[256,512]{1,0:T(8,128)S(1)}) custom-call(s32[3]{0:T(128)S(1)} %pad_add_fusion.place, bf16[128,4096]{1,0:T(8,128)(2,1)S(1)} %pad_maximum_fusion.rest_0_.act_low, bf16[128,4096]{1,0:T(8,128)(2,1)S(1)} %pad_maximum_fusion.1.act_high.rest_0_.rest_1_, ...), custom_call_target="tpu_custom_call" | custom-call | tf_op jit(solution)/shard_map/partial/pallas_call | solution.py:40
  130.4 1.0 pad_maximum_fusion.3.keys
  131.5 2.9 %collective-permute-start.28 = (bf16[256,512]{1,0:T(8,128)(2,1)S(1)}, bf16[256,512]{1,0:T(8,128)(2,1)S(1)}, u32[]{:S(2)}, u32[]{:S(2)}) collective-permute-start(bf16[256,512]{1,0:T(8,128)(2,1)S(1)} %get-tuple-element.121), channel_id=1, source_target_pairs={{0,8},{4,12},{8,0},{12,4},{1,9},{5,13},{9,1},{13,5},{2,10},{6,14},... | collective-permute-start | bytes 786440 | tf_op jit(solution)/shard_map/ppermute | solution.py:24
  134.4 3.0 %teacher.4.norm = f32[4,256,128]{2,1,0:T(8,128)S(1)} custom-call(s32[3]{0:T(128)S(1)} %pad_add_fusion.place, bf16[256,2048]{1,0:T(8,128)(2,1)S(1)} %bitcast.28, bf16[1024,256]{1,0:T(8,128)(2,1)S(1)} %pad_maximum_fusion.3.keys), custom_call_target="tpu_custom_call" | custom-call | tf_op jit(solution)/shard_map/teacher/pallas_call | solution.py:314
  138.0 1.0 fusion.1
  139.2 2.9 %collective-permute-done.31.rest_1_ = bf16[128,512]{1,0:T(8,128)(2,1)S(1)} collective-permute-done((bf16[128,512]{1,0:T(8,128)(2,1)S(1)}, bf16[128,512]{1,0:T(8,128)(2,1)S(1)}, u32[]{:S(2)}, u32[]{:S(2)}) %collective-permute-start.31) | collective-permute-done | bytes 131104 | tf_op jit(solution)/shard_map/ppermute | solution.py:24
  142.1 3.0 %teacher.5.norm = f32[4,256,128]{2,1,0:T(8,128)S(1)} custom-call(s32[3]{0:T(128)S(1)} %pad_add_fusion.place, bf16[256,2048]{1,0:T(8,128)(2,1)S(1)} %bitcast.29, bf16[1024,256]{1,0:T(8,128)(2,1)S(1)} %pad_maximum_fusion.3.keys), custom_call_target="tpu_custom_call" | custom-call | tf_op jit(solution)/shard_map/teacher/pallas_call | solution.py:314
  145.1 1.0 copy-done.12
  146.1 5.1 %partial.8 = (bf16[256,512]{1,0:T(8,128)(2,1)S(1)}, f32[256,512]{1,0:T(8,128)S(1)}) custom-call(s32[3]{0:T(128)S(1)} %pad_add_fusion.place, bf16[128,4096]{1,0:T(8,128)(2,1)S(1)} %pad_maximum_fusion.rest_0_.act_low, bf16[128,4096]{1,0:T(8,128)(2,1)S(1)} %pad_maximum_fusion.1.act_high.rest_0_.rest_1_, ...), custom_call_target="tpu_custom_call" | custom-call | tf_op jit(solution)/shard_map/partial/pallas_call | solution.py:40
  151.3 3.0 %teacher.6.norm = f32[4,256,128]{2,1,0:T(8,128)S(1)} custom-call(s32[3]{0:T(128)S(1)} %pad_add_fusion.place, bf16[256,2048]{1,0:T(8,128)(2,1)S(1)} %bitcast.30, bf16[1024,256]{1,0:T(8,128)(2,1)S(1)} %pad_maximum_fusion.3.keys), custom_call_target="tpu_custom_call" | custom-call | tf_op jit(solution)/shard_map/teacher/pallas_call | solution.py:314
  154.3 5.1 %partial.9 = (bf16[256,512]{1,0:T(8,128)(2,1)S(1)}, f32[256,512]{1,0:T(8,128)S(1)}) custom-call(s32[3]{0:T(128)S(1)} %pad_add_fusion.place, bf16[128,4096]{1,0:T(8,128)(2,1)S(1)} %pad_maximum_fusion.rest_0_.act_low, bf16[128,4096]{1,0:T(8,128)(2,1)S(1)} %pad_maximum_fusion.1.act_high.rest_0_.rest_1_, ...), custom_call_target="tpu_custom_call" | custom-call | tf_op jit(solution)/shard_map/partial/pallas_call | solution.py:40
  159.4 2.4 %collective-permute-start.33 = (bf16[256,512]{1,0:T(8,128)(2,1)S(1)}, bf16[256,512]{1,0:T(8,128)(2,1)S(1)}, u32[]{:S(2)}, u32[]{:S(2)}) collective-permute-start(bf16[256,512]{1,0:T(8,128)(2,1)S(1)} %get-tuple-element.142), channel_id=1, source_target_pairs={{0,8},{4,12},{8,0},{12,4},{1,9},{5,13},{9,1},{13,5},{2,10},{6,14},... | collective-permute-start | bytes 786440 | tf_op jit(solution)/shard_map/ppermute | solution.py:24
  161.8 3.0 %teacher.7.norm = f32[4,256,128]{2,1,0:T(8,128)S(1)} custom-call(s32[3]{0:T(128)S(1)} %pad_add_fusion.place, bf16[256,2048]{1,0:T(8,128)(2,1)S(1)} %bitcast.31, bf16[1024,256]{1,0:T(8,128)(2,1)S(1)} %pad_maximum_fusion.3.keys), custom_call_target="tpu_custom_call" | custom-call | tf_op jit(solution)/shard_map/teacher/pallas_call | solution.py:314
  164.8 1.3 decay.1
  166.2 2.8 %loss.4 = f32[4,1,256]{2,1,0:T(1,128)S(1)} custom-call(s32[3]{0:T(128)S(1)} %pad_add_fusion.place, bf16[256,2048]{1,0:T(8,128)(2,1)S(1)} %bitcast.32, f32[256,512]{1,0:T(8,128)S(1)} %get-tuple-element.114.kept, bf16[1024,256]{1,0:T(8,128)(2,1)S(1)} %pad_maximum_fusion.3.keys, bf16[1024,256]{1,0:T(8,128)(2,1)S(1)} %pad_maximum_fusion.4.inputs, ...), custom_call_target="tpu_custom_call" | custom-call | tf_op jit(solution)/shard_map/loss/pallas_call | solution.py:40
  169.0 3.0 %loss.5 = f32[4,1,256]{2,1,0:T(1,128)S(1)} custom-call(s32[3]{0:T(128)S(1)} %pad_add_fusion.place, bf16[256,2048]{1,0:T(8,128)(2,1)S(1)} %bitcast.33, f32[256,512]{1,0:T(8,128)S(1)} %get-tuple-element.122.kept, bf16[1024,256]{1,0:T(8,128)(2,1)S(1)} %pad_maximum_fusion.3.keys, bf16[1024,256]{1,0:T(8,128)(2,1)S(1)} %pad_maximum_fusion.4.inputs, ...), custom_call_target="tpu_custom_call" | custom-call | tf_op jit(solution)/shard_map/loss/pallas_call | solution.py:40
  172.0 2.8 %loss.6 = f32[4,1,256]{2,1,0:T(1,128)S(1)} custom-call(s32[3]{0:T(128)S(1)} %pad_add_fusion.place, bf16[256,2048]{1,0:T(8,128)(2,1)S(1)} %bitcast.34, f32[256,512]{1,0:T(8,128)S(1)} %get-tuple-element.138.kept, bf16[1024,256]{1,0:T(8,128)(2,1)S(1)} %pad_maximum_fusion.3.keys, bf16[1024,256]{1,0:T(8,128)(2,1)S(1)} %pad_maximum_fusion.4.inputs, ...), custom_call_target="tpu_custom_call" | custom-call | tf_op jit(solution)/shard_map/loss/pallas_call | solution.py:40
  174.8 0.6 collective-permute-done.33.rest_0_
  175.4 2.8 %loss.7 = f32[4,1,256]{2,1,0:T(1,128)S(1)} custom-call(s32[3]{0:T(128)S(1)} %pad_add_fusion.place, bf16[256,2048]{1,0:T(8,128)(2,1)S(1)} %bitcast.35, f32[256,512]{1,0:T(8,128)S(1)} %get-tuple-element.143.kept, bf16[1024,256]{1,0:T(8,128)(2,1)S(1)} %pad_maximum_fusion.3.keys, bf16[1024,256]{1,0:T(8,128)(2,1)S(1)} %pad_maximum_fusion.4.inputs, ...), custom_call_target="tpu_custom_call" | custom-call | tf_op jit(solution)/shard_map/loss/pallas_call | solution.py:40
  178.2 0.6 copy.9
  (86 shorter events, 2.3 us)
Async XLA Ops:
  0.0 44.9 %copy-start = (bf16[1,256,512]{2,1,0:T(8,128)(2,1)S(1)}, bf16[1,256,512]{2,1,0:T(8,128)(2,1)}, u32[]{:S(2)}) copy-start(bf16[1,256,512]{2,1,0:T(8,128)(2,1)} %param.9) | copy-start | bytes 786436
  2.7 15.0 %collective-permute-start.5 = (bf16[64,4096]{1,0:T(8,128)(2,1)}, bf16[64,4096]{1,0:T(8,128)(2,1)S(1)}, u32[]{:S(2)}, u32[]{:S(2)}) collective-permute-start(bf16[64,4096]{1,0:T(8,128)(2,1)} %get-tuple-element.163), channel_id=1, source_target_pairs={{0,2},{2,0},{1,3},{3,1},{4,6},{6,4},{5,7},{7,5},{8,10},{10,8},{9,1... | collective-permute-start | bytes 1572872 | tf_op jit(solution)/shard_map/ppermute | solution.py:24
  4.2 2.1 %dynamic-slice-start = ((bf16[2048,512]{1,0:T(8,128)(2,1)}, s32[]{:T(128)}, s32[]{:T(128)}), bf16[512,256]{1,0:T(8,128)(2,1)S(1)}, s32[]{:S(2)}) async-start(bf16[2048,512]{1,0:T(8,128)(2,1)} %param.11, s32[]{:T(128)} %select_n.62, s32[]{:T(128)} %select_n.64), calls=%async_computation | async-start | bytes 524800 | tf_op jit(solution)/shard_map/dynamic_slice | solution.py:290
  4.2 14.8 %copy-start.10 = (bf16[2048,16]{0,1:T(8,128)(2,1)S(1)}, bf16[2048,16]{0,1:T(8,128)(2,1)}, u32[]{:S(2)}) copy-start(bf16[2048,16]{0,1:T(8,128)(2,1)} %param.12) | copy-start | bytes 196612
  6.4 24.9 %collective-permute-start = (bf16[512,768]{1,0:T(8,128)(2,1)S(1)}, bf16[512,768]{1,0:T(8,128)(2,1)S(1)}, u32[]{:S(2)}, u32[]{:S(2)}) collective-permute-start(bf16[512,768]{1,0:T(8,128)(2,1)S(1)} %pad_maximum_fusion.2), channel_id=1, source_target_pairs={{0,4},{4,0},{8,12},{12,8},{1,5},{5,1},{9,13},{13,9},{2,6},{6,2},{1... | collective-permute-start | bytes 2359304 | tf_op jit(solution)/shard_map/ppermute | solution.py:24
  6.9 21.0 %collective-permute-start.12 = (bf16[64,4096]{1,0:T(8,128)(2,1)S(1)}, bf16[64,4096]{1,0:T(8,128)(2,1)}, u32[]{:S(2)}, u32[]{:S(2)}) collective-permute-start(bf16[64,4096]{1,0:T(8,128)(2,1)S(1)} %get-tuple-element.166), channel_id=1, source_target_pairs={{0,2},{2,0},{1,3},{3,1},{4,6},{6,4},{5,7},{7,5},{8,10},{10,8},{9,1... | collective-permute-start | bytes 1572872 | tf_op jit(solution)/shard_map/ppermute | solution.py:24
  7.5 28.8 %collective-permute-start.4 = (bf16[64,4096]{1,0:T(8,128)(2,1)}, bf16[64,4096]{1,0:T(8,128)(2,1)S(1)}, u32[]{:S(2)}, u32[]{:S(2)}) collective-permute-start(bf16[64,4096]{1,0:T(8,128)(2,1)} %get-tuple-element.97), channel_id=1, source_target_pairs={{2,10},{6,14},{8,0},{12,4},{3,11},{7,15},{9,1},{13,5},{18,26},{22,... | collective-permute-start | bytes 1572872 | tf_op jit(solution)/shard_map/ppermute | solution.py:342
  17.8 25.9 %collective-permute-start.6 = (bf16[64,4096]{1,0:T(8,128)(2,1)S(1)}, bf16[64,4096]{1,0:T(8,128)(2,1)}, u32[]{:S(2)}, u32[]{:S(2)}) collective-permute-start(bf16[64,4096]{1,0:T(8,128)(2,1)S(1)} %collective-permute-done.5), channel_id=1, source_target_pairs={{0,8},{4,12},{10,2},{14,6},{1,9},{5,13},{11,3},{15,7},{16,24},{20,... | collective-permute-start | bytes 1572872 | tf_op jit(solution)/shard_map/ppermute | solution.py:342
  19.1 74.9 %collective-permute-start.15 = (bf16[16,2048]{1,0:T(8,128)(2,1)S(1)}, bf16[16,2048]{1,0:T(8,128)(2,1)S(1)}, u32[]{:S(2)}, u32[]{:S(2)}) collective-permute-start(bf16[16,2048]{1,0:T(8,128)(2,1)S(1)} %bitcast.36), channel_id=1, source_target_pairs={{0,4},{4,0},{8,12},{12,8},{1,5},{5,1},{9,13},{13,9},{2,6},{6,2},{1... | collective-permute-start | bytes 196616 | tf_op jit(solution)/shard_map/ppermute | solution.py:24
  27.9 27.7 %collective-permute-start.8 = (bf16[512,512]{1,0:T(8,128)(2,1)}, bf16[512,512]{1,0:T(8,128)(2,1)}, u32[]{:S(2)}, u32[]{:S(2)}) collective-permute-start(bf16[512,512]{1,0:T(8,128)(2,1)} %get-tuple-element.162), channel_id=1, source_target_pairs={{0,4},{4,0},{8,12},{12,8},{1,5},{5,1},{9,13},{13,9},{2,6},{6,2},{1... | collective-permute-start | bytes 1572872 | tf_op jit(solution)/shard_map/ppermute | solution.py:24
  31.3 21.7 %collective-permute-start.17 = (bf16[64,4096]{1,0:T(8,128)(2,1)}, bf16[64,4096]{1,0:T(8,128)(2,1)S(1)}, u32[]{:S(2)}, u32[]{:S(2)}) collective-permute-start(bf16[64,4096]{1,0:T(8,128)(2,1)} %get-tuple-element.97), channel_id=1, source_target_pairs={{0,2},{4,6},{10,8},{14,12},{1,3},{5,7},{11,9},{15,13},{16,18},{20,... | collective-permute-start | bytes 1572872 | tf_op jit(solution)/shard_map/ppermute | solution.py:344
  36.3 18.1 %collective-permute-start.1 = (bf16[512,768]{1,0:T(8,128)(2,1)S(1)}, bf16[512,768]{1,0:T(8,128)(2,1)S(1)}, u32[]{:S(2)}, u32[]{:S(2)}) collective-permute-start(bf16[512,768]{1,0:T(8,128)(2,1)S(1)} %collective-permute-done.rest_2_.rest_3_), channel_id=1, source_target_pairs={{0,16},{16,0},{1,17},{17,1},{2,18},{18,2},{3,19},{19,3},{4,20},{20... | collective-permute-start | bytes 2359304 | tf_op jit(solution)/shard_map/ppermute | solution.py:24
  44.8 15.9 %collective-permute-start.7 = (bf16[64,4096]{1,0:T(8,128)(2,1)S(1)}, bf16[64,4096]{1,0:T(8,128)(2,1)S(1)}, u32[]{:S(2)}, u32[]{:S(2)}) collective-permute-start(bf16[64,4096]{1,0:T(8,128)(2,1)S(1)} %broadcast_select_fusion.5), channel_id=1, source_target_pairs={{0,2},{2,0},{1,3},{3,1},{4,6},{6,4},{5,7},{7,5},{8,10},{10,8},{9,1... | collective-permute-start | bytes 1572872 | tf_op jit(solution)/shard_map/ppermute | solution.py:24
  45.0 8.1 %copy-start.15 = (bf16[64,4096]{1,0:T(8,128)(2,1)S(1)}, bf16[64,4096]{1,0:T(8,128)(2,1)}, u32[]{:S(2)}) copy-start(bf16[64,4096]{1,0:T(8,128)(2,1)} %get-tuple-element.99) | copy-start | bytes 1572868
  53.0 12.7 %collective-permute-start.11 = (bf16[64,4096]{1,0:T(8,128)(2,1)S(1)}, bf16[64,4096]{1,0:T(8,128)(2,1)S(1)}, u32[]{:S(2)}, u32[]{:S(2)}) collective-permute-start(bf16[64,4096]{1,0:T(8,128)(2,1)S(1)} %copy-done.15), channel_id=1, source_target_pairs={{2,10},{6,14},{8,0},{12,4},{3,11},{7,15},{9,1},{13,5},{18,26},{22,... | collective-permute-start | bytes 1572872 | tf_op jit(solution)/shard_map/ppermute | solution.py:342
  54.4 36.9 %copy-start.2 = (bf16[512,768]{1,0:T(8,128)(2,1)}, bf16[512,768]{1,0:T(8,128)(2,1)S(1)}, u32[]{:S(2)}) copy-start(bf16[512,768]{1,0:T(8,128)(2,1)S(1)} %collective-permute-done.1.rest_3_.rest_4_) | copy-start | bytes 2359300
  54.4 26.3 %collective-permute-start.13 = (bf16[64,4096]{1,0:T(8,128)(2,1)}, bf16[64,4096]{1,0:T(8,128)(2,1)S(1)}, u32[]{:S(2)}, u32[]{:S(2)}) collective-permute-start(bf16[64,4096]{1,0:T(8,128)(2,1)} %collective-permute-done.12), channel_id=1, source_target_pairs={{0,8},{4,12},{10,2},{14,6},{1,9},{5,13},{11,3},{15,7},{16,24},{20,... | collective-permute-start | bytes 1572872 | tf_op jit(solution)/shard_map/ppermute | solution.py:342
  55.7 5.2 %collective-permute-start.2 = (bf16[512,768]{1,0:T(8,128)(2,1)S(1)}, bf16[512,768]{1,0:T(8,128)(2,1)S(1)}, u32[]{:S(2)}, u32[]{:S(2)}) collective-permute-start(bf16[512,768]{1,0:T(8,128)(2,1)S(1)} %collective-permute-done.rest_2_.rest_3_), channel_id=1, source_target_pairs={{0,1},{1,0},{2,3},{3,2},{4,5},{5,4},{6,7},{7,6},{8,9},{9,8},{10,11... | collective-permute-start | bytes 2359304 | tf_op jit(solution)/shard_map/ppermute | solution.py:24
  60.7 2.3 %collective-permute-start.3 = (bf16[512,768]{1,0:T(8,128)(2,1)S(1)}, bf16[512,768]{1,0:T(8,128)(2,1)S(1)}, u32[]{:S(2)}, u32[]{:S(2)}) collective-permute-start(bf16[512,768]{1,0:T(8,128)(2,1)S(1)} %collective-permute-done.1.rest_3_.rest_4_), channel_id=1, source_target_pairs={{0,1},{1,0},{2,3},{3,2},{4,5},{5,4},{6,7},{7,6},{8,9},{9,8},{10,11... | collective-permute-start | bytes 2359304 | tf_op jit(solution)/shard_map/ppermute | solution.py:24
  60.9 30.4 %copy-start.4 = (bf16[512,768]{1,0:T(8,128)(2,1)}, bf16[512,768]{1,0:T(8,128)(2,1)S(1)}, u32[]{:S(2)}) copy-start(bf16[512,768]{1,0:T(8,128)(2,1)S(1)} %collective-permute-done.2.rest_4_.rest_5_) | copy-start | bytes 2359300
  60.9 33.0 %collective-permute-start.16 = (bf16[256,256]{1,0:T(8,128)(2,1)S(1)}, bf16[256,256]{1,0:T(8,128)(2,1)S(1)}, u32[]{:S(2)}, u32[]{:S(2)}) collective-permute-start(bf16[256,256]{1,0:T(8,128)(2,1)S(1)} %dynamic-slice_bitcast_fusion), channel_id=1, source_target_pairs={{0,8},{4,12},{8,0},{12,4},{1,9},{5,13},{9,1},{13,5},{2,10},{6,14},... | collective-permute-start | bytes 393224 | tf_op jit(solution)/shard_map/ppermute | solution.py:24
  63.0 28.3 %copy-start.6 = (bf16[512,768]{1,0:T(8,128)(2,1)}, bf16[512,768]{1,0:T(8,128)(2,1)S(1)}, u32[]{:S(2)}) copy-start(bf16[512,768]{1,0:T(8,128)(2,1)S(1)} %collective-permute-done.3.rest_5_.rest_6_) | copy-start | bytes 2359300
  63.0 40.1 %collective-permute-start.10 = (bf16[512,1024]{1,0:T(8,128)(2,1)S(1)}, bf16[512,1024]{1,0:T(8,128)(2,1)}, u32[]{:S(2)}, u32[]{:S(2)}) collective-permute-start(bf16[512,1024]{1,0:T(8,128)(2,1)S(1)} %constant_dynamic-slice_fusion.2), channel_id=1, source_target_pairs={{0,4},{4,0},{8,12},{12,8},{1,5},{5,1},{9,13},{13,9},{2,6},{6,2},{1... | collective-permute-start | bytes 3145736 | tf_op jit(solution)/shard_map/ppermute | solution.py:24
  63.0 25.0 %copy-start.11 = (bf16[1,256,4096]{2,1,0:T(8,128)(2,1)S(1)}, bf16[1,256,4096]{2,1,0:T(8,128)(2,1)}, u32[]{:S(2)}) copy-start(bf16[1,256,4096]{2,1,0:T(8,128)(2,1)} %param.7) | copy-start | bytes 6291460
  65.7 22.3 %collective-permute-start.18 = (bf16[64,4096]{1,0:T(8,128)(2,1)S(1)}, bf16[64,4096]{1,0:T(8,128)(2,1)S(1)}, u32[]{:S(2)}, u32[]{:S(2)}) collective-permute-start(bf16[64,4096]{1,0:T(8,128)(2,1)S(1)} %copy-done.15), channel_id=1, source_target_pairs={{0,2},{4,6},{10,8},{14,12},{1,3},{5,7},{11,9},{15,13},{16,18},{20,... | collective-permute-start | bytes 1572872 | tf_op jit(solution)/shard_map/ppermute | solution.py:344
  80.7 13.2 %collective-permute-start.19 = (bf16[512,512]{1,0:T(8,128)(2,1)}, bf16[512,512]{1,0:T(8,128)(2,1)}, u32[]{:S(2)}, u32[]{:S(2)}) collective-permute-start(bf16[512,512]{1,0:T(8,128)(2,1)} %collective-permute-done.8.rest_4_), channel_id=1, source_target_pairs={{0,16},{16,0},{1,17},{17,1},{2,18},{18,2},{3,19},{19,3},{4,20},{20... | collective-permute-start | bytes 1572872 | tf_op jit(solution)/shard_map/ppermute | solution.py:24
  88.0 9.5 %collective-permute-start.14 = (bf16[64,4096]{1,0:T(8,128)(2,1)S(1)}, bf16[64,4096]{1,0:T(8,128)(2,1)S(1)}, u32[]{:S(2)}, u32[]{:S(2)}) collective-permute-start(bf16[64,4096]{1,0:T(8,128)(2,1)S(1)} %broadcast_select_fusion.2), channel_id=1, source_target_pairs={{0,2},{2,0},{1,3},{3,1},{4,6},{6,4},{5,7},{7,5},{8,10},{10,8},{9,1... | collective-permute-start | bytes 1572872 | tf_op jit(solution)/shard_map/ppermute | solution.py:24
  93.9 11.2 %copy-start.13 = (bf16[256,256]{1,0:T(8,128)(2,1)}, bf16[256,256]{1,0:T(8,128)(2,1)S(1)}, u32[]{:S(2)}) copy-start(bf16[256,256]{1,0:T(8,128)(2,1)S(1)} %collective-permute-done.16) | copy-start | bytes 393220
  97.6 16.7 %copy-start.16 = (f32[16]{0:T(128)S(1)}, f32[16]{0:T(128)}, u32[]{:S(2)}) copy-start(f32[16]{0:T(128)} %param.13) | copy-start | bytes 196
  102.3 0.8 copy-start.8
  103.1 34.3 %collective-permute-start.25 = (bf16[512,1024]{1,0:T(8,128)(2,1)}, bf16[512,1024]{1,0:T(8,128)(2,1)}, u32[]{:S(2)}, u32[]{:S(2)}) collective-permute-start(bf16[512,1024]{1,0:T(8,128)(2,1)} %collective-permute-done.10.rest_4_), channel_id=1, source_target_pairs={{0,16},{16,0},{1,17},{17,1},{2,18},{18,2},{3,19},{19,3},{4,20},{20... | collective-permute-start | bytes 3145736 | tf_op jit(solution)/shard_map/ppermute | solution.py:24
  104.6 17.3 %collective-permute-start.21 = (bf16[512,512]{1,0:T(8,128)(2,1)}, bf16[512,512]{1,0:T(8,128)(2,1)}, u32[]{:S(2)}, u32[]{:S(2)}) collective-permute-start(bf16[512,512]{1,0:T(8,128)(2,1)} %collective-permute-done.8.rest_4_), channel_id=1, source_target_pairs={{0,1},{1,0},{2,3},{3,2},{4,5},{5,4},{6,7},{7,6},{8,9},{9,8},{10,11... | collective-permute-start | bytes 1572872 | tf_op jit(solution)/shard_map/ppermute | solution.py:24
  104.6 20.3 %collective-permute-start.22 = (bf16[512,512]{1,0:T(8,128)(2,1)}, bf16[512,512]{1,0:T(8,128)(2,1)}, u32[]{:S(2)}, u32[]{:S(2)}) collective-permute-start(bf16[512,512]{1,0:T(8,128)(2,1)} %collective-permute-done.19.rest_5_), channel_id=1, source_target_pairs={{0,1},{1,0},{2,3},{3,2},{4,5},{5,4},{6,7},{7,6},{8,9},{9,8},{10,11... | collective-permute-start | bytes 1572872 | tf_op jit(solution)/shard_map/ppermute | solution.py:24
  105.2 9.2 %collective-permute-start.9 = (bf16[128,512]{1,0:T(8,128)(2,1)S(1)}, bf16[128,512]{1,0:T(8,128)(2,1)S(1)}, u32[]{:S(2)}, u32[]{:S(2)}) collective-permute-start(bf16[128,512]{1,0:T(8,128)(2,1)S(1)} %partial.5), channel_id=1, source_target_pairs={{0,8},{4,12},{8,0},{12,4},{1,9},{5,13},{9,1},{13,5},{2,10},{6,14},... | collective-permute-start | bytes 393224 | tf_op jit(solution)/shard_map/ppermute | solution.py:24
  105.9 24.5 %collective-permute-start.20 = (bf16[512,256]{1,0:T(8,128)(2,1)}, bf16[512,256]{1,0:T(8,128)(2,1)}, u32[]{:S(2)}, u32[]{:S(2)}) collective-permute-start(bf16[512,256]{1,0:T(8,128)(2,1)} %pad_maximum_fusion.5), channel_id=1, source_target_pairs={{0,4},{4,0},{8,12},{12,8},{1,5},{5,1},{9,13},{13,9},{2,6},{6,2},{1... | collective-permute-start | bytes 786440 | tf_op jit(solution)/shard_map/ppermute | solution.py:24
  114.4 23.6 %collective-permute-start.23 = (bf16[512,256]{1,0:T(8,128)(2,1)}, bf16[512,256]{1,0:T(8,128)(2,1)}, u32[]{:S(2)}, u32[]{:S(2)}) collective-permute-start(bf16[512,256]{1,0:T(8,128)(2,1)} %get-tuple-element.109), channel_id=1, source_target_pairs={{0,8},{4,12},{8,0},{12,4},{1,9},{5,13},{9,1},{13,5},{2,10},{6,14},... | collective-permute-start | bytes 786440 | tf_op jit(solution)/shard_map/ppermute | solution.py:24
  114.5 1.1 copy-start.3
  115.6 1.1 copy-start.5
  116.7 1.1 copy-start.7
  122.0 15.5 %collective-permute-start.24 = (f32[16,512]{1,0:T(8,128)S(1)}, f32[16,512]{1,0:T(8,128)S(1)}, u32[]{:S(2)}, u32[]{:S(2)}) collective-permute-start(f32[16,512]{1,0:T(8,128)S(1)} %get-tuple-element.110), channel_id=1, source_target_pairs={{0,8},{4,12},{8,0},{12,4},{1,9},{5,13},{9,1},{13,5},{2,10},{6,14},... | collective-permute-start | bytes 98312 | tf_op jit(solution)/shard_map/ppermute | solution.py:24
  125.0 17.1 %collective-permute-start.31 = (bf16[128,512]{1,0:T(8,128)(2,1)S(1)}, bf16[128,512]{1,0:T(8,128)(2,1)S(1)}, u32[]{:S(2)}, u32[]{:S(2)}) collective-permute-start(bf16[128,512]{1,0:T(8,128)(2,1)S(1)} %get-tuple-element.115), channel_id=1, source_target_pairs={{0,8},{4,12},{8,0},{12,4},{1,9},{5,13},{9,1},{13,5},{2,10},{6,14},... | collective-permute-start | bytes 393224 | tf_op jit(solution)/shard_map/ppermute | solution.py:24
  125.0 5.4 %copy-start.14 = (bf16[256,256]{1,0:T(8,128)(2,1)S(1)}, bf16[256,256]{1,0:T(8,128)(2,1)}, u32[]{:S(2)}) copy-start(bf16[256,256]{1,0:T(8,128)(2,1)} %copy-done.13) | copy-start | bytes 393220
  125.0 9.3 %copy-start.1 = (bf16[1,256,2048]{2,1,0:T(8,128)(2,1)S(1)}, bf16[1,256,2048]{2,1,0:T(8,128)(2,1)}, u32[]{:S(2)}) copy-start(bf16[1,256,2048]{2,1,0:T(8,128)(2,1)} %param.8) | copy-start | bytes 3145732
  130.4 8.6 %copy-start.9 = (f32[512,256]{1,0:T(8,128)S(1)}, f32[512,256]{1,0:T(8,128)}, u32[]{:S(2)}) copy-start(f32[512,256]{1,0:T(8,128)} %copy-done.8) | copy-start | bytes 1572868
  131.5 22.8 %collective-permute-start.28 = (bf16[256,512]{1,0:T(8,128)(2,1)S(1)}, bf16[256,512]{1,0:T(8,128)(2,1)S(1)}, u32[]{:S(2)}, u32[]{:S(2)}) collective-permute-start(bf16[256,512]{1,0:T(8,128)(2,1)S(1)} %get-tuple-element.121), channel_id=1, source_target_pairs={{0,8},{4,12},{8,0},{12,4},{1,9},{5,13},{9,1},{13,5},{2,10},{6,14},... | collective-permute-start | bytes 786440 | tf_op jit(solution)/shard_map/ppermute | solution.py:24
  137.4 7.7 %collective-permute-start.29 = (bf16[512,1024]{1,0:T(8,128)(2,1)}, bf16[512,1024]{1,0:T(8,128)(2,1)S(1)}, u32[]{:S(2)}, u32[]{:S(2)}) collective-permute-start(bf16[512,1024]{1,0:T(8,128)(2,1)} %collective-permute-done.10.rest_4_), channel_id=1, source_target_pairs={{0,1},{1,0},{2,3},{3,2},{4,5},{5,4},{6,7},{7,6},{8,9},{9,8},{10,11... | collective-permute-start | bytes 3145736 | tf_op jit(solution)/shard_map/ppermute | solution.py:24
  137.5 7.6 %collective-permute-start.30 = (bf16[512,1024]{1,0:T(8,128)(2,1)}, bf16[512,1024]{1,0:T(8,128)(2,1)S(1)}, u32[]{:S(2)}, u32[]{:S(2)}) collective-permute-start(bf16[512,1024]{1,0:T(8,128)(2,1)} %collective-permute-done.25.rest_5_), channel_id=1, source_target_pairs={{0,1},{1,0},{2,3},{3,2},{4,5},{5,4},{6,7},{7,6},{8,9},{9,8},{10,11... | collective-permute-start | bytes 3145736 | tf_op jit(solution)/shard_map/ppermute | solution.py:24
  139.1 25.7 %collective-permute-start.26 = (bf16[512,256]{1,0:T(8,128)(2,1)S(1)}, bf16[512,256]{1,0:T(8,128)(2,1)S(1)}, u32[]{:S(2)}, u32[]{:S(2)}) collective-permute-start(bf16[512,256]{1,0:T(8,128)(2,1)S(1)} %fusion), channel_id=1, source_target_pairs={{0,4},{4,0},{8,12},{12,8},{1,5},{5,1},{9,13},{13,9},{2,6},{6,2},{1... | collective-permute-start | bytes 786440 | tf_op jit(solution)/shard_map/ppermute | solution.py:24
  142.1 22.7 %collective-permute-start.27 = (f32[16,512]{1,0:T(8,128)S(1)}, f32[16,512]{1,0:T(8,128)S(1)}, u32[]{:S(2)}, u32[]{:S(2)}) collective-permute-start(f32[16,512]{1,0:T(8,128)S(1)} %maximum_add_fusion.1), channel_id=1, source_target_pairs={{0,4},{4,0},{8,12},{12,8},{1,5},{5,1},{9,13},{13,9},{2,6},{6,2},{1... | collective-permute-start | bytes 98312 | tf_op jit(solution)/shard_map/ppermute | solution.py:24
  145.1 1.0 copy-start.12
  151.2 20.8 %collective-permute-start.32 = (bf16[256,512]{1,0:T(8,128)(2,1)S(1)}, bf16[256,512]{1,0:T(8,128)(2,1)S(1)}, u32[]{:S(2)}, u32[]{:S(2)}) collective-permute-start(bf16[256,512]{1,0:T(8,128)(2,1)S(1)} %get-tuple-element.137), channel_id=1, source_target_pairs={{0,8},{4,12},{8,0},{12,4},{1,9},{5,13},{9,1},{13,5},{2,10},{6,14},... | collective-permute-start | bytes 786440 | tf_op jit(solution)/shard_map/ppermute | solution.py:24
  159.4 16.1 %collective-permute-start.33 = (bf16[256,512]{1,0:T(8,128)(2,1)S(1)}, bf16[256,512]{1,0:T(8,128)(2,1)S(1)}, u32[]{:S(2)}, u32[]{:S(2)}) collective-permute-start(bf16[256,512]{1,0:T(8,128)(2,1)S(1)} %get-tuple-element.142), channel_id=1, source_target_pairs={{0,8},{4,12},{8,0},{12,4},{1,9},{5,13},{9,1},{13,5},{2,10},{6,14},... | collective-permute-start | bytes 786440 | tf_op jit(solution)/shard_map/ppermute | solution.py:24

commit v4 on v3

--- a/solution.py
+++ b/solution.py
@@ -76,18 +76,40 @@
         del acts[:size]
 
 
+def pack_raw(raw, out):
+    heads, tokens = raw.shape
+    width = out.shape[1]
+    row = tokens
+    for first in range(0, tokens, width):
+        value = raw[:, first : first + width]
+        high = value.astype(BF16)
+        out[row : row + heads, :] = high
+        out[row + heads : row + 2 * heads, :] = (value - high.astype(F32)).astype(BF16)
+        row += 2 * heads
+
+
+def unpack_raw(packed, tokens, heads):
+    width = packed.shape[1]
+    parts = []
+    row = tokens
+    for _ in range(0, tokens, width):
+        parts.append(packed[row : row + heads, :].astype(F32) + packed[row + heads : row + 2 * heads, :].astype(F32))
+        row += 2 * heads
+    return jnp.concatenate(parts, axis=1)
+
+
 def extra_kernel(model, step_model, place, act_own, act_low, act_high, own, *rest):
     n = len(model)
     pieces = rest[:n]
     step_pieces = rest[n : n + len(step_model)]
-    full, rounded, raw = rest[-3:]
+    full, raw, packed = rest[-3:]
     first = 0
     for act in (act_own, act_low, act_high):
         here = slice(first, first + act.shape[0])
         first += act.shape[0]
         value = product(place, act, own, pieces, model)
         full[here, :] = value
-        rounded[here, :] = value.astype(BF16)
+        packed[here, :] = value.astype(BF16)
         total = None
         for piece, step in zip(step_pieces, step_model):
             rows = piece.shape[1]
@@ -95,15 +117,28 @@
             part = lax.dot_general(piece[...], act[:, pl.ds(start, rows)], NT, preferred_element_type=F32)
             total = part if total is None else total + part
         raw[:, here] = total
-
-
-def decay_kernel(offsets, place, raw, rate, factor, log_row, log_col, gain_col):
+    pack_raw(raw[...], packed)
+
+
+def combine_kernel(full, raw, came, out):
+    heads, tokens = raw.shape
+    half = tokens // 2
+    for a, b in ((0, half), (half, 0)):
+        out[a : a + half, :] = (full[a : a + half, :] + came[b : b + half, :].astype(F32)).astype(BF16)
+    other = unpack_raw(came, tokens, heads)
+    pack_raw(raw[...] + jnp.concatenate([other[:, half:], other[:, :half]], axis=1), out)
+
+
+def decay_kernel(offsets, tokens, place, rate, *rest):
+    packed = rest[:-4]
+    factor, log_row, log_col, gain_col = rest[-4:]
     mine = place[2]
-    heads, tokens = raw.shape[1], raw.shape[2]
+    heads = rate.shape[0]
+    pairs = [unpack_raw(p, 2 * tokens, heads) for p in packed]
     lane = lax.broadcasted_iota(jnp.int32, (heads, tokens), 1)
     steps, logs, totals = [], [], []
     for at in range(len(offsets)):
-        value = raw[at]
+        value = pairs[at // 2][:, at % 2 * tokens : (at % 2 + 1) * tokens]
         step = jnp.maximum(value, 0.0) + jnp.log1p(jnp.exp(-jnp.abs(value)))
         log = step * (-LOG2E * rate[...])
         shift = 1
@@ -152,14 +187,15 @@
         pl.when(mine == position)(functools.partial(body, earlier))
 
 
-def teacher_kernel(offsets, place, query, keys, norm):
+def teacher_kernel(offsets, place, query, *rest):
+    keys, norm = rest[:-1], rest[-1]
     tokens = query.shape[0]
 
     def body(earlier):
         asked = query[...]
         scores = []
         for at in [0] + earlier:
-            key = keys[pl.ds(at * tokens, tokens), :]
+            key = keys[at // 2][pl.ds(at % 2 * tokens, tokens), :]
             scores.append(lax.dot_general(asked, key, NT, preferred_element_type=F32) * SCALE)
         scores[0] = jnp.where(causal_of(tokens), scores[0], -jnp.inf)
         top = functools.reduce(jnp.maximum, [folded(jnp.maximum, s) for s in scores])
@@ -172,9 +208,10 @@
 
 
 def loss_kernel(
-    offsets, first, heads, place, query, kept, keys, inputs, norm, factor, log_row, log_col, gain_col, *rest
+    offsets, first, heads, number, place, query, kept, norm, factor, log_row, log_col, gain_col, *rest
 ):
-    arrived, out = rest[:-1], rest[-1]
+    arrived, rest, out = rest[:number], rest[number:-1], rest[-1]
+    keys, inputs = rest[: len(rest) // 2], rest[len(rest) // 2 :]
     tokens = query.shape[0]
 
     lane = lax.broadcasted_iota(jnp.int32, (tokens, 128), 1)
@@ -194,9 +231,9 @@
             gain = column(gain_col)
             sums = None
             for at in [0] + earlier:
-                rows = pl.ds(at * tokens, tokens)
-                score = lax.dot_general(asked, keys[rows, :], NT, preferred_element_type=F32) * SCALE
-                inner = lax.dot_general(read, inputs[rows, :], NT, preferred_element_type=F32)
+                rows = pl.ds(at % 2 * tokens, tokens)
+                score = lax.dot_general(asked, keys[at // 2][rows, :], NT, preferred_element_type=F32) * SCALE
+                inner = lax.dot_general(read, inputs[at // 2][rows, :], NT, preferred_element_type=F32)
                 inner = inner * factor[pl.ds(head, 1), at * tokens : (at + 1) * tokens]
                 prob = jnp.exp2(score - lse)
                 if at == 0:
@@ -209,7 +246,7 @@
             out[i] = jnp.sum(sums.T, axis=0, keepdims=True)
             return carry
 
-        lax.fori_loop(0, heads, one_head, 0)
+        lax.fori_loop(0, heads, one_head, 0, unroll=2 if heads % 2 == 0 else 1)
 
     for_place(place[2], offsets, body)
 
@@ -317,13 +354,13 @@
             in_specs=[
                 smem(),
                 pl.BlockSpec((tokens, HEAD_DIM), lambda h: (0, first + h)),
-                pl.BlockSpec((span, HEAD_DIM), lambda h: (0, (first + h) // per_group)),
-            ],
+            ]
+            + [pl.BlockSpec((2 * tokens, HEAD_DIM), lambda h: (0, (first + h) // per_group))] * half,
             out_specs=pl.BlockSpec((1, tokens, 128), lambda h: (h, 0, 0)),
             out_shape=jax.ShapeDtypeStruct((number, tokens, 128), F32),
             compiler_params=pltpu.CompilerParams(vmem_limit_bytes=VMEM_LIMIT),
             name="teacher",
-        )(order.gate(place), query, keys)
+        )(order.gate(place), query, *keys)
 
     spans = [(0, 1), (1, 2), (2, 4)]
     weights = []
@@ -372,7 +409,6 @@
         w1 = spread(order.wait(w1), "groups")
         others = [join(first0, second0)]
         weights.append((0, 1, order.wait(w0)))
-        early = send(partial([([others[0]], BF16)], 0)[0])
         first1, second1 = swap(1)
         moved[1] = order.wait(moved[1])
         w1 = spread(order.wait(w1), "batch")
@@ -399,70 +435,68 @@
         w1 = spread(spread(start_weights(1, 2), "groups"), "batch")
         w2 = start_weights(2, 4)
         key_rest = over_half(key_pair)
-        early = send(partial([([others[0]], BF16)], 0)[0])
-
+
+    packed_rows = 2 * tokens + 2 * padded * (2 * tokens // width_b)
+    packed_shape = jax.ShapeDtypeStruct((packed_rows, width_b), BF16)
     extra_out = [
         jax.ShapeDtypeStruct((2 * tokens, width_b), F32),
-        jax.ShapeDtypeStruct((2 * tokens, width_b), BF16),
         jax.ShapeDtypeStruct((padded, 2 * tokens), F32),
+        packed_shape,
     ]
-    extra_cols = [g[:, chunk:] for g in weights[0][2]]
     acts = (mine, *others)
-    full, rounded, raw = order.wait(
+    full, raw, packed = order.wait(
         call(
             functools.partial(extra_kernel, model, list(range(half))),
-            (order.gate(place), *acts, local_b, *extra_cols, step_t, *step_rest),
+            (order.gate(place), *acts, local_b, *weights[0][2], step_t, *step_rest),
             [smem()]
             + [whole(a.shape) for a in acts]
             + [whole(local_b.shape)]
-            + [whole((part, width_b))] * len(model)
+            + [columns(part, width_b, chunk // width_b)] * len(model)
             + [whole(step_t.shape)] * half,
             extra_out,
             "extra",
         )
     )
-    came = send(rounded)
-    came_raw = send(raw)
+    came = send(packed)
     w2 = spread(order.wait(w2), "groups")
     kept, arrived, norms = [], [], []
-    early = order.wait(early)
-    leaving, stays = partial([([others[1]], BF16), ([mine], F32)], 0)
-    arrived.append([early, send(leaving)])
-    kept.append(stays)
-
     def full_partial(j):
         leaving, stays = partial([(others, BF16), ([mine], F32)], j)
         arrived.append([send(leaving)])
         kept.append(stays)
 
+    full_partial(0)
     weights.append((1, 2, order.wait(w1)))
     full_partial(1)
+    came = order.wait(came)
+    pair = order.wait(
+        call(
+            combine_kernel,
+            (full, raw, came),
+            [whole(full.shape), whole(raw.shape), whole(came.shape)],
+            [packed_shape],
+            "combine",
+        )[0]
+    )
+    pair_rest = over_half(pair)
     key_rest = order.wait(key_rest)
-    keys = jnp.concatenate([key_pair] + key_rest, axis=0)
+    keys = [key_pair] + key_rest
+    arrived[0] = order.wait(arrived[0])
     norms.append(order.wait(teacher(0, heads)))
     w2 = spread(order.wait(w2), "batch")
-    came, came_raw = order.wait((came, came_raw))
-    came = came.astype(F32)
-    inputs_pair = (full + jnp.concatenate([came[tokens:], came[:tokens]], axis=0)).astype(BF16)
-    raw_pair = raw + jnp.concatenate([came_raw[:, tokens:], came_raw[:, :tokens]], axis=1)
-    inputs_rest = over_half(inputs_pair)
-    raw_rest = over_half(raw_pair)
     norms.append(order.wait(teacher(heads, heads)))
-    arrived[0] = order.wait(arrived[0])
     weights.append((2, 4, order.wait(w2)))
     full_partial(2)
     norms.append(order.wait(teacher(2 * heads, heads)))
     arrived[1] = order.wait(arrived[1])
     full_partial(3)
     norms.append(order.wait(teacher(3 * heads, heads)))
-    inputs_rest, raw_rest = order.wait((inputs_rest, raw_rest))
-    inputs = jnp.concatenate([inputs_pair] + inputs_rest, axis=0)
-    raw_all = jnp.stack([r[:, i * tokens : (i + 1) * tokens] for r in [raw_pair] + raw_rest for i in range(2)])
+    inputs = [pair] + order.wait(pair_rest)
     rate = jnp.pad(decay_rate, (0, padded - head_count))[:, None]
     factor, log_row, log_col, gain_col = call(
-        functools.partial(decay_kernel, offsets),
-        (order.gate(place), raw_all, rate),
-        [smem(), whole(raw_all.shape), whole(rate.shape)],
+        functools.partial(decay_kernel, offsets, tokens),
+        (order.gate(place), rate, *inputs),
+        [smem(), whole(rate.shape)] + [whole(packed_shape.shape)] * half,
         [
             jax.ShapeDtypeStruct((padded, span), F32),
             jax.ShapeDtypeStruct((padded, tokens), F32),
@@ -480,21 +514,20 @@
         losses.append(
             order.wait(
                 call(
-                    functools.partial(loss_kernel, offsets, j * heads, heads),
-                    (place, query, kept[j], keys, inputs, norms[j], factor, log_row, log_col, gain_col, *came),
+                    functools.partial(loss_kernel, offsets, j * heads, heads, len(came)),
+                    (place, query, kept[j], norms[j], factor, log_row, log_col, gain_col, *came, *keys, *inputs),
                     [
                         smem(),
                         columns(tokens, chunk, j),
                         whole((tokens, chunk)),
-                        columns(span, HEAD_DIM, group),
-                        columns(span, HEAD_DIM, group),
                         whole(norms[j].shape),
                         whole(factor.shape),
                         whole(log_row.shape),
                         whole(log_col.shape),
                         whole(gain_col.shape),
                     ]
-                    + [whole(c.shape) for c in came],
+                    + [whole(c.shape) for c in came]
+                    + [columns(2 * tokens, HEAD_DIM, group)] * (2 * half),
                     [jax.ShapeDtypeStruct((heads, 1, tokens), F32)],
                     "loss",
                 )[0]

time: 180 us -> 178 us (0.989); the launches traced: 179 us -> 175 us
  starting transfers between devices: 29.1 us -> 36.4 us
  Pallas kernels: 51.5 us -> 47.4 us
  local copies, waits for them, and re-layouts: 14.6 us -> 10.6 us
  waiting for transfers between devices: 76.4 us -> 73.8 us
    ppermute x2, waiting for transfers between devices: 11.1 us -> 3.27 us  [local(): lax.ppermute(value, both, [(flat(i, j), flat(i, 1 - j)) for i, j in even])]
    ppermute x28 -> x25, waiting for transfers between devices: 42 us -> 49.6 us  [xor_permute(): return lax.ppermute(value, axis, [(i, i ^ offset) for i in range(size)])]
    ppermute x28 -> x25, starting transfers between devices: 20.7 us -> 26.4 us  [xor_permute(): return lax.ppermute(value, axis, [(i, i ^ offset) for i in range(size)])]
    pallas_call x11, Pallas kernels: 39.5 us -> 35.4 us  [call(): pl.pallas_call(kernel, grid=(1,), in_specs=in_specs, out_specs=tuple((who...]
    unnamed x34 -> x50, local copies, waits for them, and re-layouts: 5.29 us -> 2.68 us
    ppermute x4, waiting for transfers between devices: 23.3 us -> 20.9 us  [local(): lax.ppermute(value, both, [(flat(i, j), flat(i ^ half, j)) for i, j in gr...]
  transfers between devices with their start and end apart: 34 -> 31, of which waited for: 15 -> 16; matrix products, arithmetic and copies ran while one was open for 7% -> 6% of each run, Pallas kernels for 27% -> 26%
where the time goes in v4:
time: 178 us; the launch traced here: 175 us
  waiting for transfers between devices  73.8 us (41%)
  Pallas kernels  47.4 us (27%)
  starting transfers between devices  36.4 us (20%)
  local copies, waits for them, and re-layouts  10.6 us (6%)
  other arithmetic  5.83 us (3%)
    ppermute x25, waiting for transfers between devices, xor_permute(): return lax.ppermute(value, axis, [(i, i ^ offset) for i in range(size)])  49.6 us
    pallas_call x11, Pallas kernels, call(): pl.pallas_call(kernel, grid=(1,), in_specs=in_specs, out_specs=tuple((who...  35.4 us
    ppermute x25, starting transfers between devices, xor_permute(): return lax.ppermute(value, axis, [(i, i ^ offset) for i in range(size)])  26.4 us
    ppermute x4, waiting for transfers between devices, local(): lax.ppermute(value, both, [(flat(i, j), flat(i ^ half, j)) for i, j in gr...  20.9 us
    pallas_call x4, Pallas kernels, teacher(): pl.pallas_call(functools.partial(teacher_kernel, offsets), grid=(number,)...  12 us
    ppermute x4, starting transfers between devices, local(): lax.ppermute(value, both, [(flat(i, j), flat(i ^ half, j)) for i, j in gr...  7.48 us
  transfers between devices with their start and end apart: 31, of which 16 were waited for; matrix products, arithmetic and copies ran while one was open for 6% of the time, Pallas kernels for 26%

profile of v4, /device:TPU:24, one launch (start us, length us, event | category | flops | bytes accessed | tf_op | source)
XLA Modules:
  0.0 174.5 jit_solution(13782277185471530903)
XLA Ops:
  0.0 2.7 %slice_bitcast_fusion.1 = (bf16[64,4096]{1,0:T(8,128)(2,1)S(1)}, bf16[64,4096]{1,0:T(8,128)(2,1)}, bf16[64,4096]{1,0:T(8,128)(2,1)}, bf16[64,4096]{1,0:T(8,128)(2,1)}) fusion(bf16[1,256,4096]{2,1,0:T(8,128)(2,1)} %param.7), kind=kLoop, calls=%fused_computation.5 | loop fusion | bytes 4194304 | tf_op jit(solution)/shard_map/slice | solution.py:380
  2.7 1.5 collective-permute-start.3
  4.2 2.1 %constant_dynamic-slice_fusion.1 = (bf16[512,512]{1,0:T(8,128)(2,1)S(1)}, bf16[512,512]{1,0:T(8,128)(2,1)}) fusion(bf16[2048,2048]{1,0:T(8,128)(2,1)} %rest_3_.7, s32[]{:T(128)} %select_n.62), kind=kLoop, calls=%fused_computation.18 | loop fusion | bytes 2097156 | tf_op jit(solution)/shard_map/dynamic_slice | solution.py:325
  6.4 0.5 collective-permute-start.5
  6.9 0.5 collective-permute-start.2
  7.4 2.7 %collective-permute-start.9 = (bf16[64,4096]{1,0:T(8,128)(2,1)}, bf16[64,4096]{1,0:T(8,128)(2,1)}, u32[]{:S(2)}, u32[]{:S(2)}) collective-permute-start(bf16[64,4096]{1,0:T(8,128)(2,1)} %get-tuple-element.91), channel_id=1, source_target_pairs={{2,10},{6,14},{8,0},{12,4},{3,11},{7,15},{9,1},{13,5},{18,26},{22,... | collective-permute-start | bytes 1572872 | tf_op jit(solution)/shard_map/ppermute | solution.py:379
  10.1 7.4 %collective-permute-done.3 = bf16[64,4096]{1,0:T(8,128)(2,1)S(1)} collective-permute-done((bf16[64,4096]{1,0:T(8,128)(2,1)S(1)}, bf16[64,4096]{1,0:T(8,128)(2,1)S(1)}, u32[]{:S(2)}, u32[]{:S(2)}) %collective-permute-start.3) | collective-permute-done | bytes 524320 | tf_op jit(solution)/shard_map/ppermute | solution.py:24
  17.6 1.3 collective-permute-start.10
  18.8 0.5 collective-permute-start.12
  19.4 8.4 %collective-permute-done.2 = bf16[64,4096]{1,0:T(8,128)(2,1)} collective-permute-done((bf16[64,4096]{1,0:T(8,128)(2,1)}, bf16[64,4096]{1,0:T(8,128)(2,1)}, u32[]{:S(2)}, u32[]{:S(2)}) %collective-permute-start.2) | collective-permute-done | bytes 524320 | tf_op jit(solution)/shard_map/ppermute | solution.py:24
  27.7 2.3 %collective-permute-start.1 = (bf16[64,4096]{1,0:T(8,128)(2,1)}, bf16[64,4096]{1,0:T(8,128)(2,1)S(1)}, u32[]{:S(2)}, u32[]{:S(2)}) collective-permute-start(bf16[64,4096]{1,0:T(8,128)(2,1)} %get-tuple-element.93), channel_id=1, source_target_pairs={{2,10},{6,14},{8,0},{12,4},{3,11},{7,15},{9,1},{13,5},{18,26},{22,... | collective-permute-start | bytes 1572872 | tf_op jit(solution)/shard_map/ppermute | solution.py:379
  30.0 1.5 collective-permute-done.5.rest_0_.rest_4_
  31.5 1.3 collective-permute-start.16
  32.8 3.5 %collective-permute-done.9 = bf16[64,4096]{1,0:T(8,128)(2,1)} collective-permute-done((bf16[64,4096]{1,0:T(8,128)(2,1)}, bf16[64,4096]{1,0:T(8,128)(2,1)}, u32[]{:S(2)}, u32[]{:S(2)}) %collective-permute-start.9) | collective-permute-done | bytes 524320 | tf_op jit(solution)/shard_map/ppermute | solution.py:379
  36.3 1.5 collective-permute-start.6
  37.8 5.7 %collective-permute-done.10 = bf16[64,4096]{1,0:T(8,128)(2,1)} collective-permute-done((bf16[64,4096]{1,0:T(8,128)(2,1)S(1)}, bf16[64,4096]{1,0:T(8,128)(2,1)}, u32[]{:S(2)}, u32[]{:S(2)}) %collective-permute-start.10) | collective-permute-done | bytes 524320 | tf_op jit(solution)/shard_map/ppermute | solution.py:379
  43.5 1.1 broadcast_select_fusion.5
  44.6 9.5 %collective-permute-start.11 = (bf16[64,4096]{1,0:T(8,128)(2,1)S(1)}, bf16[64,4096]{1,0:T(8,128)(2,1)S(1)}, u32[]{:S(2)}, u32[]{:S(2)}) collective-permute-start(bf16[64,4096]{1,0:T(8,128)(2,1)S(1)} %broadcast_select_fusion.5), channel_id=1, source_target_pairs={{0,2},{2,0},{1,3},{3,1},{4,6},{6,4},{5,7},{7,5},{8,10},{10,8},{9,1... | collective-permute-start | bytes 1572872 | tf_op jit(solution)/shard_map/ppermute | solution.py:24
  54.1 0.1 pad_add_fusion.place
  54.2 1.3 constant_dynamic-slice_fusion.2
  55.5 1.1 constant_dynamic-slice_fusion.own
  56.6 2.0 %collective-permute-done.16 = bf16[64,4096]{1,0:T(8,128)(2,1)S(1)} collective-permute-done((bf16[64,4096]{1,0:T(8,128)(2,1)}, bf16[64,4096]{1,0:T(8,128)(2,1)S(1)}, u32[]{:S(2)}, u32[]{:S(2)}) %collective-permute-start.16) | collective-permute-done | bytes 524320 | tf_op jit(solution)/shard_map/ppermute | solution.py:381
  58.7 1.3 collective-permute-start.4
  60.0 4.2 %collective-permute-done.11 = bf16[64,4096]{1,0:T(8,128)(2,1)S(1)} collective-permute-done((bf16[64,4096]{1,0:T(8,128)(2,1)S(1)}, bf16[64,4096]{1,0:T(8,128)(2,1)S(1)}, u32[]{:S(2)}, u32[]{:S(2)}) %collective-permute-start.11) | collective-permute-done | bytes 524320 | tf_op jit(solution)/shard_map/ppermute | solution.py:24
  64.5 2.1 %collective-permute-done.8.rest_3_.rest_7_ = bf16[512,768]{1,0:T(8,128)(2,1)S(1)} collective-permute-done((bf16[512,768]{1,0:T(8,128)(2,1)S(1)}, bf16[512,768]{1,0:T(8,128)(2,1)S(1)}, u32[]{:S(2)}, u32[]{:S(2)}) %collective-permute-start.8) | collective-permute-done | bytes 786464 | tf_op jit(solution)/shard_map/ppermute | solution.py:24
  66.6 1.3 collective-permute-start.17
  67.9 11.8 %collective-permute-done.4 = bf16[64,4096]{1,0:T(8,128)(2,1)S(1)} collective-permute-done((bf16[64,4096]{1,0:T(8,128)(2,1)}, bf16[64,4096]{1,0:T(8,128)(2,1)S(1)}, u32[]{:S(2)}, u32[]{:S(2)}) %collective-permute-start.4) | collective-permute-done | bytes 524320 | tf_op jit(solution)/shard_map/ppermute | solution.py:379
  79.6 1.5 collective-permute-start.18
  81.2 1.2 collective-permute-done.17
  82.4 3.2 %maximum_select_fusion.act_own.rest_2_ = bf16[256,4096]{1,0:T(8,128)(2,1)} fusion(bf16[64,4096]{1,0:T(8,128)(2,1)} %collective-permute-done.2, bf16[64,4096]{1,0:T(8,128)(2,1)S(1)} %collective-permute-done.17, bf16[64,4096]{1,0:T(8,128)(2,1)S(1)} %copy-done.22, bf16[64,4096]{1,0:T(8,128)(2,1)S(1)} %collective-permute-done.16, ...), kind=kLoop, calls=%fused_computation | loop fusion | flops 9437184 | bytes 6291457 | tf_op jit(solution)/shard_map/jit(_where)/select_n | solution.py:416
  85.6 4.5 %collective-permute-done.18.rest_5_ = bf16[512,512]{1,0:T(8,128)(2,1)S(1)} collective-permute-done((bf16[512,512]{1,0:T(8,128)(2,1)S(1)}, bf16[512,512]{1,0:T(8,128)(2,1)S(1)}, u32[]{:S(2)}, u32[]{:S(2)}) %collective-permute-start.18) | collective-permute-done | bytes 524320 | tf_op jit(solution)/shard_map/ppermute | solution.py:24
  90.1 5.4 %collective-permute-done.13 = bf16[64,4096]{1,0:T(8,128)(2,1)S(1)} collective-permute-done((bf16[64,4096]{1,0:T(8,128)(2,1)S(1)}, bf16[64,4096]{1,0:T(8,128)(2,1)S(1)}, u32[]{:S(2)}, u32[]{:S(2)}) %collective-permute-start.13) | collective-permute-done | bytes 524320 | tf_op jit(solution)/shard_map/ppermute | solution.py:24
  95.6 1.2 pad_maximum_fusion
  96.9 4.6 %extra.1 = (f32[512,256]{1,0:T(8,128)S(1)}, f32[16,512]{1,0:T(8,128)S(1)}, bf16[576,256]{1,0:T(8,128)(2,1)S(1)}) custom-call(s32[3]{0:T(128)S(1)} %pad_add_fusion.place, bf16[256,4096]{1,0:T(8,128)(2,1)} %maximum_select_fusion.act_own.rest_2_, bf16[128,4096]{1,0:T(8,128)(2,1)S(1)} %get-tuple-element.161.act_low.rest_0_, ...), custom_call_target="tpu_custom_call" | custom-call | tf_op jit(solution)/shard_map/extra/pallas_call | solution.py:40
  101.5 1.6 collective-permute-start.26
  103.1 0.5 collective-permute-start.23
  103.6 1.5 collective-permute-start.20
  105.1 4.6 %partial.4 = (bf16[256,512]{1,0:T(8,128)(2,1)S(1)}, f32[256,512]{1,0:T(8,128)S(1)}) custom-call(s32[3]{0:T(128)S(1)} %pad_add_fusion.place, bf16[128,4096]{1,0:T(8,128)(2,1)S(1)} %get-tuple-element.161.act_low.rest_0_, bf16[128,4096]{1,0:T(8,128)(2,1)S(1)} %copy-done.2, bf16[256,4096]{1,0:T(8,128)(2,1)} %maximum_select_fusion.act_own.rest_2_, ...), custom_call_target="tpu_custom_call" | custom-call | tf_op jit(solution)/shard_map/partial/pallas_call | solution.py:40
  109.7 3.0 %collective-permute-start.19 = (bf16[256,512]{1,0:T(8,128)(2,1)S(1)}, bf16[256,512]{1,0:T(8,128)(2,1)S(1)}, u32[]{:S(2)}, u32[]{:S(2)}) collective-permute-start(bf16[256,512]{1,0:T(8,128)(2,1)S(1)} %get-tuple-element.108), channel_id=1, source_target_pairs={{0,8},{4,12},{8,0},{12,4},{1,9},{5,13},{9,1},{13,5},{2,10},{6,14},... | collective-permute-start | bytes 786440 | tf_op jit(solution)/shard_map/ppermute | solution.py:24
  112.7 4.7 %partial.5 = (bf16[256,512]{1,0:T(8,128)(2,1)S(1)}, f32[256,512]{1,0:T(8,128)S(1)}) custom-call(s32[3]{0:T(128)S(1)} %pad_add_fusion.place, bf16[128,4096]{1,0:T(8,128)(2,1)S(1)} %get-tuple-element.161.act_low.rest_0_, bf16[128,4096]{1,0:T(8,128)(2,1)S(1)} %copy-done.2, bf16[256,4096]{1,0:T(8,128)(2,1)} %maximum_select_fusion.act_own.rest_2_, ...), custom_call_target="tpu_custom_call" | custom-call | tf_op jit(solution)/shard_map/partial/pallas_call | solution.py:40
  117.5 8.8 %collective-permute-done.21.came = bf16[576,256]{1,0:T(8,128)(2,1)S(1)} collective-permute-done((bf16[576,256]{1,0:T(8,128)(2,1)S(1)}, bf16[576,256]{1,0:T(8,128)(2,1)S(1)}, u32[]{:S(2)}, u32[]{:S(2)}) %collective-permute-start.21) | collective-permute-done | bytes 294944 | tf_op jit(solution)/shard_map/ppermute | solution.py:24
  126.3 4.6 %collective-permute-done.19.rest_0_ = bf16[256,512]{1,0:T(8,128)(2,1)S(1)} collective-permute-done((bf16[256,512]{1,0:T(8,128)(2,1)S(1)}, bf16[256,512]{1,0:T(8,128)(2,1)S(1)}, u32[]{:S(2)}, u32[]{:S(2)}) %collective-permute-start.19) | collective-permute-done | bytes 262176 | tf_op jit(solution)/shard_map/ppermute | solution.py:24
  131.0 3.0 %teacher.4.norm = f32[4,256,128]{2,1,0:T(8,128)S(1)} custom-call(s32[3]{0:T(128)S(1)} %pad_add_fusion.place, bf16[256,2048]{1,0:T(8,128)(2,1)S(1)} %bitcast.20, bf16[512,256]{1,0:T(8,128)(2,1)S(1)} %pad_maximum_fusion.3.rest_0_.rest_1_, bf16[512,256]{1,0:T(8,128)(2,1)S(1)} %collective-permute-done.20.rest_1_.rest_2_), custom_call_target="tpu_custom_call" | custom-call | tf_op jit(solution)/shard_map/teacher/pallas_call | solution.py:351
  134.1 0.5 collective-permute-start.28
  134.6 1.0 collective-permute-start.24
  135.6 3.0 %teacher.5.norm = f32[4,256,128]{2,1,0:T(8,128)S(1)} custom-call(s32[3]{0:T(128)S(1)} %pad_add_fusion.place, bf16[256,2048]{1,0:T(8,128)(2,1)S(1)} %bitcast.21, bf16[512,256]{1,0:T(8,128)(2,1)S(1)} %pad_maximum_fusion.3.rest_0_.rest_1_, bf16[512,256]{1,0:T(8,128)(2,1)S(1)} %collective-permute-done.20.rest_1_.rest_2_), custom_call_target="tpu_custom_call" | custom-call | tf_op jit(solution)/shard_map/teacher/pallas_call | solution.py:351
  138.7 1.0 copy-done.19
  139.6 4.7 %partial.6 = (bf16[256,512]{1,0:T(8,128)(2,1)}, f32[256,512]{1,0:T(8,128)S(1)}) custom-call(s32[3]{0:T(128)S(1)} %pad_add_fusion.place, bf16[128,4096]{1,0:T(8,128)(2,1)S(1)} %get-tuple-element.161.act_low.rest_0_, bf16[128,4096]{1,0:T(8,128)(2,1)S(1)} %copy-done.2, bf16[256,4096]{1,0:T(8,128)(2,1)} %maximum_select_fusion.act_own.rest_2_, ...), custom_call_target="tpu_custom_call" | custom-call | tf_op jit(solution)/shard_map/partial/pallas_call | solution.py:40
  144.4 0.8 copy-done.9
  145.2 1.4 collective-permute-start.29
  146.5 3.0 %teacher.6.norm = f32[4,256,128]{2,1,0:T(8,128)S(1)} custom-call(s32[3]{0:T(128)S(1)} %pad_add_fusion.place, bf16[256,2048]{1,0:T(8,128)(2,1)S(1)} %bitcast.22, bf16[512,256]{1,0:T(8,128)(2,1)S(1)} %pad_maximum_fusion.3.rest_0_.rest_1_, bf16[512,256]{1,0:T(8,128)(2,1)S(1)} %collective-permute-done.20.rest_1_.rest_2_), custom_call_target="tpu_custom_call" | custom-call | tf_op jit(solution)/shard_map/teacher/pallas_call | solution.py:351
  149.6 5.0 %partial.7 = (bf16[256,512]{1,0:T(8,128)(2,1)}, f32[256,512]{1,0:T(8,128)S(1)}) custom-call(s32[3]{0:T(128)S(1)} %pad_add_fusion.place, bf16[128,4096]{1,0:T(8,128)(2,1)S(1)} %get-tuple-element.161.act_low.rest_0_, bf16[128,4096]{1,0:T(8,128)(2,1)S(1)} %copy-done.2, bf16[256,4096]{1,0:T(8,128)(2,1)} %maximum_select_fusion.act_own.rest_2_, ...), custom_call_target="tpu_custom_call" | custom-call | tf_op jit(solution)/shard_map/partial/pallas_call | solution.py:40
  154.6 0.8 copy-done.11
  155.4 1.0 collective-permute-start.30
  156.4 0.1 copy.8.rate
  156.5 3.0 %teacher.7.norm = f32[4,256,128]{2,1,0:T(8,128)S(1)} custom-call(s32[3]{0:T(128)S(1)} %pad_add_fusion.place, bf16[256,2048]{1,0:T(8,128)(2,1)S(1)} %bitcast.23, bf16[512,256]{1,0:T(8,128)(2,1)S(1)} %pad_maximum_fusion.3.rest_0_.rest_1_, bf16[512,256]{1,0:T(8,128)(2,1)S(1)} %collective-permute-done.20.rest_1_.rest_2_), custom_call_target="tpu_custom_call" | custom-call | tf_op jit(solution)/shard_map/teacher/pallas_call | solution.py:351
  159.6 1.3 decay.1
  160.9 2.5 %loss.4 = f32[4,1,256]{2,1,0:T(1,128)S(1)} custom-call(s32[3]{0:T(128)S(1)} %pad_add_fusion.place, bf16[256,2048]{1,0:T(8,128)(2,1)S(1)} %bitcast.24, f32[256,512]{1,0:T(8,128)S(1)} %copy-done.6, f32[4,256,128]{2,1,0:T(8,128)S(1)} %teacher.4.norm, f32[16,1024]{1,0:T(8,128)S(1)} %get-tuple-element.139.factor, f32[16,256]{1,0:T(8,128)S(1)} %get-tuple-element.140.log_row, ...), custom_call_target="tpu_custom_call" | custom-call | tf_op jit(solution)/shard_map/loss/pallas_call | solution.py:40
  163.5 2.3 %loss.5 = f32[4,1,256]{2,1,0:T(1,128)S(1)} custom-call(s32[3]{0:T(128)S(1)} %pad_add_fusion.place, bf16[256,2048]{1,0:T(8,128)(2,1)S(1)} %bitcast.25, f32[256,512]{1,0:T(8,128)S(1)} %copy-done.8, f32[4,256,128]{2,1,0:T(8,128)S(1)} %teacher.5.norm, f32[16,1024]{1,0:T(8,128)S(1)} %get-tuple-element.139.factor, f32[16,256]{1,0:T(8,128)S(1)} %get-tuple-element.140.log_row, ...), custom_call_target="tpu_custom_call" | custom-call | tf_op jit(solution)/shard_map/loss/pallas_call | solution.py:40
  165.8 0.1 collective-permute-done.29.rest_0_
  165.9 2.8 %loss.6 = f32[4,1,256]{2,1,0:T(1,128)S(1)} custom-call(s32[3]{0:T(128)S(1)} %pad_add_fusion.place, bf16[256,2048]{1,0:T(8,128)(2,1)S(1)} %bitcast.26, f32[256,512]{1,0:T(8,128)S(1)} %copy-done.10, f32[4,256,128]{2,1,0:T(8,128)S(1)} %copy-done.4, f32[16,1024]{1,0:T(8,128)S(1)} %get-tuple-element.139.factor, f32[16,256]{1,0:T(8,128)S(1)} %get-tuple-element.140.log_row, ...), custom_call_target="tpu_custom_call" | custom-call | tf_op jit(solution)/shard_map/loss/pallas_call | solution.py:40
  168.7 2.4 %collective-permute-done.30.rest_0_ = bf16[256,512]{1,0:T(8,128)(2,1)} collective-permute-done((bf16[256,512]{1,0:T(8,128)(2,1)}, bf16[256,512]{1,0:T(8,128)(2,1)}, u32[]{:S(2)}, u32[]{:S(2)}) %collective-permute-start.30) | collective-permute-done | bytes 262176 | tf_op jit(solution)/shard_map/ppermute | solution.py:24
  171.1 2.8 %loss.7 = f32[4,1,256]{2,1,0:T(1,128)S(1)} custom-call(s32[3]{0:T(128)S(1)} %pad_add_fusion.place, bf16[256,2048]{1,0:T(8,128)(2,1)S(1)} %bitcast.27, f32[256,512]{1,0:T(8,128)S(1)} %copy-done.12, f32[4,256,128]{2,1,0:T(8,128)S(1)} %teacher.7.norm, f32[16,1024]{1,0:T(8,128)S(1)} %get-tuple-element.139.factor, f32[16,256]{1,0:T(8,128)S(1)} %get-tuple-element.140.log_row, ...), custom_call_target="tpu_custom_call" | custom-call | tf_op jit(solution)/shard_map/loss/pallas_call | solution.py:40
  173.9 0.6 copy.9
  (82 shorter events, 0.7 us)
Async XLA Ops:
  0.0 54.2 %copy-start = (bf16[1,256,512]{2,1,0:T(8,128)(2,1)S(1)}, bf16[1,256,512]{2,1,0:T(8,128)(2,1)}, u32[]{:S(2)}) copy-start(bf16[1,256,512]{2,1,0:T(8,128)(2,1)} %param.9) | copy-start | bytes 786436
  2.7 14.8 %collective-permute-start.3 = (bf16[64,4096]{1,0:T(8,128)(2,1)S(1)}, bf16[64,4096]{1,0:T(8,128)(2,1)S(1)}, u32[]{:S(2)}, u32[]{:S(2)}) collective-permute-start(bf16[64,4096]{1,0:T(8,128)(2,1)S(1)} %get-tuple-element.153), channel_id=1, source_target_pairs={{0,2},{2,0},{1,3},{3,1},{4,6},{6,4},{5,7},{7,5},{8,10},{10,8},{9,1... | collective-permute-start | bytes 1572872 | tf_op jit(solution)/shard_map/ppermute | solution.py:24
  4.2 2.1 %dynamic-slice-start = ((bf16[2048,512]{1,0:T(8,128)(2,1)}, s32[]{:T(128)}, s32[]{:T(128)}), bf16[512,256]{1,0:T(8,128)(2,1)S(1)}, s32[]{:S(2)}) async-start(bf16[2048,512]{1,0:T(8,128)(2,1)} %param.11, s32[]{:T(128)} %select_n.62, s32[]{:T(128)} %select_n.66), calls=%async_computation | async-start | bytes 524800 | tf_op jit(solution)/shard_map/dynamic_slice | solution.py:327
  6.4 25.1 %collective-permute-start.5 = (bf16[512,768]{1,0:T(8,128)(2,1)S(1)}, bf16[512,768]{1,0:T(8,128)(2,1)S(1)}, u32[]{:S(2)}, u32[]{:S(2)}) collective-permute-start(bf16[512,768]{1,0:T(8,128)(2,1)S(1)} %pad_maximum_fusion.2), channel_id=1, source_target_pairs={{0,4},{4,0},{8,12},{12,8},{1,5},{5,1},{9,13},{13,9},{2,6},{6,2},{1... | collective-permute-start | bytes 2359304 | tf_op jit(solution)/shard_map/ppermute | solution.py:24
  6.9 20.8 %collective-permute-start.2 = (bf16[64,4096]{1,0:T(8,128)(2,1)}, bf16[64,4096]{1,0:T(8,128)(2,1)}, u32[]{:S(2)}, u32[]{:S(2)}) collective-permute-start(bf16[64,4096]{1,0:T(8,128)(2,1)} %get-tuple-element.154), channel_id=1, source_target_pairs={{0,2},{2,0},{1,3},{3,1},{4,6},{6,4},{5,7},{7,5},{8,10},{10,8},{9,1... | collective-permute-start | bytes 1572872 | tf_op jit(solution)/shard_map/ppermute | solution.py:24
  7.4 28.8 %collective-permute-start.9 = (bf16[64,4096]{1,0:T(8,128)(2,1)}, bf16[64,4096]{1,0:T(8,128)(2,1)}, u32[]{:S(2)}, u32[]{:S(2)}) collective-permute-start(bf16[64,4096]{1,0:T(8,128)(2,1)} %get-tuple-element.91), channel_id=1, source_target_pairs={{2,10},{6,14},{8,0},{12,4},{3,11},{7,15},{9,1},{13,5},{18,26},{22,... | collective-permute-start | bytes 1572872 | tf_op jit(solution)/shard_map/ppermute | solution.py:379
  17.6 20.3 %copy-start.21 = (bf16[64,4096]{1,0:T(8,128)(2,1)}, bf16[64,4096]{1,0:T(8,128)(2,1)S(1)}, u32[]{:S(2)}) copy-start(bf16[64,4096]{1,0:T(8,128)(2,1)S(1)} %collective-permute-done.3) | copy-start | bytes 1572868
  17.6 25.9 %collective-permute-start.10 = (bf16[64,4096]{1,0:T(8,128)(2,1)S(1)}, bf16[64,4096]{1,0:T(8,128)(2,1)}, u32[]{:S(2)}, u32[]{:S(2)}) collective-permute-start(bf16[64,4096]{1,0:T(8,128)(2,1)S(1)} %collective-permute-done.3), channel_id=1, source_target_pairs={{0,8},{4,12},{10,2},{14,6},{1,9},{5,13},{11,3},{15,7},{16,24},{20,... | collective-permute-start | bytes 1572872 | tf_op jit(solution)/shard_map/ppermute | solution.py:379
  18.8 41.1 %collective-permute-start.12 = (bf16[512,512]{1,0:T(8,128)(2,1)}, bf16[512,512]{1,0:T(8,128)(2,1)S(1)}, u32[]{:S(2)}, u32[]{:S(2)}) collective-permute-start(bf16[512,512]{1,0:T(8,128)(2,1)} %get-tuple-element.152), channel_id=1, source_target_pairs={{0,4},{4,0},{8,12},{12,8},{1,5},{5,1},{9,13},{13,9},{2,6},{6,2},{1... | collective-permute-start | bytes 1572872 | tf_op jit(solution)/shard_map/ppermute | solution.py:24
  19.4 36.2 %copy-start.20 = (bf16[2048,512]{1,0:T(8,128)(2,1)S(1)}, bf16[2048,512]{1,0:T(8,128)(2,1)}, u32[]{:S(2)}) copy-start(bf16[2048,512]{1,0:T(8,128)(2,1)} %param.11) | copy-start | bytes 6291460
  27.7 38.8 %collective-permute-start.1 = (bf16[64,4096]{1,0:T(8,128)(2,1)}, bf16[64,4096]{1,0:T(8,128)(2,1)S(1)}, u32[]{:S(2)}, u32[]{:S(2)}) collective-permute-start(bf16[64,4096]{1,0:T(8,128)(2,1)} %get-tuple-element.93), channel_id=1, source_target_pairs={{2,10},{6,14},{8,0},{12,4},{3,11},{7,15},{9,1},{13,5},{18,26},{22,... | collective-permute-start | bytes 1572872 | tf_op jit(solution)/shard_map/ppermute | solution.py:379
  31.5 27.2 %collective-permute-start.16 = (bf16[64,4096]{1,0:T(8,128)(2,1)}, bf16[64,4096]{1,0:T(8,128)(2,1)S(1)}, u32[]{:S(2)}, u32[]{:S(2)}) collective-permute-start(bf16[64,4096]{1,0:T(8,128)(2,1)} %get-tuple-element.91), channel_id=1, source_target_pairs={{0,2},{4,6},{10,8},{14,12},{1,3},{5,7},{11,9},{15,13},{16,18},{20,... | collective-permute-start | bytes 1572872 | tf_op jit(solution)/shard_map/ppermute | solution.py:381
  36.3 22.4 %collective-permute-start.6 = (bf16[512,768]{1,0:T(8,128)(2,1)S(1)}, bf16[512,768]{1,0:T(8,128)(2,1)S(1)}, u32[]{:S(2)}, u32[]{:S(2)}) collective-permute-start(bf16[512,768]{1,0:T(8,128)(2,1)S(1)} %collective-permute-done.5.rest_0_.rest_4_), channel_id=1, source_target_pairs={{0,16},{16,0},{1,17},{17,1},{2,18},{18,2},{3,19},{19,3},{4,20},{20... | collective-permute-start | bytes 2359304 | tf_op jit(solution)/shard_map/ppermute | solution.py:24
  44.6 19.7 %collective-permute-start.11 = (bf16[64,4096]{1,0:T(8,128)(2,1)S(1)}, bf16[64,4096]{1,0:T(8,128)(2,1)S(1)}, u32[]{:S(2)}, u32[]{:S(2)}) collective-permute-start(bf16[64,4096]{1,0:T(8,128)(2,1)S(1)} %broadcast_select_fusion.5), channel_id=1, source_target_pairs={{0,2},{2,0},{1,3},{3,1},{4,6},{6,4},{5,7},{7,5},{8,10},{10,8},{9,1... | collective-permute-start | bytes 1572872 | tf_op jit(solution)/shard_map/ppermute | solution.py:24
  55.5 8.8 %copy-start.17 = (bf16[2048,16]{0,1:T(8,128)(2,1)S(1)}, bf16[2048,16]{0,1:T(8,128)(2,1)}, u32[]{:S(2)}) copy-start(bf16[2048,16]{0,1:T(8,128)(2,1)} %param.12) | copy-start | bytes 196612
  55.5 11.0 %copy-start.23 = (bf16[64,4096]{1,0:T(8,128)(2,1)S(1)}, bf16[64,4096]{1,0:T(8,128)(2,1)}, u32[]{:S(2)}) copy-start(bf16[64,4096]{1,0:T(8,128)(2,1)} %get-tuple-element.93) | copy-start | bytes 1572868
  56.6 25.8 %copy-start.18 = (bf16[1,256,4096]{2,1,0:T(8,128)(2,1)S(1)}, bf16[1,256,4096]{2,1,0:T(8,128)(2,1)}, u32[]{:S(2)}) copy-start(bf16[1,256,4096]{2,1,0:T(8,128)(2,1)} %param.7) | copy-start | bytes 6291460
  56.6 25.8 %copy-start.22 = (bf16[64,4096]{1,0:T(8,128)(2,1)S(1)}, bf16[64,4096]{1,0:T(8,128)(2,1)}, u32[]{:S(2)}) copy-start(bf16[64,4096]{1,0:T(8,128)(2,1)} %copy-done.21) | copy-start | bytes 1572868
  58.7 31.5 %collective-permute-start.15 = (bf16[256,256]{1,0:T(8,128)(2,1)S(1)}, bf16[256,256]{1,0:T(8,128)(2,1)S(1)}, u32[]{:S(2)}, u32[]{:S(2)}) collective-permute-start(bf16[256,256]{1,0:T(8,128)(2,1)S(1)} %dynamic-slice_bitcast_fusion), channel_id=1, source_target_pairs={{0,8},{4,12},{8,0},{12,4},{1,9},{5,13},{9,1},{13,5},{2,10},{6,14},... | collective-permute-start | bytes 393224 | tf_op jit(solution)/shard_map/ppermute | solution.py:24
  58.7 21.0 %collective-permute-start.4 = (bf16[64,4096]{1,0:T(8,128)(2,1)}, bf16[64,4096]{1,0:T(8,128)(2,1)S(1)}, u32[]{:S(2)}, u32[]{:S(2)}) collective-permute-start(bf16[64,4096]{1,0:T(8,128)(2,1)} %collective-permute-done.2), channel_id=1, source_target_pairs={{0,8},{4,12},{10,2},{14,6},{1,9},{5,13},{11,3},{15,7},{16,24},{20,... | collective-permute-start | bytes 1572872 | tf_op jit(solution)/shard_map/ppermute | solution.py:379
  60.0 4.4 %collective-permute-start.7 = (bf16[512,768]{1,0:T(8,128)(2,1)S(1)}, bf16[512,768]{1,0:T(8,128)(2,1)S(1)}, u32[]{:S(2)}, u32[]{:S(2)}) collective-permute-start(bf16[512,768]{1,0:T(8,128)(2,1)S(1)} %collective-permute-done.5.rest_0_.rest_4_), channel_id=1, source_target_pairs={{0,1},{1,0},{2,3},{3,2},{4,5},{5,4},{6,7},{7,6},{8,9},{9,8},{10,11... | collective-permute-start | bytes 2359304 | tf_op jit(solution)/shard_map/ppermute | solution.py:24
  64.3 2.3 %collective-permute-start.8 = (bf16[512,768]{1,0:T(8,128)(2,1)S(1)}, bf16[512,768]{1,0:T(8,128)(2,1)S(1)}, u32[]{:S(2)}, u32[]{:S(2)}) collective-permute-start(bf16[512,768]{1,0:T(8,128)(2,1)S(1)} %collective-permute-done.6.rest_1_.rest_5_), channel_id=1, source_target_pairs={{0,1},{1,0},{2,3},{3,2},{4,5},{5,4},{6,7},{7,6},{8,9},{9,8},{10,11... | collective-permute-start | bytes 2359304 | tf_op jit(solution)/shard_map/ppermute | solution.py:24
  64.4 25.8 %collective-permute-start.14 = (bf16[16,2048]{1,0:T(8,128)(2,1)S(1)}, bf16[16,2048]{1,0:T(8,128)(2,1)S(1)}, u32[]{:S(2)}, u32[]{:S(2)}) collective-permute-start(bf16[16,2048]{1,0:T(8,128)(2,1)S(1)} %bitcast.28), channel_id=1, source_target_pairs={{0,4},{4,0},{8,12},{12,8},{1,5},{5,1},{9,13},{13,9},{2,6},{6,2},{1... | collective-permute-start | bytes 196616 | tf_op jit(solution)/shard_map/ppermute | solution.py:24
  66.6 34.9 %collective-permute-start = (bf16[512,1024]{1,0:T(8,128)(2,1)S(1)}, bf16[512,1024]{1,0:T(8,128)(2,1)S(1)}, u32[]{:S(2)}, u32[]{:S(2)}) collective-permute-start(bf16[512,1024]{1,0:T(8,128)(2,1)S(1)} %constant_dynamic-slice_fusion.2), channel_id=1, source_target_pairs={{0,4},{4,0},{8,12},{12,8},{1,5},{5,1},{9,13},{13,9},{2,6},{6,2},{1... | collective-permute-start | bytes 3145736 | tf_op jit(solution)/shard_map/ppermute | solution.py:24
  66.6 15.9 %collective-permute-start.17 = (bf16[64,4096]{1,0:T(8,128)(2,1)S(1)}, bf16[64,4096]{1,0:T(8,128)(2,1)S(1)}, u32[]{:S(2)}, u32[]{:S(2)}) collective-permute-start(bf16[64,4096]{1,0:T(8,128)(2,1)S(1)} %copy-done.23), channel_id=1, source_target_pairs={{0,2},{4,6},{10,8},{14,12},{1,3},{5,7},{11,9},{15,13},{16,18},{20,... | collective-permute-start | bytes 1572872 | tf_op jit(solution)/shard_map/ppermute | solution.py:381
  79.6 10.5 %collective-permute-start.18 = (bf16[512,512]{1,0:T(8,128)(2,1)S(1)}, bf16[512,512]{1,0:T(8,128)(2,1)S(1)}, u32[]{:S(2)}, u32[]{:S(2)}) collective-permute-start(bf16[512,512]{1,0:T(8,128)(2,1)S(1)} %collective-permute-done.12.rest_4_), channel_id=1, source_target_pairs={{0,16},{16,0},{1,17},{17,1},{2,18},{18,2},{3,19},{19,3},{4,20},{20... | collective-permute-start | bytes 1572872 | tf_op jit(solution)/shard_map/ppermute | solution.py:24
  82.4 13.1 %collective-permute-start.13 = (bf16[64,4096]{1,0:T(8,128)(2,1)S(1)}, bf16[64,4096]{1,0:T(8,128)(2,1)S(1)}, u32[]{:S(2)}, u32[]{:S(2)}) collective-permute-start(bf16[64,4096]{1,0:T(8,128)(2,1)S(1)} %broadcast_select_fusion.4), channel_id=1, source_target_pairs={{0,2},{2,0},{1,3},{3,1},{4,6},{6,4},{5,7},{7,5},{8,10},{10,8},{9,1... | collective-permute-start | bytes 1572872 | tf_op jit(solution)/shard_map/ppermute | solution.py:24
  96.9 8.2 %copy-start.2 = (bf16[128,4096]{1,0:T(8,128)(2,1)S(1)}, bf16[128,4096]{1,0:T(8,128)(2,1)}, u32[]{:S(2)}) copy-start(bf16[128,4096]{1,0:T(8,128)(2,1)} %get-tuple-element.162.act_high.rest_1_) | copy-start | bytes 3145732
  101.5 32.5 %collective-permute-start.26 = (bf16[512,1024]{1,0:T(8,128)(2,1)S(1)}, bf16[512,1024]{1,0:T(8,128)(2,1)S(1)}, u32[]{:S(2)}, u32[]{:S(2)}) collective-permute-start(bf16[512,1024]{1,0:T(8,128)(2,1)S(1)} %collective-permute-done.rest_4_), channel_id=1, source_target_pairs={{0,16},{16,0},{1,17},{17,1},{2,18},{18,2},{3,19},{19,3},{4,20},{20... | collective-permute-start | bytes 3145736 | tf_op jit(solution)/shard_map/ppermute | solution.py:24
  103.1 6.6 %collective-permute-start.22 = (bf16[512,512]{1,0:T(8,128)(2,1)S(1)}, bf16[512,512]{1,0:T(8,128)(2,1)S(1)}, u32[]{:S(2)}, u32[]{:S(2)}) collective-permute-start(bf16[512,512]{1,0:T(8,128)(2,1)S(1)} %collective-permute-done.12.rest_4_), channel_id=1, source_target_pairs={{0,1},{1,0},{2,3},{3,2},{4,5},{5,4},{6,7},{7,6},{8,9},{9,8},{10,11... | collective-permute-start | bytes 1572872 | tf_op jit(solution)/shard_map/ppermute | solution.py:24
  103.1 9.6 %collective-permute-start.23 = (bf16[512,512]{1,0:T(8,128)(2,1)S(1)}, bf16[512,512]{1,0:T(8,128)(2,1)S(1)}, u32[]{:S(2)}, u32[]{:S(2)}) collective-permute-start(bf16[512,512]{1,0:T(8,128)(2,1)S(1)} %collective-permute-done.18.rest_5_), channel_id=1, source_target_pairs={{0,1},{1,0},{2,3},{3,2},{4,5},{5,4},{6,7},{7,6},{8,9},{9,8},{10,11... | collective-permute-start | bytes 1572872 | tf_op jit(solution)/shard_map/ppermute | solution.py:24
  103.6 22.7 %collective-permute-start.21 = (bf16[576,256]{1,0:T(8,128)(2,1)S(1)}, bf16[576,256]{1,0:T(8,128)(2,1)S(1)}, u32[]{:S(2)}, u32[]{:S(2)}) collective-permute-start(bf16[576,256]{1,0:T(8,128)(2,1)S(1)} %get-tuple-element.104), channel_id=1, source_target_pairs={{0,8},{4,12},{8,0},{12,4},{1,9},{5,13},{9,1},{13,5},{2,10},{6,14},... | collective-permute-start | bytes 884744 | tf_op jit(solution)/shard_map/ppermute | solution.py:24
  103.6 22.7 %collective-permute-start.20 = (bf16[512,256]{1,0:T(8,128)(2,1)S(1)}, bf16[512,256]{1,0:T(8,128)(2,1)S(1)}, u32[]{:S(2)}, u32[]{:S(2)}) collective-permute-start(bf16[512,256]{1,0:T(8,128)(2,1)S(1)} %pad_maximum_fusion.3.rest_0_.rest_1_), channel_id=1, source_target_pairs={{0,4},{4,0},{8,12},{12,8},{1,5},{5,1},{9,13},{13,9},{2,6},{6,2},{1... | collective-permute-start | bytes 786440 | tf_op jit(solution)/shard_map/ppermute | solution.py:24
  109.7 7.8 %copy-start.5 = (f32[256,512]{1,0:T(8,128)}, f32[256,512]{1,0:T(8,128)S(1)}, u32[]{:S(2)}) copy-start(f32[256,512]{1,0:T(8,128)S(1)} %get-tuple-element.107.kept) | copy-start | bytes 1572868
  109.7 21.2 %collective-permute-start.19 = (bf16[256,512]{1,0:T(8,128)(2,1)S(1)}, bf16[256,512]{1,0:T(8,128)(2,1)S(1)}, u32[]{:S(2)}, u32[]{:S(2)}) collective-permute-start(bf16[256,512]{1,0:T(8,128)(2,1)S(1)} %get-tuple-element.108), channel_id=1, source_target_pairs={{0,8},{4,12},{8,0},{12,4},{1,9},{5,13},{9,1},{13,5},{2,10},{6,14},... | collective-permute-start | bytes 786440 | tf_op jit(solution)/shard_map/ppermute | solution.py:24
  112.7 18.2 %copy-start.1 = (bf16[1,256,2048]{2,1,0:T(8,128)(2,1)S(1)}, bf16[1,256,2048]{2,1,0:T(8,128)(2,1)}, u32[]{:S(2)}) copy-start(bf16[1,256,2048]{2,1,0:T(8,128)(2,1)} %param.8) | copy-start | bytes 3145732
  117.5 21.1 %copy-start.7 = (f32[256,512]{1,0:T(8,128)}, f32[256,512]{1,0:T(8,128)S(1)}, u32[]{:S(2)}) copy-start(f32[256,512]{1,0:T(8,128)S(1)} %get-tuple-element.115.kept) | copy-start | bytes 1572868
  130.9 7.7 %copy-start.13 = (bf16[256,512]{1,0:T(8,128)(2,1)}, bf16[256,512]{1,0:T(8,128)(2,1)S(1)}, u32[]{:S(2)}) copy-start(bf16[256,512]{1,0:T(8,128)(2,1)S(1)} %collective-permute-done.19.rest_0_) | copy-start | bytes 786436
  134.0 4.7 %collective-permute-start.27 = (bf16[512,1024]{1,0:T(8,128)(2,1)S(1)}, bf16[512,1024]{1,0:T(8,128)(2,1)S(1)}, u32[]{:S(2)}, u32[]{:S(2)}) collective-permute-start(bf16[512,1024]{1,0:T(8,128)(2,1)S(1)} %collective-permute-done.rest_4_), channel_id=1, source_target_pairs={{0,1},{1,0},{2,3},{3,2},{4,5},{5,4},{6,7},{7,6},{8,9},{9,8},{10,11... | collective-permute-start | bytes 3145736 | tf_op jit(solution)/shard_map/ppermute | solution.py:24
  134.1 4.6 %collective-permute-start.28 = (bf16[512,1024]{1,0:T(8,128)(2,1)S(1)}, bf16[512,1024]{1,0:T(8,128)(2,1)S(1)}, u32[]{:S(2)}, u32[]{:S(2)}) collective-permute-start(bf16[512,1024]{1,0:T(8,128)(2,1)S(1)} %collective-permute-done.26.rest_5_), channel_id=1, source_target_pairs={{0,1},{1,0},{2,3},{3,2},{4,5},{5,4},{6,7},{7,6},{8,9},{9,8},{10,11... | collective-permute-start | bytes 3145736 | tf_op jit(solution)/shard_map/ppermute | solution.py:24
  134.5 15.0 %collective-permute-start.25 = (bf16[256,512]{1,0:T(8,128)(2,1)S(1)}, bf16[256,512]{1,0:T(8,128)(2,1)S(1)}, u32[]{:S(2)}, u32[]{:S(2)}) collective-permute-start(bf16[256,512]{1,0:T(8,128)(2,1)S(1)} %get-tuple-element.114), channel_id=1, source_target_pairs={{0,8},{4,12},{8,0},{12,4},{1,9},{5,13},{9,1},{13,5},{2,10},{6,14},... | collective-permute-start | bytes 786440 | tf_op jit(solution)/shard_map/ppermute | solution.py:24
  134.6 25.0 %collective-permute-start.24 = (bf16[576,256]{1,0:T(8,128)(2,1)S(1)}, bf16[576,256]{1,0:T(8,128)(2,1)S(1)}, u32[]{:S(2)}, u32[]{:S(2)}) collective-permute-start(bf16[576,256]{1,0:T(8,128)(2,1)S(1)} %combine.1.rest_0_.rest_3_), channel_id=1, source_target_pairs={{0,4},{4,0},{8,12},{12,8},{1,5},{5,1},{9,13},{13,9},{2,6},{6,2},{1... | collective-permute-start | bytes 884744 | tf_op jit(solution)/shard_map/ppermute | solution.py:24
  138.6 1.0 copy-start.19
  144.3 0.8 copy-start.9
  145.2 20.8 %collective-permute-start.29 = (bf16[256,512]{1,0:T(8,128)(2,1)}, bf16[256,512]{1,0:T(8,128)(2,1)}, u32[]{:S(2)}, u32[]{:S(2)}) collective-permute-start(bf16[256,512]{1,0:T(8,128)(2,1)} %get-tuple-element.129), channel_id=1, source_target_pairs={{0,8},{4,12},{8,0},{12,4},{1,9},{5,13},{9,1},{13,5},{2,10},{6,14},... | collective-permute-start | bytes 786440 | tf_op jit(solution)/shard_map/ppermute | solution.py:24
  149.5 5.0 %copy-start.3 = (f32[4,256,128]{2,1,0:T(8,128)}, f32[4,256,128]{2,1,0:T(8,128)S(1)}, u32[]{:S(2)}) copy-start(f32[4,256,128]{2,1,0:T(8,128)S(1)} %teacher.6.norm) | copy-start | bytes 1572868
  149.5 6.9 %copy-start.24 = (f32[16]{0:T(128)S(1)}, f32[16]{0:T(128)}, u32[]{:S(2)}) copy-start(f32[16]{0:T(128)} %param.13) | copy-start | bytes 196
  149.6 5.0 %copy-start.15 = (bf16[256,512]{1,0:T(8,128)(2,1)}, bf16[256,512]{1,0:T(8,128)(2,1)S(1)}, u32[]{:S(2)}) copy-start(bf16[256,512]{1,0:T(8,128)(2,1)S(1)} %collective-permute-done.25.rest_0_) | copy-start | bytes 786436
  154.6 0.8 copy-start.11
  155.4 15.7 %collective-permute-start.30 = (bf16[256,512]{1,0:T(8,128)(2,1)}, bf16[256,512]{1,0:T(8,128)(2,1)}, u32[]{:S(2)}, u32[]{:S(2)}) collective-permute-start(bf16[256,512]{1,0:T(8,128)(2,1)} %get-tuple-element.134), channel_id=1, source_target_pairs={{0,8},{4,12},{8,0},{12,4},{1,9},{5,13},{9,1},{13,5},{2,10},{6,14},... | collective-permute-start | bytes 786440 | tf_op jit(solution)/shard_map/ppermute | solution.py:24
  156.5 4.3 %copy-start.6 = (f32[256,512]{1,0:T(8,128)S(1)}, f32[256,512]{1,0:T(8,128)}, u32[]{:S(2)}) copy-start(f32[256,512]{1,0:T(8,128)} %copy-done.5) | copy-start | bytes 1572868
  156.5 4.3 %copy-start.14 = (bf16[256,512]{1,0:T(8,128)(2,1)S(1)}, bf16[256,512]{1,0:T(8,128)(2,1)}, u32[]{:S(2)}) copy-start(bf16[256,512]{1,0:T(8,128)(2,1)} %copy-done.13) | copy-start | bytes 786436
  159.5 3.9 %copy-start.8 = (f32[256,512]{1,0:T(8,128)S(1)}, f32[256,512]{1,0:T(8,128)}, u32[]{:S(2)}) copy-start(f32[256,512]{1,0:T(8,128)} %copy-done.7) | copy-start | bytes 1572868
  159.5 3.9 %copy-start.16 = (bf16[256,512]{1,0:T(8,128)(2,1)S(1)}, bf16[256,512]{1,0:T(8,128)(2,1)}, u32[]{:S(2)}) copy-start(bf16[256,512]{1,0:T(8,128)(2,1)} %copy-done.15) | copy-start | bytes 786436
  163.4 2.5 %copy-start.4 = (f32[4,256,128]{2,1,0:T(8,128)S(1)}, f32[4,256,128]{2,1,0:T(8,128)}, u32[]{:S(2)}) copy-start(f32[4,256,128]{2,1,0:T(8,128)} %copy-done.3) | copy-start | bytes 1572868
  163.4 2.5 %copy-start.10 = (f32[256,512]{1,0:T(8,128)S(1)}, f32[256,512]{1,0:T(8,128)}, u32[]{:S(2)}) copy-start(f32[256,512]{1,0:T(8,128)} %copy-done.9) | copy-start | bytes 1572868
  165.8 5.4 %copy-start.12 = (f32[256,512]{1,0:T(8,128)S(1)}, f32[256,512]{1,0:T(8,128)}, u32[]{:S(2)}) copy-start(f32[256,512]{1,0:T(8,128)} %copy-done.11) | copy-start | bytes 1572868

commit v5 on v4

--- a/solution.py
+++ b/solution.py
@@ -481,8 +481,8 @@
     pair_rest = over_half(pair)
     key_rest = order.wait(key_rest)
     keys = [key_pair] + key_rest
+    norms.append(order.wait(teacher(0, heads)))
     arrived[0] = order.wait(arrived[0])
-    norms.append(order.wait(teacher(0, heads)))
     w2 = spread(order.wait(w2), "batch")
     norms.append(order.wait(teacher(heads, heads)))
     weights.append((2, 4, order.wait(w2)))

time: 178 us -> 175 us (0.983)
  waiting for transfers between devices: 73.8 us -> 70.1 us
    ppermute x25, waiting for transfers between devices: 49.6 us -> 45.9 us  [xor_permute(): return lax.ppermute(value, axis, [(i, i ^ offset) for i in range(size)])]
  transfers between devices with their start and end apart: 31 -> 31, of which waited for: 16 -> 15; matrix products, arithmetic and copies ran while one was open for 6% -> 6% of each run, Pallas kernels for 26% -> 26%
where the time goes in v5:
time: 175 us; the launch traced here: 172 us
  waiting for transfers between devices  70.1 us (40%)
  Pallas kernels  47.6 us (27%)
  starting transfers between devices  37.1 us (21%)
  local copies, waits for them, and re-layouts  10.6 us (6%)
  other arithmetic  5.83 us (3%)
    ppermute x25, waiting for transfers between devices, xor_permute(): return lax.ppermute(value, axis, [(i, i ^ offset) for i in range(size)])  45.9 us
    pallas_call x11, Pallas kernels, call(): pl.pallas_call(kernel, grid=(1,), in_specs=in_specs, out_specs=tuple((who...  35.4 us
    ppermute x25, starting transfers between devices, xor_permute(): return lax.ppermute(value, axis, [(i, i ^ offset) for i in range(size)])  27 us
    ppermute x4, waiting for transfers between devices, local(): lax.ppermute(value, both, [(flat(i, j), flat(i ^ half, j)) for i, j in gr...  20.9 us
    pallas_call x4, Pallas kernels, teacher(): pl.pallas_call(functools.partial(teacher_kernel, offsets), grid=(number,)...  12.2 us
    ppermute x4, starting transfers between devices, local(): lax.ppermute(value, both, [(flat(i, j), flat(i ^ half, j)) for i, j in gr...  7.48 us
  transfers between devices with their start and end apart: 31, of which 15 were waited for; matrix products, arithmetic and copies ran while one was open for 6% of the time, Pallas kernels for 26%

profile of v5, /device:TPU:24, one launch (start us, length us, event | category | flops | bytes accessed | tf_op | source)
XLA Modules:
  0.0 171.8 jit_solution(18012936790102470724)
XLA Ops:
  0.0 2.7 %slice_bitcast_fusion.1 = (bf16[64,4096]{1,0:T(8,128)(2,1)S(1)}, bf16[64,4096]{1,0:T(8,128)(2,1)}, bf16[64,4096]{1,0:T(8,128)(2,1)}, bf16[64,4096]{1,0:T(8,128)(2,1)}) fusion(bf16[1,256,4096]{2,1,0:T(8,128)(2,1)} %param.7), kind=kLoop, calls=%fused_computation.5 | loop fusion | bytes 4194304 | tf_op jit(solution)/shard_map/slice | solution.py:380
  2.7 1.5 collective-permute-start.3
  4.2 2.1 %constant_dynamic-slice_fusion.1 = (bf16[512,512]{1,0:T(8,128)(2,1)S(1)}, bf16[512,512]{1,0:T(8,128)(2,1)}) fusion(bf16[2048,2048]{1,0:T(8,128)(2,1)} %rest_3_.7, s32[]{:T(128)} %select_n.62), kind=kLoop, calls=%fused_computation.18 | loop fusion | bytes 2097156 | tf_op jit(solution)/shard_map/dynamic_slice | solution.py:325
  6.4 0.5 collective-permute-start.5
  6.9 0.5 collective-permute-start.2
  7.4 2.7 %collective-permute-start.9 = (bf16[64,4096]{1,0:T(8,128)(2,1)}, bf16[64,4096]{1,0:T(8,128)(2,1)}, u32[]{:S(2)}, u32[]{:S(2)}) collective-permute-start(bf16[64,4096]{1,0:T(8,128)(2,1)} %get-tuple-element.91), channel_id=1, source_target_pairs={{2,10},{6,14},{8,0},{12,4},{3,11},{7,15},{9,1},{13,5},{18,26},{22,... | collective-permute-start | bytes 1572872 | tf_op jit(solution)/shard_map/ppermute | solution.py:379
  10.1 7.4 %collective-permute-done.3 = bf16[64,4096]{1,0:T(8,128)(2,1)S(1)} collective-permute-done((bf16[64,4096]{1,0:T(8,128)(2,1)S(1)}, bf16[64,4096]{1,0:T(8,128)(2,1)S(1)}, u32[]{:S(2)}, u32[]{:S(2)}) %collective-permute-start.3) | collective-permute-done | bytes 524320 | tf_op jit(solution)/shard_map/ppermute | solution.py:24
  17.6 1.3 collective-permute-start.10
  18.8 0.5 collective-permute-start.12
  19.4 8.4 %collective-permute-done.2 = bf16[64,4096]{1,0:T(8,128)(2,1)} collective-permute-done((bf16[64,4096]{1,0:T(8,128)(2,1)}, bf16[64,4096]{1,0:T(8,128)(2,1)}, u32[]{:S(2)}, u32[]{:S(2)}) %collective-permute-start.2) | collective-permute-done | bytes 524320 | tf_op jit(solution)/shard_map/ppermute | solution.py:24
  27.7 2.3 %collective-permute-start.1 = (bf16[64,4096]{1,0:T(8,128)(2,1)}, bf16[64,4096]{1,0:T(8,128)(2,1)S(1)}, u32[]{:S(2)}, u32[]{:S(2)}) collective-permute-start(bf16[64,4096]{1,0:T(8,128)(2,1)} %get-tuple-element.93), channel_id=1, source_target_pairs={{2,10},{6,14},{8,0},{12,4},{3,11},{7,15},{9,1},{13,5},{18,26},{22,... | collective-permute-start | bytes 1572872 | tf_op jit(solution)/shard_map/ppermute | solution.py:379
  30.0 1.5 collective-permute-done.5.rest_0_.rest_4_
  31.5 1.3 collective-permute-start.16
  32.8 3.5 %collective-permute-done.9 = bf16[64,4096]{1,0:T(8,128)(2,1)} collective-permute-done((bf16[64,4096]{1,0:T(8,128)(2,1)}, bf16[64,4096]{1,0:T(8,128)(2,1)}, u32[]{:S(2)}, u32[]{:S(2)}) %collective-permute-start.9) | collective-permute-done | bytes 524320 | tf_op jit(solution)/shard_map/ppermute | solution.py:379
  36.3 1.5 collective-permute-start.6
  37.8 5.7 %collective-permute-done.10 = bf16[64,4096]{1,0:T(8,128)(2,1)} collective-permute-done((bf16[64,4096]{1,0:T(8,128)(2,1)S(1)}, bf16[64,4096]{1,0:T(8,128)(2,1)}, u32[]{:S(2)}, u32[]{:S(2)}) %collective-permute-start.10) | collective-permute-done | bytes 524320 | tf_op jit(solution)/shard_map/ppermute | solution.py:379
  43.5 1.1 broadcast_select_fusion.5
  44.6 9.5 %collective-permute-start.11 = (bf16[64,4096]{1,0:T(8,128)(2,1)S(1)}, bf16[64,4096]{1,0:T(8,128)(2,1)S(1)}, u32[]{:S(2)}, u32[]{:S(2)}) collective-permute-start(bf16[64,4096]{1,0:T(8,128)(2,1)S(1)} %broadcast_select_fusion.5), channel_id=1, source_target_pairs={{0,2},{2,0},{1,3},{3,1},{4,6},{6,4},{5,7},{7,5},{8,10},{10,8},{9,1... | collective-permute-start | bytes 1572872 | tf_op jit(solution)/shard_map/ppermute | solution.py:24
  54.1 0.1 pad_add_fusion.place
  54.2 1.3 constant_dynamic-slice_fusion.2
  55.5 1.1 constant_dynamic-slice_fusion.own
  56.6 2.0 %collective-permute-done.16 = bf16[64,4096]{1,0:T(8,128)(2,1)S(1)} collective-permute-done((bf16[64,4096]{1,0:T(8,128)(2,1)}, bf16[64,4096]{1,0:T(8,128)(2,1)S(1)}, u32[]{:S(2)}, u32[]{:S(2)}) %collective-permute-start.16) | collective-permute-done | bytes 524320 | tf_op jit(solution)/shard_map/ppermute | solution.py:381
  58.7 1.3 collective-permute-start.4
  60.0 4.2 %collective-permute-done.11 = bf16[64,4096]{1,0:T(8,128)(2,1)S(1)} collective-permute-done((bf16[64,4096]{1,0:T(8,128)(2,1)S(1)}, bf16[64,4096]{1,0:T(8,128)(2,1)S(1)}, u32[]{:S(2)}, u32[]{:S(2)}) %collective-permute-start.11) | collective-permute-done | bytes 524320 | tf_op jit(solution)/shard_map/ppermute | solution.py:24
  64.3 0.1 broadcast_select_fusion.3
  64.5 2.1 %collective-permute-done.8.rest_3_.rest_7_ = bf16[512,768]{1,0:T(8,128)(2,1)S(1)} collective-permute-done((bf16[512,768]{1,0:T(8,128)(2,1)S(1)}, bf16[512,768]{1,0:T(8,128)(2,1)S(1)}, u32[]{:S(2)}, u32[]{:S(2)}) %collective-permute-start.8) | collective-permute-done | bytes 786464 | tf_op jit(solution)/shard_map/ppermute | solution.py:24
  66.6 1.3 collective-permute-start.17
  67.9 11.8 %collective-permute-done.4 = bf16[64,4096]{1,0:T(8,128)(2,1)S(1)} collective-permute-done((bf16[64,4096]{1,0:T(8,128)(2,1)}, bf16[64,4096]{1,0:T(8,128)(2,1)S(1)}, u32[]{:S(2)}, u32[]{:S(2)}) %collective-permute-start.4) | collective-permute-done | bytes 524320 | tf_op jit(solution)/shard_map/ppermute | solution.py:379
  79.6 1.5 collective-permute-start.18
  81.2 1.2 collective-permute-done.17
  82.4 3.2 %maximum_select_fusion.act_own.rest_2_ = bf16[256,4096]{1,0:T(8,128)(2,1)} fusion(bf16[64,4096]{1,0:T(8,128)(2,1)} %collective-permute-done.2, bf16[64,4096]{1,0:T(8,128)(2,1)S(1)} %collective-permute-done.17, bf16[64,4096]{1,0:T(8,128)(2,1)S(1)} %copy-done.22, bf16[64,4096]{1,0:T(8,128)(2,1)S(1)} %collective-permute-done.16, ...), kind=kLoop, calls=%fused_computation | loop fusion | flops 9437184 | bytes 6291457 | tf_op jit(solution)/shard_map/jit(_where)/select_n | solution.py:416
  85.6 4.5 %collective-permute-done.18.rest_5_ = bf16[512,512]{1,0:T(8,128)(2,1)S(1)} collective-permute-done((bf16[512,512]{1,0:T(8,128)(2,1)S(1)}, bf16[512,512]{1,0:T(8,128)(2,1)S(1)}, u32[]{:S(2)}, u32[]{:S(2)}) %collective-permute-start.18) | collective-permute-done | bytes 524320 | tf_op jit(solution)/shard_map/ppermute | solution.py:24
  90.1 5.4 %collective-permute-done.13 = bf16[64,4096]{1,0:T(8,128)(2,1)S(1)} collective-permute-done((bf16[64,4096]{1,0:T(8,128)(2,1)S(1)}, bf16[64,4096]{1,0:T(8,128)(2,1)S(1)}, u32[]{:S(2)}, u32[]{:S(2)}) %collective-permute-start.13) | collective-permute-done | bytes 524320 | tf_op jit(solution)/shard_map/ppermute | solution.py:24
  95.6 1.2 pad_maximum_fusion
  96.9 4.6 %extra.1 = (f32[512,256]{1,0:T(8,128)S(1)}, f32[16,512]{1,0:T(8,128)S(1)}, bf16[576,256]{1,0:T(8,128)(2,1)S(1)}) custom-call(s32[3]{0:T(128)S(1)} %pad_add_fusion.place, bf16[256,4096]{1,0:T(8,128)(2,1)} %maximum_select_fusion.act_own.rest_2_, bf16[128,4096]{1,0:T(8,128)(2,1)S(1)} %get-tuple-element.161.act_low.rest_0_, ...), custom_call_target="tpu_custom_call" | custom-call | tf_op jit(solution)/shard_map/extra/pallas_call | solution.py:40
  101.5 1.6 collective-permute-start.25
  103.1 0.5 collective-permute-start.22
  103.6 1.5 collective-permute-start.19
  105.1 4.6 %partial.4 = (bf16[256,512]{1,0:T(8,128)(2,1)S(1)}, f32[256,512]{1,0:T(8,128)S(1)}) custom-call(s32[3]{0:T(128)S(1)} %pad_add_fusion.place, bf16[128,4096]{1,0:T(8,128)(2,1)S(1)} %get-tuple-element.161.act_low.rest_0_, bf16[128,4096]{1,0:T(8,128)(2,1)S(1)} %copy-done.2, bf16[256,4096]{1,0:T(8,128)(2,1)} %maximum_select_fusion.act_own.rest_2_, ...), custom_call_target="tpu_custom_call" | custom-call | tf_op jit(solution)/shard_map/partial/pallas_call | solution.py:40
  109.7 3.0 %collective-permute-start.26 = (bf16[256,512]{1,0:T(8,128)(2,1)S(1)}, bf16[256,512]{1,0:T(8,128)(2,1)S(1)}, u32[]{:S(2)}, u32[]{:S(2)}) collective-permute-start(bf16[256,512]{1,0:T(8,128)(2,1)S(1)} %get-tuple-element.108), channel_id=1, source_target_pairs={{0,8},{4,12},{8,0},{12,4},{1,9},{5,13},{9,1},{13,5},{2,10},{6,14},... | collective-permute-start | bytes 786440 | tf_op jit(solution)/shard_map/ppermute | solution.py:24
  112.7 4.7 %partial.5 = (bf16[256,512]{1,0:T(8,128)(2,1)S(1)}, f32[256,512]{1,0:T(8,128)S(1)}) custom-call(s32[3]{0:T(128)S(1)} %pad_add_fusion.place, bf16[128,4096]{1,0:T(8,128)(2,1)S(1)} %get-tuple-element.161.act_low.rest_0_, bf16[128,4096]{1,0:T(8,128)(2,1)S(1)} %copy-done.2, bf16[256,4096]{1,0:T(8,128)(2,1)} %maximum_select_fusion.act_own.rest_2_, ...), custom_call_target="tpu_custom_call" | custom-call | tf_op jit(solution)/shard_map/partial/pallas_call | solution.py:40
  117.5 8.8 %collective-permute-done.20.came = bf16[576,256]{1,0:T(8,128)(2,1)S(1)} collective-permute-done((bf16[576,256]{1,0:T(8,128)(2,1)S(1)}, bf16[576,256]{1,0:T(8,128)(2,1)S(1)}, u32[]{:S(2)}, u32[]{:S(2)}) %collective-permute-start.20) | collective-permute-done | bytes 294944 | tf_op jit(solution)/shard_map/ppermute | solution.py:24
  126.3 3.2 %teacher.4.norm = f32[4,256,128]{2,1,0:T(8,128)S(1)} custom-call(s32[3]{0:T(128)S(1)} %pad_add_fusion.place, bf16[256,2048]{1,0:T(8,128)(2,1)S(1)} %bitcast.20, bf16[512,256]{1,0:T(8,128)(2,1)S(1)} %pad_maximum_fusion.3.rest_0_.rest_1_, bf16[512,256]{1,0:T(8,128)(2,1)S(1)} %collective-permute-done.19.rest_1_.rest_2_), custom_call_target="tpu_custom_call" | custom-call | tf_op jit(solution)/shard_map/teacher/pallas_call | solution.py:351
  129.6 1.4 collective-permute-done.26.rest_0_
  131.0 0.5 collective-permute-start.28
  131.5 1.7 %collective-permute-start.23 = (bf16[576,256]{1,0:T(8,128)(2,1)S(1)}, bf16[576,256]{1,0:T(8,128)(2,1)S(1)}, u32[]{:S(2)}, u32[]{:S(2)}) collective-permute-start(bf16[576,256]{1,0:T(8,128)(2,1)S(1)} %combine.1.rest_0_.rest_3_), channel_id=1, source_target_pairs={{0,4},{4,0},{8,12},{12,8},{1,5},{5,1},{9,13},{13,9},{2,6},{6,2},{1... | collective-permute-start | bytes 884744 | tf_op jit(solution)/shard_map/ppermute | solution.py:24
  133.2 3.0 %teacher.5.norm = f32[4,256,128]{2,1,0:T(8,128)S(1)} custom-call(s32[3]{0:T(128)S(1)} %pad_add_fusion.place, bf16[256,2048]{1,0:T(8,128)(2,1)S(1)} %bitcast.21, bf16[512,256]{1,0:T(8,128)(2,1)S(1)} %pad_maximum_fusion.3.rest_0_.rest_1_, bf16[512,256]{1,0:T(8,128)(2,1)S(1)} %collective-permute-done.19.rest_1_.rest_2_), custom_call_target="tpu_custom_call" | custom-call | tf_op jit(solution)/shard_map/teacher/pallas_call | solution.py:351
  136.3 1.0 copy-done.19
  137.2 4.7 %partial.6 = (bf16[256,512]{1,0:T(8,128)(2,1)}, f32[256,512]{1,0:T(8,128)S(1)}) custom-call(s32[3]{0:T(128)S(1)} %pad_add_fusion.place, bf16[128,4096]{1,0:T(8,128)(2,1)S(1)} %get-tuple-element.161.act_low.rest_0_, bf16[128,4096]{1,0:T(8,128)(2,1)S(1)} %copy-done.2, bf16[256,4096]{1,0:T(8,128)(2,1)} %maximum_select_fusion.act_own.rest_2_, ...), custom_call_target="tpu_custom_call" | custom-call | tf_op jit(solution)/shard_map/partial/pallas_call | solution.py:40
  142.0 0.8 copy-done.9
  142.8 0.7 collective-permute-start.29
  143.4 3.0 %teacher.6.norm = f32[4,256,128]{2,1,0:T(8,128)S(1)} custom-call(s32[3]{0:T(128)S(1)} %pad_add_fusion.place, bf16[256,2048]{1,0:T(8,128)(2,1)S(1)} %bitcast.22, bf16[512,256]{1,0:T(8,128)(2,1)S(1)} %pad_maximum_fusion.3.rest_0_.rest_1_, bf16[512,256]{1,0:T(8,128)(2,1)S(1)} %collective-permute-done.19.rest_1_.rest_2_), custom_call_target="tpu_custom_call" | custom-call | tf_op jit(solution)/shard_map/teacher/pallas_call | solution.py:351
  146.5 5.0 %partial.7 = (bf16[256,512]{1,0:T(8,128)(2,1)}, f32[256,512]{1,0:T(8,128)S(1)}) custom-call(s32[3]{0:T(128)S(1)} %pad_add_fusion.place, bf16[128,4096]{1,0:T(8,128)(2,1)S(1)} %get-tuple-element.161.act_low.rest_0_, bf16[128,4096]{1,0:T(8,128)(2,1)S(1)} %copy-done.2, bf16[256,4096]{1,0:T(8,128)(2,1)} %maximum_select_fusion.act_own.rest_2_, ...), custom_call_target="tpu_custom_call" | custom-call | tf_op jit(solution)/shard_map/partial/pallas_call | solution.py:40
  151.5 0.8 copy-done.11
  152.3 1.7 %collective-permute-start.30 = (bf16[256,512]{1,0:T(8,128)(2,1)}, bf16[256,512]{1,0:T(8,128)(2,1)}, u32[]{:S(2)}, u32[]{:S(2)}) collective-permute-start(bf16[256,512]{1,0:T(8,128)(2,1)} %get-tuple-element.134), channel_id=1, source_target_pairs={{0,8},{4,12},{8,0},{12,4},{1,9},{5,13},{9,1},{13,5},{2,10},{6,14},... | collective-permute-start | bytes 786440 | tf_op jit(solution)/shard_map/ppermute | solution.py:24
  154.0 0.1 copy.8.rate
  154.1 3.0 %teacher.7.norm = f32[4,256,128]{2,1,0:T(8,128)S(1)} custom-call(s32[3]{0:T(128)S(1)} %pad_add_fusion.place, bf16[256,2048]{1,0:T(8,128)(2,1)S(1)} %bitcast.23, bf16[512,256]{1,0:T(8,128)(2,1)S(1)} %pad_maximum_fusion.3.rest_0_.rest_1_, bf16[512,256]{1,0:T(8,128)(2,1)S(1)} %collective-permute-done.19.rest_1_.rest_2_), custom_call_target="tpu_custom_call" | custom-call | tf_op jit(solution)/shard_map/teacher/pallas_call | solution.py:351
  157.2 1.3 decay.1
  158.5 2.5 %loss.4 = f32[4,1,256]{2,1,0:T(1,128)S(1)} custom-call(s32[3]{0:T(128)S(1)} %pad_add_fusion.place, bf16[256,2048]{1,0:T(8,128)(2,1)S(1)} %bitcast.24, f32[256,512]{1,0:T(8,128)S(1)} %copy-done.6, f32[4,256,128]{2,1,0:T(8,128)S(1)} %teacher.4.norm, f32[16,1024]{1,0:T(8,128)S(1)} %get-tuple-element.139.factor, f32[16,256]{1,0:T(8,128)S(1)} %get-tuple-element.140.log_row, ...), custom_call_target="tpu_custom_call" | custom-call | tf_op jit(solution)/shard_map/loss/pallas_call | solution.py:40
  161.1 2.3 %loss.5 = f32[4,1,256]{2,1,0:T(1,128)S(1)} custom-call(s32[3]{0:T(128)S(1)} %pad_add_fusion.place, bf16[256,2048]{1,0:T(8,128)(2,1)S(1)} %bitcast.25, f32[256,512]{1,0:T(8,128)S(1)} %copy-done.8, f32[4,256,128]{2,1,0:T(8,128)S(1)} %teacher.5.norm, f32[16,1024]{1,0:T(8,128)S(1)} %get-tuple-element.139.factor, f32[16,256]{1,0:T(8,128)S(1)} %get-tuple-element.140.log_row, ...), custom_call_target="tpu_custom_call" | custom-call | tf_op jit(solution)/shard_map/loss/pallas_call | solution.py:40
  163.4 2.8 %loss.6 = f32[4,1,256]{2,1,0:T(1,128)S(1)} custom-call(s32[3]{0:T(128)S(1)} %pad_add_fusion.place, bf16[256,2048]{1,0:T(8,128)(2,1)S(1)} %bitcast.26, f32[256,512]{1,0:T(8,128)S(1)} %copy-done.10, f32[4,256,128]{2,1,0:T(8,128)S(1)} %copy-done.4, f32[16,1024]{1,0:T(8,128)S(1)} %get-tuple-element.139.factor, f32[16,256]{1,0:T(8,128)S(1)} %get-tuple-element.140.log_row, ...), custom_call_target="tpu_custom_call" | custom-call | tf_op jit(solution)/shard_map/loss/pallas_call | solution.py:40
  166.3 2.1 %collective-permute-done.30.rest_0_ = bf16[256,512]{1,0:T(8,128)(2,1)} collective-permute-done((bf16[256,512]{1,0:T(8,128)(2,1)}, bf16[256,512]{1,0:T(8,128)(2,1)}, u32[]{:S(2)}, u32[]{:S(2)}) %collective-permute-start.30) | collective-permute-done | bytes 262176 | tf_op jit(solution)/shard_map/ppermute | solution.py:24
  168.3 2.8 %loss.7 = f32[4,1,256]{2,1,0:T(1,128)S(1)} custom-call(s32[3]{0:T(128)S(1)} %pad_add_fusion.place, bf16[256,2048]{1,0:T(8,128)(2,1)S(1)} %bitcast.27, f32[256,512]{1,0:T(8,128)S(1)} %copy-done.12, f32[4,256,128]{2,1,0:T(8,128)S(1)} %teacher.7.norm, f32[16,1024]{1,0:T(8,128)S(1)} %get-tuple-element.139.factor, f32[16,256]{1,0:T(8,128)S(1)} %get-tuple-element.140.log_row, ...), custom_call_target="tpu_custom_call" | custom-call | tf_op jit(solution)/shard_map/loss/pallas_call | solution.py:40
  171.2 0.6 copy.9
  (82 shorter events, 0.6 us)
Async XLA Ops:
  0.0 54.2 %copy-start = (bf16[1,256,512]{2,1,0:T(8,128)(2,1)S(1)}, bf16[1,256,512]{2,1,0:T(8,128)(2,1)}, u32[]{:S(2)}) copy-start(bf16[1,256,512]{2,1,0:T(8,128)(2,1)} %param.9) | copy-start | bytes 786436
  2.7 14.8 %collective-permute-start.3 = (bf16[64,4096]{1,0:T(8,128)(2,1)S(1)}, bf16[64,4096]{1,0:T(8,128)(2,1)S(1)}, u32[]{:S(2)}, u32[]{:S(2)}) collective-permute-start(bf16[64,4096]{1,0:T(8,128)(2,1)S(1)} %get-tuple-element.153), channel_id=1, source_target_pairs={{0,2},{2,0},{1,3},{3,1},{4,6},{6,4},{5,7},{7,5},{8,10},{10,8},{9,1... | collective-permute-start | bytes 1572872 | tf_op jit(solution)/shard_map/ppermute | solution.py:24
  4.2 2.1 %dynamic-slice-start = ((bf16[2048,512]{1,0:T(8,128)(2,1)}, s32[]{:T(128)}, s32[]{:T(128)}), bf16[512,256]{1,0:T(8,128)(2,1)S(1)}, s32[]{:S(2)}) async-start(bf16[2048,512]{1,0:T(8,128)(2,1)} %param.11, s32[]{:T(128)} %select_n.62, s32[]{:T(128)} %select_n.66), calls=%async_computation | async-start | bytes 524800 | tf_op jit(solution)/shard_map/dynamic_slice | solution.py:327
  6.4 25.1 %collective-permute-start.5 = (bf16[512,768]{1,0:T(8,128)(2,1)S(1)}, bf16[512,768]{1,0:T(8,128)(2,1)S(1)}, u32[]{:S(2)}, u32[]{:S(2)}) collective-permute-start(bf16[512,768]{1,0:T(8,128)(2,1)S(1)} %pad_maximum_fusion.2), channel_id=1, source_target_pairs={{0,4},{4,0},{8,12},{12,8},{1,5},{5,1},{9,13},{13,9},{2,6},{6,2},{1... | collective-permute-start | bytes 2359304 | tf_op jit(solution)/shard_map/ppermute | solution.py:24
  6.9 20.8 %collective-permute-start.2 = (bf16[64,4096]{1,0:T(8,128)(2,1)}, bf16[64,4096]{1,0:T(8,128)(2,1)}, u32[]{:S(2)}, u32[]{:S(2)}) collective-permute-start(bf16[64,4096]{1,0:T(8,128)(2,1)} %get-tuple-element.154), channel_id=1, source_target_pairs={{0,2},{2,0},{1,3},{3,1},{4,6},{6,4},{5,7},{7,5},{8,10},{10,8},{9,1... | collective-permute-start | bytes 1572872 | tf_op jit(solution)/shard_map/ppermute | solution.py:24
  7.4 28.8 %collective-permute-start.9 = (bf16[64,4096]{1,0:T(8,128)(2,1)}, bf16[64,4096]{1,0:T(8,128)(2,1)}, u32[]{:S(2)}, u32[]{:S(2)}) collective-permute-start(bf16[64,4096]{1,0:T(8,128)(2,1)} %get-tuple-element.91), channel_id=1, source_target_pairs={{2,10},{6,14},{8,0},{12,4},{3,11},{7,15},{9,1},{13,5},{18,26},{22,... | collective-permute-start | bytes 1572872 | tf_op jit(solution)/shard_map/ppermute | solution.py:379
  17.6 20.3 %copy-start.21 = (bf16[64,4096]{1,0:T(8,128)(2,1)}, bf16[64,4096]{1,0:T(8,128)(2,1)S(1)}, u32[]{:S(2)}) copy-start(bf16[64,4096]{1,0:T(8,128)(2,1)S(1)} %collective-permute-done.3) | copy-start | bytes 1572868
  17.6 25.9 %collective-permute-start.10 = (bf16[64,4096]{1,0:T(8,128)(2,1)S(1)}, bf16[64,4096]{1,0:T(8,128)(2,1)}, u32[]{:S(2)}, u32[]{:S(2)}) collective-permute-start(bf16[64,4096]{1,0:T(8,128)(2,1)S(1)} %collective-permute-done.3), channel_id=1, source_target_pairs={{0,8},{4,12},{10,2},{14,6},{1,9},{5,13},{11,3},{15,7},{16,24},{20,... | collective-permute-start | bytes 1572872 | tf_op jit(solution)/shard_map/ppermute | solution.py:379
  18.8 41.1 %collective-permute-start.12 = (bf16[512,512]{1,0:T(8,128)(2,1)}, bf16[512,512]{1,0:T(8,128)(2,1)S(1)}, u32[]{:S(2)}, u32[]{:S(2)}) collective-permute-start(bf16[512,512]{1,0:T(8,128)(2,1)} %get-tuple-element.152), channel_id=1, source_target_pairs={{0,4},{4,0},{8,12},{12,8},{1,5},{5,1},{9,13},{13,9},{2,6},{6,2},{1... | collective-permute-start | bytes 1572872 | tf_op jit(solution)/shard_map/ppermute | solution.py:24
  19.4 36.2 %copy-start.20 = (bf16[2048,512]{1,0:T(8,128)(2,1)S(1)}, bf16[2048,512]{1,0:T(8,128)(2,1)}, u32[]{:S(2)}) copy-start(bf16[2048,512]{1,0:T(8,128)(2,1)} %param.11) | copy-start | bytes 6291460
  27.7 38.8 %collective-permute-start.1 = (bf16[64,4096]{1,0:T(8,128)(2,1)}, bf16[64,4096]{1,0:T(8,128)(2,1)S(1)}, u32[]{:S(2)}, u32[]{:S(2)}) collective-permute-start(bf16[64,4096]{1,0:T(8,128)(2,1)} %get-tuple-element.93), channel_id=1, source_target_pairs={{2,10},{6,14},{8,0},{12,4},{3,11},{7,15},{9,1},{13,5},{18,26},{22,... | collective-permute-start | bytes 1572872 | tf_op jit(solution)/shard_map/ppermute | solution.py:379
  31.5 27.2 %collective-permute-start.16 = (bf16[64,4096]{1,0:T(8,128)(2,1)}, bf16[64,4096]{1,0:T(8,128)(2,1)S(1)}, u32[]{:S(2)}, u32[]{:S(2)}) collective-permute-start(bf16[64,4096]{1,0:T(8,128)(2,1)} %get-tuple-element.91), channel_id=1, source_target_pairs={{0,2},{4,6},{10,8},{14,12},{1,3},{5,7},{11,9},{15,13},{16,18},{20,... | collective-permute-start | bytes 1572872 | tf_op jit(solution)/shard_map/ppermute | solution.py:381
  36.3 22.4 %collective-permute-start.6 = (bf16[512,768]{1,0:T(8,128)(2,1)S(1)}, bf16[512,768]{1,0:T(8,128)(2,1)S(1)}, u32[]{:S(2)}, u32[]{:S(2)}) collective-permute-start(bf16[512,768]{1,0:T(8,128)(2,1)S(1)} %collective-permute-done.5.rest_0_.rest_4_), channel_id=1, source_target_pairs={{0,16},{16,0},{1,17},{17,1},{2,18},{18,2},{3,19},{19,3},{4,20},{20... | collective-permute-start | bytes 2359304 | tf_op jit(solution)/shard_map/ppermute | solution.py:24
  44.6 19.7 %collective-permute-start.11 = (bf16[64,4096]{1,0:T(8,128)(2,1)S(1)}, bf16[64,4096]{1,0:T(8,128)(2,1)S(1)}, u32[]{:S(2)}, u32[]{:S(2)}) collective-permute-start(bf16[64,4096]{1,0:T(8,128)(2,1)S(1)} %broadcast_select_fusion.5), channel_id=1, source_target_pairs={{0,2},{2,0},{1,3},{3,1},{4,6},{6,4},{5,7},{7,5},{8,10},{10,8},{9,1... | collective-permute-start | bytes 1572872 | tf_op jit(solution)/shard_map/ppermute | solution.py:24
  55.5 8.8 %copy-start.17 = (bf16[2048,16]{0,1:T(8,128)(2,1)S(1)}, bf16[2048,16]{0,1:T(8,128)(2,1)}, u32[]{:S(2)}) copy-start(bf16[2048,16]{0,1:T(8,128)(2,1)} %param.12) | copy-start | bytes 196612
  55.5 11.0 %copy-start.23 = (bf16[64,4096]{1,0:T(8,128)(2,1)S(1)}, bf16[64,4096]{1,0:T(8,128)(2,1)}, u32[]{:S(2)}) copy-start(bf16[64,4096]{1,0:T(8,128)(2,1)} %get-tuple-element.93) | copy-start | bytes 1572868
  56.6 25.8 %copy-start.18 = (bf16[1,256,4096]{2,1,0:T(8,128)(2,1)S(1)}, bf16[1,256,4096]{2,1,0:T(8,128)(2,1)}, u32[]{:S(2)}) copy-start(bf16[1,256,4096]{2,1,0:T(8,128)(2,1)} %param.7) | copy-start | bytes 6291460
  56.6 25.8 %copy-start.22 = (bf16[64,4096]{1,0:T(8,128)(2,1)S(1)}, bf16[64,4096]{1,0:T(8,128)(2,1)}, u32[]{:S(2)}) copy-start(bf16[64,4096]{1,0:T(8,128)(2,1)} %copy-done.21) | copy-start | bytes 1572868
  58.7 31.5 %collective-permute-start.15 = (bf16[256,256]{1,0:T(8,128)(2,1)S(1)}, bf16[256,256]{1,0:T(8,128)(2,1)S(1)}, u32[]{:S(2)}, u32[]{:S(2)}) collective-permute-start(bf16[256,256]{1,0:T(8,128)(2,1)S(1)} %dynamic-slice_bitcast_fusion), channel_id=1, source_target_pairs={{0,8},{4,12},{8,0},{12,4},{1,9},{5,13},{9,1},{13,5},{2,10},{6,14},... | collective-permute-start | bytes 393224 | tf_op jit(solution)/shard_map/ppermute | solution.py:24
  58.7 21.0 %collective-permute-start.4 = (bf16[64,4096]{1,0:T(8,128)(2,1)}, bf16[64,4096]{1,0:T(8,128)(2,1)S(1)}, u32[]{:S(2)}, u32[]{:S(2)}) collective-permute-start(bf16[64,4096]{1,0:T(8,128)(2,1)} %collective-permute-done.2), channel_id=1, source_target_pairs={{0,8},{4,12},{10,2},{14,6},{1,9},{5,13},{11,3},{15,7},{16,24},{20,... | collective-permute-start | bytes 1572872 | tf_op jit(solution)/shard_map/ppermute | solution.py:379
  60.0 4.4 %collective-permute-start.7 = (bf16[512,768]{1,0:T(8,128)(2,1)S(1)}, bf16[512,768]{1,0:T(8,128)(2,1)S(1)}, u32[]{:S(2)}, u32[]{:S(2)}) collective-permute-start(bf16[512,768]{1,0:T(8,128)(2,1)S(1)} %collective-permute-done.5.rest_0_.rest_4_), channel_id=1, source_target_pairs={{0,1},{1,0},{2,3},{3,2},{4,5},{5,4},{6,7},{7,6},{8,9},{9,8},{10,11... | collective-permute-start | bytes 2359304 | tf_op jit(solution)/shard_map/ppermute | solution.py:24
  64.3 2.3 %collective-permute-start.8 = (bf16[512,768]{1,0:T(8,128)(2,1)S(1)}, bf16[512,768]{1,0:T(8,128)(2,1)S(1)}, u32[]{:S(2)}, u32[]{:S(2)}) collective-permute-start(bf16[512,768]{1,0:T(8,128)(2,1)S(1)} %collective-permute-done.6.rest_1_.rest_5_), channel_id=1, source_target_pairs={{0,1},{1,0},{2,3},{3,2},{4,5},{5,4},{6,7},{7,6},{8,9},{9,8},{10,11... | collective-permute-start | bytes 2359304 | tf_op jit(solution)/shard_map/ppermute | solution.py:24
  64.4 25.8 %collective-permute-start.14 = (bf16[16,2048]{1,0:T(8,128)(2,1)S(1)}, bf16[16,2048]{1,0:T(8,128)(2,1)S(1)}, u32[]{:S(2)}, u32[]{:S(2)}) collective-permute-start(bf16[16,2048]{1,0:T(8,128)(2,1)S(1)} %bitcast.28), channel_id=1, source_target_pairs={{0,4},{4,0},{8,12},{12,8},{1,5},{5,1},{9,13},{13,9},{2,6},{6,2},{1... | collective-permute-start | bytes 196616 | tf_op jit(solution)/shard_map/ppermute | solution.py:24
  66.6 34.9 %collective-permute-start = (bf16[512,1024]{1,0:T(8,128)(2,1)S(1)}, bf16[512,1024]{1,0:T(8,128)(2,1)S(1)}, u32[]{:S(2)}, u32[]{:S(2)}) collective-permute-start(bf16[512,1024]{1,0:T(8,128)(2,1)S(1)} %constant_dynamic-slice_fusion.2), channel_id=1, source_target_pairs={{0,4},{4,0},{8,12},{12,8},{1,5},{5,1},{9,13},{13,9},{2,6},{6,2},{1... | collective-permute-start | bytes 3145736 | tf_op jit(solution)/shard_map/ppermute | solution.py:24
  66.6 15.9 %collective-permute-start.17 = (bf16[64,4096]{1,0:T(8,128)(2,1)S(1)}, bf16[64,4096]{1,0:T(8,128)(2,1)S(1)}, u32[]{:S(2)}, u32[]{:S(2)}) collective-permute-start(bf16[64,4096]{1,0:T(8,128)(2,1)S(1)} %copy-done.23), channel_id=1, source_target_pairs={{0,2},{4,6},{10,8},{14,12},{1,3},{5,7},{11,9},{15,13},{16,18},{20,... | collective-permute-start | bytes 1572872 | tf_op jit(solution)/shard_map/ppermute | solution.py:381
  79.6 10.5 %collective-permute-start.18 = (bf16[512,512]{1,0:T(8,128)(2,1)S(1)}, bf16[512,512]{1,0:T(8,128)(2,1)S(1)}, u32[]{:S(2)}, u32[]{:S(2)}) collective-permute-start(bf16[512,512]{1,0:T(8,128)(2,1)S(1)} %collective-permute-done.12.rest_4_), channel_id=1, source_target_pairs={{0,16},{16,0},{1,17},{17,1},{2,18},{18,2},{3,19},{19,3},{4,20},{20... | collective-permute-start | bytes 1572872 | tf_op jit(solution)/shard_map/ppermute | solution.py:24
  82.4 13.1 %collective-permute-start.13 = (bf16[64,4096]{1,0:T(8,128)(2,1)S(1)}, bf16[64,4096]{1,0:T(8,128)(2,1)S(1)}, u32[]{:S(2)}, u32[]{:S(2)}) collective-permute-start(bf16[64,4096]{1,0:T(8,128)(2,1)S(1)} %broadcast_select_fusion.4), channel_id=1, source_target_pairs={{0,2},{2,0},{1,3},{3,1},{4,6},{6,4},{5,7},{7,5},{8,10},{10,8},{9,1... | collective-permute-start | bytes 1572872 | tf_op jit(solution)/shard_map/ppermute | solution.py:24
  96.9 8.2 %copy-start.2 = (bf16[128,4096]{1,0:T(8,128)(2,1)S(1)}, bf16[128,4096]{1,0:T(8,128)(2,1)}, u32[]{:S(2)}) copy-start(bf16[128,4096]{1,0:T(8,128)(2,1)} %get-tuple-element.162.act_high.rest_1_) | copy-start | bytes 3145732
  101.5 29.5 %collective-permute-start.25 = (bf16[512,1024]{1,0:T(8,128)(2,1)S(1)}, bf16[512,1024]{1,0:T(8,128)(2,1)S(1)}, u32[]{:S(2)}, u32[]{:S(2)}) collective-permute-start(bf16[512,1024]{1,0:T(8,128)(2,1)S(1)} %collective-permute-done.rest_4_), channel_id=1, source_target_pairs={{0,16},{16,0},{1,17},{17,1},{2,18},{18,2},{3,19},{19,3},{4,20},{20... | collective-permute-start | bytes 3145736 | tf_op jit(solution)/shard_map/ppermute | solution.py:24
  103.1 6.6 %collective-permute-start.21 = (bf16[512,512]{1,0:T(8,128)(2,1)S(1)}, bf16[512,512]{1,0:T(8,128)(2,1)S(1)}, u32[]{:S(2)}, u32[]{:S(2)}) collective-permute-start(bf16[512,512]{1,0:T(8,128)(2,1)S(1)} %collective-permute-done.12.rest_4_), channel_id=1, source_target_pairs={{0,1},{1,0},{2,3},{3,2},{4,5},{5,4},{6,7},{7,6},{8,9},{9,8},{10,11... | collective-permute-start | bytes 1572872 | tf_op jit(solution)/shard_map/ppermute | solution.py:24
  103.1 9.6 %collective-permute-start.22 = (bf16[512,512]{1,0:T(8,128)(2,1)S(1)}, bf16[512,512]{1,0:T(8,128)(2,1)S(1)}, u32[]{:S(2)}, u32[]{:S(2)}) collective-permute-start(bf16[512,512]{1,0:T(8,128)(2,1)S(1)} %collective-permute-done.18.rest_5_), channel_id=1, source_target_pairs={{0,1},{1,0},{2,3},{3,2},{4,5},{5,4},{6,7},{7,6},{8,9},{9,8},{10,11... | collective-permute-start | bytes 1572872 | tf_op jit(solution)/shard_map/ppermute | solution.py:24
  103.6 22.7 %collective-permute-start.20 = (bf16[576,256]{1,0:T(8,128)(2,1)S(1)}, bf16[576,256]{1,0:T(8,128)(2,1)S(1)}, u32[]{:S(2)}, u32[]{:S(2)}) collective-permute-start(bf16[576,256]{1,0:T(8,128)(2,1)S(1)} %get-tuple-element.104), channel_id=1, source_target_pairs={{0,8},{4,12},{8,0},{12,4},{1,9},{5,13},{9,1},{13,5},{2,10},{6,14},... | collective-permute-start | bytes 884744 | tf_op jit(solution)/shard_map/ppermute | solution.py:24
  103.6 22.7 %collective-permute-start.19 = (bf16[512,256]{1,0:T(8,128)(2,1)S(1)}, bf16[512,256]{1,0:T(8,128)(2,1)S(1)}, u32[]{:S(2)}, u32[]{:S(2)}) collective-permute-start(bf16[512,256]{1,0:T(8,128)(2,1)S(1)} %pad_maximum_fusion.3.rest_0_.rest_1_), channel_id=1, source_target_pairs={{0,4},{4,0},{8,12},{12,8},{1,5},{5,1},{9,13},{13,9},{2,6},{6,2},{1... | collective-permute-start | bytes 786440 | tf_op jit(solution)/shard_map/ppermute | solution.py:24
  109.7 7.8 %copy-start.5 = (f32[256,512]{1,0:T(8,128)}, f32[256,512]{1,0:T(8,128)S(1)}, u32[]{:S(2)}) copy-start(f32[256,512]{1,0:T(8,128)S(1)} %get-tuple-element.107.kept) | copy-start | bytes 1572868
  109.7 21.2 %collective-permute-start.26 = (bf16[256,512]{1,0:T(8,128)(2,1)S(1)}, bf16[256,512]{1,0:T(8,128)(2,1)S(1)}, u32[]{:S(2)}, u32[]{:S(2)}) collective-permute-start(bf16[256,512]{1,0:T(8,128)(2,1)S(1)} %get-tuple-element.108), channel_id=1, source_target_pairs={{0,8},{4,12},{8,0},{12,4},{1,9},{5,13},{9,1},{13,5},{2,10},{6,14},... | collective-permute-start | bytes 786440 | tf_op jit(solution)/shard_map/ppermute | solution.py:24
  112.7 13.6 %copy-start.1 = (bf16[1,256,2048]{2,1,0:T(8,128)(2,1)S(1)}, bf16[1,256,2048]{2,1,0:T(8,128)(2,1)}, u32[]{:S(2)}) copy-start(bf16[1,256,2048]{2,1,0:T(8,128)(2,1)} %param.8) | copy-start | bytes 3145732
  117.5 18.8 %copy-start.7 = (f32[256,512]{1,0:T(8,128)}, f32[256,512]{1,0:T(8,128)S(1)}, u32[]{:S(2)}) copy-start(f32[256,512]{1,0:T(8,128)S(1)} %get-tuple-element.115.kept) | copy-start | bytes 1572868
  130.9 11.0 %copy-start.13 = (bf16[256,512]{1,0:T(8,128)(2,1)}, bf16[256,512]{1,0:T(8,128)(2,1)S(1)}, u32[]{:S(2)}) copy-start(bf16[256,512]{1,0:T(8,128)(2,1)S(1)} %collective-permute-done.26.rest_0_) | copy-start | bytes 786436
  131.0 5.3 %collective-permute-start.27 = (bf16[512,1024]{1,0:T(8,128)(2,1)S(1)}, bf16[512,1024]{1,0:T(8,128)(2,1)S(1)}, u32[]{:S(2)}, u32[]{:S(2)}) collective-permute-start(bf16[512,1024]{1,0:T(8,128)(2,1)S(1)} %collective-permute-done.rest_4_), channel_id=1, source_target_pairs={{0,1},{1,0},{2,3},{3,2},{4,5},{5,4},{6,7},{7,6},{8,9},{9,8},{10,11... | collective-permute-start | bytes 3145736 | tf_op jit(solution)/shard_map/ppermute | solution.py:24
  131.0 5.3 %collective-permute-start.28 = (bf16[512,1024]{1,0:T(8,128)(2,1)S(1)}, bf16[512,1024]{1,0:T(8,128)(2,1)S(1)}, u32[]{:S(2)}, u32[]{:S(2)}) collective-permute-start(bf16[512,1024]{1,0:T(8,128)(2,1)S(1)} %collective-permute-done.25.rest_5_), channel_id=1, source_target_pairs={{0,1},{1,0},{2,3},{3,2},{4,5},{5,4},{6,7},{7,6},{8,9},{9,8},{10,11... | collective-permute-start | bytes 3145736 | tf_op jit(solution)/shard_map/ppermute | solution.py:24
  131.5 15.0 %collective-permute-start.24 = (bf16[256,512]{1,0:T(8,128)(2,1)S(1)}, bf16[256,512]{1,0:T(8,128)(2,1)S(1)}, u32[]{:S(2)}, u32[]{:S(2)}) collective-permute-start(bf16[256,512]{1,0:T(8,128)(2,1)S(1)} %get-tuple-element.114), channel_id=1, source_target_pairs={{0,8},{4,12},{8,0},{12,4},{1,9},{5,13},{9,1},{13,5},{2,10},{6,14},... | collective-permute-start | bytes 786440 | tf_op jit(solution)/shard_map/ppermute | solution.py:24
  131.5 25.7 %collective-permute-start.23 = (bf16[576,256]{1,0:T(8,128)(2,1)S(1)}, bf16[576,256]{1,0:T(8,128)(2,1)S(1)}, u32[]{:S(2)}, u32[]{:S(2)}) collective-permute-start(bf16[576,256]{1,0:T(8,128)(2,1)S(1)} %combine.1.rest_0_.rest_3_), channel_id=1, source_target_pairs={{0,4},{4,0},{8,12},{12,8},{1,5},{5,1},{9,13},{13,9},{2,6},{6,2},{1... | collective-permute-start | bytes 884744 | tf_op jit(solution)/shard_map/ppermute | solution.py:24
  136.3 1.0 copy-start.19
  142.0 0.8 copy-start.9
  142.8 20.6 %collective-permute-start.29 = (bf16[256,512]{1,0:T(8,128)(2,1)}, bf16[256,512]{1,0:T(8,128)(2,1)}, u32[]{:S(2)}, u32[]{:S(2)}) collective-permute-start(bf16[256,512]{1,0:T(8,128)(2,1)} %get-tuple-element.129), channel_id=1, source_target_pairs={{0,8},{4,12},{8,0},{12,4},{1,9},{5,13},{9,1},{13,5},{2,10},{6,14},... | collective-permute-start | bytes 786440 | tf_op jit(solution)/shard_map/ppermute | solution.py:24
  146.5 5.0 %copy-start.3 = (f32[4,256,128]{2,1,0:T(8,128)}, f32[4,256,128]{2,1,0:T(8,128)S(1)}, u32[]{:S(2)}) copy-start(f32[4,256,128]{2,1,0:T(8,128)S(1)} %teacher.6.norm) | copy-start | bytes 1572868
  146.5 7.6 %copy-start.24 = (f32[16]{0:T(128)S(1)}, f32[16]{0:T(128)}, u32[]{:S(2)}) copy-start(f32[16]{0:T(128)} %param.13) | copy-start | bytes 196
  146.5 5.0 %copy-start.15 = (bf16[256,512]{1,0:T(8,128)(2,1)}, bf16[256,512]{1,0:T(8,128)(2,1)S(1)}, u32[]{:S(2)}) copy-start(bf16[256,512]{1,0:T(8,128)(2,1)S(1)} %collective-permute-done.24.rest_0_) | copy-start | bytes 786436
  151.5 0.8 copy-start.11
  152.3 16.0 %collective-permute-start.30 = (bf16[256,512]{1,0:T(8,128)(2,1)}, bf16[256,512]{1,0:T(8,128)(2,1)}, u32[]{:S(2)}, u32[]{:S(2)}) collective-permute-start(bf16[256,512]{1,0:T(8,128)(2,1)} %get-tuple-element.134), channel_id=1, source_target_pairs={{0,8},{4,12},{8,0},{12,4},{1,9},{5,13},{9,1},{13,5},{2,10},{6,14},... | collective-permute-start | bytes 786440 | tf_op jit(solution)/shard_map/ppermute | solution.py:24
  154.1 4.3 %copy-start.6 = (f32[256,512]{1,0:T(8,128)S(1)}, f32[256,512]{1,0:T(8,128)}, u32[]{:S(2)}) copy-start(f32[256,512]{1,0:T(8,128)} %copy-done.5) | copy-start | bytes 1572868
  154.1 4.3 %copy-start.14 = (bf16[256,512]{1,0:T(8,128)(2,1)S(1)}, bf16[256,512]{1,0:T(8,128)(2,1)}, u32[]{:S(2)}) copy-start(bf16[256,512]{1,0:T(8,128)(2,1)} %copy-done.13) | copy-start | bytes 786436
  157.1 3.9 %copy-start.8 = (f32[256,512]{1,0:T(8,128)S(1)}, f32[256,512]{1,0:T(8,128)}, u32[]{:S(2)}) copy-start(f32[256,512]{1,0:T(8,128)} %copy-done.7) | copy-start | bytes 1572868
  157.2 3.9 %copy-start.16 = (bf16[256,512]{1,0:T(8,128)(2,1)S(1)}, bf16[256,512]{1,0:T(8,128)(2,1)}, u32[]{:S(2)}) copy-start(bf16[256,512]{1,0:T(8,128)(2,1)} %copy-done.15) | copy-start | bytes 786436
  161.1 2.4 %copy-start.4 = (f32[4,256,128]{2,1,0:T(8,128)S(1)}, f32[4,256,128]{2,1,0:T(8,128)}, u32[]{:S(2)}) copy-start(f32[4,256,128]{2,1,0:T(8,128)} %copy-done.3) | copy-start | bytes 1572868
  161.1 2.4 %copy-start.10 = (f32[256,512]{1,0:T(8,128)S(1)}, f32[256,512]{1,0:T(8,128)}, u32[]{:S(2)}) copy-start(f32[256,512]{1,0:T(8,128)} %copy-done.9) | copy-start | bytes 1572868
  163.4 4.9 %copy-start.12 = (f32[256,512]{1,0:T(8,128)S(1)}, f32[256,512]{1,0:T(8,128)}, u32[]{:S(2)}) copy-start(f32[256,512]{1,0:T(8,128)} %copy-done.11) | copy-start | bytes 1572868

commit v6 on v5

--- a/solution.py
+++ b/solution.py
@@ -468,6 +468,9 @@
     full_partial(0)
     weights.append((1, 2, order.wait(w1)))
     full_partial(1)
+    key_rest = order.wait(key_rest)
+    keys = [key_pair] + key_rest
+    norms.append(order.wait(teacher(0, heads)))
     came = order.wait(came)
     pair = order.wait(
         call(
@@ -479,12 +482,9 @@
         )[0]
     )
     pair_rest = over_half(pair)
-    key_rest = order.wait(key_rest)
-    keys = [key_pair] + key_rest
-    norms.append(order.wait(teacher(0, heads)))
+    norms.append(order.wait(teacher(heads, heads)))
     arrived[0] = order.wait(arrived[0])
     w2 = spread(order.wait(w2), "batch")
-    norms.append(order.wait(teacher(heads, heads)))
     weights.append((2, 4, order.wait(w2)))
     full_partial(2)
     norms.append(order.wait(teacher(2 * heads, heads)))

time: 175 us -> 174 us (level)
  transfers between devices with their start and end apart: 31 -> 31, of which waited for: 15 -> 19; matrix products, arithmetic and copies ran while one was open for 6% -> 6% of each run, Pallas kernels for 26% -> 26%
where the time goes in v6:
time: 174 us; the launch traced here: 171 us
  waiting for transfers between devices  69.9 us (40%)
  Pallas kernels  47.4 us (27%)
  starting transfers between devices  37 us (21%)
  local copies, waits for them, and re-layouts  10.6 us (6%)
  other arithmetic  5.83 us (3%)
    ppermute x25, waiting for transfers between devices, xor_permute(): return lax.ppermute(value, axis, [(i, i ^ offset) for i in range(size)])  45.6 us
    pallas_call x11, Pallas kernels, call(): pl.pallas_call(kernel, grid=(1,), in_specs=in_specs, out_specs=tuple((who...  35.2 us
    ppermute x25, starting transfers between devices, xor_permute(): return lax.ppermute(value, axis, [(i, i ^ offset) for i in range(size)])  27 us
    ppermute x4, waiting for transfers between devices, local(): lax.ppermute(value, both, [(flat(i, j), flat(i ^ half, j)) for i, j in gr...  20.9 us
    pallas_call x4, Pallas kernels, teacher(): pl.pallas_call(functools.partial(teacher_kernel, offsets), grid=(number,)...  12.2 us
    ppermute x4, starting transfers between devices, local(): lax.ppermute(value, both, [(flat(i, j), flat(i ^ half, j)) for i, j in gr...  7.48 us
  transfers between devices with their start and end apart: 31, of which 19 were waited for; matrix products, arithmetic and copies ran while one was open for 6% of the time, Pallas kernels for 26%

profile of v6, /device:TPU:24, one launch (start us, length us, event | category | flops | bytes accessed | tf_op | source)
XLA Modules:
  0.0 171.2 jit_solution(12560119490686560519)
XLA Ops:
  0.0 2.7 %slice_bitcast_fusion.1 = (bf16[64,4096]{1,0:T(8,128)(2,1)S(1)}, bf16[64,4096]{1,0:T(8,128)(2,1)}, bf16[64,4096]{1,0:T(8,128)(2,1)}, bf16[64,4096]{1,0:T(8,128)(2,1)}) fusion(bf16[1,256,4096]{2,1,0:T(8,128)(2,1)} %param.7), kind=kLoop, calls=%fused_computation.5 | loop fusion | bytes 4194304 | tf_op jit(solution)/shard_map/slice | solution.py:380
  2.7 1.5 collective-permute-start.3
  4.2 2.1 %constant_dynamic-slice_fusion.1 = (bf16[512,512]{1,0:T(8,128)(2,1)S(1)}, bf16[512,512]{1,0:T(8,128)(2,1)}) fusion(bf16[2048,2048]{1,0:T(8,128)(2,1)} %rest_3_.7, s32[]{:T(128)} %select_n.62), kind=kLoop, calls=%fused_computation.18 | loop fusion | bytes 2097156 | tf_op jit(solution)/shard_map/dynamic_slice | solution.py:325
  6.4 0.5 collective-permute-start.5
  6.9 0.5 collective-permute-start.2
  7.4 2.7 %collective-permute-start.9 = (bf16[64,4096]{1,0:T(8,128)(2,1)}, bf16[64,4096]{1,0:T(8,128)(2,1)}, u32[]{:S(2)}, u32[]{:S(2)}) collective-permute-start(bf16[64,4096]{1,0:T(8,128)(2,1)} %get-tuple-element.91), channel_id=1, source_target_pairs={{2,10},{6,14},{8,0},{12,4},{3,11},{7,15},{9,1},{13,5},{18,26},{22,... | collective-permute-start | bytes 1572872 | tf_op jit(solution)/shard_map/ppermute | solution.py:379
  10.1 7.4 %collective-permute-done.3 = bf16[64,4096]{1,0:T(8,128)(2,1)S(1)} collective-permute-done((bf16[64,4096]{1,0:T(8,128)(2,1)S(1)}, bf16[64,4096]{1,0:T(8,128)(2,1)S(1)}, u32[]{:S(2)}, u32[]{:S(2)}) %collective-permute-start.3) | collective-permute-done | bytes 524320 | tf_op jit(solution)/shard_map/ppermute | solution.py:24
  17.6 1.3 collective-permute-start.10
  18.8 0.5 collective-permute-start.12
  19.4 8.4 %collective-permute-done.2 = bf16[64,4096]{1,0:T(8,128)(2,1)} collective-permute-done((bf16[64,4096]{1,0:T(8,128)(2,1)}, bf16[64,4096]{1,0:T(8,128)(2,1)}, u32[]{:S(2)}, u32[]{:S(2)}) %collective-permute-start.2) | collective-permute-done | bytes 524320 | tf_op jit(solution)/shard_map/ppermute | solution.py:24
  27.7 2.3 %collective-permute-start.1 = (bf16[64,4096]{1,0:T(8,128)(2,1)}, bf16[64,4096]{1,0:T(8,128)(2,1)S(1)}, u32[]{:S(2)}, u32[]{:S(2)}) collective-permute-start(bf16[64,4096]{1,0:T(8,128)(2,1)} %get-tuple-element.93), channel_id=1, source_target_pairs={{2,10},{6,14},{8,0},{12,4},{3,11},{7,15},{9,1},{13,5},{18,26},{22,... | collective-permute-start | bytes 1572872 | tf_op jit(solution)/shard_map/ppermute | solution.py:379
  30.0 1.5 collective-permute-done.5.rest_0_.rest_4_
  31.5 1.3 collective-permute-start.16
  32.8 3.5 %collective-permute-done.9 = bf16[64,4096]{1,0:T(8,128)(2,1)} collective-permute-done((bf16[64,4096]{1,0:T(8,128)(2,1)}, bf16[64,4096]{1,0:T(8,128)(2,1)}, u32[]{:S(2)}, u32[]{:S(2)}) %collective-permute-start.9) | collective-permute-done | bytes 524320 | tf_op jit(solution)/shard_map/ppermute | solution.py:379
  36.3 1.5 collective-permute-start.6
  37.8 5.7 %collective-permute-done.10 = bf16[64,4096]{1,0:T(8,128)(2,1)} collective-permute-done((bf16[64,4096]{1,0:T(8,128)(2,1)S(1)}, bf16[64,4096]{1,0:T(8,128)(2,1)}, u32[]{:S(2)}, u32[]{:S(2)}) %collective-permute-start.10) | collective-permute-done | bytes 524320 | tf_op jit(solution)/shard_map/ppermute | solution.py:379
  43.5 1.1 broadcast_select_fusion.5
  44.6 9.5 %collective-permute-start.11 = (bf16[64,4096]{1,0:T(8,128)(2,1)S(1)}, bf16[64,4096]{1,0:T(8,128)(2,1)S(1)}, u32[]{:S(2)}, u32[]{:S(2)}) collective-permute-start(bf16[64,4096]{1,0:T(8,128)(2,1)S(1)} %broadcast_select_fusion.5), channel_id=1, source_target_pairs={{0,2},{2,0},{1,3},{3,1},{4,6},{6,4},{5,7},{7,5},{8,10},{10,8},{9,1... | collective-permute-start | bytes 1572872 | tf_op jit(solution)/shard_map/ppermute | solution.py:24
  54.2 1.3 constant_dynamic-slice_fusion.2
  55.5 1.1 constant_dynamic-slice_fusion.own
  56.6 2.0 %collective-permute-done.16 = bf16[64,4096]{1,0:T(8,128)(2,1)S(1)} collective-permute-done((bf16[64,4096]{1,0:T(8,128)(2,1)}, bf16[64,4096]{1,0:T(8,128)(2,1)S(1)}, u32[]{:S(2)}, u32[]{:S(2)}) %collective-permute-start.16) | collective-permute-done | bytes 524320 | tf_op jit(solution)/shard_map/ppermute | solution.py:381
  58.7 1.3 collective-permute-start.4
  60.0 4.2 %collective-permute-done.11 = bf16[64,4096]{1,0:T(8,128)(2,1)S(1)} collective-permute-done((bf16[64,4096]{1,0:T(8,128)(2,1)S(1)}, bf16[64,4096]{1,0:T(8,128)(2,1)S(1)}, u32[]{:S(2)}, u32[]{:S(2)}) %collective-permute-start.11) | collective-permute-done | bytes 524320 | tf_op jit(solution)/shard_map/ppermute | solution.py:24
  64.5 2.1 %collective-permute-done.8.rest_3_.rest_7_ = bf16[512,768]{1,0:T(8,128)(2,1)S(1)} collective-permute-done((bf16[512,768]{1,0:T(8,128)(2,1)S(1)}, bf16[512,768]{1,0:T(8,128)(2,1)S(1)}, u32[]{:S(2)}, u32[]{:S(2)}) %collective-permute-start.8) | collective-permute-done | bytes 786464 | tf_op jit(solution)/shard_map/ppermute | solution.py:24
  66.6 1.3 collective-permute-start.17
  67.9 11.8 %collective-permute-done.4 = bf16[64,4096]{1,0:T(8,128)(2,1)S(1)} collective-permute-done((bf16[64,4096]{1,0:T(8,128)(2,1)}, bf16[64,4096]{1,0:T(8,128)(2,1)S(1)}, u32[]{:S(2)}, u32[]{:S(2)}) %collective-permute-start.4) | collective-permute-done | bytes 524320 | tf_op jit(solution)/shard_map/ppermute | solution.py:379
  79.6 1.5 collective-permute-start.18
  81.2 1.2 collective-permute-done.17
  82.4 3.2 %maximum_select_fusion.act_own.rest_2_ = bf16[256,4096]{1,0:T(8,128)(2,1)} fusion(bf16[64,4096]{1,0:T(8,128)(2,1)} %collective-permute-done.2, bf16[64,4096]{1,0:T(8,128)(2,1)S(1)} %collective-permute-done.17, bf16[64,4096]{1,0:T(8,128)(2,1)S(1)} %copy-done.22, bf16[64,4096]{1,0:T(8,128)(2,1)S(1)} %collective-permute-done.16, ...), kind=kLoop, calls=%fused_computation | loop fusion | flops 9437184 | bytes 6291457 | tf_op jit(solution)/shard_map/jit(_where)/select_n | solution.py:416
  85.6 4.5 %collective-permute-done.18.rest_5_ = bf16[512,512]{1,0:T(8,128)(2,1)S(1)} collective-permute-done((bf16[512,512]{1,0:T(8,128)(2,1)S(1)}, bf16[512,512]{1,0:T(8,128)(2,1)S(1)}, u32[]{:S(2)}, u32[]{:S(2)}) %collective-permute-start.18) | collective-permute-done | bytes 524320 | tf_op jit(solution)/shard_map/ppermute | solution.py:24
  90.1 5.4 %collective-permute-done.13 = bf16[64,4096]{1,0:T(8,128)(2,1)S(1)} collective-permute-done((bf16[64,4096]{1,0:T(8,128)(2,1)S(1)}, bf16[64,4096]{1,0:T(8,128)(2,1)S(1)}, u32[]{:S(2)}, u32[]{:S(2)}) %collective-permute-start.13) | collective-permute-done | bytes 524320 | tf_op jit(solution)/shard_map/ppermute | solution.py:24
  95.6 1.2 pad_maximum_fusion
  96.9 4.6 %extra.1 = (f32[512,256]{1,0:T(8,128)S(1)}, f32[16,512]{1,0:T(8,128)S(1)}, bf16[576,256]{1,0:T(8,128)(2,1)S(1)}) custom-call(s32[3]{0:T(128)S(1)} %pad_add_fusion.place, bf16[256,4096]{1,0:T(8,128)(2,1)} %maximum_select_fusion.act_own.rest_2_, bf16[128,4096]{1,0:T(8,128)(2,1)S(1)} %get-tuple-element.161.act_low.rest_0_, ...), custom_call_target="tpu_custom_call" | custom-call | tf_op jit(solution)/shard_map/extra/pallas_call | solution.py:40
  101.5 1.6 collective-permute-start.25
  103.1 0.5 collective-permute-start.21
  103.6 1.5 collective-permute-start.19
  105.1 4.6 %partial.4 = (bf16[256,512]{1,0:T(8,128)(2,1)S(1)}, f32[256,512]{1,0:T(8,128)S(1)}) custom-call(s32[3]{0:T(128)S(1)} %pad_add_fusion.place, bf16[128,4096]{1,0:T(8,128)(2,1)S(1)} %get-tuple-element.161.act_low.rest_0_, bf16[128,4096]{1,0:T(8,128)(2,1)S(1)} %copy-done.2, bf16[256,4096]{1,0:T(8,128)(2,1)} %maximum_select_fusion.act_own.rest_2_, ...), custom_call_target="tpu_custom_call" | custom-call | tf_op jit(solution)/shard_map/partial/pallas_call | solution.py:40
  109.7 3.0 %collective-permute-start.26 = (bf16[256,512]{1,0:T(8,128)(2,1)S(1)}, bf16[256,512]{1,0:T(8,128)(2,1)S(1)}, u32[]{:S(2)}, u32[]{:S(2)}) collective-permute-start(bf16[256,512]{1,0:T(8,128)(2,1)S(1)} %get-tuple-element.108), channel_id=1, source_target_pairs={{0,8},{4,12},{8,0},{12,4},{1,9},{5,13},{9,1},{13,5},{2,10},{6,14},... | collective-permute-start | bytes 786440 | tf_op jit(solution)/shard_map/ppermute | solution.py:24
  112.7 4.7 %partial.5 = (bf16[256,512]{1,0:T(8,128)(2,1)S(1)}, f32[256,512]{1,0:T(8,128)S(1)}) custom-call(s32[3]{0:T(128)S(1)} %pad_add_fusion.place, bf16[128,4096]{1,0:T(8,128)(2,1)S(1)} %get-tuple-element.161.act_low.rest_0_, bf16[128,4096]{1,0:T(8,128)(2,1)S(1)} %copy-done.2, bf16[256,4096]{1,0:T(8,128)(2,1)} %maximum_select_fusion.act_own.rest_2_, ...), custom_call_target="tpu_custom_call" | custom-call | tf_op jit(solution)/shard_map/partial/pallas_call | solution.py:40
  117.5 3.2 %teacher.4.norm = f32[4,256,128]{2,1,0:T(8,128)S(1)} custom-call(s32[3]{0:T(128)S(1)} %pad_add_fusion.place, bf16[256,2048]{1,0:T(8,128)(2,1)S(1)} %bitcast.20, bf16[512,256]{1,0:T(8,128)(2,1)S(1)} %pad_maximum_fusion.3.rest_0_.rest_1_, bf16[512,256]{1,0:T(8,128)(2,1)S(1)} %collective-permute-done.19.rest_1_.rest_2_), custom_call_target="tpu_custom_call" | custom-call | tf_op jit(solution)/shard_map/teacher/pallas_call | solution.py:351
  120.7 5.6 %collective-permute-done.22.came = bf16[576,256]{1,0:T(8,128)(2,1)S(1)} collective-permute-done((bf16[576,256]{1,0:T(8,128)(2,1)S(1)}, bf16[576,256]{1,0:T(8,128)(2,1)S(1)}, u32[]{:S(2)}, u32[]{:S(2)}) %collective-permute-start.22) | collective-permute-done | bytes 294944 | tf_op jit(solution)/shard_map/ppermute | solution.py:24
  126.3 3.0 %teacher.5.norm = f32[4,256,128]{2,1,0:T(8,128)S(1)} custom-call(s32[3]{0:T(128)S(1)} %pad_add_fusion.place, bf16[256,2048]{1,0:T(8,128)(2,1)S(1)} %bitcast.21, bf16[512,256]{1,0:T(8,128)(2,1)S(1)} %pad_maximum_fusion.3.rest_0_.rest_1_, bf16[512,256]{1,0:T(8,128)(2,1)S(1)} %collective-permute-done.19.rest_1_.rest_2_), custom_call_target="tpu_custom_call" | custom-call | tf_op jit(solution)/shard_map/teacher/pallas_call | solution.py:351
  129.4 1.6 collective-permute-done.26.rest_0_
  131.0 0.5 collective-permute-start.28
  131.5 1.7 %collective-permute-start.23 = (bf16[576,256]{1,0:T(8,128)(2,1)S(1)}, bf16[576,256]{1,0:T(8,128)(2,1)S(1)}, u32[]{:S(2)}, u32[]{:S(2)}) collective-permute-start(bf16[576,256]{1,0:T(8,128)(2,1)S(1)} %combine.1.rest_0_.rest_3_), channel_id=1, source_target_pairs={{0,4},{4,0},{8,12},{12,8},{1,5},{5,1},{9,13},{13,9},{2,6},{6,2},{1... | collective-permute-start | bytes 884744 | tf_op jit(solution)/shard_map/ppermute | solution.py:24
  133.2 0.4 collective-permute-done.27.rest_6_
  133.6 1.5 collective-permute-done.28.rest_7_
  135.1 1.0 copy-done.19
  136.1 4.7 %partial.6 = (bf16[256,512]{1,0:T(8,128)(2,1)}, f32[256,512]{1,0:T(8,128)S(1)}) custom-call(s32[3]{0:T(128)S(1)} %pad_add_fusion.place, bf16[128,4096]{1,0:T(8,128)(2,1)S(1)} %get-tuple-element.161.act_low.rest_0_, bf16[128,4096]{1,0:T(8,128)(2,1)S(1)} %copy-done.2, bf16[256,4096]{1,0:T(8,128)(2,1)} %maximum_select_fusion.act_own.rest_2_, ...), custom_call_target="tpu_custom_call" | custom-call | tf_op jit(solution)/shard_map/partial/pallas_call | solution.py:40
  140.8 0.8 copy-done.9
  141.6 3.0 %teacher.6.norm = f32[4,256,128]{2,1,0:T(8,128)S(1)} custom-call(s32[3]{0:T(128)S(1)} %pad_add_fusion.place, bf16[256,2048]{1,0:T(8,128)(2,1)S(1)} %bitcast.22, bf16[512,256]{1,0:T(8,128)(2,1)S(1)} %pad_maximum_fusion.3.rest_0_.rest_1_, bf16[512,256]{1,0:T(8,128)(2,1)S(1)} %collective-permute-done.19.rest_1_.rest_2_), custom_call_target="tpu_custom_call" | custom-call | tf_op jit(solution)/shard_map/teacher/pallas_call | solution.py:351
  144.7 0.2 collective-permute-done.24.rest_0_
  144.9 4.8 %partial.7 = (bf16[256,512]{1,0:T(8,128)(2,1)}, f32[256,512]{1,0:T(8,128)S(1)}) custom-call(s32[3]{0:T(128)S(1)} %pad_add_fusion.place, bf16[128,4096]{1,0:T(8,128)(2,1)S(1)} %get-tuple-element.161.act_low.rest_0_, bf16[128,4096]{1,0:T(8,128)(2,1)S(1)} %copy-done.2, bf16[256,4096]{1,0:T(8,128)(2,1)} %maximum_select_fusion.act_own.rest_2_, ...), custom_call_target="tpu_custom_call" | custom-call | tf_op jit(solution)/shard_map/partial/pallas_call | solution.py:40
  149.7 0.8 copy-done.11
  150.5 2.4 %collective-permute-start.30 = (bf16[256,512]{1,0:T(8,128)(2,1)}, bf16[256,512]{1,0:T(8,128)(2,1)}, u32[]{:S(2)}, u32[]{:S(2)}) collective-permute-start(bf16[256,512]{1,0:T(8,128)(2,1)} %get-tuple-element.134), channel_id=1, source_target_pairs={{0,8},{4,12},{8,0},{12,4},{1,9},{5,13},{9,1},{13,5},{2,10},{6,14},... | collective-permute-start | bytes 786440 | tf_op jit(solution)/shard_map/ppermute | solution.py:24
  153.0 3.0 %teacher.7.norm = f32[4,256,128]{2,1,0:T(8,128)S(1)} custom-call(s32[3]{0:T(128)S(1)} %pad_add_fusion.place, bf16[256,2048]{1,0:T(8,128)(2,1)S(1)} %bitcast.23, bf16[512,256]{1,0:T(8,128)(2,1)S(1)} %pad_maximum_fusion.3.rest_0_.rest_1_, bf16[512,256]{1,0:T(8,128)(2,1)S(1)} %collective-permute-done.19.rest_1_.rest_2_), custom_call_target="tpu_custom_call" | custom-call | tf_op jit(solution)/shard_map/teacher/pallas_call | solution.py:351
  156.0 1.3 decay.1
  157.3 2.5 %loss.4 = f32[4,1,256]{2,1,0:T(1,128)S(1)} custom-call(s32[3]{0:T(128)S(1)} %pad_add_fusion.place, bf16[256,2048]{1,0:T(8,128)(2,1)S(1)} %bitcast.24, f32[256,512]{1,0:T(8,128)S(1)} %copy-done.6, f32[4,256,128]{2,1,0:T(8,128)S(1)} %teacher.4.norm, f32[16,1024]{1,0:T(8,128)S(1)} %get-tuple-element.139.factor, f32[16,256]{1,0:T(8,128)S(1)} %get-tuple-element.140.log_row, ...), custom_call_target="tpu_custom_call" | custom-call | tf_op jit(solution)/shard_map/loss/pallas_call | solution.py:40
  159.9 2.3 %loss.5 = f32[4,1,256]{2,1,0:T(1,128)S(1)} custom-call(s32[3]{0:T(128)S(1)} %pad_add_fusion.place, bf16[256,2048]{1,0:T(8,128)(2,1)S(1)} %bitcast.25, f32[256,512]{1,0:T(8,128)S(1)} %copy-done.8, f32[4,256,128]{2,1,0:T(8,128)S(1)} %teacher.5.norm, f32[16,1024]{1,0:T(8,128)S(1)} %get-tuple-element.139.factor, f32[16,256]{1,0:T(8,128)S(1)} %get-tuple-element.140.log_row, ...), custom_call_target="tpu_custom_call" | custom-call | tf_op jit(solution)/shard_map/loss/pallas_call | solution.py:40
  162.3 0.3 collective-permute-done.29.rest_0_
  162.6 2.8 %loss.6 = f32[4,1,256]{2,1,0:T(1,128)S(1)} custom-call(s32[3]{0:T(128)S(1)} %pad_add_fusion.place, bf16[256,2048]{1,0:T(8,128)(2,1)S(1)} %bitcast.26, f32[256,512]{1,0:T(8,128)S(1)} %copy-done.10, f32[4,256,128]{2,1,0:T(8,128)S(1)} %copy-done.4, f32[16,1024]{1,0:T(8,128)S(1)} %get-tuple-element.139.factor, f32[16,256]{1,0:T(8,128)S(1)} %get-tuple-element.140.log_row, ...), custom_call_target="tpu_custom_call" | custom-call | tf_op jit(solution)/shard_map/loss/pallas_call | solution.py:40
  165.4 2.4 %collective-permute-done.30.rest_0_ = bf16[256,512]{1,0:T(8,128)(2,1)} collective-permute-done((bf16[256,512]{1,0:T(8,128)(2,1)}, bf16[256,512]{1,0:T(8,128)(2,1)}, u32[]{:S(2)}, u32[]{:S(2)}) %collective-permute-start.30) | collective-permute-done | bytes 262176 | tf_op jit(solution)/shard_map/ppermute | solution.py:24
  167.8 2.8 %loss.7 = f32[4,1,256]{2,1,0:T(1,128)S(1)} custom-call(s32[3]{0:T(128)S(1)} %pad_add_fusion.place, bf16[256,2048]{1,0:T(8,128)(2,1)S(1)} %bitcast.27, f32[256,512]{1,0:T(8,128)S(1)} %copy-done.12, f32[4,256,128]{2,1,0:T(8,128)S(1)} %teacher.7.norm, f32[16,1024]{1,0:T(8,128)S(1)} %get-tuple-element.139.factor, f32[16,256]{1,0:T(8,128)S(1)} %get-tuple-element.140.log_row, ...), custom_call_target="tpu_custom_call" | custom-call | tf_op jit(solution)/shard_map/loss/pallas_call | solution.py:40
  170.6 0.6 copy.9
  (82 shorter events, 0.8 us)
Async XLA Ops:
  0.0 54.2 %copy-start = (bf16[1,256,512]{2,1,0:T(8,128)(2,1)S(1)}, bf16[1,256,512]{2,1,0:T(8,128)(2,1)}, u32[]{:S(2)}) copy-start(bf16[1,256,512]{2,1,0:T(8,128)(2,1)} %param.9) | copy-start | bytes 786436
  2.7 14.8 %collective-permute-start.3 = (bf16[64,4096]{1,0:T(8,128)(2,1)S(1)}, bf16[64,4096]{1,0:T(8,128)(2,1)S(1)}, u32[]{:S(2)}, u32[]{:S(2)}) collective-permute-start(bf16[64,4096]{1,0:T(8,128)(2,1)S(1)} %get-tuple-element.153), channel_id=1, source_target_pairs={{0,2},{2,0},{1,3},{3,1},{4,6},{6,4},{5,7},{7,5},{8,10},{10,8},{9,1... | collective-permute-start | bytes 1572872 | tf_op jit(solution)/shard_map/ppermute | solution.py:24
  4.2 2.1 %dynamic-slice-start = ((bf16[2048,512]{1,0:T(8,128)(2,1)}, s32[]{:T(128)}, s32[]{:T(128)}), bf16[512,256]{1,0:T(8,128)(2,1)S(1)}, s32[]{:S(2)}) async-start(bf16[2048,512]{1,0:T(8,128)(2,1)} %param.11, s32[]{:T(128)} %select_n.62, s32[]{:T(128)} %select_n.66), calls=%async_computation | async-start | bytes 524800 | tf_op jit(solution)/shard_map/dynamic_slice | solution.py:327
  6.4 25.1 %collective-permute-start.5 = (bf16[512,768]{1,0:T(8,128)(2,1)S(1)}, bf16[512,768]{1,0:T(8,128)(2,1)S(1)}, u32[]{:S(2)}, u32[]{:S(2)}) collective-permute-start(bf16[512,768]{1,0:T(8,128)(2,1)S(1)} %pad_maximum_fusion.2), channel_id=1, source_target_pairs={{0,4},{4,0},{8,12},{12,8},{1,5},{5,1},{9,13},{13,9},{2,6},{6,2},{1... | collective-permute-start | bytes 2359304 | tf_op jit(solution)/shard_map/ppermute | solution.py:24
  6.9 20.8 %collective-permute-start.2 = (bf16[64,4096]{1,0:T(8,128)(2,1)}, bf16[64,4096]{1,0:T(8,128)(2,1)}, u32[]{:S(2)}, u32[]{:S(2)}) collective-permute-start(bf16[64,4096]{1,0:T(8,128)(2,1)} %get-tuple-element.154), channel_id=1, source_target_pairs={{0,2},{2,0},{1,3},{3,1},{4,6},{6,4},{5,7},{7,5},{8,10},{10,8},{9,1... | collective-permute-start | bytes 1572872 | tf_op jit(solution)/shard_map/ppermute | solution.py:24
  7.4 28.8 %collective-permute-start.9 = (bf16[64,4096]{1,0:T(8,128)(2,1)}, bf16[64,4096]{1,0:T(8,128)(2,1)}, u32[]{:S(2)}, u32[]{:S(2)}) collective-permute-start(bf16[64,4096]{1,0:T(8,128)(2,1)} %get-tuple-element.91), channel_id=1, source_target_pairs={{2,10},{6,14},{8,0},{12,4},{3,11},{7,15},{9,1},{13,5},{18,26},{22,... | collective-permute-start | bytes 1572872 | tf_op jit(solution)/shard_map/ppermute | solution.py:379
  17.6 20.3 %copy-start.21 = (bf16[64,4096]{1,0:T(8,128)(2,1)}, bf16[64,4096]{1,0:T(8,128)(2,1)S(1)}, u32[]{:S(2)}) copy-start(bf16[64,4096]{1,0:T(8,128)(2,1)S(1)} %collective-permute-done.3) | copy-start | bytes 1572868
  17.6 25.9 %collective-permute-start.10 = (bf16[64,4096]{1,0:T(8,128)(2,1)S(1)}, bf16[64,4096]{1,0:T(8,128)(2,1)}, u32[]{:S(2)}, u32[]{:S(2)}) collective-permute-start(bf16[64,4096]{1,0:T(8,128)(2,1)S(1)} %collective-permute-done.3), channel_id=1, source_target_pairs={{0,8},{4,12},{10,2},{14,6},{1,9},{5,13},{11,3},{15,7},{16,24},{20,... | collective-permute-start | bytes 1572872 | tf_op jit(solution)/shard_map/ppermute | solution.py:379
  18.8 41.1 %collective-permute-start.12 = (bf16[512,512]{1,0:T(8,128)(2,1)}, bf16[512,512]{1,0:T(8,128)(2,1)S(1)}, u32[]{:S(2)}, u32[]{:S(2)}) collective-permute-start(bf16[512,512]{1,0:T(8,128)(2,1)} %get-tuple-element.152), channel_id=1, source_target_pairs={{0,4},{4,0},{8,12},{12,8},{1,5},{5,1},{9,13},{13,9},{2,6},{6,2},{1... | collective-permute-start | bytes 1572872 | tf_op jit(solution)/shard_map/ppermute | solution.py:24
  19.4 36.2 %copy-start.20 = (bf16[2048,512]{1,0:T(8,128)(2,1)S(1)}, bf16[2048,512]{1,0:T(8,128)(2,1)}, u32[]{:S(2)}) copy-start(bf16[2048,512]{1,0:T(8,128)(2,1)} %param.11) | copy-start | bytes 6291460
  27.7 38.8 %collective-permute-start.1 = (bf16[64,4096]{1,0:T(8,128)(2,1)}, bf16[64,4096]{1,0:T(8,128)(2,1)S(1)}, u32[]{:S(2)}, u32[]{:S(2)}) collective-permute-start(bf16[64,4096]{1,0:T(8,128)(2,1)} %get-tuple-element.93), channel_id=1, source_target_pairs={{2,10},{6,14},{8,0},{12,4},{3,11},{7,15},{9,1},{13,5},{18,26},{22,... | collective-permute-start | bytes 1572872 | tf_op jit(solution)/shard_map/ppermute | solution.py:379
  31.5 27.2 %collective-permute-start.16 = (bf16[64,4096]{1,0:T(8,128)(2,1)}, bf16[64,4096]{1,0:T(8,128)(2,1)S(1)}, u32[]{:S(2)}, u32[]{:S(2)}) collective-permute-start(bf16[64,4096]{1,0:T(8,128)(2,1)} %get-tuple-element.91), channel_id=1, source_target_pairs={{0,2},{4,6},{10,8},{14,12},{1,3},{5,7},{11,9},{15,13},{16,18},{20,... | collective-permute-start | bytes 1572872 | tf_op jit(solution)/shard_map/ppermute | solution.py:381
  36.3 22.4 %collective-permute-start.6 = (bf16[512,768]{1,0:T(8,128)(2,1)S(1)}, bf16[512,768]{1,0:T(8,128)(2,1)S(1)}, u32[]{:S(2)}, u32[]{:S(2)}) collective-permute-start(bf16[512,768]{1,0:T(8,128)(2,1)S(1)} %collective-permute-done.5.rest_0_.rest_4_), channel_id=1, source_target_pairs={{0,16},{16,0},{1,17},{17,1},{2,18},{18,2},{3,19},{19,3},{4,20},{20... | collective-permute-start | bytes 2359304 | tf_op jit(solution)/shard_map/ppermute | solution.py:24
  44.6 19.7 %collective-permute-start.11 = (bf16[64,4096]{1,0:T(8,128)(2,1)S(1)}, bf16[64,4096]{1,0:T(8,128)(2,1)S(1)}, u32[]{:S(2)}, u32[]{:S(2)}) collective-permute-start(bf16[64,4096]{1,0:T(8,128)(2,1)S(1)} %broadcast_select_fusion.5), channel_id=1, source_target_pairs={{0,2},{2,0},{1,3},{3,1},{4,6},{6,4},{5,7},{7,5},{8,10},{10,8},{9,1... | collective-permute-start | bytes 1572872 | tf_op jit(solution)/shard_map/ppermute | solution.py:24
  55.5 8.8 %copy-start.17 = (bf16[2048,16]{0,1:T(8,128)(2,1)S(1)}, bf16[2048,16]{0,1:T(8,128)(2,1)}, u32[]{:S(2)}) copy-start(bf16[2048,16]{0,1:T(8,128)(2,1)} %param.12) | copy-start | bytes 196612
  55.5 11.0 %copy-start.23 = (bf16[64,4096]{1,0:T(8,128)(2,1)S(1)}, bf16[64,4096]{1,0:T(8,128)(2,1)}, u32[]{:S(2)}) copy-start(bf16[64,4096]{1,0:T(8,128)(2,1)} %get-tuple-element.93) | copy-start | bytes 1572868
  56.6 25.8 %copy-start.18 = (bf16[1,256,4096]{2,1,0:T(8,128)(2,1)S(1)}, bf16[1,256,4096]{2,1,0:T(8,128)(2,1)}, u32[]{:S(2)}) copy-start(bf16[1,256,4096]{2,1,0:T(8,128)(2,1)} %param.7) | copy-start | bytes 6291460
  56.6 25.8 %copy-start.22 = (bf16[64,4096]{1,0:T(8,128)(2,1)S(1)}, bf16[64,4096]{1,0:T(8,128)(2,1)}, u32[]{:S(2)}) copy-start(bf16[64,4096]{1,0:T(8,128)(2,1)} %copy-done.21) | copy-start | bytes 1572868
  58.7 31.5 %collective-permute-start.15 = (bf16[256,256]{1,0:T(8,128)(2,1)S(1)}, bf16[256,256]{1,0:T(8,128)(2,1)S(1)}, u32[]{:S(2)}, u32[]{:S(2)}) collective-permute-start(bf16[256,256]{1,0:T(8,128)(2,1)S(1)} %dynamic-slice_bitcast_fusion), channel_id=1, source_target_pairs={{0,8},{4,12},{8,0},{12,4},{1,9},{5,13},{9,1},{13,5},{2,10},{6,14},... | collective-permute-start | bytes 393224 | tf_op jit(solution)/shard_map/ppermute | solution.py:24
  58.7 21.0 %collective-permute-start.4 = (bf16[64,4096]{1,0:T(8,128)(2,1)}, bf16[64,4096]{1,0:T(8,128)(2,1)S(1)}, u32[]{:S(2)}, u32[]{:S(2)}) collective-permute-start(bf16[64,4096]{1,0:T(8,128)(2,1)} %collective-permute-done.2), channel_id=1, source_target_pairs={{0,8},{4,12},{10,2},{14,6},{1,9},{5,13},{11,3},{15,7},{16,24},{20,... | collective-permute-start | bytes 1572872 | tf_op jit(solution)/shard_map/ppermute | solution.py:379
  60.0 4.4 %collective-permute-start.7 = (bf16[512,768]{1,0:T(8,128)(2,1)S(1)}, bf16[512,768]{1,0:T(8,128)(2,1)S(1)}, u32[]{:S(2)}, u32[]{:S(2)}) collective-permute-start(bf16[512,768]{1,0:T(8,128)(2,1)S(1)} %collective-permute-done.5.rest_0_.rest_4_), channel_id=1, source_target_pairs={{0,1},{1,0},{2,3},{3,2},{4,5},{5,4},{6,7},{7,6},{8,9},{9,8},{10,11... | collective-permute-start | bytes 2359304 | tf_op jit(solution)/shard_map/ppermute | solution.py:24
  64.3 2.3 %collective-permute-start.8 = (bf16[512,768]{1,0:T(8,128)(2,1)S(1)}, bf16[512,768]{1,0:T(8,128)(2,1)S(1)}, u32[]{:S(2)}, u32[]{:S(2)}) collective-permute-start(bf16[512,768]{1,0:T(8,128)(2,1)S(1)} %collective-permute-done.6.rest_1_.rest_5_), channel_id=1, source_target_pairs={{0,1},{1,0},{2,3},{3,2},{4,5},{5,4},{6,7},{7,6},{8,9},{9,8},{10,11... | collective-permute-start | bytes 2359304 | tf_op jit(solution)/shard_map/ppermute | solution.py:24
  64.4 25.8 %collective-permute-start.14 = (bf16[16,2048]{1,0:T(8,128)(2,1)S(1)}, bf16[16,2048]{1,0:T(8,128)(2,1)S(1)}, u32[]{:S(2)}, u32[]{:S(2)}) collective-permute-start(bf16[16,2048]{1,0:T(8,128)(2,1)S(1)} %bitcast.28), channel_id=1, source_target_pairs={{0,4},{4,0},{8,12},{12,8},{1,5},{5,1},{9,13},{13,9},{2,6},{6,2},{1... | collective-permute-start | bytes 196616 | tf_op jit(solution)/shard_map/ppermute | solution.py:24
  66.6 34.9 %collective-permute-start = (bf16[512,1024]{1,0:T(8,128)(2,1)S(1)}, bf16[512,1024]{1,0:T(8,128)(2,1)S(1)}, u32[]{:S(2)}, u32[]{:S(2)}) collective-permute-start(bf16[512,1024]{1,0:T(8,128)(2,1)S(1)} %constant_dynamic-slice_fusion.2), channel_id=1, source_target_pairs={{0,4},{4,0},{8,12},{12,8},{1,5},{5,1},{9,13},{13,9},{2,6},{6,2},{1... | collective-permute-start | bytes 3145736 | tf_op jit(solution)/shard_map/ppermute | solution.py:24
  66.6 15.9 %collective-permute-start.17 = (bf16[64,4096]{1,0:T(8,128)(2,1)S(1)}, bf16[64,4096]{1,0:T(8,128)(2,1)S(1)}, u32[]{:S(2)}, u32[]{:S(2)}) collective-permute-start(bf16[64,4096]{1,0:T(8,128)(2,1)S(1)} %copy-done.23), channel_id=1, source_target_pairs={{0,2},{4,6},{10,8},{14,12},{1,3},{5,7},{11,9},{15,13},{16,18},{20,... | collective-permute-start | bytes 1572872 | tf_op jit(solution)/shard_map/ppermute | solution.py:381
  79.6 10.5 %collective-permute-start.18 = (bf16[512,512]{1,0:T(8,128)(2,1)S(1)}, bf16[512,512]{1,0:T(8,128)(2,1)S(1)}, u32[]{:S(2)}, u32[]{:S(2)}) collective-permute-start(bf16[512,512]{1,0:T(8,128)(2,1)S(1)} %collective-permute-done.12.rest_4_), channel_id=1, source_target_pairs={{0,16},{16,0},{1,17},{17,1},{2,18},{18,2},{3,19},{19,3},{4,20},{20... | collective-permute-start | bytes 1572872 | tf_op jit(solution)/shard_map/ppermute | solution.py:24
  82.4 13.1 %collective-permute-start.13 = (bf16[64,4096]{1,0:T(8,128)(2,1)S(1)}, bf16[64,4096]{1,0:T(8,128)(2,1)S(1)}, u32[]{:S(2)}, u32[]{:S(2)}) collective-permute-start(bf16[64,4096]{1,0:T(8,128)(2,1)S(1)} %broadcast_select_fusion.4), channel_id=1, source_target_pairs={{0,2},{2,0},{1,3},{3,1},{4,6},{6,4},{5,7},{7,5},{8,10},{10,8},{9,1... | collective-permute-start | bytes 1572872 | tf_op jit(solution)/shard_map/ppermute | solution.py:24
  96.9 8.2 %copy-start.2 = (bf16[128,4096]{1,0:T(8,128)(2,1)S(1)}, bf16[128,4096]{1,0:T(8,128)(2,1)}, u32[]{:S(2)}) copy-start(bf16[128,4096]{1,0:T(8,128)(2,1)} %get-tuple-element.162.act_high.rest_1_) | copy-start | bytes 3145732
  101.5 29.5 %collective-permute-start.25 = (bf16[512,1024]{1,0:T(8,128)(2,1)S(1)}, bf16[512,1024]{1,0:T(8,128)(2,1)S(1)}, u32[]{:S(2)}, u32[]{:S(2)}) collective-permute-start(bf16[512,1024]{1,0:T(8,128)(2,1)S(1)} %collective-permute-done.rest_4_), channel_id=1, source_target_pairs={{0,16},{16,0},{1,17},{17,1},{2,18},{18,2},{3,19},{19,3},{4,20},{20... | collective-permute-start | bytes 3145736 | tf_op jit(solution)/shard_map/ppermute | solution.py:24
  103.1 6.6 %collective-permute-start.20 = (bf16[512,512]{1,0:T(8,128)(2,1)S(1)}, bf16[512,512]{1,0:T(8,128)(2,1)S(1)}, u32[]{:S(2)}, u32[]{:S(2)}) collective-permute-start(bf16[512,512]{1,0:T(8,128)(2,1)S(1)} %collective-permute-done.12.rest_4_), channel_id=1, source_target_pairs={{0,1},{1,0},{2,3},{3,2},{4,5},{5,4},{6,7},{7,6},{8,9},{9,8},{10,11... | collective-permute-start | bytes 1572872 | tf_op jit(solution)/shard_map/ppermute | solution.py:24
  103.1 9.6 %collective-permute-start.21 = (bf16[512,512]{1,0:T(8,128)(2,1)S(1)}, bf16[512,512]{1,0:T(8,128)(2,1)S(1)}, u32[]{:S(2)}, u32[]{:S(2)}) collective-permute-start(bf16[512,512]{1,0:T(8,128)(2,1)S(1)} %collective-permute-done.18.rest_5_), channel_id=1, source_target_pairs={{0,1},{1,0},{2,3},{3,2},{4,5},{5,4},{6,7},{7,6},{8,9},{9,8},{10,11... | collective-permute-start | bytes 1572872 | tf_op jit(solution)/shard_map/ppermute | solution.py:24
  103.6 22.7 %collective-permute-start.22 = (bf16[576,256]{1,0:T(8,128)(2,1)S(1)}, bf16[576,256]{1,0:T(8,128)(2,1)S(1)}, u32[]{:S(2)}, u32[]{:S(2)}) collective-permute-start(bf16[576,256]{1,0:T(8,128)(2,1)S(1)} %get-tuple-element.104), channel_id=1, source_target_pairs={{0,8},{4,12},{8,0},{12,4},{1,9},{5,13},{9,1},{13,5},{2,10},{6,14},... | collective-permute-start | bytes 884744 | tf_op jit(solution)/shard_map/ppermute | solution.py:24
  103.6 13.9 %collective-permute-start.19 = (bf16[512,256]{1,0:T(8,128)(2,1)S(1)}, bf16[512,256]{1,0:T(8,128)(2,1)S(1)}, u32[]{:S(2)}, u32[]{:S(2)}) collective-permute-start(bf16[512,256]{1,0:T(8,128)(2,1)S(1)} %pad_maximum_fusion.3.rest_0_.rest_1_), channel_id=1, source_target_pairs={{0,4},{4,0},{8,12},{12,8},{1,5},{5,1},{9,13},{13,9},{2,6},{6,2},{1... | collective-permute-start | bytes 786440 | tf_op jit(solution)/shard_map/ppermute | solution.py:24
  109.7 7.8 %copy-start.5 = (f32[256,512]{1,0:T(8,128)}, f32[256,512]{1,0:T(8,128)S(1)}, u32[]{:S(2)}) copy-start(f32[256,512]{1,0:T(8,128)S(1)} %get-tuple-element.107.kept) | copy-start | bytes 1572868
  109.7 21.2 %collective-permute-start.26 = (bf16[256,512]{1,0:T(8,128)(2,1)S(1)}, bf16[256,512]{1,0:T(8,128)(2,1)S(1)}, u32[]{:S(2)}, u32[]{:S(2)}) collective-permute-start(bf16[256,512]{1,0:T(8,128)(2,1)S(1)} %get-tuple-element.108), channel_id=1, source_target_pairs={{0,8},{4,12},{8,0},{12,4},{1,9},{5,13},{9,1},{13,5},{2,10},{6,14},... | collective-permute-start | bytes 786440 | tf_op jit(solution)/shard_map/ppermute | solution.py:24
  112.7 4.8 %copy-start.1 = (bf16[1,256,2048]{2,1,0:T(8,128)(2,1)S(1)}, bf16[1,256,2048]{2,1,0:T(8,128)(2,1)}, u32[]{:S(2)}) copy-start(bf16[1,256,2048]{2,1,0:T(8,128)(2,1)} %param.8) | copy-start | bytes 3145732
  117.5 11.9 %copy-start.7 = (f32[256,512]{1,0:T(8,128)}, f32[256,512]{1,0:T(8,128)S(1)}, u32[]{:S(2)}) copy-start(f32[256,512]{1,0:T(8,128)S(1)} %get-tuple-element.115.kept) | copy-start | bytes 1572868
  130.9 9.9 %copy-start.13 = (bf16[256,512]{1,0:T(8,128)(2,1)}, bf16[256,512]{1,0:T(8,128)(2,1)S(1)}, u32[]{:S(2)}) copy-start(bf16[256,512]{1,0:T(8,128)(2,1)S(1)} %collective-permute-done.26.rest_0_) | copy-start | bytes 786436
  131.0 2.7 %collective-permute-start.27 = (bf16[512,1024]{1,0:T(8,128)(2,1)S(1)}, bf16[512,1024]{1,0:T(8,128)(2,1)S(1)}, u32[]{:S(2)}, u32[]{:S(2)}) collective-permute-start(bf16[512,1024]{1,0:T(8,128)(2,1)S(1)} %collective-permute-done.rest_4_), channel_id=1, source_target_pairs={{0,1},{1,0},{2,3},{3,2},{4,5},{5,4},{6,7},{7,6},{8,9},{9,8},{10,11... | collective-permute-start | bytes 3145736 | tf_op jit(solution)/shard_map/ppermute | solution.py:24
  131.0 4.2 %collective-permute-start.28 = (bf16[512,1024]{1,0:T(8,128)(2,1)S(1)}, bf16[512,1024]{1,0:T(8,128)(2,1)S(1)}, u32[]{:S(2)}, u32[]{:S(2)}) collective-permute-start(bf16[512,1024]{1,0:T(8,128)(2,1)S(1)} %collective-permute-done.25.rest_5_), channel_id=1, source_target_pairs={{0,1},{1,0},{2,3},{3,2},{4,5},{5,4},{6,7},{7,6},{8,9},{9,8},{10,11... | collective-permute-start | bytes 3145736 | tf_op jit(solution)/shard_map/ppermute | solution.py:24
  131.5 13.4 %collective-permute-start.24 = (bf16[256,512]{1,0:T(8,128)(2,1)S(1)}, bf16[256,512]{1,0:T(8,128)(2,1)S(1)}, u32[]{:S(2)}, u32[]{:S(2)}) collective-permute-start(bf16[256,512]{1,0:T(8,128)(2,1)S(1)} %get-tuple-element.114), channel_id=1, source_target_pairs={{0,8},{4,12},{8,0},{12,4},{1,9},{5,13},{9,1},{13,5},{2,10},{6,14},... | collective-permute-start | bytes 786440 | tf_op jit(solution)/shard_map/ppermute | solution.py:24
  131.5 24.6 %collective-permute-start.23 = (bf16[576,256]{1,0:T(8,128)(2,1)S(1)}, bf16[576,256]{1,0:T(8,128)(2,1)S(1)}, u32[]{:S(2)}, u32[]{:S(2)}) collective-permute-start(bf16[576,256]{1,0:T(8,128)(2,1)S(1)} %combine.1.rest_0_.rest_3_), channel_id=1, source_target_pairs={{0,4},{4,0},{8,12},{12,8},{1,5},{5,1},{9,13},{13,9},{2,6},{6,2},{1... | collective-permute-start | bytes 884744 | tf_op jit(solution)/shard_map/ppermute | solution.py:24
  135.1 1.0 copy-start.19
  140.8 0.8 copy-start.9
  141.6 20.9 %collective-permute-start.29 = (bf16[256,512]{1,0:T(8,128)(2,1)}, bf16[256,512]{1,0:T(8,128)(2,1)}, u32[]{:S(2)}, u32[]{:S(2)}) collective-permute-start(bf16[256,512]{1,0:T(8,128)(2,1)} %get-tuple-element.129), channel_id=1, source_target_pairs={{0,8},{4,12},{8,0},{12,4},{1,9},{5,13},{9,1},{13,5},{2,10},{6,14},... | collective-permute-start | bytes 786440 | tf_op jit(solution)/shard_map/ppermute | solution.py:24
  144.7 5.1 %copy-start.3 = (f32[4,256,128]{2,1,0:T(8,128)}, f32[4,256,128]{2,1,0:T(8,128)S(1)}, u32[]{:S(2)}) copy-start(f32[4,256,128]{2,1,0:T(8,128)S(1)} %teacher.6.norm) | copy-start | bytes 1572868
  144.7 8.2 %copy-start.24 = (f32[16]{0:T(128)S(1)}, f32[16]{0:T(128)}, u32[]{:S(2)}) copy-start(f32[16]{0:T(128)} %param.13) | copy-start | bytes 196
  144.9 4.8 %copy-start.15 = (bf16[256,512]{1,0:T(8,128)(2,1)}, bf16[256,512]{1,0:T(8,128)(2,1)S(1)}, u32[]{:S(2)}) copy-start(bf16[256,512]{1,0:T(8,128)(2,1)S(1)} %collective-permute-done.24.rest_0_) | copy-start | bytes 786436
  149.7 0.8 copy-start.11
  150.5 17.3 %collective-permute-start.30 = (bf16[256,512]{1,0:T(8,128)(2,1)}, bf16[256,512]{1,0:T(8,128)(2,1)}, u32[]{:S(2)}, u32[]{:S(2)}) collective-permute-start(bf16[256,512]{1,0:T(8,128)(2,1)} %get-tuple-element.134), channel_id=1, source_target_pairs={{0,8},{4,12},{8,0},{12,4},{1,9},{5,13},{9,1},{13,5},{2,10},{6,14},... | collective-permute-start | bytes 786440 | tf_op jit(solution)/shard_map/ppermute | solution.py:24
  153.0 4.3 %copy-start.6 = (f32[256,512]{1,0:T(8,128)S(1)}, f32[256,512]{1,0:T(8,128)}, u32[]{:S(2)}) copy-start(f32[256,512]{1,0:T(8,128)} %copy-done.5) | copy-start | bytes 1572868
  153.0 4.3 %copy-start.14 = (bf16[256,512]{1,0:T(8,128)(2,1)S(1)}, bf16[256,512]{1,0:T(8,128)(2,1)}, u32[]{:S(2)}) copy-start(bf16[256,512]{1,0:T(8,128)(2,1)} %copy-done.13) | copy-start | bytes 786436
  156.0 3.9 %copy-start.8 = (f32[256,512]{1,0:T(8,128)S(1)}, f32[256,512]{1,0:T(8,128)}, u32[]{:S(2)}) copy-start(f32[256,512]{1,0:T(8,128)} %copy-done.7) | copy-start | bytes 1572868
  156.0 3.9 %copy-start.16 = (bf16[256,512]{1,0:T(8,128)(2,1)S(1)}, bf16[256,512]{1,0:T(8,128)(2,1)}, u32[]{:S(2)}) copy-start(bf16[256,512]{1,0:T(8,128)(2,1)} %copy-done.15) | copy-start | bytes 786436
  159.9 2.7 %copy-start.4 = (f32[4,256,128]{2,1,0:T(8,128)S(1)}, f32[4,256,128]{2,1,0:T(8,128)}, u32[]{:S(2)}) copy-start(f32[4,256,128]{2,1,0:T(8,128)} %copy-done.3) | copy-start | bytes 1572868
  159.9 2.7 %copy-start.10 = (f32[256,512]{1,0:T(8,128)S(1)}, f32[256,512]{1,0:T(8,128)}, u32[]{:S(2)}) copy-start(f32[256,512]{1,0:T(8,128)} %copy-done.9) | copy-start | bytes 1572868
  162.3 5.6 %copy-start.12 = (f32[256,512]{1,0:T(8,128)S(1)}, f32[256,512]{1,0:T(8,128)}, u32[]{:S(2)}) copy-start(f32[256,512]{1,0:T(8,128)} %copy-done.11) | copy-start | bytes 1572868
